TPU v7x, 32 devices: a whole 2x2x4 slice. The times are simulated.
32 devices in a mesh: dp: 8 (over z, y), tensor: 4 (over x, core).
Axes of the slice: x: 2, y: 2, z: 4, core: 2. Of those that a mesh axis runs over, the one named last changes fastest.
Arguments:
- tokens: bfloat16 [18688, 1024], P(('dp', 'tensor')), may hold values from -6 to 6
- cotangent: bfloat16 [18688, 1024], P(('dp', 'tensor')), may hold values from -6 to 6
- image_mask: int32 [32], P('dp'), may hold values 0 or 1
- norm_gains: bfloat16 [2, 1024], P(None, 'dp'), may hold values from 0.25 to 1.75
- norm_shifts: bfloat16 [4, 1024], P(None, 'dp'), may hold values from -1.796875 to 1.796875
- w_qkv: bfloat16 [3, 1024, 1024], P(None, 'dp', 'tensor'), may hold values from -0.25 to 0.25
- b_qv: bfloat16 [2, 1024], P(None, ('tensor', 'dp')), may hold values from -3 to 3
- w_out: bfloat16 [1024, 1024], P('tensor', 'dp'), may hold values from -0.4375 to 0.4375
- w_up: bfloat16 [1024, 4096], P('dp', 'tensor'), may hold values from -0.1875 to 0.1875
- up_bias: bfloat16 [4096], P(('tensor', 'dp')), may hold values from -3 to 3
- w_down: bfloat16 [4096, 1024], P('tensor', 'dp'), may hold values from -0.125 to 0.125
Outputs:
- layer_out: bfloat16 [18688, 1024], P(('dp', 'tensor'))
- grad_tokens: bfloat16 [18688, 1024], P(('dp', 'tensor'))
- grad_norm_gains: float32 [2, 1024], P(None, ('dp', 'tensor'))
- grad_norm_shifts: float32 [4, 1024], P(None, ('dp', 'tensor'))
- grad_w_qkv: float32 [3, 1024, 1024], P(None, 'dp', 'tensor')
- grad_b_qv: float32 [2, 1024], P(None, ('tensor', 'dp'))
- grad_w_out: float32 [1024, 1024], P('tensor', 'dp')
- grad_w_up: float32 [1024, 4096], P('dp', 'tensor')
- grad_up_bias: float32 [4096], P(('tensor', 'dp'))
- grad_w_down: float32 [4096, 1024], P('tensor', 'dp')
All inputs are finite; a program needn't handle non-finite values. No bound on the sum of `image_mask` on one device may be relied on, other than what follows from the above.
Results may differ from a plain program's by a relative error of at most 0.02.
Values may be sent and summed in bfloat16 or wider, within the bound.
No kernel may reach another device: no remote copies, remote signals or barrier semaphores. Data moves between devices by JAX's collectives and lax.ppermute only.
A program may use at most 320 MiB of HBM per device.

v0:
```python
import jax
import jax.numpy as jnp
from jax import lax
from jax.sharding import PartitionSpec as P

HEAD_DIM = 64
VALID = 577
SEQ = 584


def layer_norm(rows_in, gain_row, shift_row):
    center = rows_in - jnp.mean(rows_in, axis=1, keepdims=True)
    inverse = lax.rsqrt(jnp.mean(center * center, axis=1, keepdims=True) + 1e-05)
    scaled = center * inverse
    return (scaled, inverse, scaled * gain_row + shift_row)


def norm_back(grad_norm, scaled, inverse, gain_row):
    grad_hat = grad_norm * gain_row
    first_mean = jnp.mean(grad_hat, axis=1, keepdims=True)
    second_mean = jnp.mean(grad_hat * scaled, axis=1, keepdims=True)
    return inverse * (grad_hat - first_mean - scaled * second_mean)


def per_device(
    tokens,
    cotangent,
    image_mask,
    norm_gains,
    norm_shifts,
    w_qkv,
    b_qv,
    w_out,
    w_up,
    up_bias,
    w_down,
):
    tensor_pos = lax.axis_index("tensor")
    local_rows = tokens.shape[0]
    images_dp = image_mask.shape[0]
    score_scale = HEAD_DIM ** (-0.5)
    qkv_full, out_full, bias_full, gains_full, shifts_full = (
        lax.all_gather(w_qkv, "dp", axis=1, tiled=True),
        lax.all_gather(w_out, "dp", axis=1, tiled=True),
        lax.all_gather(b_qv, "dp", axis=1, tiled=True),
        lax.all_gather(norm_gains, "dp", axis=1, tiled=True),
        lax.all_gather(norm_shifts, "dp", axis=1, tiled=True),
    )
    up_full, down_full, cup_full = (
        lax.all_gather(w_up, "dp", axis=0, tiled=True),
        lax.all_gather(w_down, "dp", axis=1, tiled=True),
        lax.all_gather(up_bias, "dp", axis=0, tiled=True),
    )
    gains = gains_full.astype(jnp.float32)
    shifts = shifts_full.astype(jnp.float32)
    width_here = qkv_full.shape[2]
    heads_here = width_here // HEAD_DIM
    owner_image = (tensor_pos * local_rows + lax.iota(jnp.int32, local_rows)) // SEQ
    row_keep = jnp.sum(
        jnp.where(
            owner_image[:, None] == lax.iota(jnp.int32, images_dp)[None, :], image_mask[None, :], 0
        ),
        axis=1,
    ).astype(jnp.float32)[:, None]
    rows_in = tokens.astype(jnp.float32)
    hat_one, inv_one, normed_one = layer_norm(rows_in, gains[0], shifts[0])
    low_one = normed_one.astype(jnp.bfloat16)
    full_one = lax.all_gather(low_one, "tensor", axis=0, tiled=True)
    work_rows = full_one.shape[0]
    head_shape = (work_rows // SEQ, SEQ, heads_here, HEAD_DIM)
    projected = jnp.einsum("rd,cde->cre", full_one, qkv_full, preferred_element_type=jnp.float32)
    bias_wide = bias_full.astype(jnp.float32)
    queries = (projected[0] + bias_wide[0]).astype(jnp.bfloat16).reshape(head_shape)
    keys_all = projected[1].astype(jnp.bfloat16).reshape(head_shape)
    values = (projected[2] + bias_wide[1]).astype(jnp.bfloat16).reshape(head_shape)
    valid_keys = lax.iota(jnp.int32, SEQ) < VALID

    def scores_of(query_blk, key_blk):
        raw_scores = (
            jnp.einsum("qhd,khd->hqk", query_blk, key_blk, preferred_element_type=jnp.float32)
            * score_scale
        )
        return jnp.where(valid_keys[None, None, :], raw_scores, -1e30)

    def attend(blocks):
        query_blk, key_blk, value_blk = blocks
        scores = scores_of(query_blk, key_blk)
        row_max = jnp.max(scores, axis=2, keepdims=True)
        exponent = jnp.exp(scores - row_max)
        row_total = jnp.sum(exponent, axis=2, keepdims=True)
        attn_probs = (exponent / row_total).astype(jnp.bfloat16)
        result = jnp.einsum(
            "hqk,khd->qhd", attn_probs, value_blk, preferred_element_type=jnp.float32
        )
        return (result.astype(jnp.bfloat16), (row_max + jnp.log(row_total))[:, :, 0])

    attended, log_total = lax.map(attend, (queries, keys_all, values))
    flat_out = attended.reshape(work_rows, width_here)
    attn_part = jnp.dot(flat_out, out_full, preferred_element_type=jnp.float32)
    attn_sum = lax.psum_scatter(
        attn_part.astype(jnp.bfloat16), "tensor", scatter_dimension=0, tiled=True
    ).astype(jnp.float32)
    middle = rows_in + row_keep * (attn_sum + shifts[2])
    hat_two, inv_two, normed_two = layer_norm(middle, gains[1], shifts[1])
    low_two = normed_two.astype(jnp.bfloat16)
    full_two = lax.all_gather(low_two, "tensor", axis=0, tiled=True)
    hidden_pre = jnp.dot(full_two, up_full, preferred_element_type=jnp.float32) + cup_full.astype(
        jnp.float32
    )
    gating = jax.nn.sigmoid(1.702 * hidden_pre)
    activated = (hidden_pre * gating).astype(jnp.bfloat16)
    mlp_part = jnp.dot(activated, down_full, preferred_element_type=jnp.float32)
    mlp_sum = lax.psum_scatter(
        mlp_part.astype(jnp.bfloat16), "tensor", scatter_dimension=0, tiled=True
    ).astype(jnp.float32)
    layer_out = (middle + row_keep * (mlp_sum + shifts[3])).astype(jnp.bfloat16)
    grad_top = cotangent.astype(jnp.float32)
    grad_mlp = row_keep * grad_top
    send_mlp = grad_mlp.astype(jnp.bfloat16)
    mlp_grad_full = lax.all_gather(send_mlp, "tensor", axis=0, tiled=True)
    grad_act = jnp.einsum("rd,fd->rf", mlp_grad_full, down_full, preferred_element_type=jnp.float32)
    grad_pre = grad_act * (gating + 1.702 * hidden_pre * gating * (1.0 - gating))
    low_pre = grad_pre.astype(jnp.bfloat16)
    grad_down = jnp.einsum(
        "rf,rd->fd", activated, mlp_grad_full, preferred_element_type=jnp.float32
    )
    grad_up = jnp.einsum("rd,rf->df", full_two, low_pre, preferred_element_type=jnp.float32)
    grad_cup = jnp.sum(grad_pre, axis=0)
    two_part = jnp.einsum("rf,df->rd", low_pre, up_full, preferred_element_type=jnp.float32)
    grad_two = lax.psum_scatter(
        two_part.astype(jnp.bfloat16), "tensor", scatter_dimension=0, tiled=True
    ).astype(jnp.float32)
    grad_mid = grad_top + norm_back(grad_two, hat_two, inv_two, gains[1])
    grad_attn = row_keep * grad_mid
    send_attn = grad_attn.astype(jnp.bfloat16)
    attn_grad_full = lax.all_gather(send_attn, "tensor", axis=0, tiled=True)
    grad_flat = jnp.einsum(
        "rd,ed->re", attn_grad_full, out_full, preferred_element_type=jnp.float32
    ).astype(jnp.bfloat16)
    grad_wout = jnp.einsum(
        "re,rd->ed", flat_out, attn_grad_full, preferred_element_type=jnp.float32
    )
    grad_heads = grad_flat.reshape(head_shape)

    def attend_back(blocks):
        query_blk, key_blk, value_blk, grad_blk, log_blk = blocks
        attn_probs = jnp.exp(scores_of(query_blk, key_blk) - log_blk[:, :, None])
        grad_probs = jnp.einsum(
            "qhd,khd->hqk", grad_blk, value_blk, preferred_element_type=jnp.float32
        )
        row_dot = jnp.sum(attn_probs * grad_probs, axis=2, keepdims=True)
        grad_scores = (attn_probs * (grad_probs - row_dot)).astype(jnp.bfloat16)
        grad_q = (
            jnp.einsum("hqk,khd->qhd", grad_scores, key_blk, preferred_element_type=jnp.float32)
            * score_scale
        )
        grad_k = (
            jnp.einsum("hqk,qhd->khd", grad_scores, query_blk, preferred_element_type=jnp.float32)
            * score_scale
        )
        grad_v = jnp.einsum(
            "hqk,qhd->khd",
            attn_probs.astype(jnp.bfloat16),
            grad_blk,
            preferred_element_type=jnp.float32,
        )
        return (grad_q, grad_k, grad_v)

    grad_q, grad_k, grad_v = lax.map(
        attend_back, (queries, keys_all, values, grad_heads, log_total)
    )
    grad_proj = jnp.stack([grad_q, grad_k, grad_v]).reshape(3, work_rows, width_here)
    grad_bias_qv = jnp.stack([jnp.sum(grad_proj[0], axis=0), jnp.sum(grad_proj[2], axis=0)])
    low_proj = grad_proj.astype(jnp.bfloat16)
    grad_qkv = jnp.einsum("rd,cre->cde", full_one, low_proj, preferred_element_type=jnp.float32)
    one_part = jnp.einsum("cre,cde->rd", low_proj, qkv_full, preferred_element_type=jnp.float32)
    grad_one = lax.psum_scatter(
        one_part.astype(jnp.bfloat16), "tensor", scatter_dimension=0, tiled=True
    ).astype(jnp.float32)
    grad_in = grad_mid + norm_back(grad_one, hat_one, inv_one, gains[0])
    gain_grads = jnp.stack(
        [jnp.sum(grad_one * hat_one, axis=0), jnp.sum(grad_two * hat_two, axis=0)]
    )
    shift_grads = jnp.stack(
        [
            jnp.sum(grad_one, axis=0),
            jnp.sum(grad_two, axis=0),
            jnp.sum(grad_attn, axis=0),
            jnp.sum(grad_mlp, axis=0),
        ]
    )
    qkv_share, wout_share, bias_share, up_share, down_share, cup_share = (
        lax.psum_scatter(
            grad_qkv.astype(jnp.bfloat16), "dp", scatter_dimension=1, tiled=True
        ).astype(jnp.float32),
        lax.psum_scatter(
            grad_wout.astype(jnp.bfloat16), "dp", scatter_dimension=1, tiled=True
        ).astype(jnp.float32),
        lax.psum_scatter(
            grad_bias_qv.astype(jnp.bfloat16), "dp", scatter_dimension=1, tiled=True
        ).astype(jnp.float32),
        lax.psum_scatter(
            grad_up.astype(jnp.bfloat16), "dp", scatter_dimension=0, tiled=True
        ).astype(jnp.float32),
        lax.psum_scatter(
            grad_down.astype(jnp.bfloat16), "dp", scatter_dimension=1, tiled=True
        ).astype(jnp.float32),
        lax.psum_scatter(
            grad_cup.astype(jnp.bfloat16), "dp", scatter_dimension=0, tiled=True
        ).astype(jnp.float32),
    )
    gain_share, shift_share = (
        lax.psum_scatter(gain_grads, ("dp", "tensor"), scatter_dimension=1, tiled=True),
        lax.psum_scatter(shift_grads, ("dp", "tensor"), scatter_dimension=1, tiled=True),
    )
    return (
        layer_out,
        grad_in.astype(jnp.bfloat16),
        gain_share,
        shift_share,
        qkv_share,
        bias_share,
        wout_share,
        up_share,
        cup_share,
        down_share,
    )


def solution(mesh):
    in_specs = (
        P(("dp", "tensor"), None),
        P(("dp", "tensor"), None),
        P("dp"),
        P(None, "dp"),
        P(None, "dp"),
        P(None, "dp", "tensor"),
        P(None, ("tensor", "dp")),
        P("tensor", "dp"),
        P("dp", "tensor"),
        P(("tensor", "dp")),
        P("tensor", "dp"),
    )
    out_specs = (
        P(("dp", "tensor"), None),
        P(("dp", "tensor"), None),
        P(None, ("dp", "tensor")),
        P(None, ("dp", "tensor")),
        P(None, "dp", "tensor"),
        P(None, ("tensor", "dp")),
        P("tensor", "dp"),
        P("dp", "tensor"),
        P(("tensor", "dp")),
        P("tensor", "dp"),
    )
    return jax.shard_map(
        per_device, mesh=mesh, in_specs=in_specs, out_specs=out_specs, check_vma=False
    )
```

profile of v0, /device:TPU:0, one launch (start us, length us, event | category | flops | bytes accessed | tf_op | source)
XLA Modules:
  0.0 1240.6 jit_solution(2609150840192611639)
XLA Ops:
  8.0 22.4 %all_gather.36 = bf16[2,1024]{1,0:T(2,128)(2,1)S(1)} all-gather(bf16[2,128]{1,0:T(2,128)(2,1)} %param.18), channel_id=1, replica_groups=mesh['dp'=8,'tensor'=4] {'dp'}, dimensions={1}, use_global_device_ids=true | all-gather | bytes 4608 | tf_op jit(solution)/shard_map/all_gather | solution.py:46
  30.3 16.6 %all_gather.37 = bf16[4,1024]{1,0:T(4,128)(2,1)S(1)} all-gather(bf16[4,128]{1,0:T(4,128)(2,1)} %param.19), channel_id=1, replica_groups=mesh['dp'=8,'tensor'=4] {'dp'}, dimensions={1}, use_global_device_ids=true | all-gather | bytes 9216 | tf_op jit(solution)/shard_map/all_gather | solution.py:47
  52.5 18.1 %all-gather = bf16[8,32,2]{1,2,0:T(2,128)(2,1)S(1)} all-gather(bf16[1,32,2]{1,2,0:T(2,128)(2,1)S(1)} %bitcast.216), channel_id=1, replica_groups=mesh['dp'=8,'tensor'=4] {'dp'}, dimensions={0}, use_global_device_ids=true | all-gather | bytes 1152 | tf_op jit(solution)/shard_map/all_gather | solution.py:45
  70.9 27.0 %all_gather.41 = bf16[256,1024]{1,0:T(8,128)(2,1)S(1)} all-gather(bf16[256,128]{1,0:T(8,128)(2,1)S(1)} %copy-done.18), channel_id=1, replica_groups=mesh['dp'=8,'tensor'=4] {'dp'}, dimensions={1}, use_global_device_ids=true | all-gather | bytes 589824 | tf_op jit(solution)/shard_map/all_gather | solution.py:44
  97.9 6.2 convolution_bitcast_fusion
  107.8 3.2 copy.112
  110.9 4.3 squeeze.35
  117.7 4.6 reshape.173
  122.3 4.2 copy.116
  126.5 3.2 copy.110
  129.7 4.3 squeeze.34
  137.5 29.4 %while.28 = (s32[]{:T(128)}, bf16[4,584,4,64]{1,3,2,0:T(8,128)(2,1)}, f32[4,4,584]{2,1,0:T(4,128)S(1)}, bf16[4,584,4,64]{1,3,2,0:T(8,128)(2,1)}, bf16[4,584,4,64...) while((s32[]{:T(128)}, bf16[4,584,4,64]{1,3,2,0:T(8,128)(2,1)}, ...), condition=%wide.region_6.7_spmd.clone, body=%wide.region_3.6_spmd.clone.sunk | while | flops 365759776 | bytes 17763760 | solution.py:97
  141.3 3.4 fusion.149
  148.5 3.5 fusion.149
  155.8 3.5 fusion.149
  163.1 3.5 fusion.149
  167.0 3.9 copy.117
  170.8 3.5 reshape.146
  174.4 4.9 convolution_convert_fusion.2
  180.0 45.5 %reduce-scatter.24.cloned.1.call-done = bf16[584,1024]{1,0:T(8,128)(2,1)} async-done(((bf16[2336,1024]{1,0:T(8,128)(2,1)}), bf16[584,1024]{1,0:T(8,128)(2,1)}) %reduce-scatter.24.cloned.1.call-update) | async-done | bytes 1196048 | tf_op jit(solution)/shard_map/reduce_scatter | solution.py:100
  227.5 3.1 fusion.68
  233.9 20.4 %all-gather.1 = bf16[8,1,128]{2,1,0:T(2,128)(2,1)S(1)} all-gather(bf16[1,1,128]{2,1,0:T(2,128)(2,1)S(1)} %bitcast.217), channel_id=1, replica_groups=mesh['dp'=8,'tensor'=4] {'dp'}, dimensions={0}, use_global_device_ids=true | all-gather | bytes 2304 | tf_op jit(solution)/shard_map/all_gather | solution.py:52
  254.3 22.8 %all-gather.16.cloned.1.call-done = bf16[1024,1024]{1,0:T(8,128)(2,1)} async-done(((bf16[128,1024]{1,0:T(8,128)(2,1)}), bf16[1024,1024]{1,0:T(8,128)(2,1)}) %all-gather.16.cloned.1.call-update) | async-done | bytes 2097168 | tf_op jit(solution)/shard_map/all_gather | solution.py:50
  277.1 38.4 %all-gather.14.cloned.1.call-done = bf16[2336,1024]{1,0:T(8,128)(2,1)} async-done(((bf16[584,1024]{1,0:T(8,128)(2,1)}), bf16[2336,1024]{1,0:T(8,128)(2,1)}) %all-gather.14.cloned.1.call-update) | async-done | bytes 4784144 | tf_op jit(solution)/shard_map/all_gather | solution.py:106
  315.5 12.6 %multiply_convert_fusion.1 = (bf16[2336,1024]{1,0:T(8,128)(2,1)}, f32[2336,1024]{1,0:T(8,128)}) fusion(f32[1024]{0:T(1024)S(1)} %bitcast.214, bf16[2336,1024]{1,0:T(8,128)(2,1)} %all-gather.14.cloned.1.call-done, bf16[1024,1024]{1,0:T(8,128)(2,1)} %all-gather.16.cloned.1.call-done), kind=kOutput, calls=%fused_computation.65 | convolution fusion | flops 4915691520 | bytes 21237760 | tf_op jit(solution)/shard_map/dot_general | solution.py:107
  328.1 40.6 %all-gather.18.cloned.1.call-done = bf16[1024,1024]{1,0:T(8,128)(2,1)} async-done(((bf16[1024,128]{1,0:T(8,128)(2,1)}), bf16[1024,1024]{1,0:T(8,128)(2,1)}) %all-gather.18.cloned.1.call-update) | async-done | bytes 2097168 | tf_op jit(solution)/shard_map/all_gather | solution.py:51
  368.8 38.3 %all-gather.20.cloned.1.call-done = bf16[2336,1024]{1,0:T(8,128)(2,1)} async-done(((bf16[584,1024]{1,0:T(8,128)(2,1)}), bf16[2336,1024]{1,0:T(8,128)(2,1)}) %all-gather.20.cloned.1.call-update) | async-done | bytes 4784144 | tf_op jit(solution)/shard_map/all_gather | solution.py:120
  407.0 12.7 %fusion.105 = (bf16[1024]{0:T(1024)(128)(2,1)S(1)}, bf16[2336,1024]{1,0:T(8,128)(2,1)S(1)}) fusion(f32[2336,1024]{1,0:T(8,128)} %get-tuple-element.329, f32[1024]{0:T(1024)S(1)} %bitcast.215, bf16[2336,1024]{1,0:T(8,128)(2,1)} %all-gather.20.cloned.1.call-done, bf16[1024,1024]{1,0:T(8,128)(2,1)} %all-gather.18.cloned.1.call-done), kind=kOutput, calls=%fused_computation.159 | convolution fusion | flops 4927650816 | bytes 21239808 | tf_op jit(solution)/shard_map/rd,fd->rf/dot_general | solution.py:121
  421.9 6.9 convolution_convert_fusion
  428.9 9.6 convolution_convert_fusion.1
  438.7 38.5 %reduce-scatter.28.cloned.1.call-done = bf16[584,1024]{1,0:T(8,128)(2,1)} async-done(((bf16[2336,1024]{1,0:T(8,128)(2,1)}), bf16[584,1024]{1,0:T(8,128)(2,1)}) %reduce-scatter.28.cloned.1.call-update) | async-done | bytes 1196048 | tf_op jit(solution)/shard_map/reduce_scatter | solution.py:130
  477.2 3.5 fusion.84
  480.7 47.3 %reduce-scatter.26.cloned.1.call-done = bf16[584,1024]{1,0:T(8,128)(2,1)} async-done(((bf16[2336,1024]{1,0:T(8,128)(2,1)}), bf16[584,1024]{1,0:T(8,128)(2,1)}) %reduce-scatter.26.cloned.1.call-update) | async-done | bytes 1196048 | tf_op jit(solution)/shard_map/reduce_scatter | solution.py:113
  528.1 4.2 multiply_reduce_fusion.2
  535.1 10.0 convolution_convert_fusion.4
  545.0 4.0 copy.149
  549.1 10.0 fusion.89
  559.4 13.6 %all-gather.22.cloned.1.call-done = bf16[2336,1024]{1,0:T(8,128)(2,1)} async-done(((bf16[584,1024]{1,0:T(8,128)(2,1)}), bf16[2336,1024]{1,0:T(8,128)(2,1)}) %all-gather.22.cloned.1.call-update) | async-done | bytes 4784144 | tf_op jit(solution)/shard_map/all_gather | solution.py:136
  573.0 3.8 convolution_convert_fusion.3
  578.9 4.3 copy.121
  583.3 53.3 %while.29 = (s32[]{:T(128)}, f32[4,584,4,64]{1,3,2,0:T(8,128)}, bf16[4,584,4,64]{1,3,2,0:T(8,128)(2,1)}, f32[4,584,4,64]{1,3,2,0:T(8,128)}, bf16[4,584,4,64]{1,3...) while((s32[]{:T(128)}, f32[4,584,4,64]{1,3,2,0:T(8,128)}, ...), condition=%wide.region_16.17_spmd.clone, body=%wide.region_14.16_spmd.clone.sunk | while | flops 893863936 | bytes 60922836 | solution.py:169
  588.0 3.0 multiply_reduce_fusion.4
  601.3 3.0 multiply_reduce_fusion.4
  607.3 2.7 fusion.159
  614.6 3.0 multiply_reduce_fusion.4
  627.9 3.0 multiply_reduce_fusion.4
  633.9 2.7 fusion.159
  636.6 5.8 fusion.101
  646.0 4.7 reshape.157
  651.0 4.0 convolution_convert_fusion.5
  659.8 3.8 reshape.159
  663.6 4.2 copy.137
  667.8 4.6 reshape.158
  676.0 9.0 fusion.95
  685.0 2.9 copy.143
  689.6 8.6 bitcast_convert_fusion
  700.1 21.7 %all-reduce = bf16[1024]{0:T(1024)(128)(2,1)S(1)} all-reduce(bf16[1024]{0:T(1024)(128)(2,1)S(1)} %get-tuple-element.330), channel_id=12, replica_groups=mesh['dp'=8,'tensor'=4] {'dp'}, use_global_device_ids=true, to_apply=%region_35.36.clone | all-reduce | flops 1024 | bytes 4096
  726.1 54.3 %reduce-scatter.40.cloned.1.call-done = bf16[32,2]{1,0:T(8,128)(2,1)} async-done(((bf16[256,2]{1,0:T(8,128)(2,1)}), bf16[32,2]{1,0:T(8,128)(2,1)}) %reduce-scatter.40.cloned.1.call-update) | async-done | bytes 144
  781.7 63.2 %reduce-scatter.42.cloned.1.call-done = bf16[128,256]{1,0:T(8,128)(2,1)} async-done(((bf16[1024,256]{1,0:T(8,128)(2,1)}), bf16[128,256]{1,0:T(8,128)(2,1)}) %reduce-scatter.42.cloned.1.call-update) | async-done | bytes 65552
  846.5 65.7 %reduce-scatter.38.cloned.1.call-done = bf16[128,768]{1,0:T(8,128)(2,1)} async-done(((bf16[1024,768]{1,0:T(8,128)(2,1)}), bf16[128,768]{1,0:T(8,128)(2,1)}) %reduce-scatter.38.cloned.1.call-update) | async-done | bytes 196624
  914.3 47.6 %reduce-scatter.30.cloned.1.call-done = bf16[584,1024]{1,0:T(8,128)(2,1)} async-done(((bf16[2336,1024]{1,0:T(8,128)(2,1)}), bf16[584,1024]{1,0:T(8,128)(2,1)}) %reduce-scatter.30.cloned.1.call-update) | async-done | bytes 1196048 | tf_op jit(solution)/shard_map/reduce_scatter | solution.py:177
  966.7 3.6 fusion.78
  970.3 129.4 %reduce-scatter.34.cloned.1.call-done = f32[32,2]{1,0:T(8,128)} async-done(((f32[1024,2]{1,0:T(8,128)}), f32[32,2]{1,0:T(8,128)}) %reduce-scatter.34.cloned.1.call-update) | async-done | bytes 272
  1101.1 130.8 %reduce-scatter.36.cloned.1.call-done = f32[32,4]{1,0:T(8,128)} async-done(((f32[1024,4]{1,0:T(8,128)}), f32[32,4]{1,0:T(8,128)}) %reduce-scatter.36.cloned.1.call-update) | async-done | bytes 528
  (219 shorter events, 112.5 us)
Async XLA Ops:
  7.2 43.7 %copy-start = (bf16[584,1024]{1,0:T(8,128)(2,1)S(1)}, bf16[584,1024]{1,0:T(8,128)(2,1)}, u32[]{:S(2)}) copy-start(bf16[584,1024]{1,0:T(8,128)(2,1)} %param.15) | copy-start | bytes 3588100
  7.2 90.8 %all-gather.12.cloned.1.call-start = ((), (), s32[]{:S(2)}) async-start(), calls=%async_computation.12 | async-start | bytes 1769472 | tf_op jit(solution)/shard_map/all_gather | solution.py:43
  7.9 90.0 %all-gather.10.cloned.1.call-start = ((), (), s32[]{:S(2)}) async-start(), calls=%async_computation.11 | async-start | bytes 5980160 | tf_op jit(solution)/shard_map/all_gather | solution.py:68
  48.5 2.5 copy-start.12
  48.5 4.1 copy-start.20
  48.5 22.4 %copy-start.18 = (bf16[256,128]{1,0:T(8,128)(2,1)S(1)}, bf16[256,128]{1,0:T(8,128)(2,1)}, u32[]{:S(2)}) copy-start(bf16[256,128]{1,0:T(8,128)(2,1)} %param.22) | copy-start | bytes 196612
  50.3 0.6 copy-start.14
  50.3 0.6 copy-start.16
  52.5 173.1 %reduce-scatter.24.cloned.1.call-start = ((), (), s32[]{:S(2)}) async-start(), calls=%async_computation.13 | async-start | bytes 5980160 | tf_op jit(solution)/shard_map/reduce_scatter | solution.py:100
  167.0 7.4 copy-start.2
  179.2 0.7 copy-start.21
  179.3 97.9 %all-gather.16.cloned.1.call-start = ((), (), s32[]{:S(2)}) async-start(), calls=%async_computation.15 | async-start | bytes 2359296 | tf_op jit(solution)/shard_map/all_gather | solution.py:50
  179.8 135.7 %all-gather.14.cloned.1.call-start = ((), (), s32[]{:S(2)}) async-start(), calls=%async_computation.14 | async-start | bytes 5980160 | tf_op jit(solution)/shard_map/all_gather | solution.py:106
  225.5 2.0 copy-start.1
  230.7 3.2 copy-start.22
  232.5 136.3 %all-gather.18.cloned.1.call-start = ((), (), s32[]{:S(2)}) async-start(), calls=%async_computation.16 | async-start | bytes 2359296 | tf_op jit(solution)/shard_map/all_gather | solution.py:51
  233.1 173.9 %all-gather.20.cloned.1.call-start = ((), (), s32[]{:S(2)}) async-start(), calls=%async_computation.18 | async-start | bytes 5980160 | tf_op jit(solution)/shard_map/all_gather | solution.py:120
  233.8 243.4 %reduce-scatter.28.cloned.1.call-start = ((), (), s32[]{:S(2)}) async-start(), calls=%async_computation.19 | async-start | bytes 5980160 | tf_op jit(solution)/shard_map/reduce_scatter | solution.py:130
  407.0 14.9 %copy-start.23 = (bf16[1024,1024]{1,0:T(8,128)(2,1)S(1)}, bf16[1024,1024]{1,0:T(8,128)(2,1)}, u32[]{:S(2)}) copy-start(bf16[1024,1024]{1,0:T(8,128)(2,1)} %all-gather.16.cloned.1.call-done) | copy-start | bytes 6291460
  419.7 2.2 copy-start.25
  428.8 99.3 %reduce-scatter.26.cloned.1.call-start = ((), (), s32[]{:S(2)}) async-start(), calls=%async_computation.17 | async-start | bytes 5980160 | tf_op jit(solution)/shard_map/reduce_scatter | solution.py:113
  438.4 89.6 %copy-start.19 = (f32[1,1024]{1,0:T(1,128)S(1)}, f32[1,1024]{1,0:T(1,128)}, u32[]{:S(2)}) copy-start(f32[1,1024]{1,0:T(1,128)} %get-tuple-element.320) | copy-start | bytes 12292
  438.5 134.6 %all-gather.22.cloned.1.call-start = ((), (), s32[]{:S(2)}) async-start(), calls=%async_computation.20 | async-start | bytes 5980160 | tf_op jit(solution)/shard_map/all_gather | solution.py:136
  532.3 1.5 copy-start.4
  535.0 187.3 %reduce-scatter.44.cloned.1.call-start = ((), (), s32[]{:S(2)}) async-start(), calls=%async_computation.28 | async-start | bytes 2359296
  549.1 175.2 %reduce-scatter.32.cloned.1.call-start = ((), (), s32[]{:S(2)}) async-start(), calls=%async_computation.22 | async-start | bytes 2359296 | tf_op jit(solution)/shard_map/reduce_scatter | solution.py:202
  559.2 221.2 %reduce-scatter.40.cloned.1.call-start = ((), (), s32[]{:S(2)}) async-start(), calls=%async_computation.26 | async-start | bytes 73728
  578.9 4.3 copy-start.3
  583.3 2.3 copy-start.6
  591.0 1.9 copy-start.10
  594.0 2.7 copy-start.11
  596.7 2.2 copy-start.6
  604.3 1.9 copy-start.10
  607.3 2.7 copy-start.11
  610.0 2.2 copy-start.6
  617.6 1.9 copy-start.10
  620.6 2.7 copy-start.11
  623.3 2.2 copy-start.6
  630.9 1.9 copy-start.10
  633.9 2.7 copy-start.11
  646.0 5.0 copy-start.5
  650.7 194.2 %reduce-scatter.42.cloned.1.call-start = ((), (), s32[]{:S(2)}) async-start(), calls=%async_computation.27 | async-start | bytes 589824
  651.0 4.0 copy-start.9
  655.0 2.2 copy-start.7
  672.5 239.8 %reduce-scatter.38.cloned.1.call-start = ((), (), s32[]{:S(2)}) async-start(), calls=%async_computation.25 | async-start | bytes 1769472
  689.6 272.4 %reduce-scatter.30.cloned.1.call-start = ((), (), s32[]{:S(2)}) async-start(), calls=%async_computation.21 | async-start | bytes 5980160 | tf_op jit(solution)/shard_map/reduce_scatter | solution.py:177
  698.2 0.7 copy-start.24
  698.2 263.8 %copy-start.13 = (f32[584]{0:T(1024)S(1)}, f32[584]{0:T(1024)}, u32[]{:S(2)}) copy-start(f32[584]{0:T(1024)} %copy-done.12) | copy-start | bytes 7012
  698.2 263.8 %copy-start.15 = (f32[584]{0:T(1024)S(1)}, f32[584]{0:T(1024)}, u32[]{:S(2)}) copy-start(f32[584]{0:T(1024)} %copy-done.14) | copy-start | bytes 7012
  698.2 263.7 %copy-start.17 = (f32[1,1024]{1,0:T(1,128)S(1)}, f32[1,1024]{1,0:T(1,128)}, u32[]{:S(2)}) copy-start(f32[1,1024]{1,0:T(1,128)} %copy-done.16) | copy-start | bytes 12292
  698.2 401.5 %reduce-scatter.34.cloned.1.call-start = ((), (), s32[]{:S(2)}) async-start(), calls=%async_computation.23 | async-start | bytes 540672
  962.0 4.8 copy-start.8
  965.6 266.3 %reduce-scatter.36.cloned.1.call-start = ((), (), s32[]{:S(2)}) async-start(), calls=%async_computation.24 | async-start | bytes 540672
Sparse Core Ops, SparseCore 0:
  10.2 46.6 all-gather.11
  59.1 36.6 all-gather.9
  179.4 46.1 reduce-scatter.23
  227.7 49.3 all-gather.15
  279.2 36.3 all-gather.13
  317.6 51.0 all-gather.17
  371.0 35.9 all-gather.19
  428.9 48.2 reduce-scatter.27
  479.8 48.2 reduce-scatter.25
  535.1 37.8 all-gather.21
  577.0 67.9 reduce-scatter.43
  648.8 66.9 reduce-scatter.31
  720.2 60.1 reduce-scatter.39
  784.0 60.8 reduce-scatter.41
  848.2 64.0 reduce-scatter.37
  914.8 47.1 reduce-scatter.29
  965.7 133.9 reduce-scatter.33
  1101.9 129.9 reduce-scatter.35
where the time goes:
time: 1250 us; the launch traced here: 1240 us
  waiting for transfers between devices  779 us (62%)
  matrix products  167 us (13%)
  blocking collectives  126 us (10%)
  local copies, waits for them, and re-layouts  95.9 us (8%)
  other arithmetic  55 us (4%)
  between operations  15.9 us (1%)
    unnamed x24, waiting for transfers between devices  446 us
    reduce_scatter x1, waiting for transfers between devices, per_device(): lax.psum_scatter(one_part.astype(jnp.bfloat16), 'tensor', scatter_dimensi...  47.6 us
    reduce_scatter x1, waiting for transfers between devices, per_device(): lax.psum_scatter(mlp_part.astype(jnp.bfloat16), 'tensor', scatter_dimensi...  47.3 us
    reduce_scatter x1, waiting for transfers between devices, per_device(): lax.psum_scatter(attn_part.astype(jnp.bfloat16), 'tensor', scatter_dimens...  45.5 us
    all_gather x1, waiting for transfers between devices, per_device(): lax.all_gather(w_down, 'dp', axis=1, tiled=True)  40.6 us
    reduce_scatter x1, waiting for transfers between devices, per_device(): lax.psum_scatter(two_part.astype(jnp.bfloat16), 'tensor', scatter_dimensi...  38.5 us
    unnamed x68, local copies, waits for them, and re-layouts  38.5 us
    all_gather x1, waiting for transfers between devices, per_device(): full_two = lax.all_gather(low_two, 'tensor', axis=0, tiled=True)  38.4 us
  transfers between devices with their start and end apart: 18, of which 14 were waited for; matrix products, arithmetic and copies ran while one was open for 16% of the time, Pallas kernels for 0%

commit v1 on v0

v1 whole, which is shorter than its diff:
```python
import functools

import jax
import jax.numpy as jnp
from jax import lax
from jax.experimental import pallas as pl
from jax.experimental.pallas import tpu as pltpu
from jax.sharding import Mesh, PartitionSpec as P

HEAD_DIM = 64
VALID = 577
SEQ = 584
BF = jnp.bfloat16
F32 = jnp.float32
VMEM_LIMIT = 60 * 1024 * 1024
NT = (((1,), (1,)), ((), ()))
TN = (((0,), (0,)), ((), ()))
NN = (((1,), (0,)), ((), ()))


def dot(left, right, dims):
    return lax.dot_general(left, right, dims, preferred_element_type=F32)


class Loads:
    def __init__(self, sems):
        self.sems, self.groups = sems, []

    def start(self, pairs):
        sem = self.sems.at[len(self.groups)]
        copies = [pltpu.make_async_copy(src, dst, sem) for src, dst in pairs]
        for copy in copies:
            copy.start()
        self.groups.append(copies)
        return len(self.groups) - 1

    def wait(self, group):
        for copy in self.groups[group]:
            copy.wait()


def call(body, ins, outs, scratch, name, flops, aliases=None, smem=(), sems=12, vmem_ins=()):
    n_smem, n_vmem, n_in, n_out = len(smem), len(vmem_ins), len(ins), len(outs)
    moved = sum(a.size * a.dtype.itemsize for a in ins) + sum(
        o.size * o.dtype.itemsize for o in outs
    )

    def kernel(*refs):
        first = n_smem + n_vmem
        small = refs[:first]
        in_refs = refs[first : first + n_in]
        out_refs = refs[first + n_in : first + n_in + n_out]
        rest = refs[first + n_in + n_out :]
        body(small, in_refs, out_refs, rest[:-1], Loads(rest[-1]))

    any_spec = pl.BlockSpec(memory_space=pl.ANY)
    return pl.pallas_call(
        kernel,
        out_shape=outs,
        in_specs=[pl.BlockSpec(memory_space=pltpu.SMEM)] * n_smem
        + [pl.BlockSpec(memory_space=pltpu.VMEM)] * n_vmem
        + [any_spec] * n_in,
        out_specs=[any_spec] * n_out,
        scratch_shapes=list(scratch) + [pltpu.SemaphoreType.DMA((sems,))],
        input_output_aliases={n_smem + n_vmem + i: o for i, o in (aliases or {}).items()},
        compiler_params=pltpu.CompilerParams(vmem_limit_bytes=VMEM_LIMIT),
        cost_estimate=pl.CostEstimate(flops=int(flops), bytes_accessed=int(moved), transcendentals=0),
        name=name,
    )(*smem, *vmem_ins, *ins)


def norm_parts(rows):
    center = rows - jnp.mean(rows, axis=1, keepdims=True)
    inverse = lax.rsqrt(jnp.mean(center * center, axis=1, keepdims=True) + 1e-05)
    return center * inverse, inverse


def norm_back(grad_norm, scaled, inverse, gain_row):
    grad_hat = grad_norm * gain_row
    first_mean = jnp.mean(grad_hat, axis=1, keepdims=True)
    second_mean = jnp.mean(grad_hat * scaled, axis=1, keepdims=True)
    return inverse * (grad_hat - first_mean - scaled * second_mean)


def sds(shape, dtype):
    return jax.ShapeDtypeStruct(shape, dtype)


def arrange_pair(ids, own, other, nd):
    n = len(own)
    rows, width = own[0].shape
    bd = width // nd

    def body(small, ins, outs, scratch, loads):
        (ids_ref,) = small
        mine = ids_ref[0]
        pairs = []
        for i in range(n):
            for p in range(nd):
                src = pl.ds(pl.multiple_of(ids_ref[2 + p] * bd, 128), bd)
                dst = pl.ds(p * bd, bd)
                pairs.append((ins[i].at[:, src], outs[i].at[mine, :, dst]))
                pairs.append((ins[n + i].at[:, src], outs[i].at[1 - mine, :, dst]))
        loads.wait(loads.start(pairs))

    return call(
        body,
        list(own) + list(other),
        [sds((2, rows, width), BF)] * n,
        [],
        "arrange_pair",
        0,
        smem=(ids,),
    )


def weight_loads(loads, plan, refs, scratch):
    return loads.start([(refs[a].at[src], scratch[s].at[dst]) for a, src, s, dst in plan])


def softmax_rows(q2, k2):
    scores = dot(q2, k2, NT)
    lane = lax.broadcasted_iota(jnp.int32, scores.shape, 1)
    scores = jnp.where(lane < VALID, scores, -1e30)
    e = jnp.exp(scores - jnp.max(scores, axis=1, keepdims=True))
    return e * (1.0 / jnp.sum(e, axis=1, keepdims=True))


def attn_forward(image, tok, nv, bq, wqkv, wout, prev):
    seq, width = tok.shape[1:]
    qkv_arrays, qkv_plan, qkv_scratch = wqkv
    out_arrays, out_plan, out_scratch = wout
    ext = qkv_scratch[-1]
    n_prev = 0 if prev is None else len(prev)
    nq, no = len(qkv_arrays), len(out_arrays)

    def body(small, ins, outs, scratch, loads):
        nv_ref, bq_ref = small
        tok_ref, ins = ins[0], ins[1 + n_prev :]
        w_s, wo_s, tok_s, first_s, q_s, k_s, v_s, att_s, part_s = scratch
        g_tok = loads.start([(tok_ref.at[image], tok_s)])
        g_w = weight_loads(loads, qkv_plan, ins[:nq], (w_s,))
        g_o = weight_loads(loads, out_plan, ins[nq:], (wo_s,))
        loads.wait(g_tok)
        hat, _ = norm_parts(tok_s[...].astype(F32))
        first_s[...] = (hat * nv_ref[0:1, :] + nv_ref[2:3, :]).astype(BF)
        g_first = loads.start([(first_s, outs[0].at[image])])
        loads.wait(g_w)
        low = first_s[...]
        for i, ref in enumerate((q_s, k_s, v_s)):
            proj = dot(low, w_s[i].reshape(width, ext), NN)
            if i == 0:
                proj = proj + bq_ref[0:1, :]
            if i == 2:
                proj = proj + bq_ref[1:2, :]
            low_proj = proj.astype(BF)
            if i == 0:
                low_proj = low_proj * jnp.asarray(HEAD_DIM**-0.5, BF)
            ref[...] = low_proj
        g_qkv = loads.start(
            [(q_s, outs[1].at[image]), (k_s, outs[2].at[image]), (v_s, outs[3].at[image])]
        )
        half = lax.broadcasted_iota(jnp.int32, (1, 128), 1) // HEAD_DIM

        def pair(i, carry):
            cols = pl.ds(pl.multiple_of(i * 128, 128), 128)
            q2, k2, v2 = q_s[:, cols], k_s[:, cols], v_s[:, cols]
            total = None
            for h in range(2):
                keep = (half == h).astype(BF)
                probs = softmax_rows(q2, k2 * keep).astype(BF)
                piece = dot(probs, v2 * keep, NN)
                total = piece if total is None else total + piece
            att_s[:, cols] = total.astype(BF)
            return carry

        lax.fori_loop(0, ext // 128, pair, 0)
        g_att = loads.start([(att_s, outs[4].at[image])])
        loads.wait(g_o)
        part_s[...] = dot(att_s[...], wo_s[...], NN).astype(BF)
        g_part = loads.start([(part_s, outs[5])])
        for group in (g_first, g_qkv, g_att, g_part):
            loads.wait(group)

    shapes = [(2, seq, width)] + [(2, seq, ext)] * 4
    return call(
        body,
        [tok] + list(prev or []) + qkv_arrays + out_arrays,
        [sds(s, BF) for s in shapes] + [sds((seq, width), BF)],
        [
            pltpu.VMEM(qkv_scratch, BF),
            pltpu.VMEM(out_scratch, BF),
            pltpu.VMEM((seq, width), BF),
            pltpu.VMEM((seq, width), BF),
            pltpu.VMEM((seq, ext), BF),
            pltpu.VMEM((seq, ext), BF),
            pltpu.VMEM((seq, ext), BF),
            pltpu.VMEM((seq, ext), BF),
            pltpu.VMEM((seq, width), BF),
        ],
        "attn_forward",
        2 * seq * width * ext * 4 + 16 * seq * seq * ext,
        aliases={1 + i: i for i in range(n_prev)},
        vmem_ins=(nv, bq),
    )


def mlp_up(image, tok, part, recv, keep, nv, bu, wup, prev):
    seq, width = tok.shape[1:]
    up_arrays, up_plan, up_scratch = wup
    hid = up_scratch[-1]
    n_prev = 0 if prev is None else len(prev)
    step = min(512, hid)

    def body(small, ins, outs, scratch, loads):
        keep_ref, nv_ref, bu_ref = small
        tok_ref, part_ref, recv_ref = ins[:3]
        w_s, tok_s, part_s, recv_s, mid_s, sec_s, act_s, dact_s = scratch
        g_in = loads.start([(tok_ref.at[image], tok_s), (part_ref, part_s), (recv_ref, recv_s)])
        g_w = weight_loads(loads, up_plan, ins[3 + n_prev :], (w_s,))
        loads.wait(g_in)
        total = part_s[...].astype(F32) + recv_s[...].astype(F32) + nv_ref[4:5, :]
        middle = tok_s[...].astype(F32) + keep_ref[image] * total
        mid_s[...] = middle
        hat, _ = norm_parts(middle)
        sec_s[...] = (hat * nv_ref[1:2, :] + nv_ref[3:4, :]).astype(BF)
        g_mid = loads.start([(mid_s, outs[0].at[image]), (sec_s, outs[1].at[image])])
        loads.wait(g_w)
        second = sec_s[...]
        for lo in range(0, hid, step):
            cols = slice(lo, lo + step)
            pre = dot(second, w_s[:, cols], NN) + bu_ref[0:1, cols]
            gate = 1.0 / (1.0 + jnp.exp(-1.702 * pre))
            act_s[:, cols] = (pre * gate).astype(BF)
            dact_s[:, cols] = (gate + 1.702 * pre * gate * (1.0 - gate)).astype(BF)
        g_out = loads.start([(act_s, outs[2].at[image]), (dact_s, outs[3].at[image])])
        loads.wait(g_mid)
        loads.wait(g_out)

    outs = [
        sds((2, seq, width), F32),
        sds((2, seq, width), BF),
        sds((2, seq, hid), BF),
        sds((2, seq, hid), BF),
    ]
    return call(
        body,
        [tok, part, recv] + list(prev or []) + up_arrays,
        outs,
        [
            pltpu.VMEM(up_scratch, BF),
            pltpu.VMEM((seq, width), BF),
            pltpu.VMEM((seq, width), BF),
            pltpu.VMEM((seq, width), BF),
            pltpu.VMEM((seq, width), F32),
            pltpu.VMEM((seq, width), BF),
            pltpu.VMEM((seq, hid), BF),
            pltpu.VMEM((seq, hid), BF),
        ],
        "mlp_up",
        2 * seq * width * hid,
        aliases={3 + i: i for i in range(n_prev)},
        smem=(keep,),
        vmem_ins=(nv, bu),
    )


def weight_grad(left, right, tasks, out_shapes, name):
    rows = left.shape[0]
    n_right = len(right)

    def body(small, ins, outs, scratch, loads):
        left_s = scratch[0]
        right_s = scratch[1 : 1 + n_right]
        out_s = scratch[1 + n_right :]
        g_l = loads.start([(ins[0], left_s)])
        g_r = [loads.start([(ins[1 + i], right_s[i])]) for i in range(n_right)]
        loads.wait(g_l)
        for g in g_r:
            loads.wait(g)
        for l_cols, index, r_cols, stores in tasks:
            value = dot(left_s[:, l_cols], right_s[index][:, r_cols], TN).astype(BF)
            for which, spot, r_sl, c_sl in stores:
                out_s[which][spot] = value[r_sl, c_sl]
        done = loads.start([(out_s[i], outs[i]) for i in range(len(outs))])
        loads.wait(done)

    flops = sum(
        2 * rows * (l.stop - l.start) * (r.stop - r.start) for l, _, r, _ in tasks
    )
    return call(
        body,
        [left] + list(right),
        [sds(s, BF) for s in out_shapes],
        [pltpu.VMEM(a.shape, BF) for a in [left] + list(right)]
        + [pltpu.VMEM(s, BF) for s in out_shapes],
        name,
        flops,
    )


def mlp_back(grad, dact, wdown):
    rows, width = grad.shape
    hid = dact.shape[1]
    down_arrays, down_plan, down_scratch = wdown
    step = min(512, hid)

    def body(small, ins, outs, scratch, loads):
        w_s, g_s, d_s, low_s, sum_s = scratch
        g_g = loads.start([(ins[0], g_s)])
        g_w = weight_loads(loads, down_plan, ins[2:], (w_s,))
        g_d = loads.start([(ins[1], d_s)])
        for g in (g_g, g_w, g_d):
            loads.wait(g)
        left = g_s[...]
        for lo in range(0, hid, step):
            cols = slice(lo, lo + step)
            pre = dot(left, w_s[cols, :], NT) * d_s[:, cols].astype(F32)
            low_s[:, cols] = pre.astype(BF)
            sum_s[0:1, cols] = jnp.sum(pre, axis=0, keepdims=True)
        done = loads.start([(low_s, outs[0]), (sum_s, outs[1])])
        loads.wait(done)

    return call(
        body,
        [grad, dact] + down_arrays,
        [sds((rows, hid), BF), sds((1, hid), F32)],
        [
            pltpu.VMEM(down_scratch, BF),
            pltpu.VMEM((rows, width), BF),
            pltpu.VMEM((rows, hid), BF),
            pltpu.VMEM((rows, hid), BF),
            pltpu.VMEM((1, hid), F32),
        ],
        "mlp_back",
        2 * rows * width * hid,
    )


def rows_times(lefts, row_range, weight, dims, split, width, name):
    arrays, plan, shape = weight
    lo, hi = row_range
    rows = hi - lo
    n = len(lefts)

    def body(small, ins, outs, scratch, loads):
        w_s, out_s = scratch[0], scratch[1]
        l_s = scratch[2:]
        g_l = loads.start([(ins[i].at[lo:hi], l_s[i]) for i in range(n)])
        g_w = weight_loads(loads, plan, ins[n:], (w_s,))
        loads.wait(g_l)
        loads.wait(g_w)
        total = None
        for i in range(n):
            w = w_s[i].reshape(-1, shape[-1]) if split else w_s[...]
            piece = dot(l_s[i][...], w, dims)
            total = piece if total is None else total + piece
        out_s[...] = total.astype(BF)
        loads.wait(loads.start([(out_s, outs[0])]))

    return call(
        body,
        list(lefts) + arrays,
        [sds((rows, width), BF)],
        [pltpu.VMEM(shape, BF), pltpu.VMEM((rows, width), BF)]
        + [pltpu.VMEM((rows, a.shape[1]), BF) for a in lefts],
        name,
        2 * rows * width * sum(a.shape[1] for a in lefts),
    )[0]


def attn_backward(image, middle, part, recv, cot, keep, nv, wout, q, k, v, prev):
    seq, width = middle.shape[1:]
    out_arrays, out_plan, out_scratch = wout
    ext = q.shape[2]
    n_prev = 0 if prev is None else len(prev)

    def body(small, ins, outs, scratch, loads):
        keep_ref, nv_ref = small
        mid_ref, part_ref, recv_ref, cot_ref, q_ref, k_ref, v_ref = ins[:7]
        (wo_s, mid_s, part_s, recv_s, cot_s, q_s, k_s, v_s) = scratch[:8]
        (gmid_s, gat_s, do_s, dq_s, dk_s, dv_s, cs_s, bs_s) = scratch[8:]
        g_in = loads.start(
            [
                (mid_ref.at[image], mid_s),
                (part_ref, part_s),
                (recv_ref, recv_s),
                (cot_ref.at[image], cot_s),
            ]
        )
        g_o = weight_loads(loads, out_plan, ins[7 + n_prev :], (wo_s,))
        g_q = loads.start(
            [(q_ref.at[image], q_s), (k_ref.at[image], k_s), (v_ref.at[image], v_s)]
        )
        loads.wait(g_in)
        keep_here = keep_ref[image]
        hat, inverse = norm_parts(mid_s[...])
        grad_two = part_s[...].astype(F32) + recv_s[...].astype(F32)
        top = cot_s[...].astype(F32)
        cs_s[0:1, :] = jnp.sum(grad_two * hat, axis=0, keepdims=True)
        cs_s[1:2, :] = jnp.sum(grad_two, axis=0, keepdims=True)
        cs_s[3:4, :] = jnp.sum(top, axis=0, keepdims=True) * keep_here
        grad_mid = top + norm_back(grad_two, hat, inverse, nv_ref[1:2, :])
        gmid_s[...] = grad_mid
        grad_attn = grad_mid * keep_here
        cs_s[2:3, :] = jnp.sum(grad_attn, axis=0, keepdims=True)
        gat_s[...] = grad_attn.astype(BF)
        g_mid = loads.start([(gmid_s, outs[0].at[image]), (gat_s, outs[1].at[image])])
        loads.wait(g_o)
        do_s[...] = dot(gat_s[...], wo_s[...], NT).astype(BF)
        loads.wait(g_q)
        half = lax.broadcasted_iota(jnp.int32, (1, 128), 1) // HEAD_DIM

        def pair(i, carry):
            cols = pl.ds(pl.multiple_of(i * 128, 128), 128)
            q2, k2, v2, do2 = q_s[:, cols], k_s[:, cols], v_s[:, cols], do_s[:, cols]
            dq = dk = dv = None
            for h in range(2):
                mask = (half == h).astype(BF)
                km, qm, dom = k2 * mask, q2 * mask, do2 * mask
                scores = dot(km, q2, NT)
                row = lax.broadcasted_iota(jnp.int32, scores.shape, 0)
                scores = jnp.where(row < VALID, scores, -1e30)
                e = jnp.exp(scores - jnp.max(scores, axis=0, keepdims=True))
                probs = e * (1.0 / jnp.sum(e, axis=0, keepdims=True))
                grad_probs = dot(v2, dom, NT)
                row_dot = jnp.sum(probs * grad_probs, axis=0, keepdims=True)
                grad_scores = (probs * (grad_probs - row_dot)).astype(BF)
                v_piece = dot(probs.astype(BF), dom, NN)
                k_piece = dot(grad_scores, qm, NN)
                q_piece = dot(grad_scores, km, TN)
                dq = q_piece if dq is None else dq + q_piece
                dk = k_piece if dk is None else dk + k_piece
                dv = v_piece if dv is None else dv + v_piece
            dq = dq * HEAD_DIM**-0.5
            bs_s[0:1, cols] = jnp.sum(dq, axis=0, keepdims=True)
            bs_s[1:2, cols] = jnp.sum(dv, axis=0, keepdims=True)
            dq_s[:, cols] = dq.astype(BF)
            dk_s[:, cols] = dk.astype(BF)
            dv_s[:, cols] = dv.astype(BF)
            return carry

        lax.fori_loop(0, ext // 128, pair, 0)
        g_out = loads.start(
            [
                (dq_s, outs[2].at[image]),
                (dk_s, outs[3].at[image]),
                (dv_s, outs[4].at[image]),
                (cs_s, outs[5]),
                (bs_s, outs[6]),
            ]
        )
        loads.wait(g_mid)
        loads.wait(g_out)

    return call(
        body,
        [middle, part, recv, cot, q, k, v] + list(prev or []) + out_arrays,
        [sds((2, seq, width), F32), sds((2, seq, width), BF)]
        + [sds((2, seq, ext), BF)] * 3
        + [sds((4, width), F32), sds((2, ext), F32)],
        [
            pltpu.VMEM(out_scratch, BF),
            pltpu.VMEM((seq, width), F32),
            pltpu.VMEM((seq, width), BF),
            pltpu.VMEM((seq, width), BF),
            pltpu.VMEM((seq, width), BF),
            pltpu.VMEM((seq, ext), BF),
            pltpu.VMEM((seq, ext), BF),
            pltpu.VMEM((seq, ext), BF),
            pltpu.VMEM((seq, width), F32),
            pltpu.VMEM((seq, width), BF),
            pltpu.VMEM((seq, ext), BF),
            pltpu.VMEM((seq, ext), BF),
            pltpu.VMEM((seq, ext), BF),
            pltpu.VMEM((seq, ext), BF),
            pltpu.VMEM((4, width), F32),
            pltpu.VMEM((2, ext), F32),
        ],
        "attn_backward",
        2 * seq * width * ext + 40 * seq * seq * ext,
        aliases={7 + i: i for i in range(n_prev)},
        smem=(keep,),
        vmem_ins=(nv,),
    )


def store_blocks(ids_ref, out_s, value, nd, aligned):
    width = value.shape[1]
    bd = width // nd
    if not aligned:
        out_s[...] = value
        return
    for p in range(nd):
        cols = pl.ds(pl.multiple_of(ids_ref[2 + p] * bd, 128), bd)
        out_s[:, cols] = value[:, p * bd : (p + 1) * bd]


def finish_layer(ids, keep, nv, middle, part, recv, nd, aligned):
    seq, width = middle.shape[1:]

    def body(small, ins, outs, scratch, loads):
        ids_ref, keep_ref, nv_ref = small
        mine = ids_ref[0]
        mid_s, part_s, recv_s, out_s = scratch
        loads.wait(
            loads.start(
                [
                    (ins[0].at[mine], mid_s),
                    (ins[1].at[mine], part_s),
                    (ins[2].at[mine], recv_s),
                ]
            )
        )
        total = part_s[...].astype(F32) + recv_s[...].astype(F32) + nv_ref[5:6, :]
        value = (mid_s[...] + keep_ref[mine] * total).astype(BF)
        store_blocks(ids_ref, out_s, value, nd, aligned)
        loads.wait(loads.start([(out_s, outs[0])]))

    return call(
        body,
        [middle, part, recv],
        [sds((seq, width), BF)],
        [
            pltpu.VMEM((seq, width), F32),
            pltpu.VMEM((seq, width), BF),
            pltpu.VMEM((seq, width), BF),
            pltpu.VMEM((seq, width), BF),
        ],
        "finish_layer",
        0,
        smem=(ids, keep),
        vmem_ins=(nv,),
    )[0]


def finish_tokens(ids, nv, tok, part, recv, gmid, nd, aligned):
    seq, width = tok.shape[1:]

    def body(small, ins, outs, scratch, loads):
        ids_ref, nv_ref = small
        mine = ids_ref[0]
        tok_s, part_s, recv_s, mid_s, out_s, cs_s = scratch
        groups = [
            loads.start(
                [(ins[0].at[a], tok_s.at[a]), (ins[1].at[a], part_s.at[a]), (ins[2].at[a], recv_s.at[a])]
            )
            for a in range(2)
        ]
        g_mid = loads.start([(ins[3].at[mine], mid_s)])
        loads.wait(g_mid)
        for group in groups:
            loads.wait(group)
        for i in range(2):
            a = mine if i == 0 else 1 - mine
            hat, inverse = norm_parts(tok_s[a].astype(F32))
            grad_one = part_s[a].astype(F32) + recv_s[a].astype(F32)
            gain_sum = jnp.sum(grad_one * hat, axis=0, keepdims=True)
            shift_sum = jnp.sum(grad_one, axis=0, keepdims=True)
            if i == 0:
                cs_s[0:1, :] = gain_sum
                cs_s[1:2, :] = shift_sum
                value = mid_s[...] + norm_back(grad_one, hat, inverse, nv_ref[0:1, :])
                store_blocks(ids_ref, out_s, value.astype(BF), nd, aligned)
            else:
                cs_s[0:1, :] = cs_s[0:1, :] + gain_sum
                cs_s[1:2, :] = cs_s[1:2, :] + shift_sum
        loads.wait(loads.start([(out_s, outs[0]), (cs_s, outs[1])]))

    return call(
        body,
        [tok, part, recv, gmid],
        [sds((seq, width), BF), sds((2, width), F32)],
        [
            pltpu.VMEM((2, seq, width), BF),
            pltpu.VMEM((2, seq, width), BF),
            pltpu.VMEM((2, seq, width), BF),
            pltpu.VMEM((seq, width), F32),
            pltpu.VMEM((seq, width), BF),
            pltpu.VMEM((2, width), F32),
        ],
        "finish_tokens",
        0,
        smem=(ids,),
        vmem_ins=(nv,),
    )


class Grid3:
    def __init__(self, dp, tx):
        self.dp, self.tx = dp, tx
        self.y = 2 if dp % 2 == 0 else 1
        self.z = dp // self.y

    def send_z(self, value, k):
        return lax.ppermute(value, "dp", [(i, i ^ (k * self.y)) for i in range(self.dp)])

    def send_y(self, value, k):
        return lax.ppermute(value, "dp", [(i, i ^ k) for i in range(self.dp)])

    def send_x(self, value, k):
        return lax.ppermute(value, "tx", [(i, i ^ k) for i in range(self.tx)])


def swap_core(value):
    return lax.ppermute(value, "core", [(0, 1), (1, 0)])


def gather(grid, part_a, part_b):
    rows = part_a.shape[0]
    both = jnp.concatenate([part_a, part_b], axis=0)
    all_z = [both] + [grid.send_z(both, k) for k in range(1, grid.z)]
    a_z = jnp.stack([v[:rows] for v in all_z])
    b_z = jnp.stack([v[rows:] for v in all_z])
    a_y = jnp.concatenate([a_z] + [grid.send_y(a_z, k) for k in range(1, grid.y)])
    b_x = jnp.concatenate([b_z] + [grid.send_x(b_z, k) for k in range(1, grid.tx)])
    a_all = [a_y] + [grid.send_x(a_y, k) for k in range(1, grid.tx)]
    b_all = [b_x] + [grid.send_y(b_x, k) for k in range(1, grid.y)]
    return a_all, b_all


def add_low(first, *others):
    total = first.astype(F32)
    for other in others:
        total = total + other.astype(F32)
    return total.astype(BF)


def scatter(grid, a_all, b_all):
    z = grid.z
    a_got = [grid.send_x(a_all[k], k) for k in range(1, grid.tx)]
    b_got = [grid.send_y(b_all[k], k) for k in range(1, grid.y)]
    a_y = [add_low(*[v[k * z : (k + 1) * z] for v in [a_all[0]] + a_got]) for k in range(grid.y)]
    b_x = [add_low(*[v[k * z : (k + 1) * z] for v in [b_all[0]] + b_got]) for k in range(grid.tx)]
    a_got = [grid.send_y(a_y[k], k) for k in range(1, grid.y)]
    b_got = [grid.send_x(b_x[k], k) for k in range(1, grid.tx)]
    both = [
        jnp.concatenate(
            [add_low(*[v[k] for v in [a_y[0]] + a_got]), add_low(*[v[k] for v in [b_x[0]] + b_got])]
        )
        for k in range(z)
    ]
    got = [grid.send_z(both[k], k) for k in range(1, z)]
    total = both[0].astype(F32)
    for value in got:
        total = total + value.astype(F32)
    rows = a_all[0].shape[1]
    return total[:rows], total[rows:]


def xor_blocks(value, mask, axis):
    count = value.shape[axis]
    bit = 1
    while bit < count:
        shape = value.shape
        split = value.reshape(shape[:axis] + (count // (2 * bit), 2, bit) + shape[axis + 1 :])
        turned = jnp.flip(split, axis=axis + 1).reshape(shape)
        value = jnp.where(jnp.bitwise_and(mask, bit) != 0, turned, value)
        bit *= 2
    return value


def pad_cols(value, width):
    return jnp.pad(value, ((0, 0), (0, width - value.shape[1])))


def per_device(
    tokens,
    cotangent,
    image_mask,
    norm_gains,
    norm_shifts,
    w_qkv,
    b_qv,
    w_out,
    w_up,
    up_bias,
    w_down,
    *,
    dp,
    tx,
):
    grid = Grid3(dp, tx)
    y_n, z_n = grid.y, grid.z
    core = lax.axis_index("core").astype(jnp.int32)
    me_d = lax.axis_index("dp").astype(jnp.int32)
    me_x = lax.axis_index("tx").astype(jnp.int32)
    seq, width = tokens.shape
    _, bd, hw = w_qkv.shape
    fw = w_up.shape[1]
    ext, hid = tx * hw, tx * fw
    hh, fh = hw // 2, fw // 2
    aligned = bd % 128 == 0 and hh % 128 == 0 and fh % 128 == 0
    rel = [kz * y_n + ky for ky in range(y_n) for kz in range(z_n)]

    def from_abs(value, axis):
        shape = value.shape
        value = value.reshape(shape[:axis] + (z_n, y_n) + shape[axis + 1 :])
        return jnp.swapaxes(value, axis, axis + 1).reshape(shape)

    def to_rel(value, axis):
        shape = value.shape
        value = value.reshape(shape[:axis] + (y_n, z_n) + shape[axis + 1 :])
        return jnp.swapaxes(value, axis, axis + 1).reshape(shape)

    ids = jnp.stack([core, me_d] + [jnp.bitwise_xor(me_d, k) for k in rel])
    keep = lax.dynamic_slice(image_mask, (2 * me_x,), (2,)).astype(F32)

    lane = max(bd, hh)
    small = jnp.concatenate(
        [
            pad_cols(norm_gains, lane),
            pad_cols(norm_shifts, lane),
            pad_cols(b_qv, lane),
            pad_cols(up_bias[None], lane),
            jnp.zeros((7, lane), BF),
        ]
    )
    qkv_a = pad_cols(w_qkv[:, :, :hh].reshape(3 * bd, hh), lane)
    qkv_b = pad_cols(w_qkv[:, :, hh:].reshape(3 * bd, hh), lane)
    first_a = jnp.concatenate([qkv_a, pad_cols(w_out[:hh], lane), small])
    first_b = jnp.concatenate([qkv_b, pad_cols(w_out[hh:], lane)])
    c1a, c1b = gather(grid, first_a, first_b)
    upa, upb = gather(grid, w_up[:, :fh], w_up[:, fh:])
    dna, dnb = gather(grid, w_down[:fh], w_down[fh:])

    tok_other, cot_other = swap_core(tokens), swap_core(cotangent)
    if aligned:
        tok, cot = arrange_pair(ids, [tokens, cotangent], [tok_other, cot_other], dp)
    else:

        def arrange(own, other):
            pair = jnp.where(core == 0, jnp.stack([own, other]), jnp.stack([other, own]))
            pair = xor_blocks(pair.reshape(2, seq, dp, bd), me_d, 2)
            return from_abs(pair, 2).reshape(2, seq, width)

        tok, cot = arrange(tokens, tok_other), arrange(cotangent, cot_other)
    grad_top = cot * keep.astype(BF)[:, None, None]

    row0 = 3 * bd + hh
    nv = (
        c1a[0][:, row0 : row0 + 6, :bd].transpose(1, 0, 2).reshape(6, width).astype(F32)
    )
    tail = jnp.stack([v[:, row0 + 6 : row0 + 9] for v in c1a])
    tail = xor_blocks(to_rel(tail, 1), me_d, 1)
    bq = (
        tail[:, :, :2, : hw // dp].transpose(2, 0, 1, 3).reshape(2, ext).astype(F32)
    )
    bu = tail[:, :, 2, : fw // dp].reshape(1, hid).astype(F32)

    if aligned:
        wq_plan, wo_plan, up_plan, dn_plan = [], [], [], []
        for kx in range(tx):
            for i in range(3):
                src = slice(i * bd, (i + 1) * bd)
                cols = slice(kx * hw, kx * hw + hh)
                wq_plan.append((kx, (slice(None), src), 0, (i, slice(None), slice(None), cols)))
                cols = slice(kx * hw + hh, (kx + 1) * hw)
                for ky in range(y_n):
                    own = slice(kx * z_n, (kx + 1) * z_n)
                    dst = (i, slice(ky * z_n, (ky + 1) * z_n), slice(None), cols)
                    wq_plan.append((tx + ky, (own, src), 0, dst))
            src = slice(3 * bd, 3 * bd + hh)
            for ky in range(y_n):
                for kz in range(z_n):
                    p = ky * z_n + kz
                    cols = slice(p * bd, (p + 1) * bd)
                    wo_plan.append((kx, (p, src), 0, (slice(kx * hw, kx * hw + hh), cols)))
                    dst = (slice(kx * hw + hh, (kx + 1) * hw), cols)
                    wo_plan.append((tx + ky, (kx * z_n + kz, src), 0, dst))
                    dst = (slice(kx * fw, kx * fw + fh), cols)
                    dn_plan.append((kx, (p,), 0, dst))
                    dst = (slice(kx * fw + fh, (kx + 1) * fw), cols)
                    dn_plan.append((tx + ky, (kx * z_n + kz,), 0, dst))
            dst = (slice(None), slice(kx * fw, kx * fw + fh))
            up_plan.append((kx, (slice(None),), 0, dst))
            for ky in range(y_n):
                rows = slice(kx * z_n * bd, (kx + 1) * z_n * bd)
                dst = (
                    slice(ky * z_n * bd, (ky + 1) * z_n * bd),
                    slice(kx * fw + fh, (kx + 1) * fw),
                )
                up_plan.append((tx + ky, (rows,), 0, dst))
        c1 = c1a + c1b
        wqkv = (c1, wq_plan, (3, dp, bd, ext))
        wout = (c1, wo_plan, (ext, width))
        up = [v.reshape(-1, fh) for v in upa + upb]
        wup = (up, up_plan, (width, hid))
        wdown = (dna + dnb, dn_plan, (hid, width))
    else:

        def whole(a_all, b_all):
            a = jnp.stack(a_all)
            b = jnp.stack(b_all).reshape((y_n, tx, z_n) + b_all[0].shape[1:])
            b = b.transpose(1, 0, 2, 3, 4).reshape(a.shape[:2] + b.shape[3:])
            return jnp.stack([a, b], axis=1)

        a_rows = first_b.shape[0]
        c1 = whole([v[:, :a_rows] for v in c1a], c1b)
        qkv = c1[:, :, :, : 3 * bd, :hh].reshape(tx, 2, dp, 3, bd, hh)
        qkv = qkv.transpose(3, 2, 4, 0, 1, 5).reshape(3, dp, bd, ext)
        out = c1[:, :, :, 3 * bd :, :bd].transpose(0, 1, 3, 2, 4).reshape(ext, width)
        up = whole(upa, upb).transpose(2, 3, 0, 1, 4).reshape(width, hid)
        down = whole(dna, dnb).transpose(0, 1, 3, 2, 4).reshape(hid, width)
        wqkv = ([qkv], [(0, (slice(None),), 0, (slice(None),))], qkv.shape)
        wout = ([out], [(0, (slice(None),), 0, (slice(None),))], out.shape)
        wup = ([up], [(0, (slice(None),), 0, (slice(None),))], up.shape)
        wdown = ([down], [(0, (slice(None),), 0, (slice(None),))], down.shape)

    rows2 = 2 * seq

    state, parts = None, []
    for image in range(2):
        res = attn_forward(image, tok, nv, bq, wqkv, wout, state)
        state = res[:5]
        parts.append((res[5], swap_core(res[5])))
    first, q, k, v, att = state
    state = None
    for image in range(2):
        part, recv = parts[image]
        state = mlp_up(image, tok, part, recv, keep, nv, bu, wup, state)
    middle, second, act, dact = state
    flat = lambda value: value.reshape(rows2, value.shape[2])
    act2, sec2, grad2 = flat(act), flat(second), flat(grad_top)

    def down_tasks(kxs, kys):
        tasks, shapes = [], []
        for n, kx in enumerate(kxs):
            stores = [
                (n, (p,), slice(None), slice(p * bd, (p + 1) * bd)) for p in range(dp)
            ]
            tasks.append((slice(kx * fw, kx * fw + fh), 0, slice(0, width), stores))
            shapes.append((dp, fh, bd))
        for n, ky in enumerate(kys):
            for kx in range(tx):
                stores = [
                    (len(kxs) + n, (kx * z_n + kz,), slice(None), slice(kz * bd, (kz + 1) * bd))
                    for kz in range(z_n)
                ]
                cols = slice(ky * z_n * bd, (ky + 1) * z_n * bd)
                tasks.append((slice(kx * fw + fh, (kx + 1) * fw), 0, cols, stores))
            shapes.append((tx * z_n, fh, bd))
        return tasks, shapes

    def out_tasks(kxs, kys):
        tasks, shapes = [], []
        for n, kx in enumerate(kxs):
            stores = [
                (n, (p,), slice(None), slice(p * bd, (p + 1) * bd)) for p in range(dp)
            ]
            tasks.append((slice(kx * hw, kx * hw + hh), 0, slice(0, width), stores))
            shapes.append((dp, hh, bd))
        for n, ky in enumerate(kys):
            for kx in range(tx):
                stores = [
                    (len(kxs) + n, (kx * z_n + kz,), slice(None), slice(kz * bd, (kz + 1) * bd))
                    for kz in range(z_n)
                ]
                cols = slice(ky * z_n * bd, (ky + 1) * z_n * bd)
                tasks.append((slice(kx * hw + hh, (kx + 1) * hw), 0, cols, stores))
            shapes.append((tx * z_n, hh, bd))
        return tasks, shapes

    def up_tasks(kxs, kys):
        tasks, shapes = [], []
        for n, kx in enumerate(kxs):
            stores = [
                (n, (p,), slice(p * bd, (p + 1) * bd), slice(None)) for p in range(dp)
            ]
            tasks.append((slice(0, width), 0, slice(kx * fw, kx * fw + fh), stores))
            shapes.append((dp, bd, fh))
        for n, ky in enumerate(kys):
            for kx in range(tx):
                stores = [
                    (len(kxs) + n, (kx * z_n + kz,), slice(kz * bd, (kz + 1) * bd), slice(None))
                    for kz in range(z_n)
                ]
                rows = slice(ky * z_n * bd, (ky + 1) * z_n * bd)
                tasks.append((rows, 0, slice(kx * fw + fh, (kx + 1) * fw), stores))
            shapes.append((tx * z_n, bd, fh))
        return tasks, shapes

    def qkv_tasks(kxs, kys):
        tasks, shapes = [], []
        for n, kx in enumerate(kxs):
            for i in range(3):
                stores = [
                    (n, (p, slice(i * bd, (i + 1) * bd)), slice(p * bd, (p + 1) * bd), slice(None))
                    for p in range(dp)
                ]
                tasks.append((slice(0, width), i, slice(kx * hw, kx * hw + hh), stores))
            shapes.append((dp, 3 * bd, hh))
        for n, ky in enumerate(kys):
            for kx in range(tx):
                for i in range(3):
                    stores = [
                        (
                            len(kxs) + n,
                            (kx * z_n + kz, slice(i * bd, (i + 1) * bd)),
                            slice(kz * bd, (kz + 1) * bd),
                            slice(None),
                        )
                        for kz in range(z_n)
                    ]
                    rows = slice(ky * z_n * bd, (ky + 1) * z_n * bd)
                    tasks.append((rows, i, slice(kx * hw + hh, (kx + 1) * hw), stores))
            shapes.append((tx * z_n, 3 * bd, hh))
        return tasks, shapes

    def reduce_grad(make, left, right, name):
        away_x, away_y = list(range(1, tx)), list(range(1, y_n))
        sent = weight_grad(left, right, *make(away_x, away_y), name + "_send")
        kept = weight_grad(left, right, *make([0], [0]), name + "_keep")
        return scatter(
            grid, [kept[0]] + list(sent[: tx - 1]), [kept[1]] + list(sent[tx - 1 :])
        )

    down_a, down_b = reduce_grad(down_tasks, act2, [grad2], "down_grad")
    low_pre, bias_up = mlp_back(grad2, flat(dact), wdown)
    parts = []
    for image in range(2):
        span = (image * seq, (image + 1) * seq)
        part = rows_times([low_pre], span, wup, NT, False, width, "grad_two")
        parts.append((part, swap_core(part)))
    up_a, up_b = reduce_grad(up_tasks, sec2, [low_pre], "up_grad")
    mlp_part = rows_times([act2], (0, rows2), wdown, NN, False, width, "mlp_out")
    mlp_part = mlp_part.reshape(2, seq, width)
    mlp_recv = swap_core(mlp_part)
    layer_out = finish_layer(ids, keep, nv, middle, mlp_part, mlp_recv, dp, aligned)

    state, sums = None, []
    for image in range(2):
        part, recv = parts[image]
        res = attn_backward(image, middle, part, recv, cot, keep, nv, wout, q, k, v, state)
        state = res[:5]
        sums.append(res[5:])
    gmid, gattn, dq, dk, dv = state
    out_a, out_b = reduce_grad(out_tasks, flat(att), [flat(gattn)], "out_grad")
    low_proj = [flat(dq), flat(dk), flat(dv)]
    qkv_ga, qkv_gb = reduce_grad(qkv_tasks, flat(first), low_proj, "qkv_grad")
    one_part = rows_times(low_proj, (0, rows2), wqkv, NT, True, width, "grad_one")
    one_part = one_part.reshape(2, seq, width)
    one_recv = swap_core(one_part)
    grad_tokens, one_sums = finish_tokens(ids, nv, tok, one_part, one_recv, gmid, dp, aligned)
    if not aligned:

        def restore(value):
            value = xor_blocks(to_rel(value.reshape(seq, dp, bd), 1), me_d, 1)
            return value.reshape(seq, width)

        layer_out, grad_tokens = restore(layer_out), restore(grad_tokens)

    col = sums[0][0] + sums[1][0]
    bias_qv = sums[0][1] + sums[1][1]
    vec = jnp.stack([one_sums[0], col[0], one_sums[1], col[1], col[2], col[3]])
    wide = max(bd, hw // dp, fw // dp)
    vec = vec.reshape(6, dp, bd).transpose(1, 0, 2)
    vec = jnp.pad(vec, ((0, 0), (0, 0), (0, wide - bd)))
    bias_qv = bias_qv.reshape(2, tx, dp, hw // dp).transpose(2, 1, 0, 3).reshape(dp, 2 * tx, -1)
    bias_up = bias_up.reshape(tx, dp, fw // dp).transpose(1, 0, 2)
    bias = jnp.concatenate(
        [
            jnp.pad(bias_qv, ((0, 0), (0, 0), (0, wide - hw // dp))),
            jnp.pad(bias_up, ((0, 0), (0, 0), (0, wide - fw // dp))),
        ],
        axis=1,
    )
    bias = from_abs(xor_blocks(bias, me_d, 0), 0)
    both = jnp.concatenate([vec, bias], axis=1)
    got = [both] + [grid.send_x(both, k) for k in range(1, tx)]
    vec = sum(value[:, :6] for value in got)
    bqv_mine = sum(value[:, 6 + 2 * k : 8 + 2 * k] for k, value in enumerate(got))
    bup_mine = sum(
        value[:, 6 + 2 * tx + k : 7 + 2 * tx + k] for k, value in enumerate(got)
    )
    both = jnp.concatenate([vec, bqv_mine, bup_mine], axis=1)
    both = both[:z_n] + sum(
        grid.send_y(both[k * z_n : (k + 1) * z_n], k) for k in range(1, y_n)
    )
    both = both[0] + sum(grid.send_z(both[k], k) for k in range(1, z_n))
    share = bd // (2 * tx)
    mine = lax.dynamic_slice(both[:6, :bd], (0, (2 * me_x + core) * share), (6, share))

    grad_qkv = jnp.concatenate(
        [qkv_ga.reshape(3, bd, hh), qkv_gb.reshape(3, bd, hh)], axis=2
    )
    grad_out = jnp.concatenate([out_a, out_b], axis=0)
    grad_up = jnp.concatenate([up_a, up_b], axis=1)
    grad_down = jnp.concatenate([down_a, down_b], axis=0)
    return (
        layer_out,
        grad_tokens,
        mine[:2],
        mine[2:6],
        grad_qkv,
        both[6:8, : hw // dp],
        grad_out,
        grad_up,
        both[8, : fw // dp],
        grad_down,
    )


def solution(mesh):
    dp, tensor = mesh.shape["dp"], mesh.shape["tensor"]
    split = Mesh(mesh.devices.reshape(dp, tensor // 2, 2), ("dp", "tx", "core"))
    every = ("dp", "tx", "core")
    tensor_axes = ("tx", "core")
    in_specs = (
        P(every, None),
        P(every, None),
        P("dp"),
        P(None, "dp"),
        P(None, "dp"),
        P(None, "dp", tensor_axes),
        P(None, ("tx", "core", "dp")),
        P(tensor_axes, "dp"),
        P("dp", tensor_axes),
        P(("tx", "core", "dp")),
        P(tensor_axes, "dp"),
    )
    out_specs = (
        P(every, None),
        P(every, None),
        P(None, every),
        P(None, every),
        P(None, "dp", tensor_axes),
        P(None, ("tx", "core", "dp")),
        P(tensor_axes, "dp"),
        P("dp", tensor_axes),
        P(("tx", "core", "dp")),
        P(tensor_axes, "dp"),
    )
    return jax.shard_map(
        functools.partial(per_device, dp=dp, tx=tensor // 2),
        mesh=split,
        in_specs=in_specs,
        out_specs=out_specs,
        check_vma=False,
    )
```

time: 1250 us -> 644 us (0.52)
  waiting for transfers between devices: 779 us -> 132 us
  Pallas kernels: 0 us -> 353 us
  matrix products: 167 us -> 0 us
  blocking collectives: 126 us -> 0 us
  starting transfers between devices: 1.37 us -> 79.7 us
  local copies, waits for them, and re-layouts: 95.9 us -> 37.5 us
  other arithmetic: 55 us -> 32.6 us
  between operations: 15.9 us -> 2.14 us
    unnamed x24 -> x0, waiting for transfers between devices: 446 us -> none
    pallas_call x0 -> x22, Pallas kernels: none -> 353 us  [call(): pl.pallas_call(kernel, out_shape=outs, in_specs=[pl.BlockSpec(memory_spac...]
    reduce_scatter x5 -> x0, waiting for transfers between devices: 179 us -> none  [the longest x1 47.6 us: per_device(): lax.psum_scatter(one_part.astype(jnp.bfloat16), 'tensor', scatter_dimensi...]
    dot_general x40 -> x0, matrix products: 167 us -> none  [the longest x8 18.5 us: scores_of(): jnp.einsum('qhd,khd->hqk', query_blk, key_blk, preferred_element_type=jnp...]
    all_gather x7 -> x0, waiting for transfers between devices: 154 us -> none  [the longest x1 40.6 us: per_device(): lax.all_gather(w_down, 'dp', axis=1, tiled=True)]
    ppermute x0 -> x62, waiting for transfers between devices: none -> 132 us  [the longest x24 63.8 us: send_z(): lax.ppermute(value, 'dp', [(i, i ^ k * self.y) for i in range(self.dp)])]
    all_gather x5 -> x0, blocking collectives: 104 us -> none  [the longest x1 27 us: per_device(): lax.all_gather(w_out, 'dp', axis=1, tiled=True)]
    ppermute x0 -> x62, starting transfers between devices: none -> 79.7 us  [the longest x24 45.9 us: send_z(): lax.ppermute(value, 'dp', [(i, i ^ k * self.y) for i in range(self.dp)])]
  transfers between devices with their start and end apart: 18 -> 62, of which waited for: 14 -> 18; matrix products, arithmetic and copies ran while one was open for 16% -> 9% of each run, Pallas kernels for 0% -> 55%
where the time goes in v1:
time: 644 us; the launch traced here: 637 us
  Pallas kernels  353 us (55%)
  waiting for transfers between devices  132 us (20%)
  starting transfers between devices  79.7 us (12%)
  local copies, waits for them, and re-layouts  37.5 us (6%)
  other arithmetic  32.6 us (5%)
    pallas_call x22, Pallas kernels, call(): pl.pallas_call(kernel, out_shape=outs, in_specs=[pl.BlockSpec(memory_spac...  353 us
    ppermute x24, waiting for transfers between devices, send_z(): lax.ppermute(value, 'dp', [(i, i ^ k * self.y) for i in range(self.dp)])  63.8 us
    ppermute x24, starting transfers between devices, send_z(): lax.ppermute(value, 'dp', [(i, i ^ k * self.y) for i in range(self.dp)])  45.9 us
    ppermute x15, waiting for transfers between devices, send_x(): return lax.ppermute(value, 'tx', [(i, i ^ k) for i in range(self.tx)])  37.9 us
    ppermute x15, waiting for transfers between devices, send_y(): return lax.ppermute(value, 'dp', [(i, i ^ k) for i in range(self.dp)])  30.8 us
    ppermute x15, starting transfers between devices, send_x(): return lax.ppermute(value, 'tx', [(i, i ^ k) for i in range(self.tx)])  16.9 us
    convert_element_type x16, other arithmetic, add_low(): return total.astype(BF)  15.1 us
    ppermute x15, starting transfers between devices, send_y(): return lax.ppermute(value, 'dp', [(i, i ^ k) for i in range(self.dp)])  14.8 us
  transfers between devices with their start and end apart: 62, of which 18 were waited for; matrix products, arithmetic and copies ran while one was open for 9% of the time, Pallas kernels for 55%

profile of v1, /device:TPU:0, one launch (start us, length us, event | category | flops | bytes accessed | tf_op | source)
XLA Modules:
  0.0 637.5 jit_solution(1116266694529141180)
XLA Ops:
  3.1 5.1 concatenate.132
  8.2 3.0 collective-permute-start
  11.3 2.6 collective-permute-start.1
  16.2 3.5 collective-permute-start.12
  19.8 1.8 constant_dynamic-update-slice_fusion.29
  21.6 1.7 slice_bitcast_fusion.18
  26.5 9.0 %collective-permute-done.11 = bf16[256,512]{1,0:T(8,128)(2,1)} collective-permute-done((bf16[256,512]{1,0:T(8,128)(2,1)}, bf16[256,512]{1,0:T(8,128)(2,1)}, u32[]{:S(2)}, u32[]{:S(2)}) %collective-permute-start.11) | collective-permute-done | bytes 262176 | tf_op jit(solution)/shard_map/ppermute | solution.py:596
  35.5 3.3 collective-permute-start.13
  39.8 16.0 %collective-permute-done.12 = bf16[256,512]{1,0:T(8,128)(2,1)} collective-permute-done((bf16[256,512]{1,0:T(8,128)(2,1)}, bf16[256,512]{1,0:T(8,128)(2,1)}, u32[]{:S(2)}, u32[]{:S(2)}) %collective-permute-start.12) | collective-permute-done | bytes 262176 | tf_op jit(solution)/shard_map/ppermute | solution.py:596
  56.8 4.7 collective-permute-start.19
  61.5 2.4 collective-permute-done.18
  63.8 3.0 collective-permute-start.20
  67.9 11.6 %collective-permute-done.19 = bf16[1024,128]{1,0:T(8,128)(2,1)S(1)} collective-permute-done((bf16[1024,128]{1,0:T(8,128)(2,1)S(1)}, bf16[1024,128]{1,0:T(8,128)(2,1)S(1)}, u32[]{:S(2)}, u32[]{:S(2)}) %collective-permute-start.19) | collective-permute-done | bytes 262176 | tf_op jit(solution)/shard_map/ppermute | solution.py:596
  87.1 1.6 collective-permute-start.16
  92.0 19.0 %collective-permute-done.3 = bf16[4,528,128]{2,1,0:T(8,128)(2,1)S(1)} collective-permute-done((bf16[4,528,128]{2,1,0:T(8,128)(2,1)S(1)}, bf16[4,528,128]{2,1,0:T(8,128)(2,1)S(1)}, u32[]{:S(2)}, u32[]{:S(2)}) %collective-permute-start.3) | collective-permute-done | bytes 540704 | tf_op jit(solution)/shard_map/ppermute | solution.py:599
  115.4 1.6 collective-permute-start.21
  117.0 31.2 %collective-permute-done.7 = bf16[4,512,128]{2,1,0:T(8,128)(2,1)S(1)} collective-permute-done((bf16[4,512,128]{2,1,0:T(8,128)(2,1)S(1)}, bf16[4,512,128]{2,1,0:T(8,128)(2,1)S(1)}, u32[]{:S(2)}, u32[]{:S(2)}) %collective-permute-start.7) | collective-permute-done | bytes 524320 | tf_op jit(solution)/shard_map/ppermute | solution.py:602
  152.7 1.6 collective-permute-start.23
  156.2 146.8 %arrange_pair.1 = (bf16[2,584,1024]{2,1,0:T(8,128)(2,1)}, bf16[2,584,1024]{2,1,0:T(8,128)(2,1)}) custom-call(s32[10]{0:T(128)} %stack.143.refs_0_, bf16[584,1024]{1,0:T(8,128)(2,1)} %refs_1_.1, bf16[584,1024]{1,0:T(8,128)(2,1)} %refs_2_.1, bf16[584,1024]{1,0:T(8,128)(2,1)} %copy-done.8, bf16[584,1024]{1,0:T(8,128)(2,1)} %copy-done.9), custom_call_target="tpu_custom_call" | custom-call | bytes 9568256 | tf_op jit(solution)/shard_map/arrange_pair/pallas_call | solution.py:57
  305.3 15.3 %attn_forward.2 = (bf16[2,584,1024]{2,1,0:T(8,128)(2,1)}, bf16[2,584,512]{2,1,0:T(8,128)(2,1)}, bf16[2,584,512]{2,1,0:T(8,128)(2,1)}, bf16[2,584,512]{2,1,0:T(8,...) custom-call(f32[6,1024]{1,0:T(8,128)} %convert_bitcast_fusion.refs_0_.refs_1_.refs_2_, ...), custom_call_target="tpu_custom_call" | custom-call | flops 5243404288 | bytes 19283968 | tf_op jit(solution)/shard_map/attn_forward/pallas_call | solution.py:57
  320.7 15.6 %attn_forward.3 = (bf16[2,584,1024]{2,1,0:T(8,128)(2,1)}, bf16[2,584,512]{2,1,0:T(8,128)(2,1)}, bf16[2,584,512]{2,1,0:T(8,128)(2,1)}, bf16[2,584,512]{2,1,0:T(8,...) custom-call(f32[6,1024]{1,0:T(8,128)} %convert_bitcast_fusion.refs_0, ...), custom_call_target="tpu_custom_call", output_to_operand_aliasing={{0}: (3, {}), {1}: (4, {}), {2}: (5, {}), {3}: (6, {}), {4}... | custom-call | flops 5243404288 | bytes 26460160 | tf_op jit(solution)/shard_map/attn_forward/pallas_call | solution.py:57
  337.6 2.0 constant_dynamic-update-slice_fusion.20.refs_1_.refs_2_
  340.7 1.9 constant_dynamic-update-slice_fusion.25.refs_3_.refs_4_
  344.1 1.6 broadcast_multiply_fusion
  346.3 10.6 %mlp_up.2 = (f32[2,584,1024]{2,1,0:T(8,128)}, bf16[2,584,1024]{2,1,0:T(8,128)(2,1)}, bf16[2,584,2048]{2,1,0:T(8,128)(2,1)}, bf16[2,584,2048]{2,1,0:T(8,128)(2,1)}) custom-call(f32[2]{0:T(128)} %get-tuple-element.123.refs_0_.refs_1_, f32[6,1024]{1,0:T(8,128)} %convert_bitcast_fusion.refs_0_.refs_1_.refs_2_, f32[1,2048]{1,0:T(1,128)} %bitcast.330, ...), custom_call_target="tpu_custom_call" | custom-call | flops 2449473536 | bytes 25722880 | tf_op jit(solution)/shard_map/mlp_up/pallas_call | solution.py:57
  356.9 10.5 %mlp_up.3 = (f32[2,584,1024]{2,1,0:T(8,128)}, bf16[2,584,1024]{2,1,0:T(8,128)(2,1)}, bf16[2,584,2048]{2,1,0:T(8,128)(2,1)}, bf16[2,584,2048]{2,1,0:T(8,128)(2,1)}) custom-call(f32[2]{0:T(128)} %get-tuple-element.123.refs_0_.refs_1_, ...), custom_call_target="tpu_custom_call", output_to_operand_aliasing={{0}: (6, {}), {1}: (7, {}), {2}: (8, {}), {3}: (9, {})} | custom-call | flops 2449473536 | bytes 42467328 | tf_op jit(solution)/shard_map/mlp_up/pallas_call | solution.py:57
  367.4 7.3 %down_grad_send.1 = (bf16[8,512,128]{2,1,0:T(8,128)(2,1)}, bf16[8,512,128]{2,1,0:T(8,128)(2,1)}) custom-call(bf16[1168,2048]{1,0:T(8,128)(2,1)} %bitcast.276, bf16[1168,1024]{1,0:T(8,128)(2,1)} %bitcast.280), custom_call_target="tpu_custom_call" | custom-call | flops 2449473536 | bytes 9273344 | tf_op jit(solution)/shard_map/down_grad_send/pallas_call | solution.py:57
  376.2 11.9 %mlp_back.1 = (bf16[1168,2048]{1,0:T(8,128)(2,1)}, f32[1,2048]{1,0:T(1,128)}) custom-call(bf16[1168,1024]{1,0:T(8,128)(2,1)} %bitcast.281, bf16[1168,2048]{1,0:T(8,128)(2,1)} %bitcast.279, bf16[8,512,128]{2,1,0:T(8,128)(2,1)} %constant_dynamic-update-slice_fusion.20.refs_1_.refs_2_, bf16[8,512,128]{2,1,0:T(8,128)(2,1)} %collective-permute-done.22.refs_2_.refs_3_, ...), custom_call_target="tpu_custom_call" | custom-call | flops 4898947072 | bytes 16162816 | tf_op jit(solution)/shard_map/mlp_back/pallas_call | solution.py:57
  388.1 6.7 %grad_two.3.refs_3_ = bf16[584,1024]{1,0:T(8,128)(2,1)} custom-call(bf16[1168,2048]{1,0:T(8,128)(2,1)} %get-tuple-element.82.refs_0_.refs_1_, bf16[1024,512]{1,0:T(8,128)(2,1)} %bitcast.268, bf16[1024,512]{1,0:T(8,128)(2,1)} %bitcast.272, bf16[1024,512]{1,0:T(8,128)(2,1)} %bitcast.264, bf16[1024,512]{1,0:T(8,128)(2,1)} %bitcast.45.refs_9_.refs_13_.refs_4_), custom_call_target="tpu_custom_call" | custom-call | flops 2449473536 | bytes 10174464 | tf_op jit(solution)/shard_map/grad_two/pallas_call | solution.py:57
  394.8 7.2 %up_grad_send.1 = (bf16[8,128,512]{2,1,0:T(8,128)(2,1)}, bf16[8,128,512]{2,1,0:T(8,128)(2,1)}) custom-call(bf16[1168,1024]{1,0:T(8,128)(2,1)} %bitcast.287, bf16[1168,2048]{1,0:T(8,128)(2,1)} %get-tuple-element.82.refs_0_.refs_1_), custom_call_target="tpu_custom_call" | custom-call | flops 2449473536 | bytes 9273344 | tf_op jit(solution)/shard_map/up_grad_send/pallas_call | solution.py:57
  404.7 10.4 %mlp_out.1 = bf16[1168,1024]{1,0:T(8,128)(2,1)} custom-call(bf16[1168,2048]{1,0:T(8,128)(2,1)} %bitcast.277, bf16[8,512,128]{2,1,0:T(8,128)(2,1)} %constant_dynamic-update-slice_fusion.20.refs_1_.refs_2_, bf16[8,512,128]{2,1,0:T(8,128)(2,1)} %collective-permute-done.22.refs_2_.refs_3_, ...), custom_call_target="tpu_custom_call" | custom-call | flops 4898947072 | bytes 11370496 | tf_op jit(solution)/shard_map/mlp_out/pallas_call | solution.py:57
  415.1 7.1 %down_grad_keep.1 = (bf16[8,512,128]{2,1,0:T(8,128)(2,1)}, bf16[8,512,128]{2,1,0:T(8,128)(2,1)}) custom-call(bf16[1168,2048]{1,0:T(8,128)(2,1)} %bitcast.278, bf16[1168,1024]{1,0:T(8,128)(2,1)} %bitcast.282), custom_call_target="tpu_custom_call" | custom-call | flops 2449473536 | bytes 9273344 | tf_op jit(solution)/shard_map/down_grad_keep/pallas_call | solution.py:57
  422.2 7.1 %up_grad_keep.1 = (bf16[8,128,512]{2,1,0:T(8,128)(2,1)}, bf16[8,128,512]{2,1,0:T(8,128)(2,1)}) custom-call(bf16[1168,1024]{1,0:T(8,128)(2,1)} %bitcast.288, bf16[1168,2048]{1,0:T(8,128)(2,1)} %get-tuple-element.82.refs_0_.refs_1_), custom_call_target="tpu_custom_call" | custom-call | flops 2449473536 | bytes 9273344 | tf_op jit(solution)/shard_map/up_grad_keep/pallas_call | solution.py:57
  429.3 6.7 %grad_two.2.refs_3_ = bf16[584,1024]{1,0:T(8,128)(2,1)} custom-call(bf16[1168,2048]{1,0:T(8,128)(2,1)} %get-tuple-element.82.refs_0_.refs_1_, bf16[1024,512]{1,0:T(8,128)(2,1)} %bitcast.269, bf16[1024,512]{1,0:T(8,128)(2,1)} %bitcast.273, bf16[1024,512]{1,0:T(8,128)(2,1)} %bitcast.265, bf16[1024,512]{1,0:T(8,128)(2,1)} %bitcast.45.refs_9_.refs_13_.refs_4_), custom_call_target="tpu_custom_call" | custom-call | flops 2449473536 | bytes 10174464 | tf_op jit(solution)/shard_map/grad_two/pallas_call | solution.py:57
  436.9 2.7 add_convert_fusion.3
  442.2 2.4 add_convert_fusion.7
  446.1 2.3 add_convert_fusion.5
  448.4 22.1 %attn_backward.2 = (f32[2,584,1024]{2,1,0:T(8,128)}, bf16[2,584,1024]{2,1,0:T(8,128)(2,1)}, bf16[2,584,512]{2,1,0:T(8,128)(2,1)}, bf16[2,584,512]{2,1,0:T(8,128)...) custom-call(f32[2]{0:T(128)} %get-tuple-element.123.refs_0_.refs_1_, ...), custom_call_target="tpu_custom_call" | custom-call | flops 7597195264 | bytes 28200960 | tf_op jit(solution)/shard_map/attn_backward/pallas_call | solution.py:57
  470.5 21.7 %attn_backward.3 = (f32[2,584,1024]{2,1,0:T(8,128)}, bf16[2,584,1024]{2,1,0:T(8,128)(2,1)}, bf16[2,584,512]{2,1,0:T(8,128)(2,1)}, bf16[2,584,512]{2,1,0:T(8,128)...) custom-call(f32[2]{0:T(128)} %get-tuple-element.123.refs_0_.refs_1_,, ...), custom_call_target="tpu_custom_call", output_to_operand_aliasing={{0}: (9, {}), {1}: (10, {}), {2}: (11, {}), {3}: (12, {}), ... | custom-call | flops 7597195264 | bytes 38965248 | tf_op jit(solution)/shard_map/attn_backward/pallas_call | solution.py:57
  492.2 3.7 out_grad_send.1
  497.9 8.0 %qkv_grad_keep.1 = (bf16[8,384,128]{2,1,0:T(8,128)(2,1)}, bf16[8,384,128]{2,1,0:T(8,128)(2,1)}) custom-call(bf16[1168,1024]{1,0:T(8,128)(2,1)} %bitcast.339, bf16[1168,512]{1,0:T(8,128)(2,1)} %bitcast.293, bf16[1168,512]{1,0:T(8,128)(2,1)} %bitcast.296, bf16[1168,512]{1,0:T(8,128)(2,1)} %bitcast.299), custom_call_target="tpu_custom_call" | custom-call | flops 1837105152 | bytes 7553024 | tf_op jit(solution)/shard_map/qkv_grad_keep/pallas_call | solution.py:57
  506.0 8.3 %grad_one.1 = bf16[1168,1024]{1,0:T(8,128)(2,1)} custom-call(bf16[1168,512]{1,0:T(8,128)(2,1)} %bitcast.294, bf16[1168,512]{1,0:T(8,128)(2,1)} %bitcast.297, bf16[1168,512]{1,0:T(8,128)(2,1)} %bitcast.300, bf16[8,528,128]{2,1,0:T(8,128)(2,1)} %constant_dynamic-update-slice_fusion.refs_3_.refs_7_.refs_8_.refs_12_.refs_9_.refs_14_, ...), custom_call_target="tpu_custom_call" | custom-call | flops 3674210304 | bytes 10240000 | tf_op jit(solution)/shard_map/grad_one/pallas_call | solution.py:57
  514.4 3.8 out_grad_keep.1
  520.3 1.6 collective-permute-start.42
  526.7 5.0 collective-permute-start.59
  534.1 5.0 collective-permute-start.45
  539.2 2.4 collective-permute-start.47
  542.4 2.6 collective-permute-done.45
  545.5 9.4 %collective-permute-done.46 = bf16[256,128]{1,0:T(8,128)(2,1)S(1)} collective-permute-done((bf16[256,128]{1,0:T(8,128)(2,1)S(1)}, bf16[256,128]{1,0:T(8,128)(2,1)S(1)}, u32[]{:S(2)}, u32[]{:S(2)}) %collective-permute-start.46) | collective-permute-done | bytes 65568 | tf_op jit(solution)/shard_map/ppermute | solution.py:596
  557.6 8.3 %qkv_grad_send.1 = (bf16[8,384,128]{2,1,0:T(8,128)(2,1)}, bf16[8,384,128]{2,1,0:T(8,128)(2,1)}) custom-call(bf16[1168,1024]{1,0:T(8,128)(2,1)} %bitcast.340, bf16[1168,512]{1,0:T(8,128)(2,1)} %bitcast.295, bf16[1168,512]{1,0:T(8,128)(2,1)} %bitcast.298, bf16[1168,512]{1,0:T(8,128)(2,1)} %bitcast.301), custom_call_target="tpu_custom_call" | custom-call | flops 1837105152 | bytes 7553024 | tf_op jit(solution)/shard_map/qkv_grad_send/pallas_call | solution.py:57
  567.6 5.1 collective-permute-done.53
  574.1 1.6 convert_add_fusion.3
  575.7 2.1 convert_add_fusion
  577.8 3.9 collective-permute-done.54
  585.1 2.6 collective-permute-done.36
  589.9 5.7 collective-permute-done.35
  595.8 2.4 collective-permute-done.37
  598.4 3.5 collective-permute-start.39
  602.9 4.9 finish_layer.1
  607.9 9.2 %finish_tokens.1 = (bf16[584,1024]{1,0:T(8,128)(2,1)}, f32[2,1024]{1,0:T(2,128)}) custom-call(s32[10]{0:T(128)} %stack.143.refs_0_, f32[6,1024]{1,0:T(8,128)} %convert_bitcast_fusion.refs_0_.refs_1_.refs_2_, bf16[2,584,1024]{2,1,0:T(8,128)(2,1)} %get-tuple-element.66.refs_2_.refs_3_, bf16[2,584,1024]{2,1,0:T(8,128)(2,1)} %bitcast.286, ...), custom_call_target="tpu_custom_call" | custom-call | bytes 13164544 | tf_op jit(solution)/shard_map/finish_tokens/pallas_call | solution.py:57
  619.1 2.9 collective-permute-done.29
  622.5 3.5 collective-permute-done.30
  626.1 3.4 collective-permute-start.32
  631.2 3.7 collective-permute-done.33
  (301 shorter events, 80.4 us)
Async XLA Ops:
  8.2 80.4 %collective-permute-start = (bf16[1040,128]{1,0:T(8,128)(2,1)}, bf16[1040,128]{1,0:T(8,128)(2,1)S(1)}, u32[]{:S(2)}, u32[]{:S(2)}) collective-permute-start(bf16[1040,128]{1,0:T(8,128)(2,1)} %concatenate.132), channel_id=1, source_target_pairs={{0,8},{4,12},{8,0},{12,4},{16,24},{20,28},{24,16},{28,20},{1,9},{5... | collective-permute-start | bytes 798728 | tf_op jit(solution)/shard_map/ppermute | solution.py:596
  11.3 75.8 %collective-permute-start.1 = (bf16[1040,128]{1,0:T(8,128)(2,1)}, bf16[1040,128]{1,0:T(8,128)(2,1)S(1)}, u32[]{:S(2)}, u32[]{:S(2)}) collective-permute-start(bf16[1040,128]{1,0:T(8,128)(2,1)} %concatenate.132), channel_id=1, source_target_pairs={{0,16},{4,20},{8,24},{12,28},{16,0},{20,4},{24,8},{28,12},{1,17},{... | collective-permute-start | bytes 798728 | tf_op jit(solution)/shard_map/ppermute | solution.py:596
  13.8 71.7 %collective-permute-start.2 = (bf16[1040,128]{1,0:T(8,128)(2,1)}, bf16[1040,128]{1,0:T(8,128)(2,1)S(1)}, u32[]{:S(2)}, u32[]{:S(2)}) collective-permute-start(bf16[1040,128]{1,0:T(8,128)(2,1)} %concatenate.132), channel_id=1, source_target_pairs={{0,24},{4,28},{8,16},{12,20},{16,8},{20,12},{24,0},{28,4},{1,25},{... | collective-permute-start | bytes 798728 | tf_op jit(solution)/shard_map/ppermute | solution.py:596
  15.3 20.2 %collective-permute-start.11 = (bf16[256,512]{1,0:T(8,128)(2,1)}, bf16[256,512]{1,0:T(8,128)(2,1)}, u32[]{:S(2)}, u32[]{:S(2)}) collective-permute-start(bf16[256,512]{1,0:T(8,128)(2,1)} %pad_maximum_fusion.8), channel_id=1, source_target_pairs={{0,8},{4,12},{8,0},{12,4},{16,24},{20,28},{24,16},{28,20},{1,9},{5... | collective-permute-start | bytes 786440 | tf_op jit(solution)/shard_map/ppermute | solution.py:596
  16.2 39.6 %collective-permute-start.12 = (bf16[256,512]{1,0:T(8,128)(2,1)}, bf16[256,512]{1,0:T(8,128)(2,1)}, u32[]{:S(2)}, u32[]{:S(2)}) collective-permute-start(bf16[256,512]{1,0:T(8,128)(2,1)} %pad_maximum_fusion.8), channel_id=1, source_target_pairs={{0,16},{4,20},{8,24},{12,28},{16,0},{20,4},{24,8},{28,12},{1,17},{... | collective-permute-start | bytes 786440 | tf_op jit(solution)/shard_map/ppermute | solution.py:596
  35.5 21.3 %collective-permute-start.13 = (bf16[256,512]{1,0:T(8,128)(2,1)}, bf16[256,512]{1,0:T(8,128)(2,1)S(1)}, u32[]{:S(2)}, u32[]{:S(2)}) collective-permute-start(bf16[256,512]{1,0:T(8,128)(2,1)} %pad_maximum_fusion.8), channel_id=1, source_target_pairs={{0,24},{4,28},{8,16},{12,20},{16,8},{20,12},{24,0},{28,4},{1,25},{... | collective-permute-start | bytes 786440 | tf_op jit(solution)/shard_map/ppermute | solution.py:596
  55.8 8.1 %collective-permute-start.18 = (bf16[1024,128]{1,0:T(8,128)(2,1)S(1)}, bf16[1024,128]{1,0:T(8,128)(2,1)S(1)}, u32[]{:S(2)}, u32[]{:S(2)}) collective-permute-start(bf16[1024,128]{1,0:T(8,128)(2,1)S(1)} %copy-done.15), channel_id=1, source_target_pairs={{0,8},{4,12},{8,0},{12,4},{16,24},{20,28},{24,16},{28,20},{1,9},{5... | collective-permute-start | bytes 786440 | tf_op jit(solution)/shard_map/ppermute | solution.py:596
  56.8 22.7 %collective-permute-start.19 = (bf16[1024,128]{1,0:T(8,128)(2,1)S(1)}, bf16[1024,128]{1,0:T(8,128)(2,1)S(1)}, u32[]{:S(2)}, u32[]{:S(2)}) collective-permute-start(bf16[1024,128]{1,0:T(8,128)(2,1)S(1)} %copy-done.15), channel_id=1, source_target_pairs={{0,16},{4,20},{8,24},{12,28},{16,0},{20,4},{24,8},{28,12},{1,17},{... | collective-permute-start | bytes 786440 | tf_op jit(solution)/shard_map/ppermute | solution.py:596
  63.8 15.7 %collective-permute-start.20 = (bf16[1024,128]{1,0:T(8,128)(2,1)S(1)}, bf16[1024,128]{1,0:T(8,128)(2,1)S(1)}, u32[]{:S(2)}, u32[]{:S(2)}) collective-permute-start(bf16[1024,128]{1,0:T(8,128)(2,1)S(1)} %copy-done.15), channel_id=1, source_target_pairs={{0,24},{4,28},{8,16},{12,20},{16,8},{20,12},{24,0},{28,4},{1,25},{... | collective-permute-start | bytes 786440 | tf_op jit(solution)/shard_map/ppermute | solution.py:596
  79.5 73.1 %collective-permute-start.5 = (bf16[584,1024]{1,0:T(8,128)(2,1)S(1)}, bf16[584,1024]{1,0:T(8,128)(2,1)S(1)}, u32[]{:S(2)}, u32[]{:S(2)}) collective-permute-start(bf16[584,1024]{1,0:T(8,128)(2,1)S(1)} %copy-done.6), channel_id=1, source_target_pairs={{0,1},{1,0},{2,3},{3,2},{4,5},{5,4},{6,7},{7,6},{8,9},{9,8},{10,11... | collective-permute-start | bytes 3588104 | tf_op jit(solution)/shard_map/ppermute | solution.py:606
  79.6 74.7 %collective-permute-start.6 = (bf16[584,1024]{1,0:T(8,128)(2,1)S(1)}, bf16[584,1024]{1,0:T(8,128)(2,1)S(1)}, u32[]{:S(2)}, u32[]{:S(2)}) collective-permute-start(bf16[584,1024]{1,0:T(8,128)(2,1)S(1)} %copy-done.7), channel_id=1, source_target_pairs={{0,1},{1,0},{2,3},{3,2},{4,5},{5,4},{6,7},{7,6},{8,9},{9,8},{10,11... | collective-permute-start | bytes 3588104 | tf_op jit(solution)/shard_map/ppermute | solution.py:606
  85.5 27.8 %collective-permute-start.14 = (bf16[4,128,512]{2,1,0:T(8,128)(2,1)S(1)}, bf16[4,128,512]{2,1,0:T(8,128)(2,1)S(1)}, u32[]{:S(2)}, u32[]{:S(2)}) collective-permute-start(bf16[4,128,512]{2,1,0:T(8,128)(2,1)S(1)} %pad_maximum_fusion.2), channel_id=1, source_target_pairs={{0,4},{4,0},{8,12},{12,8},{16,20},{20,16},{24,28},{28,24},{1,5},{5... | collective-permute-start | bytes 1572872 | tf_op jit(solution)/shard_map/ppermute | solution.py:599
  87.1 28.3 %collective-permute-start.16 = (bf16[4,128,512]{2,1,0:T(8,128)(2,1)S(1)}, bf16[4,128,512]{2,1,0:T(8,128)(2,1)S(1)}, u32[]{:S(2)}, u32[]{:S(2)}) collective-permute-start(bf16[4,128,512]{2,1,0:T(8,128)(2,1)S(1)} %pad_maximum_fusion.3), channel_id=1, source_target_pairs={{0,2},{2,0},{1,3},{3,1},{4,6},{6,4},{5,7},{7,5},{8,10},{10,8},{9,1... | collective-permute-start | bytes 1572872 | tf_op jit(solution)/shard_map/ppermute | solution.py:602
  88.7 22.2 %collective-permute-start.3 = (bf16[4,528,128]{2,1,0:T(8,128)(2,1)S(1)}, bf16[4,528,128]{2,1,0:T(8,128)(2,1)S(1)}, u32[]{:S(2)}, u32[]{:S(2)}) collective-permute-start(bf16[4,528,128]{2,1,0:T(8,128)(2,1)S(1)} %pad_maximum_fusion), channel_id=1, source_target_pairs={{0,4},{4,0},{8,12},{12,8},{16,20},{20,16},{24,28},{28,24},{1,5},{5... | collective-permute-start | bytes 1622024 | tf_op jit(solution)/shard_map/ppermute | solution.py:599
  111.8 191.2 %collective-permute-start.4 = (bf16[8,528,128]{2,1,0:T(8,128)(2,1)}, bf16[8,528,128]{2,1,0:T(8,128)(2,1)}, u32[]{:S(2)}, u32[]{:S(2)}) collective-permute-start(bf16[8,528,128]{2,1,0:T(8,128)(2,1)} %constant_dynamic-update-slice_fusion.refs_3_.refs_7_.refs_8_.refs_12_.refs_9_.refs_14_), channel_id=1, source_target_pairs={{0,2},{2,0},{1,3},{3,1},{4,6},{6,4},{5,7},{7,5},{8,10},{10,8},{9,1... | collective-permute-start | bytes 3244040 | tf_op jit(solution)/shard_map/ppermute | solution.py:602
  113.4 34.8 %collective-permute-start.7 = (bf16[4,512,128]{2,1,0:T(8,128)(2,1)S(1)}, bf16[4,512,128]{2,1,0:T(8,128)(2,1)S(1)}, u32[]{:S(2)}, u32[]{:S(2)}) collective-permute-start(bf16[4,512,128]{2,1,0:T(8,128)(2,1)S(1)} %pad_maximum_fusion.1), channel_id=1, source_target_pairs={{0,2},{2,0},{1,3},{3,1},{4,6},{6,4},{5,7},{7,5},{8,10},{10,8},{9,1... | collective-permute-start | bytes 1572872 | tf_op jit(solution)/shard_map/ppermute | solution.py:602
  115.3 187.6 %copy-start.1 = (bf16[8,128,512]{2,1,0:T(8,128)(2,1)}, bf16[8,128,512]{2,1,0:T(8,128)(2,1)S(1)}, u32[]{:S(2)}) copy-start(bf16[8,128,512]{2,1,0:T(8,128)(2,1)S(1)} %constant_dynamic-update-slice_fusion.10) | copy-start | bytes 3145732
  115.4 221.0 %collective-permute-start.21 = (bf16[4,512,128]{2,1,0:T(8,128)(2,1)}, bf16[4,512,128]{2,1,0:T(8,128)(2,1)}, u32[]{:S(2)}, u32[]{:S(2)}) collective-permute-start(bf16[4,512,128]{2,1,0:T(8,128)(2,1)} %pad_maximum_fusion.4), channel_id=1, source_target_pairs={{0,4},{4,0},{8,12},{12,8},{16,20},{20,16},{24,28},{28,24},{1,5},{5... | collective-permute-start | bytes 1572872 | tf_op jit(solution)/shard_map/ppermute | solution.py:599
  117.0 186.0 %copy-start = (bf16[8,128,512]{2,1,0:T(8,128)(2,1)}, bf16[8,128,512]{2,1,0:T(8,128)(2,1)S(1)}, u32[]{:S(2)}) copy-start(bf16[8,128,512]{2,1,0:T(8,128)(2,1)S(1)} %constant_dynamic-update-slice_fusion.15) | copy-start | bytes 3145732
  149.0 156.3 %collective-permute-start.8 = (bf16[8,512,128]{2,1,0:T(8,128)(2,1)}, bf16[8,512,128]{2,1,0:T(8,128)(2,1)}, u32[]{:S(2)}, u32[]{:S(2)}) collective-permute-start(bf16[8,512,128]{2,1,0:T(8,128)(2,1)} %constant_dynamic-update-slice_fusion.5.refs_5_.refs_9_.refs_10_.refs_14_.refs_11_.refs_16_), channel_id=1, source_target_pairs={{0,4},{4,0},{8,12},{12,8},{16,20},{20,16},{24,28},{28,24},{1,5},{5... | collective-permute-start | bytes 3145736 | tf_op jit(solution)/shard_map/ppermute | solution.py:599
  152.7 186.9 %collective-permute-start.23 = (bf16[4,512,128]{2,1,0:T(8,128)(2,1)}, bf16[4,512,128]{2,1,0:T(8,128)(2,1)}, u32[]{:S(2)}, u32[]{:S(2)}) collective-permute-start(bf16[4,512,128]{2,1,0:T(8,128)(2,1)} %pad_maximum_fusion.5), channel_id=1, source_target_pairs={{0,2},{2,0},{1,3},{3,1},{4,6},{6,4},{5,7},{7,5},{8,10},{10,8},{9,1... | collective-permute-start | bytes 1572872 | tf_op jit(solution)/shard_map/ppermute | solution.py:602
  155.2 187.3 %collective-permute-start.15 = (bf16[8,128,512]{2,1,0:T(8,128)(2,1)S(1)}, bf16[8,128,512]{2,1,0:T(8,128)(2,1)S(1)}, u32[]{:S(2)}, u32[]{:S(2)}) collective-permute-start(bf16[8,128,512]{2,1,0:T(8,128)(2,1)S(1)} %constant_dynamic-update-slice_fusion.10), channel_id=1, source_target_pairs={{0,2},{2,0},{1,3},{3,1},{4,6},{6,4},{5,7},{7,5},{8,10},{10,8},{9,1... | collective-permute-start | bytes 3145736 | tf_op jit(solution)/shard_map/ppermute | solution.py:602
  303.0 43.3 %collective-permute-start.17 = (bf16[8,128,512]{2,1,0:T(8,128)(2,1)S(1)}, bf16[8,128,512]{2,1,0:T(8,128)(2,1)}, u32[]{:S(2)}, u32[]{:S(2)}) collective-permute-start(bf16[8,128,512]{2,1,0:T(8,128)(2,1)S(1)} %constant_dynamic-update-slice_fusion.15), channel_id=1, source_target_pairs={{0,4},{4,0},{8,12},{12,8},{16,20},{20,16},{24,28},{28,24},{1,5},{5... | collective-permute-start | bytes 3145736 | tf_op jit(solution)/shard_map/ppermute | solution.py:599
  320.6 25.6 %collective-permute-start.10 = (bf16[584,1024]{1,0:T(8,128)(2,1)}, bf16[584,1024]{1,0:T(8,128)(2,1)}, u32[]{:S(2)}, u32[]{:S(2)}) collective-permute-start(bf16[584,1024]{1,0:T(8,128)(2,1)} %get-tuple-element.73.refs_4_), channel_id=1, source_target_pairs={{0,1},{1,0},{2,3},{3,2},{4,5},{5,4},{6,7},{7,6},{8,9},{9,8},{10,11... | collective-permute-start | bytes 3588104 | tf_op jit(solution)/shard_map/ppermute | solution.py:606
  336.3 20.6 %collective-permute-start.9 = (bf16[584,1024]{1,0:T(8,128)(2,1)}, bf16[584,1024]{1,0:T(8,128)(2,1)}, u32[]{:S(2)}, u32[]{:S(2)}) collective-permute-start(bf16[584,1024]{1,0:T(8,128)(2,1)} %get-tuple-element.72.refs_4_), channel_id=1, source_target_pairs={{0,1},{1,0},{2,3},{3,2},{4,5},{5,4},{6,7},{7,6},{8,9},{9,8},{10,11... | collective-permute-start | bytes 3588104 | tf_op jit(solution)/shard_map/ppermute | solution.py:606
  339.6 36.6 %collective-permute-start.22 = (bf16[8,512,128]{2,1,0:T(8,128)(2,1)}, bf16[8,512,128]{2,1,0:T(8,128)(2,1)}, u32[]{:S(2)}, u32[]{:S(2)}) collective-permute-start(bf16[8,512,128]{2,1,0:T(8,128)(2,1)} %constant_dynamic-update-slice_fusion.20.refs_1_.refs_2_), channel_id=1, source_target_pairs={{0,2},{2,0},{1,3},{3,1},{4,6},{6,4},{5,7},{7,5},{8,10},{10,8},{9,1... | collective-permute-start | bytes 3145736 | tf_op jit(solution)/shard_map/ppermute | solution.py:602
  342.5 33.7 %collective-permute-start.24 = (bf16[8,512,128]{2,1,0:T(8,128)(2,1)}, bf16[8,512,128]{2,1,0:T(8,128)(2,1)}, u32[]{:S(2)}, u32[]{:S(2)}) collective-permute-start(bf16[8,512,128]{2,1,0:T(8,128)(2,1)} %constant_dynamic-update-slice_fusion.25.refs_3_.refs_4_), channel_id=1, source_target_pairs={{0,4},{4,0},{8,12},{12,8},{16,20},{20,16},{24,28},{28,24},{1,5},{5... | collective-permute-start | bytes 3145736 | tf_op jit(solution)/shard_map/ppermute | solution.py:599
  374.7 61.3 %collective-permute-start.55 = (bf16[8,512,128]{2,1,0:T(8,128)(2,1)}, bf16[8,512,128]{2,1,0:T(8,128)(2,1)S(1)}, u32[]{:S(2)}, u32[]{:S(2)}) collective-permute-start(bf16[8,512,128]{2,1,0:T(8,128)(2,1)} %get-tuple-element.119), channel_id=1, source_target_pairs={{0,2},{2,0},{1,3},{3,1},{4,6},{6,4},{5,7},{7,5},{8,10},{10,8},{9,1... | collective-permute-start | bytes 3145736 | tf_op jit(solution)/shard_map/ppermute | solution.py:602
  375.7 63.9 %collective-permute-start.57 = (bf16[8,512,128]{2,1,0:T(8,128)(2,1)}, bf16[8,512,128]{2,1,0:T(8,128)(2,1)S(1)}, u32[]{:S(2)}, u32[]{:S(2)}) collective-permute-start(bf16[8,512,128]{2,1,0:T(8,128)(2,1)} %get-tuple-element.121), channel_id=1, source_target_pairs={{0,4},{4,0},{8,12},{12,8},{16,20},{20,16},{24,28},{28,24},{1,5},{5... | collective-permute-start | bytes 3145736 | tf_op jit(solution)/shard_map/ppermute | solution.py:599
  402.0 39.2 %collective-permute-start.48 = (bf16[8,128,512]{2,1,0:T(8,128)(2,1)}, bf16[8,128,512]{2,1,0:T(8,128)(2,1)}, u32[]{:S(2)}, u32[]{:S(2)}) collective-permute-start(bf16[8,128,512]{2,1,0:T(8,128)(2,1)} %get-tuple-element.115), channel_id=1, source_target_pairs={{0,2},{2,0},{1,3},{3,1},{4,6},{6,4},{5,7},{7,5},{8,10},{10,8},{9,1... | collective-permute-start | bytes 3145736 | tf_op jit(solution)/shard_map/ppermute | solution.py:602
  403.2 41.4 %collective-permute-start.50 = (bf16[8,128,512]{2,1,0:T(8,128)(2,1)}, bf16[8,128,512]{2,1,0:T(8,128)(2,1)}, u32[]{:S(2)}, u32[]{:S(2)}) collective-permute-start(bf16[8,128,512]{2,1,0:T(8,128)(2,1)} %get-tuple-element.117), channel_id=1, source_target_pairs={{0,4},{4,0},{8,12},{12,8},{16,20},{20,16},{24,28},{28,24},{1,5},{5... | collective-permute-start | bytes 3145736 | tf_op jit(solution)/shard_map/ppermute | solution.py:599
  404.7 43.7 %collective-permute-start.27 = (bf16[584,1024]{1,0:T(8,128)(2,1)S(1)}, bf16[584,1024]{1,0:T(8,128)(2,1)}, u32[]{:S(2)}, u32[]{:S(2)}) collective-permute-start(bf16[584,1024]{1,0:T(8,128)(2,1)S(1)} %copy-done.5), channel_id=1, source_target_pairs={{0,1},{1,0},{2,3},{3,2},{4,5},{5,4},{6,7},{7,6},{8,9},{9,8},{10,11... | collective-permute-start | bytes 3588104 | tf_op jit(solution)/shard_map/ppermute | solution.py:606
  436.0 34.5 %collective-permute-start.26 = (bf16[584,1024]{1,0:T(8,128)(2,1)}, bf16[584,1024]{1,0:T(8,128)(2,1)}, u32[]{:S(2)}, u32[]{:S(2)}) collective-permute-start(bf16[584,1024]{1,0:T(8,128)(2,1)} %grad_two.2.refs_3_), channel_id=1, source_target_pairs={{0,1},{1,0},{2,3},{3,2},{4,5},{5,4},{6,7},{7,6},{8,9},{9,8},{10,11... | collective-permute-start | bytes 3588104 | tf_op jit(solution)/shard_map/ppermute | solution.py:606
  439.6 83.3 %collective-permute-start.56 = (bf16[4,512,128]{2,1,0:T(8,128)(2,1)}, bf16[4,512,128]{2,1,0:T(8,128)(2,1)}, u32[]{:S(2)}, u32[]{:S(2)}) collective-permute-start(bf16[4,512,128]{2,1,0:T(8,128)(2,1)} %get-tuple-element.125), channel_id=1, source_target_pairs={{0,4},{4,0},{8,12},{12,8},{16,20},{20,16},{24,28},{28,24},{1,5},{5... | collective-permute-start | bytes 1572872 | tf_op jit(solution)/shard_map/ppermute | solution.py:599
  441.2 84.2 %collective-permute-start.58 = (bf16[4,512,128]{2,1,0:T(8,128)(2,1)}, bf16[4,512,128]{2,1,0:T(8,128)(2,1)}, u32[]{:S(2)}, u32[]{:S(2)}) collective-permute-start(bf16[4,512,128]{2,1,0:T(8,128)(2,1)} %get-tuple-element.127), channel_id=1, source_target_pairs={{0,2},{2,0},{1,3},{3,1},{4,6},{6,4},{5,7},{7,5},{8,10},{10,8},{9,1... | collective-permute-start | bytes 1572872 | tf_op jit(solution)/shard_map/ppermute | solution.py:602
  444.6 87.1 %collective-permute-start.49 = (bf16[4,128,512]{2,1,0:T(8,128)(2,1)}, bf16[4,128,512]{2,1,0:T(8,128)(2,1)}, u32[]{:S(2)}, u32[]{:S(2)}) collective-permute-start(bf16[4,128,512]{2,1,0:T(8,128)(2,1)} %get-tuple-element.129), channel_id=1, source_target_pairs={{0,4},{4,0},{8,12},{12,8},{16,20},{20,16},{24,28},{28,24},{1,5},{5... | collective-permute-start | bytes 1572872 | tf_op jit(solution)/shard_map/ppermute | solution.py:599
  496.0 22.3 %collective-permute-start.41 = (bf16[8,128,128]{2,1,0:T(8,128)(2,1)}, bf16[8,128,128]{2,1,0:T(8,128)(2,1)S(1)}, u32[]{:S(2)}, u32[]{:S(2)}) collective-permute-start(bf16[8,128,128]{2,1,0:T(8,128)(2,1)} %get-tuple-element.110), channel_id=1, source_target_pairs={{0,2},{2,0},{1,3},{3,1},{4,6},{6,4},{5,7},{7,5},{8,10},{10,8},{9,1... | collective-permute-start | bytes 786440 | tf_op jit(solution)/shard_map/ppermute | solution.py:602
  497.1 23.2 %collective-permute-start.43 = (bf16[8,128,128]{2,1,0:T(8,128)(2,1)}, bf16[8,128,128]{2,1,0:T(8,128)(2,1)S(1)}, u32[]{:S(2)}, u32[]{:S(2)}) collective-permute-start(bf16[8,128,128]{2,1,0:T(8,128)(2,1)} %get-tuple-element.112), channel_id=1, source_target_pairs={{0,4},{4,0},{8,12},{12,8},{16,20},{20,16},{24,28},{28,24},{1,5},{5... | collective-permute-start | bytes 786440 | tf_op jit(solution)/shard_map/ppermute | solution.py:599
  518.3 14.7 %collective-permute-start.51 = (bf16[4,128,512]{2,1,0:T(8,128)(2,1)S(1)}, bf16[4,128,512]{2,1,0:T(8,128)(2,1)S(1)}, u32[]{:S(2)}, u32[]{:S(2)}) collective-permute-start(bf16[4,128,512]{2,1,0:T(8,128)(2,1)S(1)} %copy-done.20), channel_id=1, source_target_pairs={{0,2},{2,0},{1,3},{3,1},{4,6},{6,4},{5,7},{7,5},{8,10},{10,8},{9,1... | collective-permute-start | bytes 1572872 | tf_op jit(solution)/shard_map/ppermute | solution.py:602
  520.3 13.6 %collective-permute-start.42 = (bf16[4,128,128]{2,1,0:T(8,128)(2,1)S(1)}, bf16[4,128,128]{2,1,0:T(8,128)(2,1)S(1)}, u32[]{:S(2)}, u32[]{:S(2)}) collective-permute-start(bf16[4,128,128]{2,1,0:T(8,128)(2,1)S(1)} %get-tuple-element.163), channel_id=1, source_target_pairs={{0,4},{4,0},{8,12},{12,8},{16,20},{20,16},{24,28},{28,24},{1,5},{5... | collective-permute-start | bytes 393224 | tf_op jit(solution)/shard_map/ppermute | solution.py:599
  523.0 11.1 %collective-permute-start.44 = (bf16[4,128,128]{2,1,0:T(8,128)(2,1)S(1)}, bf16[4,128,128]{2,1,0:T(8,128)(2,1)S(1)}, u32[]{:S(2)}, u32[]{:S(2)}) collective-permute-start(bf16[4,128,128]{2,1,0:T(8,128)(2,1)S(1)} %get-tuple-element.165), channel_id=1, source_target_pairs={{0,2},{2,0},{1,3},{3,1},{4,6},{6,4},{5,7},{7,5},{8,10},{10,8},{9,1... | collective-permute-start | bytes 393224 | tf_op jit(solution)/shard_map/ppermute | solution.py:602
  526.7 39.2 %collective-permute-start.59 = (bf16[1024,128]{1,0:T(8,128)(2,1)S(1)}, bf16[1024,128]{1,0:T(8,128)(2,1)}, u32[]{:S(2)}, u32[]{:S(2)}) collective-permute-start(bf16[1024,128]{1,0:T(8,128)(2,1)S(1)} %pad_maximum_fusion.12), channel_id=1, source_target_pairs={{0,8},{4,12},{8,0},{12,4},{16,24},{20,28},{24,16},{28,20},{1,9},{5... | collective-permute-start | bytes 786440 | tf_op jit(solution)/shard_map/ppermute | solution.py:596
  531.7 35.2 %collective-permute-start.60 = (bf16[1024,128]{1,0:T(8,128)(2,1)S(1)}, bf16[1024,128]{1,0:T(8,128)(2,1)}, u32[]{:S(2)}, u32[]{:S(2)}) collective-permute-start(bf16[1024,128]{1,0:T(8,128)(2,1)S(1)} %pad_maximum_fusion.13), channel_id=1, source_target_pairs={{0,16},{4,20},{8,24},{12,28},{16,0},{20,4},{24,8},{28,12},{1,17},{... | collective-permute-start | bytes 786440 | tf_op jit(solution)/shard_map/ppermute | solution.py:596
  534.1 10.8 %collective-permute-start.45 = (bf16[256,128]{1,0:T(8,128)(2,1)S(1)}, bf16[256,128]{1,0:T(8,128)(2,1)S(1)}, u32[]{:S(2)}, u32[]{:S(2)}) collective-permute-start(bf16[256,128]{1,0:T(8,128)(2,1)S(1)} %pad_maximum_fusion.18), channel_id=1, source_target_pairs={{0,8},{4,12},{8,0},{12,4},{16,24},{20,28},{24,16},{28,20},{1,9},{5... | collective-permute-start | bytes 196616 | tf_op jit(solution)/shard_map/ppermute | solution.py:596
  539.2 15.7 %collective-permute-start.46 = (bf16[256,128]{1,0:T(8,128)(2,1)S(1)}, bf16[256,128]{1,0:T(8,128)(2,1)S(1)}, u32[]{:S(2)}, u32[]{:S(2)}) collective-permute-start(bf16[256,128]{1,0:T(8,128)(2,1)S(1)} %pad_maximum_fusion.19), channel_id=1, source_target_pairs={{0,16},{4,20},{8,24},{12,28},{16,0},{20,4},{24,8},{28,12},{1,17},{... | collective-permute-start | bytes 196616 | tf_op jit(solution)/shard_map/ppermute | solution.py:596
  539.2 15.7 %collective-permute-start.47 = (bf16[256,128]{1,0:T(8,128)(2,1)S(1)}, bf16[256,128]{1,0:T(8,128)(2,1)S(1)}, u32[]{:S(2)}, u32[]{:S(2)}) collective-permute-start(bf16[256,128]{1,0:T(8,128)(2,1)S(1)} %pad_maximum_fusion.20), channel_id=1, source_target_pairs={{0,24},{4,28},{8,16},{12,20},{16,8},{20,12},{24,0},{28,4},{1,25},{... | collective-permute-start | bytes 196616 | tf_op jit(solution)/shard_map/ppermute | solution.py:596
  545.0 22.1 %collective-permute-start.61 = (bf16[1024,128]{1,0:T(8,128)(2,1)}, bf16[1024,128]{1,0:T(8,128)(2,1)}, u32[]{:S(2)}, u32[]{:S(2)}) collective-permute-start(bf16[1024,128]{1,0:T(8,128)(2,1)} %pad_maximum_fusion.14), channel_id=1, source_target_pairs={{0,24},{4,28},{8,16},{12,20},{16,8},{20,12},{24,0},{28,4},{1,25},{... | collective-permute-start | bytes 786440 | tf_op jit(solution)/shard_map/ppermute | solution.py:596
  554.8 12.5 %collective-permute-start.52 = (bf16[256,512]{1,0:T(8,128)(2,1)S(1)}, bf16[256,512]{1,0:T(8,128)(2,1)}, u32[]{:S(2)}, u32[]{:S(2)}) collective-permute-start(bf16[256,512]{1,0:T(8,128)(2,1)S(1)} %pad_maximum_fusion.9), channel_id=1, source_target_pairs={{0,8},{4,12},{8,0},{12,4},{16,24},{20,28},{24,16},{28,20},{1,9},{5... | collective-permute-start | bytes 786440 | tf_op jit(solution)/shard_map/ppermute | solution.py:596
  556.1 16.6 %collective-permute-start.53 = (bf16[256,512]{1,0:T(8,128)(2,1)}, bf16[256,512]{1,0:T(8,128)(2,1)}, u32[]{:S(2)}, u32[]{:S(2)}) collective-permute-start(bf16[256,512]{1,0:T(8,128)(2,1)} %pad_maximum_fusion.10), channel_id=1, source_target_pairs={{0,16},{4,20},{8,24},{12,28},{16,0},{20,4},{24,8},{28,12},{1,17},{... | collective-permute-start | bytes 786440 | tf_op jit(solution)/shard_map/ppermute | solution.py:596
  565.9 18.3 %collective-permute-start.34 = (bf16[8,384,128]{2,1,0:T(8,128)(2,1)}, bf16[8,384,128]{2,1,0:T(8,128)(2,1)S(1)}, u32[]{:S(2)}, u32[]{:S(2)}) collective-permute-start(bf16[8,384,128]{2,1,0:T(8,128)(2,1)} %get-tuple-element.104), channel_id=1, source_target_pairs={{0,2},{2,0},{1,3},{3,1},{4,6},{6,4},{5,7},{7,5},{8,10},{10,8},{9,1... | collective-permute-start | bytes 2359304 | tf_op jit(solution)/shard_map/ppermute | solution.py:602
  567.0 36.0 %collective-permute-start.25 = (bf16[2,584,1024]{2,1,0:T(8,128)(2,1)S(1)}, bf16[2,584,1024]{2,1,0:T(8,128)(2,1)}, u32[]{:S(2)}, u32[]{:S(2)}) collective-permute-start(bf16[2,584,1024]{2,1,0:T(8,128)(2,1)S(1)} %bitcast.284), channel_id=1, source_target_pairs={{0,1},{1,0},{2,3},{3,2},{4,5},{5,4},{6,7},{7,6},{8,9},{9,8},{10,11... | collective-permute-start | bytes 7176200 | tf_op jit(solution)/shard_map/ppermute | solution.py:606
  567.1 20.6 %collective-permute-start.36 = (bf16[8,384,128]{2,1,0:T(8,128)(2,1)}, bf16[8,384,128]{2,1,0:T(8,128)(2,1)S(1)}, u32[]{:S(2)}, u32[]{:S(2)}) collective-permute-start(bf16[8,384,128]{2,1,0:T(8,128)(2,1)} %get-tuple-element.106), channel_id=1, source_target_pairs={{0,4},{4,0},{8,12},{12,8},{16,20},{20,16},{24,28},{28,24},{1,5},{5... | collective-permute-start | bytes 2359304 | tf_op jit(solution)/shard_map/ppermute | solution.py:599
  567.4 40.4 %collective-permute-start.28 = (bf16[2,584,1024]{2,1,0:T(8,128)(2,1)}, bf16[2,584,1024]{2,1,0:T(8,128)(2,1)}, u32[]{:S(2)}, u32[]{:S(2)}) collective-permute-start(bf16[2,584,1024]{2,1,0:T(8,128)(2,1)} %bitcast.285), channel_id=1, source_target_pairs={{0,1},{1,0},{2,3},{3,2},{4,5},{5,4},{6,7},{7,6},{8,9},{9,8},{10,11... | collective-permute-start | bytes 7176200 | tf_op jit(solution)/shard_map/ppermute | solution.py:606
  572.7 9.0 %collective-permute-start.54 = (bf16[256,512]{1,0:T(8,128)(2,1)S(1)}, bf16[256,512]{1,0:T(8,128)(2,1)S(1)}, u32[]{:S(2)}, u32[]{:S(2)}) collective-permute-start(bf16[256,512]{1,0:T(8,128)(2,1)S(1)} %pad_maximum_fusion.11), channel_id=1, source_target_pairs={{0,24},{4,28},{8,16},{12,20},{16,8},{20,12},{24,0},{28,4},{1,25},{... | collective-permute-start | bytes 786440 | tf_op jit(solution)/shard_map/ppermute | solution.py:596
  584.4 11.3 %collective-permute-start.35 = (bf16[4,384,128]{2,1,0:T(8,128)(2,1)S(1)}, bf16[4,384,128]{2,1,0:T(8,128)(2,1)S(1)}, u32[]{:S(2)}, u32[]{:S(2)}) collective-permute-start(bf16[4,384,128]{2,1,0:T(8,128)(2,1)S(1)} %get-tuple-element.133), channel_id=1, source_target_pairs={{0,4},{4,0},{8,12},{12,8},{16,20},{20,16},{24,28},{28,24},{1,5},{5... | collective-permute-start | bytes 1179656 | tf_op jit(solution)/shard_map/ppermute | solution.py:599
  587.9 10.3 %collective-permute-start.37 = (bf16[4,384,128]{2,1,0:T(8,128)(2,1)S(1)}, bf16[4,384,128]{2,1,0:T(8,128)(2,1)S(1)}, u32[]{:S(2)}, u32[]{:S(2)}) collective-permute-start(bf16[4,384,128]{2,1,0:T(8,128)(2,1)S(1)} %get-tuple-element.135), channel_id=1, source_target_pairs={{0,2},{2,0},{1,3},{3,1},{4,6},{6,4},{5,7},{7,5},{8,10},{10,8},{9,1... | collective-permute-start | bytes 1179656 | tf_op jit(solution)/shard_map/ppermute | solution.py:602
  598.3 20.7 %collective-permute-start.38 = (bf16[768,128]{1,0:T(8,128)(2,1)S(1)}, bf16[768,128]{1,0:T(8,128)(2,1)S(1)}, u32[]{:S(2)}, u32[]{:S(2)}) collective-permute-start(bf16[768,128]{1,0:T(8,128)(2,1)S(1)} %pad_maximum_fusion.15), channel_id=1, source_target_pairs={{0,8},{4,12},{8,0},{12,4},{16,24},{20,28},{24,16},{28,20},{1,9},{5... | collective-permute-start | bytes 589832 | tf_op jit(solution)/shard_map/ppermute | solution.py:596
  598.4 20.6 %collective-permute-start.39 = (bf16[768,128]{1,0:T(8,128)(2,1)S(1)}, bf16[768,128]{1,0:T(8,128)(2,1)S(1)}, u32[]{:S(2)}, u32[]{:S(2)}) collective-permute-start(bf16[768,128]{1,0:T(8,128)(2,1)S(1)} %pad_maximum_fusion.16), channel_id=1, source_target_pairs={{0,16},{4,20},{8,24},{12,28},{16,0},{20,4},{24,8},{28,12},{1,17},{... | collective-permute-start | bytes 589832 | tf_op jit(solution)/shard_map/ppermute | solution.py:596
  601.9 17.1 %collective-permute-start.40 = (bf16[768,128]{1,0:T(8,128)(2,1)S(1)}, bf16[768,128]{1,0:T(8,128)(2,1)S(1)}, u32[]{:S(2)}, u32[]{:S(2)}) collective-permute-start(bf16[768,128]{1,0:T(8,128)(2,1)S(1)} %pad_maximum_fusion.17), channel_id=1, source_target_pairs={{0,24},{4,28},{8,16},{12,20},{16,8},{20,12},{24,0},{28,4},{1,25},{... | collective-permute-start | bytes 589832 | tf_op jit(solution)/shard_map/ppermute | solution.py:596
  617.9 4.2 collective-permute-start.29
  622.1 3.8 collective-permute-start.30
  626.0 5.2 collective-permute-start.31
  626.1 5.1 collective-permute-start.32
  629.5 5.4 collective-permute-start.33
  (35 other events, 322.2 us)

commit v2 on v1

v2 whole, which is shorter than its diff:
```python
import functools

import jax
import jax.numpy as jnp
from jax import lax
from jax.experimental import pallas as pl
from jax.experimental.pallas import tpu as pltpu
from jax.sharding import Mesh, PartitionSpec as P

HEAD_DIM = 64
VALID = 577
SEQ = 584
BF = jnp.bfloat16
F32 = jnp.float32
VMEM_LIMIT = 60 * 1024 * 1024
SLOW = 0.05
NT = (((1,), (1,)), ((), ()))
TN = (((0,), (0,)), ((), ()))
NN = (((1,), (0,)), ((), ()))


def dot(left, right, dims):
    return lax.dot_general(left, right, dims, preferred_element_type=F32)


class Loads:
    def __init__(self, sems):
        self.sems, self.groups = sems, []

    def start(self, pairs):
        sem = self.sems.at[len(self.groups)]
        copies = [pltpu.make_async_copy(src, dst, sem) for src, dst in pairs]
        for copy in copies:
            copy.start()
        self.groups.append(copies)
        return len(self.groups) - 1

    def wait(self, group):
        for copy in self.groups[group]:
            copy.wait()


def call(body, ins, outs, scratch, name, flops, aliases=None, smem=(), sems=48, vmem_ins=()):
    n_smem, n_vmem, n_in, n_out = len(smem), len(vmem_ins), len(ins), len(outs)
    moved = sum(a.size * a.dtype.itemsize for a in ins) + sum(
        o.size * o.dtype.itemsize for o in outs
    )

    def kernel(*refs):
        first = n_smem + n_vmem
        small = refs[:first]
        in_refs = refs[first : first + n_in]
        out_refs = refs[first + n_in : first + n_in + n_out]
        rest = refs[first + n_in + n_out :]
        body(small, in_refs, out_refs, rest[:-1], Loads(rest[-1]))

    any_spec = pl.BlockSpec(memory_space=pl.ANY)
    return pl.pallas_call(
        kernel,
        out_shape=outs,
        in_specs=[pl.BlockSpec(memory_space=pltpu.SMEM)] * n_smem
        + [pl.BlockSpec(memory_space=pltpu.VMEM)] * n_vmem
        + [any_spec] * n_in,
        out_specs=[any_spec] * n_out,
        scratch_shapes=list(scratch) + [pltpu.SemaphoreType.DMA((sems,))],
        input_output_aliases={n_smem + n_vmem + i: o for i, o in (aliases or {}).items()},
        compiler_params=pltpu.CompilerParams(vmem_limit_bytes=VMEM_LIMIT),
        cost_estimate=pl.CostEstimate(flops=int(flops / SLOW), bytes_accessed=int(moved / SLOW), transcendentals=0),
        name=name,
    )(*smem, *vmem_ins, *ins)


def norm_parts(rows):
    center = rows - jnp.mean(rows, axis=1, keepdims=True)
    inverse = lax.rsqrt(jnp.mean(center * center, axis=1, keepdims=True) + 1e-05)
    return center * inverse, inverse


def norm_back(grad_norm, scaled, inverse, gain_row):
    grad_hat = grad_norm * gain_row
    first_mean = jnp.mean(grad_hat, axis=1, keepdims=True)
    second_mean = jnp.mean(grad_hat * scaled, axis=1, keepdims=True)
    return inverse * (grad_hat - first_mean - scaled * second_mean)


def sds(shape, dtype):
    return jax.ShapeDtypeStruct(shape, dtype)


def arrange_pair(ids, own, other, nd):
    n = len(own)
    rows, width = own[0].shape
    bd = width // nd

    def body(small, ins, outs, scratch, loads):
        (ids_ref,) = small
        mine = ids_ref[0]
        in_s, out_s = scratch[: 2 * n], scratch[2 * n :]
        groups = [loads.start([(ins[i], in_s[i])]) for i in range(2 * n)]
        done = []
        for i in range(2 * n):
            loads.wait(groups[i])
            for p in range(nd):
                src = pl.ds(pl.multiple_of(ids_ref[2 + p] * bd, 128), bd)
                out_s[i][:, p * bd : (p + 1) * bd] = in_s[i][:, src]
            spot = mine if i < n else 1 - mine
            done.append(loads.start([(out_s[i], outs[i % n].at[spot])]))
        for group in done:
            loads.wait(group)

    return call(
        body,
        list(own) + list(other),
        [sds((2, rows, width), BF)] * n,
        [pltpu.VMEM((rows, width), BF)] * (4 * n),
        "arrange_pair",
        0,
        smem=(ids,),
    )


def weight_loads(loads, groups, refs, scratch):
    return [
        loads.start([(refs[a].at[src], scratch.at[dst]) for a, src, dst in plan])
        for plan in groups
    ]


def softmax_rows(q2, k2):
    scores = dot(q2, k2, NT)
    lane = lax.broadcasted_iota(jnp.int32, scores.shape, 1)
    scores = jnp.where(lane < VALID, scores, -1e30)
    e = jnp.exp(scores - jnp.max(scores, axis=1, keepdims=True))
    return e * (1.0 / jnp.sum(e, axis=1, keepdims=True))


def attn_forward(image, tok, nv, bq, wqkv, wout, prev):
    seq, width = tok.shape[1:]
    qkv_arrays, qkv_plan, qkv_scratch = wqkv
    out_arrays, out_plan, out_scratch = wout
    ext = qkv_scratch[-1]
    n_prev = 0 if prev is None else len(prev)
    nq, no = len(qkv_arrays), len(out_arrays)

    def body(small, ins, outs, scratch, loads):
        nv_ref, bq_ref = small
        tok_ref, ins = ins[0], ins[1 + n_prev :]
        w_s, wo_s, tok_s, first_s, q_s, k_s, v_s, att_s, part_s = scratch
        g_tok = loads.start([(tok_ref.at[image], tok_s)])
        g_w = weight_loads(loads, qkv_plan, ins[:nq], w_s)
        g_o = weight_loads(loads, out_plan, ins[nq:], wo_s)
        loads.wait(g_tok)
        hat, _ = norm_parts(tok_s[...].astype(F32))
        first_s[...] = (hat * nv_ref[0:1, :] + nv_ref[2:3, :]).astype(BF)
        g_first = loads.start([(first_s, outs[0].at[image])])
        low = first_s[...]
        for i, ref in enumerate((q_s, k_s, v_s)):
            if i < len(g_w):
                loads.wait(g_w[i])
            proj = dot(low, w_s[i].reshape(width, ext), NN)
            if i == 0:
                proj = proj + bq_ref[0:1, :]
            if i == 2:
                proj = proj + bq_ref[1:2, :]
            low_proj = proj.astype(BF)
            if i == 0:
                low_proj = low_proj * jnp.asarray(HEAD_DIM**-0.5, BF)
            ref[...] = low_proj
        g_qkv = loads.start(
            [(q_s, outs[1].at[image]), (k_s, outs[2].at[image]), (v_s, outs[3].at[image])]
        )
        half = lax.broadcasted_iota(jnp.int32, (1, 128), 1) // HEAD_DIM

        def pair(i, carry):
            cols = pl.ds(pl.multiple_of(i * 128, 128), 128)
            q2, k2, v2 = q_s[:, cols], k_s[:, cols], v_s[:, cols]
            total = None
            for h in range(2):
                keep = (half == h).astype(BF)
                probs = softmax_rows(q2, k2 * keep).astype(BF)
                piece = dot(probs, v2 * keep, NN)
                total = piece if total is None else total + piece
            att_s[:, cols] = total.astype(BF)
            return carry

        lax.fori_loop(0, ext // 128, pair, 0)
        g_att = loads.start([(att_s, outs[4].at[image])])
        loads.wait(g_o[0])
        part_s[...] = dot(att_s[...], wo_s[...], NN).astype(BF)
        g_part = loads.start([(part_s, outs[5])])
        for group in (g_first, g_qkv, g_att, g_part):
            loads.wait(group)

    shapes = [(2, seq, width)] + [(2, seq, ext)] * 4
    return call(
        body,
        [tok] + list(prev or []) + qkv_arrays + out_arrays,
        [sds(s, BF) for s in shapes] + [sds((seq, width), BF)],
        [
            pltpu.VMEM(qkv_scratch, BF),
            pltpu.VMEM(out_scratch, BF),
            pltpu.VMEM((seq, width), BF),
            pltpu.VMEM((seq, width), BF),
            pltpu.VMEM((seq, ext), BF),
            pltpu.VMEM((seq, ext), BF),
            pltpu.VMEM((seq, ext), BF),
            pltpu.VMEM((seq, ext), BF),
            pltpu.VMEM((seq, width), BF),
        ],
        "attn_forward",
        2 * seq * width * ext * 4 + 16 * seq * seq * ext,
        aliases={1 + i: i for i in range(n_prev)},
        vmem_ins=(nv, bq),
    )


def mlp_up(image, tok, part, recv, keep, nv, bu, wup, step, prev):
    seq, width = tok.shape[1:]
    up_arrays, up_plan, up_scratch = wup
    hid = up_scratch[-1]
    n_prev = 0 if prev is None else len(prev)

    def body(small, ins, outs, scratch, loads):
        keep_ref, nv_ref, bu_ref = small
        tok_ref, part_ref, recv_ref = ins[:3]
        w_s, tok_s, part_s, recv_s, mid_s, sec_s, act_s, dact_s = scratch
        g_in = loads.start([(tok_ref.at[image], tok_s), (part_ref, part_s), (recv_ref, recv_s)])
        g_w = weight_loads(loads, up_plan, ins[3 + n_prev :], w_s)
        loads.wait(g_in)
        total = part_s[...].astype(F32) + recv_s[...].astype(F32) + nv_ref[4:5, :]
        middle = tok_s[...].astype(F32) + keep_ref[image] * total
        mid_s[...] = middle
        hat, _ = norm_parts(middle)
        sec_s[...] = (hat * nv_ref[1:2, :] + nv_ref[3:4, :]).astype(BF)
        g_mid = loads.start([(mid_s, outs[0].at[image]), (sec_s, outs[1].at[image])])
        second = sec_s[...]
        done = []
        for block in range(hid // step):
            if block < len(g_w):
                loads.wait(g_w[block])
            cols = slice(block * step, (block + 1) * step)
            pre = dot(second, w_s[:, cols], NN) + bu_ref[0:1, cols]
            gate = 1.0 / (1.0 + jnp.exp(-1.702 * pre))
            act_s[:, cols] = (pre * gate).astype(BF)
            dact_s[:, cols] = (gate + 1.702 * pre * gate * (1.0 - gate)).astype(BF)
            done.append(
                loads.start(
                    [
                        (act_s.at[:, cols], outs[2].at[image, :, cols]),
                        (dact_s.at[:, cols], outs[3].at[image, :, cols]),
                    ]
                )
            )
        for group in [g_mid] + done:
            loads.wait(group)

    outs = [
        sds((2, seq, width), F32),
        sds((2, seq, width), BF),
        sds((2, seq, hid), BF),
        sds((2, seq, hid), BF),
    ]
    return call(
        body,
        [tok, part, recv] + list(prev or []) + up_arrays,
        outs,
        [
            pltpu.VMEM(up_scratch, BF),
            pltpu.VMEM((seq, width), BF),
            pltpu.VMEM((seq, width), BF),
            pltpu.VMEM((seq, width), BF),
            pltpu.VMEM((seq, width), F32),
            pltpu.VMEM((seq, width), BF),
            pltpu.VMEM((seq, hid), BF),
            pltpu.VMEM((seq, hid), BF),
        ],
        "mlp_up",
        2 * seq * width * hid,
        aliases={3 + i: i for i in range(n_prev)},
        smem=(keep,),
        vmem_ins=(nv, bu),
    )


def weight_grad(lefts, rights, tasks, out_shapes, name):
    rows = lefts[0].shape[0]
    arrays = list(lefts) + list(rights)
    n_left, n_in = len(lefts), len(arrays)
    last = {}
    for n, task in enumerate(tasks):
        for store in task[4]:
            last[store[0]] = n

    def body(small, ins, outs, scratch, loads):
        in_s, out_s = scratch[:n_in], scratch[n_in:]
        order = []
        for l_index, _, r_index, _, _ in tasks:
            for i in (l_index, n_left + r_index):
                if i not in order:
                    order.append(i)
        groups = {i: loads.start([(ins[i], in_s[i])]) for i in order}
        ready, done = set(), []
        for n, (l_index, l_cols, r_index, r_cols, stores) in enumerate(tasks):
            for i in (l_index, n_left + r_index):
                if i not in ready:
                    loads.wait(groups[i])
                    ready.add(i)
            left, right = in_s[l_index][:, l_cols], in_s[n_left + r_index][:, r_cols]
            value = dot(left, right, TN).astype(BF)
            for which, spot, r_sl, c_sl in stores:
                out_s[which][spot] = value[r_sl, c_sl]
            for which in sorted(w for w in last if last[w] == n):
                done.append(loads.start([(out_s[which], outs[which])]))
        for group in done:
            loads.wait(group)

    flops = sum(
        2 * rows * (t[1].stop - t[1].start) * (t[3].stop - t[3].start) for t in tasks
    )
    return call(
        body,
        arrays,
        [sds(s, BF) for s in out_shapes],
        [pltpu.VMEM(a.shape, BF) for a in arrays] + [pltpu.VMEM(s, BF) for s in out_shapes],
        name,
        flops,
    )


def mlp_back(grad, act, dact, wdown, wup, step):
    rows, width = grad.shape
    hid = dact.shape[1]
    down_arrays, down_plan, down_scratch = wdown
    up_arrays, up_plan, up_scratch = wup
    n_down = len(down_arrays)

    def body(small, ins, outs, scratch, loads):
        wd_s, wu_s, g_s, a_s, d_s, low_s, sum_s, two_s, mlp_s = scratch
        g_g = loads.start([(ins[0], g_s)])
        g_wd = weight_loads(loads, down_plan, ins[3 : 3 + n_down], wd_s)
        g_d = []
        for block in range(hid // step):
            cols = slice(block * step, (block + 1) * step)
            g_d.append(loads.start([(ins[2].at[:, cols], d_s.at[:, cols])]))
        g_wu = weight_loads(loads, up_plan, ins[3 + n_down :], wu_s)
        g_a = loads.start([(ins[1], a_s)])
        loads.wait(g_g)
        left = g_s[...]
        done = []
        for block in range(hid // step):
            if block < len(g_wd):
                loads.wait(g_wd[block])
            loads.wait(g_d[block])
            cols = slice(block * step, (block + 1) * step)
            pre = dot(left, wd_s[cols, :], NT) * d_s[:, cols].astype(F32)
            low_s[:, cols] = pre.astype(BF)
            sum_s[0:1, cols] = jnp.sum(pre, axis=0, keepdims=True)
            done.append(loads.start([(low_s.at[:, cols], outs[0].at[:, cols])]))
        done.append(loads.start([(sum_s, outs[1])]))
        for group in g_wu:
            loads.wait(group)
        two_s[...] = dot(low_s[...], wu_s[...], NT).astype(BF)
        done.append(loads.start([(two_s, outs[2])]))
        loads.wait(g_a)
        mlp_s[...] = dot(a_s[...], wd_s[...], NN).astype(BF)
        done.append(loads.start([(mlp_s, outs[3])]))
        for group in done:
            loads.wait(group)

    return call(
        body,
        [grad, act, dact] + down_arrays + up_arrays,
        [sds((rows, hid), BF), sds((1, hid), F32), sds((rows, width), BF), sds((rows, width), BF)],
        [
            pltpu.VMEM(down_scratch, BF),
            pltpu.VMEM(up_scratch, BF),
            pltpu.VMEM((rows, width), BF),
            pltpu.VMEM((rows, hid), BF),
            pltpu.VMEM((rows, hid), BF),
            pltpu.VMEM((rows, hid), BF),
            pltpu.VMEM((1, hid), F32),
            pltpu.VMEM((rows, width), BF),
            pltpu.VMEM((rows, width), BF),
        ],
        "mlp_back",
        6 * rows * width * hid,
        sems=64,
    )


def rows_times(lefts, row_range, weight, dims, split, width, name):
    arrays, plan, shape = weight
    lo, hi = row_range
    rows = hi - lo
    n = len(lefts)

    def body(small, ins, outs, scratch, loads):
        w_s, out_s = scratch[0], scratch[1]
        l_s = scratch[2:]
        g_l = loads.start([(ins[i].at[lo:hi], l_s[i]) for i in range(n)])
        g_w = weight_loads(loads, plan, ins[n:], w_s)
        loads.wait(g_l)
        for group in g_w:
            loads.wait(group)
        total = None
        for i in range(n):
            w = w_s[i].reshape(-1, shape[-1]) if split else w_s[...]
            piece = dot(l_s[i][...], w, dims)
            total = piece if total is None else total + piece
        out_s[...] = total.astype(BF)
        loads.wait(loads.start([(out_s, outs[0])]))

    return call(
        body,
        list(lefts) + arrays,
        [sds((rows, width), BF)],
        [pltpu.VMEM(shape, BF), pltpu.VMEM((rows, width), BF)]
        + [pltpu.VMEM((rows, a.shape[1]), BF) for a in lefts],
        name,
        2 * rows * width * sum(a.shape[1] for a in lefts),
    )[0]


def store_blocks(ids_ref, out_s, value, nd, aligned):
    width = value.shape[1]
    bd = width // nd
    if not aligned:
        out_s[...] = value
        return
    for p in range(nd):
        cols = pl.ds(pl.multiple_of(ids_ref[2 + p] * bd, 128), bd)
        out_s[:, cols] = value[:, p * bd : (p + 1) * bd]


def middle_back(ids, middle, part, recvs, cot, keep, nv, wout):
    _, seq, width = middle.shape
    out_arrays, out_plan, out_scratch = wout
    ext = out_scratch[0]

    def body(small, ins, outs, scratch, loads):
        ids_ref, keep_ref, nv_ref = small
        mine = ids_ref[0]
        wo_s, mid_s, part_s, recv_s, cot_s, gmid_s, gat_s, do_s = scratch[:8]
        cs_s = scratch[8]
        g_in = [
            loads.start(
                [
                    (ins[0].at[a], mid_s.at[a]),
                    (ins[1].at[a], part_s.at[a]),
                    (ins[2].at[a], cot_s.at[a]),
                    (ins[3 + a], recv_s.at[a]),
                ]
            )
            for a in range(2)
        ]
        g_o = weight_loads(loads, out_plan, ins[5:], wo_s)
        done = []
        for a in range(2):
            loads.wait(g_in[a])
            keep_here = keep_ref[a]
            hat, inverse = norm_parts(mid_s[a])
            grad_two = part_s[a].astype(F32) + recv_s[a].astype(F32)
            top = cot_s[a].astype(F32)
            grad_mid = top + norm_back(grad_two, hat, inverse, nv_ref[1:2, :])
            grad_attn = grad_mid * keep_here
            sums = [
                jnp.sum(grad_two * hat, axis=0, keepdims=True),
                jnp.sum(grad_two, axis=0, keepdims=True),
                jnp.sum(grad_attn, axis=0, keepdims=True),
                jnp.sum(top, axis=0, keepdims=True) * keep_here,
            ]
            for i, value in enumerate(sums):
                cs_s[i : i + 1, :] = value if a == 0 else cs_s[i : i + 1, :] + value
            gmid_s[a] = grad_mid
            gat_s[a] = grad_attn.astype(BF)
            done.append(loads.start([(gat_s.at[a], outs[1].at[a])]))
            if a == 0:
                loads.wait(g_o[0])
            do_s[a] = dot(gat_s[a], wo_s[...], NT).astype(BF)
            done.append(loads.start([(do_s.at[a], outs[2].at[a])]))
        done.append(loads.start([(gmid_s.at[mine], outs[0]), (cs_s, outs[3])]))
        for group in done:
            loads.wait(group)

    return call(
        body,
        [middle, part, cot] + list(recvs) + out_arrays,
        [
            sds((seq, width), F32),
            sds((2, seq, width), BF),
            sds((2, seq, ext), BF),
            sds((4, width), F32),
        ],
        [
            pltpu.VMEM(out_scratch, BF),
            pltpu.VMEM((2, seq, width), F32),
            pltpu.VMEM((2, seq, width), BF),
            pltpu.VMEM((2, seq, width), BF),
            pltpu.VMEM((2, seq, width), BF),
            pltpu.VMEM((2, seq, width), F32),
            pltpu.VMEM((2, seq, width), BF),
            pltpu.VMEM((2, seq, ext), BF),
            pltpu.VMEM((4, width), F32),
        ],
        "middle_back",
        4 * seq * width * ext,
        smem=(ids, keep),
        vmem_ins=(nv,),
    )


def attn_backward(image, grad, q, k, v, prev):
    _, seq, ext = q.shape
    n_prev = 0 if prev is None else len(prev)

    def body(small, ins, outs, scratch, loads):
        q_s, k_s, v_s, do_s, dq_s, dk_s, dv_s, bs_s = scratch
        n_pairs = ext // 128
        groups = []
        for i in range(n_pairs):
            cols = slice(i * 128, (i + 1) * 128)
            groups.append(
                loads.start(
                    [
                        (ins[j].at[image, :, cols], scratch[j].at[:, cols])
                        for j in range(4)
                    ]
                )
            )
        half = lax.broadcasted_iota(jnp.int32, (1, 128), 1) // HEAD_DIM
        for group in groups:
            loads.wait(group)

        def pair(i, carry):
            cols = pl.ds(pl.multiple_of(i * 128, 128), 128)
            q2, k2, v2, do2 = q_s[:, cols], k_s[:, cols], v_s[:, cols], do_s[:, cols]
            dq = dk = dv = None
            for h in range(2):
                mask = (half == h).astype(BF)
                km, qm, dom = k2 * mask, q2 * mask, do2 * mask
                scores = dot(km, q2, NT)
                row = lax.broadcasted_iota(jnp.int32, scores.shape, 0)
                scores = jnp.where(row < VALID, scores, -1e30)
                e = jnp.exp(scores - jnp.max(scores, axis=0, keepdims=True))
                probs = e * (1.0 / jnp.sum(e, axis=0, keepdims=True))
                grad_probs = dot(v2, dom, NT)
                row_dot = jnp.sum(probs * grad_probs, axis=0, keepdims=True)
                grad_scores = (probs * (grad_probs - row_dot)).astype(BF)
                v_piece = dot(probs.astype(BF), dom, NN)
                k_piece = dot(grad_scores, qm, NN)
                q_piece = dot(grad_scores, km, TN)
                dq = q_piece if dq is None else dq + q_piece
                dk = k_piece if dk is None else dk + k_piece
                dv = v_piece if dv is None else dv + v_piece
            dq = dq * HEAD_DIM**-0.5
            bs_s[0:1, cols] = jnp.sum(dq, axis=0, keepdims=True)
            bs_s[1:2, cols] = jnp.sum(dv, axis=0, keepdims=True)
            dq_s[:, cols] = dq.astype(BF)
            dk_s[:, cols] = dk.astype(BF)
            dv_s[:, cols] = dv.astype(BF)
            return carry

        lax.fori_loop(0, n_pairs, pair, 0)
        g_out = loads.start(
            [
                (dq_s, outs[0].at[image]),
                (dk_s, outs[1].at[image]),
                (dv_s, outs[2].at[image]),
                (bs_s, outs[3]),
            ]
        )
        loads.wait(g_out)

    return call(
        body,
        [q, k, v, grad] + list(prev or []),
        [sds((2, seq, ext), BF)] * 3 + [sds((2, ext), F32)],
        [pltpu.VMEM((seq, ext), BF)] * 7 + [pltpu.VMEM((2, ext), F32)],
        "attn_backward",
        40 * seq * seq * ext,
        aliases={4 + i: i for i in range(n_prev)},
    )


def finish_layer(ids, keep, nv, middle, part, recv, nd, aligned):
    _, seq, width = middle.shape

    def body(small, ins, outs, scratch, loads):
        ids_ref, keep_ref, nv_ref = small
        mine = ids_ref[0]
        mid_s, part_s, recv_s, out_s = scratch
        groups = [loads.start([(ins[i].at[mine], scratch[i])]) for i in range(3)]
        for group in groups:
            loads.wait(group)
        total = part_s[...].astype(F32) + recv_s[...].astype(F32) + nv_ref[5:6, :]
        value = (mid_s[...] + keep_ref[mine] * total).astype(BF)
        store_blocks(ids_ref, out_s, value, nd, aligned)
        loads.wait(loads.start([(out_s, outs[0])]))

    return call(
        body,
        [middle, part, recv],
        [sds((seq, width), BF)],
        [pltpu.VMEM((seq, width), F32)] + [pltpu.VMEM((seq, width), BF)] * 3,
        "finish_layer",
        100 * seq * width,
        smem=(ids, keep),
        vmem_ins=(nv,),
    )[0]


def finish_tokens(ids, nv, tok, part, recvs, gmid, nd, aligned):
    _, seq, width = tok.shape

    def body(small, ins, outs, scratch, loads):
        ids_ref, nv_ref = small
        mine = ids_ref[0]
        tok_s, part_s, recv_s, gm_s, out_s, cs_s = scratch
        groups = [
            loads.start(
                [
                    (ins[0].at[a], tok_s.at[a]),
                    (ins[1].at[a], part_s.at[a]),
                    (ins[3 + a], recv_s.at[a]),
                ]
            )
            for a in range(2)
        ]
        g_mid = loads.start([(ins[2], gm_s)])
        for group in groups:
            loads.wait(group)
        done = []
        for i in range(2):
            a = mine if i == 0 else 1 - mine
            hat, inverse = norm_parts(tok_s[a].astype(F32))
            grad_one = part_s[a].astype(F32) + recv_s[a].astype(F32)
            gain_sum = jnp.sum(grad_one * hat, axis=0, keepdims=True)
            shift_sum = jnp.sum(grad_one, axis=0, keepdims=True)
            if i == 0:
                cs_s[0:1, :] = gain_sum
                cs_s[1:2, :] = shift_sum
                loads.wait(g_mid)
                value = gm_s[...] + norm_back(grad_one, hat, inverse, nv_ref[0:1, :])
                store_blocks(ids_ref, out_s, value.astype(BF), nd, aligned)
                done.append(loads.start([(out_s, outs[0])]))
            else:
                cs_s[0:1, :] = cs_s[0:1, :] + gain_sum
                cs_s[1:2, :] = cs_s[1:2, :] + shift_sum
        done.append(loads.start([(cs_s, outs[1])]))
        for group in done:
            loads.wait(group)

    return call(
        body,
        [tok, part, gmid] + list(recvs),
        [sds((seq, width), BF), sds((2, width), F32)],
        [pltpu.VMEM((2, seq, width), BF)] * 3
        + [pltpu.VMEM((seq, width), F32), pltpu.VMEM((seq, width), BF), pltpu.VMEM((2, width), F32)],
        "finish_tokens",
        200 * seq * width,
        smem=(ids,),
        vmem_ins=(nv,),
    )


class Grid3:
    def __init__(self, dp, tx):
        self.dp, self.tx = dp, tx
        self.y = 2 if dp % 2 == 0 else 1
        self.z = dp // self.y

    def send_z(self, value, k):
        return lax.ppermute(value, "dp", [(i, i ^ (k * self.y)) for i in range(self.dp)])

    def send_y(self, value, k):
        return lax.ppermute(value, "dp", [(i, i ^ k) for i in range(self.dp)])

    def send_x(self, value, k):
        return lax.ppermute(value, "tx", [(i, i ^ k) for i in range(self.tx)])


def swap_core(value):
    return lax.ppermute(value, "core", [(0, 1), (1, 0)])


def after(values, gate):
    return lax.optimization_barrier((values, gate))[0]


def gather_z(grid, part_a, part_b, gate=None):
    rows = part_a.shape[0]
    both = jnp.concatenate([part_a, part_b], axis=0)
    all_z = [both] + [grid.send_z(both, k) for k in range(1, grid.z)]
    if gate is not None:
        all_z = after(all_z, gate)
    return jnp.stack([v[:rows] for v in all_z]), jnp.stack([v[rows:] for v in all_z])


def gather_first(grid, a_z, b_z):
    a_y = [a_z] + [grid.send_y(a_z, k) for k in range(1, grid.y)]
    b_x = [b_z] + [grid.send_x(b_z, k) for k in range(1, grid.tx)]
    return a_y, b_x


def gather_last(grid, a_y, b_x):
    a_y, b_x = jnp.concatenate(a_y), jnp.concatenate(b_x)
    a_all = [a_y] + [grid.send_x(a_y, k) for k in range(1, grid.tx)]
    b_all = [b_x] + [grid.send_y(b_x, k) for k in range(1, grid.y)]
    return a_all, b_all


def add_low(first, *others):
    total = first.astype(F32)
    for other in others:
        total = total + other.astype(F32)
    return total.astype(BF)


class Scatter:
    def __init__(self, grid, a_all, b_all):
        self.grid, self.rows = grid, a_all[0].shape[1]
        a_got = [grid.send_x(a_all[k], k) for k in range(1, grid.tx)]
        b_got = [grid.send_y(b_all[k], k) for k in range(1, grid.y)]
        self.state = ([a_all[0]] + a_got, [b_all[0]] + b_got)

    def second(self, gate):
        grid, z = self.grid, self.grid.z
        a_in, b_in = after(self.state, gate)
        a_y = [add_low(*[v[k * z : (k + 1) * z] for v in a_in]) for k in range(grid.y)]
        b_x = [add_low(*[v[k * z : (k + 1) * z] for v in b_in]) for k in range(grid.tx)]
        a_got = [grid.send_y(a_y[k], k) for k in range(1, grid.y)]
        b_got = [grid.send_x(b_x[k], k) for k in range(1, grid.tx)]
        self.state = ([a_y[0]] + a_got, [b_x[0]] + b_got)
        return a_y[0], b_x[0]

    def along_z(self, gate):
        grid = self.grid
        a_in, b_in = after(self.state, gate)
        both = [
            jnp.concatenate([add_low(*[v[k] for v in a_in]), add_low(*[v[k] for v in b_in])])
            for k in range(grid.z)
        ]
        got = [grid.send_z(both[k], k) for k in range(1, grid.z)]
        self.state = [both[0]] + got
        return both

    def finish(self, gate):
        parts = after(self.state, gate)
        total = parts[0].astype(F32)
        for value in parts[1:]:
            total = total + value.astype(F32)
        return total[: self.rows], total[self.rows :]


def xor_blocks(value, mask, axis):
    count = value.shape[axis]
    bit = 1
    while bit < count:
        shape = value.shape
        split = value.reshape(shape[:axis] + (count // (2 * bit), 2, bit) + shape[axis + 1 :])
        turned = jnp.flip(split, axis=axis + 1).reshape(shape)
        value = jnp.where(jnp.bitwise_and(mask, bit) != 0, turned, value)
        bit *= 2
    return value


def pad_cols(value, width):
    return jnp.pad(value, ((0, 0), (0, width - value.shape[1])))


def per_device(
    tokens,
    cotangent,
    image_mask,
    norm_gains,
    norm_shifts,
    w_qkv,
    b_qv,
    w_out,
    w_up,
    up_bias,
    w_down,
    *,
    dp,
    tx,
):
    grid = Grid3(dp, tx)
    y_n, z_n = grid.y, grid.z
    core = lax.axis_index("core").astype(jnp.int32)
    me_d = lax.axis_index("dp").astype(jnp.int32)
    me_x = lax.axis_index("tx").astype(jnp.int32)
    seq, width = tokens.shape
    _, bd, hw = w_qkv.shape
    fw = w_up.shape[1]
    ext, hid = tx * hw, tx * fw
    hh, fh = hw // 2, fw // 2
    aligned = bd % 128 == 0 and hh % 128 == 0 and fh % 128 == 0
    rel = [kz * y_n + ky for ky in range(y_n) for kz in range(z_n)]

    def from_abs(value, axis):
        shape = value.shape
        value = value.reshape(shape[:axis] + (z_n, y_n) + shape[axis + 1 :])
        return jnp.swapaxes(value, axis, axis + 1).reshape(shape)

    def to_rel(value, axis):
        shape = value.shape
        value = value.reshape(shape[:axis] + (y_n, z_n) + shape[axis + 1 :])
        return jnp.swapaxes(value, axis, axis + 1).reshape(shape)

    ids = jnp.stack([core, me_d] + [jnp.bitwise_xor(me_d, k) for k in rel])
    keep = lax.dynamic_slice(image_mask, (2 * me_x,), (2,)).astype(F32)

    lane = max(bd, hh)
    small = jnp.concatenate(
        [
            pad_cols(norm_gains, lane),
            pad_cols(norm_shifts, lane),
            pad_cols(b_qv, lane),
            pad_cols(up_bias[None], lane),
            jnp.zeros((7, lane), BF),
        ]
    )
    qkv_a = pad_cols(w_qkv[:, :, :hh].reshape(3 * bd, hh), lane)
    qkv_b = pad_cols(w_qkv[:, :, hh:].reshape(3 * bd, hh), lane)
    first_a = jnp.concatenate([qkv_a, pad_cols(w_out[:hh], lane)])
    first_b = jnp.concatenate([qkv_b, pad_cols(w_out[hh:], lane)])
    tok_other, cot_other = swap_core(tokens), swap_core(cotangent)
    if aligned:
        tok, cot = arrange_pair(ids, [tokens, cotangent], [tok_other, cot_other], dp)
    else:

        def arrange(own, other):
            pair = jnp.where(core == 0, jnp.stack([own, other]), jnp.stack([other, own]))
            pair = xor_blocks(pair.reshape(2, seq, dp, bd), me_d, 2)
            return from_abs(pair, 2).reshape(2, seq, width)

        tok, cot = arrange(tokens, tok_other), arrange(cotangent, cot_other)
    c1_z = gather_z(grid, first_a, first_b, gate=tok)
    small = jnp.stack([small] + [grid.send_z(small, k) for k in range(1, z_n)])
    small = jnp.concatenate([small] + [grid.send_y(small, k) for k in range(1, y_n)])
    small = [small] + [grid.send_x(small, k) for k in range(1, tx)]
    up_halves = after((w_up[:, :fh], w_up[:, fh:]), c1_z)
    c1_h = gather_first(grid, *c1_z)
    c1a, c1b = gather_last(grid, *c1_h)
    up_z = gather_z(grid, *up_halves, gate=(c1a, c1b))
    dn_halves = after((w_down[:fh], w_down[fh:]), (c1a, c1b))
    up_h = gather_first(grid, *up_z)

    grad_top = cot * keep.astype(BF)[:, None, None]

    nv = small[0][:, :6, :bd].transpose(1, 0, 2).reshape(6, width).astype(F32)
    tail = jnp.stack([v[:, 6:9] for v in small])
    tail = xor_blocks(to_rel(tail, 1), me_d, 1)
    bq = (
        tail[:, :, :2, : hw // dp].transpose(2, 0, 1, 3).reshape(2, ext).astype(F32)
    )
    bu = tail[:, :, 2, : fw // dp].reshape(1, hid).astype(F32)

    if aligned:
        every, wq_plan, wo_plan, up_plan, dn_plan = slice(None), [[], [], []], [], [], []
        for kx in range(tx):
            halves = [slice(kx * hw, kx * hw + hh), slice(kx * hw + hh, (kx + 1) * hw)]
            f_halves = [slice(kx * fw, kx * fw + fh), slice(kx * fw + fh, (kx + 1) * fw)]
            own = slice(kx * z_n, (kx + 1) * z_n)
            for i in range(3):
                src = slice(i * bd, (i + 1) * bd)
                wq_plan[i].append((kx, (every, src), (i, every, every, halves[0])))
                for ky in range(y_n):
                    dst = (i, slice(ky * z_n, (ky + 1) * z_n), every, halves[1])
                    wq_plan[i].append((tx + ky, (own, src), dst))
            src = slice(3 * bd, 3 * bd + hh)
            dn_plan += [[], []]
            for ky in range(y_n):
                for kz in range(z_n):
                    p, r = ky * z_n + kz, kx * z_n + kz
                    cols = slice(p * bd, (p + 1) * bd)
                    wo_plan.append((kx, (p, src), (halves[0], cols)))
                    wo_plan.append((tx + ky, (r, src), (halves[1], cols)))
                    dn_plan[-2].append((kx, (p,), (f_halves[0], cols)))
                    dn_plan[-1].append((tx + ky, (r,), (f_halves[1], cols)))
            up_plan += [[(kx, (every,), (every, f_halves[0]))], []]
            for ky in range(y_n):
                rows = slice(kx * z_n * bd, (kx + 1) * z_n * bd)
                dst = (slice(ky * z_n * bd, (ky + 1) * z_n * bd), f_halves[1])
                up_plan[-1].append((tx + ky, (rows,), dst))
        c1 = c1a + c1b
        wqkv = (c1, wq_plan, (3, dp, bd, ext))
        wout = (c1, [wo_plan], (ext, width))
    else:

        def whole(a_all, b_all):
            a = jnp.stack(a_all)
            b = jnp.stack(b_all).reshape((y_n, tx, z_n) + b_all[0].shape[1:])
            b = b.transpose(1, 0, 2, 3, 4).reshape(a.shape[:2] + b.shape[3:])
            return jnp.stack([a, b], axis=1)

        c1 = whole(c1a, c1b)
        qkv = c1[:, :, :, : 3 * bd, :hh].reshape(tx, 2, dp, 3, bd, hh)
        qkv = qkv.transpose(3, 2, 4, 0, 1, 5).reshape(3, dp, bd, ext)
        out = c1[:, :, :, 3 * bd :, :bd].transpose(0, 1, 3, 2, 4).reshape(ext, width)
        all_of = [[(0, (slice(None),), (slice(None),))]]
        wqkv = ([qkv], all_of, qkv.shape)
        wout = ([out], all_of, out.shape)

    rows2 = 2 * seq

    res = attn_forward(0, after(tok, up_z), nv, bq, wqkv, wout, None)
    parts = [(res[5], swap_core(res[5]))]
    upa, upb = gather_last(grid, *after(up_h, res[5]))
    dn_z = gather_z(grid, *dn_halves, gate=res[5])
    dn_h = gather_first(grid, *dn_z)
    res = attn_forward(1, after(tok, dn_z), nv, bq, wqkv, wout, res[:5])
    parts.append((res[5], swap_core(res[5])))
    first, q, k, v, att = res[:5]
    upa, upb = after((upa, upb), res[5])
    dna, dnb = gather_last(grid, *after(dn_h, (upa, upb)))
    if aligned:
        wup = ([v.reshape(-1, fh) for v in upa + upb], up_plan, (width, hid))
        wdown = (dna + dnb, dn_plan, (hid, width))
    else:
        up_w = whole(upa, upb).transpose(2, 3, 0, 1, 4).reshape(width, hid)
        down_w = whole(dna, dnb).transpose(0, 1, 3, 2, 4).reshape(hid, width)
        wup = ([up_w], all_of, up_w.shape)
        wdown = ([down_w], all_of, down_w.shape)
    state = None
    for image in range(2):
        part, recv = parts[image]
        state = mlp_up(image, tok, part, recv, keep, nv, bu, wup, fh, state)
    middle, second, act, dact = state
    flat = lambda value: value.reshape(rows2, value.shape[2])
    act2, sec2, grad2 = flat(act), flat(second), flat(grad_top)

    order_x, order_y = list(range(1, tx)) + [0], list(range(1, y_n)) + [0]
    d_all = slice(0, width)
    d_half = [slice(ky * z_n * bd, (ky + 1) * z_n * bd) for ky in range(y_n)]

    def spots(ky, kx):
        if ky is None:
            return [(order_x.index(kx), p, slice(p * bd, (p + 1) * bd)) for p in range(dp)]
        which = tx + order_y.index(ky)
        return [(which, kx * z_n + kz, slice(kz * bd, (kz + 1) * bd)) for kz in range(z_n)]

    def cut(kx, size, ky):
        start = kx * size + (0 if ky is None else size // 2)
        return slice(start, start + size // 2)

    def visits():
        for kx in order_x:
            yield None, kx, d_all
        for ky in order_y:
            for kx in range(tx):
                yield ky, kx, d_half[ky]

    full = slice(None)

    def by_left(l_index, r_index, size, row0):
        rows = slice(row0, row0 + size // 2)
        return [
            (
                l_index,
                cut(kx, size, ky),
                r_index,
                d_cols,
                [(w, (spot, rows), full, cols) for w, spot, cols in spots(ky, kx)],
            )
            for ky, kx, d_cols in visits()
        ]

    def by_right(l_index, r_index, size, row0, lanes):
        tasks = []
        for ky, kx, d_cols in visits():
            stores = []
            for j in range(size // 2 // lanes):
                rows = slice(row0 + j * bd, row0 + (j + 1) * bd)
                cols = slice(j * lanes, (j + 1) * lanes)
                stores += [(w, (spot, rows), r_sl, cols) for w, spot, r_sl in spots(ky, kx)]
            tasks.append((l_index, d_cols, r_index, cut(kx, size, ky), stores))
        return tasks

    def start_grad(lefts, rights, makers, rows, lanes, name):
        tasks = []
        for group in zip(*makers):
            tasks += group
        shapes = [(dp, rows, lanes)] * tx + [(tx * z_n, rows, lanes)] * y_n
        parts = weight_grad(lefts, rights, tasks, shapes, name)
        by_x, by_y = list(parts[:tx]), list(parts[tx:])
        return Scatter(grid, by_x[-1:] + by_x[:-1], by_y[-1:] + by_y[:-1]), parts[-1]

    down_rs, gate = start_grad([act2], [grad2], [by_left(0, 0, fw, 0)], fh, bd, "down_grad")
    grad_in = after(grad2, gate)
    low_pre, bias_up, two_part, mlp_part = mlp_back(grad_in, act2, flat(dact), wdown, wup, fh)
    two_part = two_part.reshape(2, seq, width)
    mlp_part = mlp_part.reshape(2, seq, width)
    mlp_recv = swap_core(mlp_part)
    two_recvs = [swap_core(two_part[a]) for a in range(2)]
    down_half = down_rs.second(bias_up)
    gmid, gattn, grad_att, col = middle_back(
        ids, middle, two_part, after(two_recvs, down_half), cot, keep, nv, wout
    )
    down_zs = down_rs.along_z(col)
    up_rows = fh // bd * bd
    up_rs, gate = start_grad(
        [sec2, flat(att)],
        [low_pre, after(flat(gattn), down_zs)],
        [by_right(0, 0, fw, 0, bd), by_left(1, 1, hw, up_rows)],
        up_rows + hh,
        bd,
        "up_out_grad",
    )

    down_a, down_b = down_rs.finish(gate)
    res = attn_backward(0, after(grad_att, (gate, down_a)), q, k, v, None)
    bias_qv = res[3]
    up_half = up_rs.second(bias_qv)
    res = attn_backward(1, after(grad_att, up_half), q, k, v, res[:3])
    bias_qv = bias_qv + res[3]
    up_zs = up_rs.along_z(res[3])
    low_proj = [flat(value) for value in res[:3]]
    makers = [by_right(0, i, hw, i * bd, hh) for i in range(3)]
    first_in = after(flat(first), up_zs)
    qkv_rs, gate = start_grad([first_in], low_proj, makers, 3 * bd, hh, "qkv_grad")
    low_in = after(low_proj, gate)
    one_part = rows_times(low_in, (0, rows2), wqkv, NT, True, width, "grad_one")
    one_part = one_part.reshape(2, seq, width)
    one_recvs = [swap_core(one_part[a]) for a in range(2)]
    up_a, up_b = up_rs.finish(one_part)
    qkv_half = qkv_rs.second(up_a)
    layer_out = finish_layer(
        ids, keep, nv, middle, after(mlp_part, qkv_half), mlp_recv, dp, aligned
    )
    grad_tokens, one_sums = finish_tokens(
        ids, nv, tok, one_part, after(one_recvs, layer_out), gmid, dp, aligned
    )
    qkv_rs.along_z(one_sums)
    qkv_ga, qkv_gb = qkv_rs.finish(one_sums)
    out_a, out_b = up_a[up_rows:], up_b[up_rows:]

    def lanes_back(value):
        value = value[:up_rows].reshape(fh // bd, bd, bd)
        return value.transpose(1, 0, 2).reshape(bd, fh)

    up_a, up_b = lanes_back(up_a), lanes_back(up_b)
    if not aligned:

        def restore(value):
            value = xor_blocks(to_rel(value.reshape(seq, dp, bd), 1), me_d, 1)
            return value.reshape(seq, width)

        layer_out, grad_tokens = restore(layer_out), restore(grad_tokens)

    vec = jnp.stack([one_sums[0], col[0], one_sums[1], col[1], col[2], col[3]])
    wide = max(bd, hw // dp, fw // dp)
    vec = vec.reshape(6, dp, bd).transpose(1, 0, 2)
    vec = jnp.pad(vec, ((0, 0), (0, 0), (0, wide - bd)))
    bias_qv = bias_qv.reshape(2, tx, dp, hw // dp).transpose(2, 1, 0, 3).reshape(dp, 2 * tx, -1)
    bias_up = bias_up.reshape(tx, dp, fw // dp).transpose(1, 0, 2)
    bias = jnp.concatenate(
        [
            jnp.pad(bias_qv, ((0, 0), (0, 0), (0, wide - hw // dp))),
            jnp.pad(bias_up, ((0, 0), (0, 0), (0, wide - fw // dp))),
        ],
        axis=1,
    )
    bias = from_abs(xor_blocks(bias, me_d, 0), 0)
    both = jnp.concatenate([vec, bias], axis=1)
    got = [both] + [grid.send_x(both, k) for k in range(1, tx)]
    vec = sum(value[:, :6] for value in got)
    bqv_mine = sum(value[:, 6 + 2 * k : 8 + 2 * k] for k, value in enumerate(got))
    bup_mine = sum(
        value[:, 6 + 2 * tx + k : 7 + 2 * tx + k] for k, value in enumerate(got)
    )
    both = jnp.concatenate([vec, bqv_mine, bup_mine], axis=1)
    both = both[:z_n] + sum(
        grid.send_y(both[k * z_n : (k + 1) * z_n], k) for k in range(1, y_n)
    )
    both = both[0] + sum(grid.send_z(both[k], k) for k in range(1, z_n))
    share = bd // (2 * tx)
    mine = lax.dynamic_slice(both[:6, :bd], (0, (2 * me_x + core) * share), (6, share))

    grad_qkv = jnp.concatenate(
        [qkv_ga.reshape(3, bd, hh), qkv_gb.reshape(3, bd, hh)], axis=2
    )
    grad_out = jnp.concatenate([out_a, out_b], axis=0)
    grad_up = jnp.concatenate([up_a, up_b], axis=1)
    grad_down = jnp.concatenate([down_a, down_b], axis=0)
    return (
        layer_out,
        grad_tokens,
        mine[:2],
        mine[2:6],
        grad_qkv,
        both[6:8, : hw // dp],
        grad_out,
        grad_up,
        both[8, : fw // dp],
        grad_down,
    )


def solution(mesh):
    dp, tensor = mesh.shape["dp"], mesh.shape["tensor"]
    split = Mesh(mesh.devices.reshape(dp, tensor // 2, 2), ("dp", "tx", "core"))
    every = ("dp", "tx", "core")
    tensor_axes = ("tx", "core")
    in_specs = (
        P(every, None),
        P(every, None),
        P("dp"),
        P(None, "dp"),
        P(None, "dp"),
        P(None, "dp", tensor_axes),
        P(None, ("tx", "core", "dp")),
        P(tensor_axes, "dp"),
        P("dp", tensor_axes),
        P(("tx", "core", "dp")),
        P(tensor_axes, "dp"),
    )
    out_specs = (
        P(every, None),
        P(every, None),
        P(None, every),
        P(None, every),
        P(None, "dp", tensor_axes),
        P(None, ("tx", "core", "dp")),
        P(tensor_axes, "dp"),
        P("dp", tensor_axes),
        P(("tx", "core", "dp")),
        P(tensor_axes, "dp"),
    )
    return jax.shard_map(
        functools.partial(per_device, dp=dp, tx=tensor // 2),
        mesh=split,
        in_specs=in_specs,
        out_specs=out_specs,
        check_vma=False,
    )
```

time: 644 us -> 408 us (0.63)
  Pallas kernels: 353 us -> 184 us
  waiting for transfers between devices: 132 us -> 64.5 us
  starting transfers between devices: 79.7 us -> 88 us
    pallas_call x22 -> x15, Pallas kernels: 353 us -> 184 us  [call(): pl.pallas_call(kernel, out_shape=outs, in_specs=[pl.BlockSpec(memory_spac...]
    ppermute x24, waiting for transfers between devices: 63.8 us -> 7.44 us  [send_z(): lax.ppermute(value, 'dp', [(i, i ^ k * self.y) for i in range(self.dp)])]
    ppermute x15 -> x14, waiting for transfers between devices: 37.9 us -> 30.9 us  [send_x(): return lax.ppermute(value, 'tx', [(i, i ^ k) for i in range(self.tx)])]
    ppermute x15 -> x14, waiting for transfers between devices: 30.8 us -> 26.1 us  [send_y(): return lax.ppermute(value, 'dp', [(i, i ^ k) for i in range(self.dp)])]
    unnamed x91 -> x74, local copies, waits for them, and re-layouts: 13.4 us -> 8.88 us
    ppermute x15 -> x14, starting transfers between devices: 14.8 us -> 17.4 us  [send_y(): return lax.ppermute(value, 'dp', [(i, i ^ k) for i in range(self.dp)])]
    convert_element_type x16 -> x12, other arithmetic: 15.1 us -> 12.8 us  [add_low(): return total.astype(BF)]
    ppermute x15 -> x14, starting transfers between devices: 16.9 us -> 16.6 us  [send_x(): return lax.ppermute(value, 'tx', [(i, i ^ k) for i in range(self.tx)])]
  transfers between devices with their start and end apart: 62 -> 61, of which waited for: 18 -> 17; matrix products, arithmetic and copies ran while one was open for 9% -> 14% of each run, Pallas kernels for 55% -> 46%
where the time goes in v2:
time: 408 us; the launch traced here: 401 us
  Pallas kernels  184 us (45%)
  starting transfers between devices  88 us (22%)
  waiting for transfers between devices  64.5 us (16%)
  local copies, waits for them, and re-layouts  33.5 us (8%)
  other arithmetic  29.3 us (7%)
    pallas_call x15, Pallas kernels, call(): pl.pallas_call(kernel, out_shape=outs, in_specs=[pl.BlockSpec(memory_spac...  184 us
    ppermute x24, starting transfers between devices, send_z(): lax.ppermute(value, 'dp', [(i, i ^ k * self.y) for i in range(self.dp)])  52.3 us
    ppermute x14, waiting for transfers between devices, send_x(): return lax.ppermute(value, 'tx', [(i, i ^ k) for i in range(self.tx)])  30.9 us
    ppermute x14, waiting for transfers between devices, send_y(): return lax.ppermute(value, 'dp', [(i, i ^ k) for i in range(self.dp)])  26.1 us
    ppermute x14, starting transfers between devices, send_y(): return lax.ppermute(value, 'dp', [(i, i ^ k) for i in range(self.dp)])  17.4 us
    ppermute x14, starting transfers between devices, send_x(): return lax.ppermute(value, 'tx', [(i, i ^ k) for i in range(self.tx)])  16.6 us
    convert_element_type x12, other arithmetic, add_low(): return total.astype(BF)  12.8 us
    unnamed x74, local copies, waits for them, and re-layouts  8.88 us
  transfers between devices with their start and end apart: 61, of which 17 were waited for; matrix products, arithmetic and copies ran while one was open for 14% of the time, Pallas kernels for 46%

profile of v2, /device:TPU:0, one launch (start us, length us, event | category | flops | bytes accessed | tf_op | source)
XLA Modules:
  0.0 401.3 jit_solution(265421478579794821)
XLA Ops:
  2.8 3.0 collective-permute-start
  5.9 2.6 collective-permute-start.1
  11.2 3.5 collective-permute-start.8
  14.7 1.7 fusion.36
  18.8 1.6 collective-permute-start.3
  20.4 2.2 collective-permute-done.3
  22.6 1.5 collective-permute-start.4
  24.7 1.8 collective-permute-done.4
  27.8 4.9 %arrange_pair.1 = (bf16[2,584,1024]{2,1,0:T(8,128)(2,1)}, bf16[2,584,1024]{2,1,0:T(8,128)(2,1)}) custom-call(s32[10]{0:T(128)} %stack.158.refs_0_, bf16[584,1024]{1,0:T(8,128)(2,1)} %refs_1_.1, bf16[584,1024]{1,0:T(8,128)(2,1)} %refs_2_.1, bf16[584,1024]{1,0:T(8,128)(2,1)} %copy-done.8, bf16[584,1024]{1,0:T(8,128)(2,1)} %collective-permute-done.6.refs_4_), custom_call_target="tpu_custom_call" | custom-call | bytes 191365120 | tf_op jit(solution)/shard_map/arrange_pair/pallas_call | solution.py:58
  32.7 2.3 collective-permute-done.9
  35.9 1.6 collective-permute-start.10
  37.5 1.6 collective-permute-start.12
  41.3 5.9 %collective-permute-done.10 = bf16[4,512,128]{2,1,0:T(8,128)(2,1)S(1)} collective-permute-done((bf16[4,512,128]{2,1,0:T(8,128)(2,1)S(1)}, bf16[4,512,128]{2,1,0:T(8,128)(2,1)S(1)}, u32[]{:S(2)}, u32[]{:S(2)}) %collective-permute-start.10) | collective-permute-done | bytes 524320 | tf_op jit(solution)/shard_map/ppermute | solution.py:676
  48.0 1.5 collective-permute-start.11
  53.2 3.5 collective-permute-start.17
  56.7 1.7 collective-permute-start.18
  59.8 1.8 broadcast_multiply_fusion
  61.6 9.5 %collective-permute-done.11.refs_4_.refs_8_.refs_9_.refs_13_ = bf16[8,512,128]{2,1,0:T(8,128)(2,1)} collective-permute-done((bf16[8,512,128]{2,1,0:T(8,128)(2,1)}, bf16[8,512,128]{2,1,0:T(8,128)(2,1)}, u32[]{:S(2)}, u32[]{:S(2)}) %collective-permute-start.11) | collective-permute-done | bytes 1048608 | tf_op jit(solution)/shard_map/ppermute | solution.py:679
  72.1 3.5 collective-permute-start.14
  75.5 3.1 collective-permute-start.15
  80.2 1.6 collective-permute-start.22
  82.4 15.9 %attn_forward.2 = (bf16[2,584,1024]{2,1,0:T(8,128)(2,1)}, bf16[2,584,512]{2,1,0:T(8,128)(2,1)}, bf16[2,584,512]{2,1,0:T(8,128)(2,1)}, bf16[2,584,512]{2,1,0:T(8,...) custom-call(f32[6,1024]{1,0:T(8,128)} %convert_bitcast_fusion.refs_0_.refs_1_.refs_2_, ...), custom_call_target="tpu_custom_call" | custom-call | flops 104868085760 | bytes 383057920 | tf_op jit(solution)/shard_map/attn_forward/pallas_call | solution.py:58
  99.2 1.6 collective-permute-start.27
  104.7 1.9 collective-permute-start.25
  106.5 16.1 %attn_forward.3 = (bf16[2,584,1024]{2,1,0:T(8,128)(2,1)}, bf16[2,584,512]{2,1,0:T(8,128)(2,1)}, bf16[2,584,512]{2,1,0:T(8,128)(2,1)}, bf16[2,584,512]{2,1,0:T(8,...) custom-call(f32[6,1024]{1,0:T(8,128)} %convert_bitcast_fusion.refs_0, ...), custom_call_target="tpu_custom_call", output_to_operand_aliasing={{0}: (3, {}), {1}: (4, {}), {2}: (5, {}), {3}: (6, {}), {4}... | custom-call | flops 104868085760 | bytes 526581760 | tf_op jit(solution)/shard_map/attn_forward/pallas_call | solution.py:58
  122.6 13.3 %collective-permute-done.24 = bf16[8,128,512]{2,1,0:T(8,128)(2,1)} collective-permute-done((bf16[8,128,512]{2,1,0:T(8,128)(2,1)}, bf16[8,128,512]{2,1,0:T(8,128)(2,1)}, u32[]{:S(2)}, u32[]{:S(2)}) %collective-permute-start.24) | collective-permute-done | bytes 1048608 | tf_op jit(solution)/shard_map/ppermute | solution.py:679
  137.7 1.5 collective-permute-start.28
  140.1 1.9 constant_dynamic-update-slice_fusion.25.refs_5_
  141.9 1.5 collective-permute-start.29
  143.5 10.2 %mlp_up.2 = (f32[2,584,1024]{2,1,0:T(8,128)}, bf16[2,584,1024]{2,1,0:T(8,128)(2,1)}, bf16[2,584,2048]{2,1,0:T(8,128)(2,1)}, bf16[2,584,2048]{2,1,0:T(8,128)(2,1)}) custom-call(f32[2]{0:T(128)} %get-tuple-element.273.refs_0_.refs_1_, f32[6,1024]{1,0:T(8,128)} %convert_bitcast_fusion.refs_0_.refs_1_.refs_2_, f32[1,2048]{1,0:T(1,128)} %bitcast.285, ...), custom_call_target="tpu_custom_call" | custom-call | flops 48989470720 | bytes 514457600 | tf_op jit(solution)/shard_map/mlp_up/pallas_call | solution.py:58
  153.7 10.2 %mlp_up.3 = (f32[2,584,1024]{2,1,0:T(8,128)}, bf16[2,584,1024]{2,1,0:T(8,128)(2,1)}, bf16[2,584,2048]{2,1,0:T(8,128)(2,1)}, bf16[2,584,2048]{2,1,0:T(8,128)(2,1)}) custom-call(f32[2]{0:T(128)} %get-tuple-element.273.refs_0_.refs_1_, ...), custom_call_target="tpu_custom_call", output_to_operand_aliasing={{0}: (6, {}), {1}: (7, {}), {2}: (8, {}), {3}: (9, {})} | custom-call | flops 48989470720 | bytes 849346560 | tf_op jit(solution)/shard_map/mlp_up/pallas_call | solution.py:58
  164.0 10.4 %down_grad.1 = (bf16[8,512,128]{2,1,0:T(8,128)(2,1)}, bf16[8,512,128]{2,1,0:T(8,128)(2,1)}, bf16[8,512,128]{2,1,0:T(8,128)(2,1)}, bf16[8,512,128]{2,1,0:T(8,128)(2,1)}) custom-call(bf16[1168,2048]{1,0:T(8,128)(2,1)} %bitcast.294, bf16[1168,1024]{1,0:T(8,128)(2,1)} %bitcast.243), custom_call_target="tpu_custom_call" | custom-call | flops 97978941440 | bytes 227409920 | tf_op jit(solution)/shard_map/down_grad/pallas_call | solution.py:58
  175.5 21.9 %mlp_back.1 = (bf16[1168,2048]{1,0:T(8,128)(2,1)}, f32[1,2048]{1,0:T(1,128)}, bf16[1168,1024]{1,0:T(8,128)(2,1)}, bf16[1168,1024]{1,0:T(8,128)(2,1)}) custom-call(bf16[1168,1024]{1,0:T(8,128)(2,1)} %bitcast.244, bf16[1168,2048]{1,0:T(8,128)(2,1)} %bitcast.295, bf16[1168,2048]{1,0:T(8,128)(2,1)} %bitcast.296, ...), custom_call_target="tpu_custom_call" | custom-call | flops 293936824320 | bytes 598507520 | tf_op jit(solution)/shard_map/mlp_back/pallas_call | solution.py:58
  197.4 1.9 fusion.31
  200.0 2.4 add_convert_fusion.5
  203.8 2.3 add_convert_fusion.4
  206.1 1.5 collective-permute-start.35
  207.6 11.4 %middle_back.1 = (f32[584,1024]{1,0:T(8,128)}, bf16[2,584,1024]{2,1,0:T(8,128)(2,1)}, bf16[2,584,512]{2,1,0:T(8,128)(2,1)}, f32[4,1024]{1,0:T(4,128)}) custom-call(s32[10]{0:T(128)} %stack.158.refs_0_, f32[2]{0:T(128)} %get-tuple-element.273.refs_0_.refs_1_, f32[6,1024]{1,0:T(8,128)} %convert_bitcast_fusion.refs_0_.refs_1_.refs_2_, ...), custom_call_target="tpu_custom_call" | custom-call | flops 24494735360 | bytes 443023360 | tf_op jit(solution)/shard_map/middle_back/pallas_call | solution.py:58
  222.1 11.0 %collective-permute-start.58 = (bf16[1024,128]{1,0:T(8,128)(2,1)}, bf16[1024,128]{1,0:T(8,128)(2,1)}, u32[]{:S(2)}, u32[]{:S(2)}) collective-permute-start(bf16[1024,128]{1,0:T(8,128)(2,1)} %pad_maximum_fusion.14), channel_id=1, source_target_pairs={{0,8},{4,12},{8,0},{12,4},{16,24},{20,28},{24,16},{28,20},{1,9},{5... | collective-permute-start | bytes 786440 | tf_op jit(solution)/shard_map/ppermute | solution.py:673
  233.8 1.9 collective-permute-start.59
  238.7 11.9 %up_out_grad.1 = (bf16[8,640,128]{2,1,0:T(8,128)(2,1)}, bf16[8,640,128]{2,1,0:T(8,128)(2,1)}, bf16[8,640,128]{2,1,0:T(8,128)(2,1)}, bf16[8,640,128]{2,1,0:T(8,128)(2,1)}) custom-call(bf16[1168,1024]{1,0:T(8,128)(2,1)} %bitcast.299, bf16[1168,512]{1,0:T(8,128)(2,1)} %bitcast.300, bf16[1168,2048]{1,0:T(8,128)(2,1)} %get-tuple-element.193.refs_2_, ...), custom_call_target="tpu_custom_call" | custom-call | flops 122473676800 | bytes 320143360 | tf_op jit(solution)/shard_map/up_out_grad/pallas_call | solution.py:58
  250.6 1.6 collective-permute-start.36
  252.3 1.6 collective-permute-start.37
  253.9 17.4 %attn_backward.2 = (bf16[2,584,512]{2,1,0:T(8,128)(2,1)}, bf16[2,584,512]{2,1,0:T(8,128)(2,1)}, bf16[2,584,512]{2,1,0:T(8,128)(2,1)}, f32[2,512]{1,0:T(2,128)}) custom-call(bf16[2,584,512]{2,1,0:T(8,128)(2,1)} %get-tuple-element.216.refs_0_, bf16[2,584,512]{2,1,0:T(8,128)(2,1)} %get-tuple-element.217.refs_1_, ...), custom_call_target="tpu_custom_call" | custom-call | flops 139696537600 | bytes 167526400 | tf_op jit(solution)/shard_map/attn_backward/pallas_call | solution.py:58
  272.5 2.0 convert_add_fusion.1
  274.6 5.0 %collective-permute-done.36 = bf16[8,640,128]{2,1,0:T(8,128)(2,1)S(1)} collective-permute-done((bf16[8,640,128]{2,1,0:T(8,128)(2,1)}, bf16[8,640,128]{2,1,0:T(8,128)(2,1)S(1)}, u32[]{:S(2)}, u32[]{:S(2)}) %collective-permute-start.36) | collective-permute-done | bytes 1310752 | tf_op jit(solution)/shard_map/ppermute | solution.py:679
  279.6 1.5 collective-permute-done.37
  281.1 2.6 add_convert_fusion.2
  283.7 1.7 collective-permute-start.38
  288.0 17.3 %attn_backward.3 = (bf16[2,584,512]{2,1,0:T(8,128)(2,1)}, bf16[2,584,512]{2,1,0:T(8,128)(2,1)}, bf16[2,584,512]{2,1,0:T(8,128)(2,1)}, f32[2,512]{1,0:T(2,128)}) custom-call(bf16[2,584,512]{2,1,0:T(8,128)(2,1)} %get-tuple-element.216.refs_0_, ...), custom_call_target="tpu_custom_call", output_to_operand_aliasing={{0}: (4, {}), {1}: (5, {}), {2}: (6, {})} | custom-call | flops 139696537600 | bytes 239288320 | tf_op jit(solution)/shard_map/attn_backward/pallas_call | solution.py:58
  309.4 2.4 collective-permute-start.56
  312.5 1.5 collective-permute-start.57
  314.8 13.4 %qkv_grad.1 = (bf16[8,384,128]{2,1,0:T(8,128)(2,1)}, bf16[8,384,128]{2,1,0:T(8,128)(2,1)}, bf16[8,384,128]{2,1,0:T(8,128)(2,1)}, bf16[8,384,128]{2,1,0:T(8,128)(2,1)}) custom-call(bf16[1168,1024]{1,0:T(8,128)(2,1)} %bitcast.297, bf16[1168,512]{1,0:T(8,128)(2,1)} %bitcast.301, bf16[1168,512]{1,0:T(8,128)(2,1)} %bitcast.303, bf16[1168,512]{1,0:T(8,128)(2,1)} %bitcast.305), custom_call_target="tpu_custom_call" | custom-call | flops 73484206080 | bytes 182517760 | tf_op jit(solution)/shard_map/qkv_grad/pallas_call | solution.py:58
  328.9 8.9 %grad_one.1 = bf16[1168,1024]{1,0:T(8,128)(2,1)} custom-call(bf16[1168,512]{1,0:T(8,128)(2,1)} %bitcast.302, bf16[1168,512]{1,0:T(8,128)(2,1)} %bitcast.304, bf16[1168,512]{1,0:T(8,128)(2,1)} %bitcast.306, bf16[8,512,128]{2,1,0:T(8,128)(2,1)} %constant_dynamic-update-slice_fusion.5.refs_3_.refs_7_.refs_8_.refs_12_, ...), custom_call_target="tpu_custom_call" | custom-call | flops 73484206080 | bytes 203489280 | tf_op jit(solution)/shard_map/grad_one/pallas_call | solution.py:58
  337.8 3.4 fusion.30
  345.0 13.4 %collective-permute-done.41 = bf16[8,384,128]{2,1,0:T(8,128)(2,1)S(1)} collective-permute-done((bf16[8,384,128]{2,1,0:T(8,128)(2,1)S(1)}, bf16[8,384,128]{2,1,0:T(8,128)(2,1)S(1)}, u32[]{:S(2)}, u32[]{:S(2)}) %collective-permute-start.41) | collective-permute-done | bytes 786464 | tf_op jit(solution)/shard_map/ppermute | solution.py:676
  360.4 5.2 %finish_layer.1 = bf16[584,1024]{1,0:T(8,128)(2,1)} custom-call(s32[10]{0:T(128)} %stack.158.refs_0_, f32[2]{0:T(128)} %get-tuple-element.273.refs_0_.refs_1_, f32[6,1024]{1,0:T(8,128)} %convert_bitcast_fusion.refs_0_.refs_1_.refs_2_, f32[2,584,1024]{2,1,0:T(8,128)} %get-tuple-element.179.refs_3_, bf16[2,584,1024]{2,1,0:T(8,128)(2,1)} %bitcast.61.refs_4_, ...), custom_call_target="tpu_custom_call" | custom-call | flops 1196032000 | bytes 215285760 | tf_op jit(solution)/shard_map/finish_layer/pallas_call | solution.py:58
  367.1 8.8 %finish_tokens.1 = (bf16[584,1024]{1,0:T(8,128)(2,1)}, f32[2,1024]{1,0:T(2,128)}) custom-call(s32[10]{0:T(128)} %stack.158.refs_0_, f32[6,1024]{1,0:T(8,128)} %convert_bitcast_fusion.refs_0_.refs_1_.refs_2_, bf16[2,584,1024]{2,1,0:T(8,128)(2,1)} %get-tuple-element.160.refs_2_.refs_3_, bf16[2,584,1024]{2,1,0:T(8,128)(2,1)} %bitcast.242, ...), custom_call_target="tpu_custom_call" | custom-call | flops 2392064000 | bytes 215449600 | tf_op jit(solution)/shard_map/finish_tokens/pallas_call | solution.py:58
  380.1 3.0 collective-permute-start.53
  383.1 1.8 collective-permute-start.46
  385.0 2.0 collective-permute-done.46
  387.0 1.5 collective-permute-start.49
  388.5 2.9 collective-permute-start.48
  396.3 3.7 collective-permute-done.54
  (270 shorter events, 65.6 us)
Async XLA Ops:
  0.7 17.6 %copy-start.7 = (bf16[584,1024]{1,0:T(8,128)(2,1)S(1)}, bf16[584,1024]{1,0:T(8,128)(2,1)}, u32[]{:S(2)}) copy-start(bf16[584,1024]{1,0:T(8,128)(2,1)} %refs_1_.1) | copy-start | bytes 3588100
  2.8 15.4 %collective-permute-start = (bf16[16,128]{1,0:T(8,128)(2,1)S(1)}, bf16[16,128]{1,0:T(8,128)(2,1)S(1)}, u32[]{:S(2)}, u32[]{:S(2)}) collective-permute-start(bf16[16,128]{1,0:T(8,128)(2,1)S(1)} %concatenate.119), channel_id=1, source_target_pairs={{0,8},{4,12},{8,0},{12,4},{16,24},{20,28},{24,16},{28,20},{1,9},{5... | collective-permute-start | bytes 12296 | tf_op jit(solution)/shard_map/ppermute | solution.py:673
  5.9 12.4 %collective-permute-start.1 = (bf16[16,128]{1,0:T(8,128)(2,1)S(1)}, bf16[16,128]{1,0:T(8,128)(2,1)S(1)}, u32[]{:S(2)}, u32[]{:S(2)}) collective-permute-start(bf16[16,128]{1,0:T(8,128)(2,1)S(1)} %concatenate.119), channel_id=1, source_target_pairs={{0,16},{4,20},{8,24},{12,28},{16,0},{20,4},{24,8},{28,12},{1,17},{... | collective-permute-start | bytes 12296 | tf_op jit(solution)/shard_map/ppermute | solution.py:673
  8.5 10.3 %collective-permute-start.2 = (bf16[16,128]{1,0:T(8,128)(2,1)S(1)}, bf16[16,128]{1,0:T(8,128)(2,1)S(1)}, u32[]{:S(2)}, u32[]{:S(2)}) collective-permute-start(bf16[16,128]{1,0:T(8,128)(2,1)S(1)} %concatenate.119), channel_id=1, source_target_pairs={{0,24},{4,28},{8,16},{12,20},{16,8},{20,12},{24,0},{28,4},{1,25},{... | collective-permute-start | bytes 12296 | tf_op jit(solution)/shard_map/ppermute | solution.py:673
  10.2 22.4 %collective-permute-start.7 = (bf16[1024,128]{1,0:T(8,128)(2,1)S(1)}, bf16[1024,128]{1,0:T(8,128)(2,1)S(1)}, u32[]{:S(2)}, u32[]{:S(2)}) collective-permute-start(bf16[1024,128]{1,0:T(8,128)(2,1)S(1)} %pad_maximum_fusion.12), channel_id=1, source_target_pairs={{0,8},{4,12},{8,0},{12,4},{16,24},{20,28},{24,16},{28,20},{1,9},{5... | collective-permute-start | bytes 786440 | tf_op jit(solution)/shard_map/ppermute | solution.py:673
  11.2 21.5 %collective-permute-start.8 = (bf16[1024,128]{1,0:T(8,128)(2,1)S(1)}, bf16[1024,128]{1,0:T(8,128)(2,1)S(1)}, u32[]{:S(2)}, u32[]{:S(2)}) collective-permute-start(bf16[1024,128]{1,0:T(8,128)(2,1)S(1)} %pad_maximum_fusion.12), channel_id=1, source_target_pairs={{0,16},{4,20},{8,24},{12,28},{16,0},{20,4},{24,8},{28,12},{1,17},{... | collective-permute-start | bytes 786440 | tf_op jit(solution)/shard_map/ppermute | solution.py:673
  18.2 8.5 %collective-permute-start.5 = (bf16[584,1024]{1,0:T(8,128)(2,1)S(1)}, bf16[584,1024]{1,0:T(8,128)(2,1)S(1)}, u32[]{:S(2)}, u32[]{:S(2)}) collective-permute-start(bf16[584,1024]{1,0:T(8,128)(2,1)S(1)} %copy-done.7), channel_id=1, source_target_pairs={{0,1},{1,0},{2,3},{3,2},{4,5},{5,4},{6,7},{7,6},{8,9},{9,8},{10,11... | collective-permute-start | bytes 3588104 | tf_op jit(solution)/shard_map/ppermute | solution.py:683
  18.3 8.5 %collective-permute-start.6 = (bf16[584,1024]{1,0:T(8,128)(2,1)}, bf16[584,1024]{1,0:T(8,128)(2,1)}, u32[]{:S(2)}, u32[]{:S(2)}) collective-permute-start(bf16[584,1024]{1,0:T(8,128)(2,1)} %refs_2_.1), channel_id=1, source_target_pairs={{0,1},{1,0},{2,3},{3,2},{4,5},{5,4},{6,7},{7,6},{8,9},{9,8},{10,11... | collective-permute-start | bytes 3588104 | tf_op jit(solution)/shard_map/ppermute | solution.py:683
  18.8 3.8 collective-permute-start.3
  22.6 3.9 collective-permute-start.4
  26.5 8.5 %collective-permute-start.9 = (bf16[1024,128]{1,0:T(8,128)(2,1)S(1)}, bf16[1024,128]{1,0:T(8,128)(2,1)S(1)}, u32[]{:S(2)}, u32[]{:S(2)}) collective-permute-start(bf16[1024,128]{1,0:T(8,128)(2,1)S(1)} %pad_maximum_fusion.12), channel_id=1, source_target_pairs={{0,24},{4,28},{8,16},{12,20},{16,8},{20,12},{24,0},{28,4},{1,25},{... | collective-permute-start | bytes 786440 | tf_op jit(solution)/shard_map/ppermute | solution.py:673
  35.9 11.3 %collective-permute-start.10 = (bf16[4,512,128]{2,1,0:T(8,128)(2,1)S(1)}, bf16[4,512,128]{2,1,0:T(8,128)(2,1)S(1)}, u32[]{:S(2)}, u32[]{:S(2)}) collective-permute-start(bf16[4,512,128]{2,1,0:T(8,128)(2,1)S(1)} %pad_maximum_fusion), channel_id=1, source_target_pairs={{0,4},{4,0},{8,12},{12,8},{16,20},{20,16},{24,28},{28,24},{1,5},{5... | collective-permute-start | bytes 1572872 | tf_op jit(solution)/shard_map/ppermute | solution.py:676
  37.5 12.2 %collective-permute-start.12 = (bf16[4,512,128]{2,1,0:T(8,128)(2,1)S(1)}, bf16[4,512,128]{2,1,0:T(8,128)(2,1)S(1)}, u32[]{:S(2)}, u32[]{:S(2)}) collective-permute-start(bf16[4,512,128]{2,1,0:T(8,128)(2,1)S(1)} %pad_maximum_fusion.1), channel_id=1, source_target_pairs={{0,2},{2,0},{1,3},{3,1},{4,6},{6,4},{5,7},{7,5},{8,10},{10,8},{9,1... | collective-permute-start | bytes 1572872 | tf_op jit(solution)/shard_map/ppermute | solution.py:679
  48.0 23.1 %collective-permute-start.11 = (bf16[8,512,128]{2,1,0:T(8,128)(2,1)}, bf16[8,512,128]{2,1,0:T(8,128)(2,1)}, u32[]{:S(2)}, u32[]{:S(2)}) collective-permute-start(bf16[8,512,128]{2,1,0:T(8,128)(2,1)} %constant_dynamic-update-slice_fusion.5.refs_3_.refs_7_.refs_8_.refs_12_), channel_id=1, source_target_pairs={{0,2},{2,0},{1,3},{3,1},{4,6},{6,4},{5,7},{7,5},{8,10},{10,8},{9,1... | collective-permute-start | bytes 3145736 | tf_op jit(solution)/shard_map/ppermute | solution.py:679
  50.6 21.4 %collective-permute-start.13 = (bf16[8,512,128]{2,1,0:T(8,128)(2,1)}, bf16[8,512,128]{2,1,0:T(8,128)(2,1)}, u32[]{:S(2)}, u32[]{:S(2)}) collective-permute-start(bf16[8,512,128]{2,1,0:T(8,128)(2,1)} %constant_dynamic-update-slice_fusion.10.refs_5_.refs_9_.refs_10_.refs_14_), channel_id=1, source_target_pairs={{0,4},{4,0},{8,12},{12,8},{16,20},{20,16},{24,28},{28,24},{1,5},{5... | collective-permute-start | bytes 3145736 | tf_op jit(solution)/shard_map/ppermute | solution.py:676
  53.2 25.4 %collective-permute-start.17 = (bf16[256,512]{1,0:T(8,128)(2,1)S(1)}, bf16[256,512]{1,0:T(8,128)(2,1)S(1)}, u32[]{:S(2)}, u32[]{:S(2)}) collective-permute-start(bf16[256,512]{1,0:T(8,128)(2,1)S(1)} %constant_dynamic-update-slice_fusion.17), channel_id=1, source_target_pairs={{0,8},{4,12},{8,0},{12,4},{16,24},{20,28},{24,16},{28,20},{1,9},{5... | collective-permute-start | bytes 786440 | tf_op jit(solution)/shard_map/ppermute | solution.py:673
  56.7 23.3 %collective-permute-start.18 = (bf16[256,512]{1,0:T(8,128)(2,1)S(1)}, bf16[256,512]{1,0:T(8,128)(2,1)S(1)}, u32[]{:S(2)}, u32[]{:S(2)}) collective-permute-start(bf16[256,512]{1,0:T(8,128)(2,1)S(1)} %constant_dynamic-update-slice_fusion.17), channel_id=1, source_target_pairs={{0,16},{4,20},{8,24},{12,28},{16,0},{20,4},{24,8},{28,12},{1,17},{... | collective-permute-start | bytes 786440 | tf_op jit(solution)/shard_map/ppermute | solution.py:673
  58.4 21.6 %collective-permute-start.19 = (bf16[256,512]{1,0:T(8,128)(2,1)S(1)}, bf16[256,512]{1,0:T(8,128)(2,1)S(1)}, u32[]{:S(2)}, u32[]{:S(2)}) collective-permute-start(bf16[256,512]{1,0:T(8,128)(2,1)S(1)} %constant_dynamic-update-slice_fusion.17), channel_id=1, source_target_pairs={{0,24},{4,28},{8,16},{12,20},{16,8},{20,12},{24,0},{28,4},{1,25},{... | collective-permute-start | bytes 786440 | tf_op jit(solution)/shard_map/ppermute | solution.py:673
  72.1 26.3 %collective-permute-start.14 = (bf16[1024,128]{1,0:T(8,128)(2,1)S(1)}, bf16[1024,128]{1,0:T(8,128)(2,1)S(1)}, u32[]{:S(2)}, u32[]{:S(2)}) collective-permute-start(bf16[1024,128]{1,0:T(8,128)(2,1)S(1)} %constant_dynamic-update-slice_fusion.15), channel_id=1, source_target_pairs={{0,8},{4,12},{8,0},{12,4},{16,24},{20,28},{24,16},{28,20},{1,9},{5... | collective-permute-start | bytes 786440 | tf_op jit(solution)/shard_map/ppermute | solution.py:673
  75.5 23.3 %collective-permute-start.15 = (bf16[1024,128]{1,0:T(8,128)(2,1)S(1)}, bf16[1024,128]{1,0:T(8,128)(2,1)S(1)}, u32[]{:S(2)}, u32[]{:S(2)}) collective-permute-start(bf16[1024,128]{1,0:T(8,128)(2,1)S(1)} %constant_dynamic-update-slice_fusion.15), channel_id=1, source_target_pairs={{0,16},{4,20},{8,24},{12,28},{16,0},{20,4},{24,8},{28,12},{1,17},{... | collective-permute-start | bytes 786440 | tf_op jit(solution)/shard_map/ppermute | solution.py:673
  78.6 20.2 %collective-permute-start.16 = (bf16[1024,128]{1,0:T(8,128)(2,1)S(1)}, bf16[1024,128]{1,0:T(8,128)(2,1)S(1)}, u32[]{:S(2)}, u32[]{:S(2)}) collective-permute-start(bf16[1024,128]{1,0:T(8,128)(2,1)S(1)} %constant_dynamic-update-slice_fusion.15), channel_id=1, source_target_pairs={{0,24},{4,28},{8,16},{12,20},{16,8},{20,12},{24,0},{28,4},{1,25},{... | collective-permute-start | bytes 786440 | tf_op jit(solution)/shard_map/ppermute | solution.py:673
  80.2 20.6 %collective-permute-start.22 = (bf16[4,128,512]{2,1,0:T(8,128)(2,1)S(1)}, bf16[4,128,512]{2,1,0:T(8,128)(2,1)S(1)}, u32[]{:S(2)}, u32[]{:S(2)}) collective-permute-start(bf16[4,128,512]{2,1,0:T(8,128)(2,1)S(1)} %pad_maximum_fusion.2), channel_id=1, source_target_pairs={{0,4},{4,0},{8,12},{12,8},{16,20},{20,16},{24,28},{28,24},{1,5},{5... | collective-permute-start | bytes 1572872 | tf_op jit(solution)/shard_map/ppermute | solution.py:676
  81.8 19.0 %collective-permute-start.23 = (bf16[4,128,512]{2,1,0:T(8,128)(2,1)S(1)}, bf16[4,128,512]{2,1,0:T(8,128)(2,1)S(1)}, u32[]{:S(2)}, u32[]{:S(2)}) collective-permute-start(bf16[4,128,512]{2,1,0:T(8,128)(2,1)S(1)} %pad_maximum_fusion.3), channel_id=1, source_target_pairs={{0,2},{2,0},{1,3},{3,1},{4,6},{6,4},{5,7},{7,5},{8,10},{10,8},{9,1... | collective-permute-start | bytes 1572872 | tf_op jit(solution)/shard_map/ppermute | solution.py:679
  98.3 45.1 %collective-permute-start.21 = (bf16[584,1024]{1,0:T(8,128)(2,1)}, bf16[584,1024]{1,0:T(8,128)(2,1)}, u32[]{:S(2)}, u32[]{:S(2)}) collective-permute-start(bf16[584,1024]{1,0:T(8,128)(2,1)} %get-tuple-element.155.refs_4_), channel_id=1, source_target_pairs={{0,1},{1,0},{2,3},{3,2},{4,5},{5,4},{6,7},{7,6},{8,9},{9,8},{10,11... | collective-permute-start | bytes 3588104 | tf_op jit(solution)/shard_map/ppermute | solution.py:683
  99.0 37.0 %collective-permute-start.26 = (bf16[4,512,128]{2,1,0:T(8,128)(2,1)S(1)}, bf16[4,512,128]{2,1,0:T(8,128)(2,1)S(1)}, u32[]{:S(2)}, u32[]{:S(2)}) collective-permute-start(bf16[4,512,128]{2,1,0:T(8,128)(2,1)S(1)} %pad_maximum_fusion.4), channel_id=1, source_target_pairs={{0,4},{4,0},{8,12},{12,8},{16,20},{20,16},{24,28},{28,24},{1,5},{5... | collective-permute-start | bytes 1572872 | tf_op jit(solution)/shard_map/ppermute | solution.py:676
  99.2 36.7 %collective-permute-start.27 = (bf16[4,512,128]{2,1,0:T(8,128)(2,1)S(1)}, bf16[4,512,128]{2,1,0:T(8,128)(2,1)}, u32[]{:S(2)}, u32[]{:S(2)}) collective-permute-start(bf16[4,512,128]{2,1,0:T(8,128)(2,1)S(1)} %pad_maximum_fusion.5), channel_id=1, source_target_pairs={{0,2},{2,0},{1,3},{3,1},{4,6},{6,4},{5,7},{7,5},{8,10},{10,8},{9,1... | collective-permute-start | bytes 1572872 | tf_op jit(solution)/shard_map/ppermute | solution.py:679
  102.5 33.4 %collective-permute-start.24 = (bf16[8,128,512]{2,1,0:T(8,128)(2,1)}, bf16[8,128,512]{2,1,0:T(8,128)(2,1)}, u32[]{:S(2)}, u32[]{:S(2)}) collective-permute-start(bf16[8,128,512]{2,1,0:T(8,128)(2,1)} %constant_dynamic-update-slice_fusion.19), channel_id=1, source_target_pairs={{0,2},{2,0},{1,3},{3,1},{4,6},{6,4},{5,7},{7,5},{8,10},{10,8},{9,1... | collective-permute-start | bytes 3145736 | tf_op jit(solution)/shard_map/ppermute | solution.py:679
  104.7 31.2 %collective-permute-start.25 = (bf16[8,128,512]{2,1,0:T(8,128)(2,1)}, bf16[8,128,512]{2,1,0:T(8,128)(2,1)S(1)}, u32[]{:S(2)}, u32[]{:S(2)}) collective-permute-start(bf16[8,128,512]{2,1,0:T(8,128)(2,1)} %constant_dynamic-update-slice_fusion.21), channel_id=1, source_target_pairs={{0,4},{4,0},{8,12},{12,8},{16,20},{20,16},{24,28},{28,24},{1,5},{5... | collective-permute-start | bytes 3145736 | tf_op jit(solution)/shard_map/ppermute | solution.py:676
  135.9 17.8 %collective-permute-start.20 = (bf16[584,1024]{1,0:T(8,128)(2,1)}, bf16[584,1024]{1,0:T(8,128)(2,1)}, u32[]{:S(2)}, u32[]{:S(2)}) collective-permute-start(bf16[584,1024]{1,0:T(8,128)(2,1)} %get-tuple-element.166.refs_4_), channel_id=1, source_target_pairs={{0,1},{1,0},{2,3},{3,2},{4,5},{5,4},{6,7},{7,6},{8,9},{9,8},{10,11... | collective-permute-start | bytes 3588104 | tf_op jit(solution)/shard_map/ppermute | solution.py:683
  137.7 37.8 %collective-permute-start.28 = (bf16[8,512,128]{2,1,0:T(8,128)(2,1)}, bf16[8,512,128]{2,1,0:T(8,128)(2,1)}, u32[]{:S(2)}, u32[]{:S(2)}) collective-permute-start(bf16[8,512,128]{2,1,0:T(8,128)(2,1)} %constant_dynamic-update-slice_fusion.23.refs_3_), channel_id=1, source_target_pairs={{0,2},{2,0},{1,3},{3,1},{4,6},{6,4},{5,7},{7,5},{8,10},{10,8},{9,1... | collective-permute-start | bytes 3145736 | tf_op jit(solution)/shard_map/ppermute | solution.py:679
  141.9 33.6 %collective-permute-start.29 = (bf16[8,512,128]{2,1,0:T(8,128)(2,1)}, bf16[8,512,128]{2,1,0:T(8,128)(2,1)}, u32[]{:S(2)}, u32[]{:S(2)}) collective-permute-start(bf16[8,512,128]{2,1,0:T(8,128)(2,1)} %constant_dynamic-update-slice_fusion.25.refs_5_), channel_id=1, source_target_pairs={{0,4},{4,0},{8,12},{12,8},{16,20},{20,16},{24,28},{28,24},{1,5},{5... | collective-permute-start | bytes 3145736 | tf_op jit(solution)/shard_map/ppermute | solution.py:676
  174.4 25.5 %collective-permute-start.32 = (bf16[8,512,128]{2,1,0:T(8,128)(2,1)}, bf16[8,512,128]{2,1,0:T(8,128)(2,1)}, u32[]{:S(2)}, u32[]{:S(2)}) collective-permute-start(bf16[8,512,128]{2,1,0:T(8,128)(2,1)} %get-tuple-element.196), channel_id=1, source_target_pairs={{0,2},{2,0},{1,3},{3,1},{4,6},{6,4},{5,7},{7,5},{8,10},{10,8},{9,1... | collective-permute-start | bytes 3145736 | tf_op jit(solution)/shard_map/ppermute | solution.py:679
  175.0 25.0 %collective-permute-start.33 = (bf16[8,512,128]{2,1,0:T(8,128)(2,1)}, bf16[8,512,128]{2,1,0:T(8,128)(2,1)}, u32[]{:S(2)}, u32[]{:S(2)}) collective-permute-start(bf16[8,512,128]{2,1,0:T(8,128)(2,1)} %get-tuple-element.197), channel_id=1, source_target_pairs={{0,4},{4,0},{8,12},{12,8},{16,20},{20,16},{24,28},{28,24},{1,5},{5... | collective-permute-start | bytes 3145736 | tf_op jit(solution)/shard_map/ppermute | solution.py:676
  199.3 8.2 %collective-permute-start.30 = (bf16[584,1024]{1,0:T(8,128)(2,1)S(1)}, bf16[584,1024]{1,0:T(8,128)(2,1)}, u32[]{:S(2)}, u32[]{:S(2)}) collective-permute-start(bf16[584,1024]{1,0:T(8,128)(2,1)S(1)} %get-tuple-element.281), channel_id=1, source_target_pairs={{0,1},{1,0},{2,3},{3,2},{4,5},{5,4},{6,7},{7,6},{8,9},{9,8},{10,11... | collective-permute-start | bytes 3588104 | tf_op jit(solution)/shard_map/ppermute | solution.py:683
  199.4 8.2 %collective-permute-start.31 = (bf16[584,1024]{1,0:T(8,128)(2,1)S(1)}, bf16[584,1024]{1,0:T(8,128)(2,1)}, u32[]{:S(2)}, u32[]{:S(2)}) collective-permute-start(bf16[584,1024]{1,0:T(8,128)(2,1)S(1)} %get-tuple-element.280), channel_id=1, source_target_pairs={{0,1},{1,0},{2,3},{3,2},{4,5},{5,4},{6,7},{7,6},{8,9},{9,8},{10,11... | collective-permute-start | bytes 3588104 | tf_op jit(solution)/shard_map/ppermute | solution.py:683
  202.4 16.6 %collective-permute-start.34 = (bf16[4,512,128]{2,1,0:T(8,128)(2,1)}, bf16[4,512,128]{2,1,0:T(8,128)(2,1)S(1)}, u32[]{:S(2)}, u32[]{:S(2)}) collective-permute-start(bf16[4,512,128]{2,1,0:T(8,128)(2,1)} %get-tuple-element.284), channel_id=1, source_target_pairs={{0,4},{4,0},{8,12},{12,8},{16,20},{20,16},{24,28},{28,24},{1,5},{5... | collective-permute-start | bytes 1572872 | tf_op jit(solution)/shard_map/ppermute | solution.py:676
  206.1 13.9 %collective-permute-start.35 = (bf16[4,512,128]{2,1,0:T(8,128)(2,1)}, bf16[4,512,128]{2,1,0:T(8,128)(2,1)}, u32[]{:S(2)}, u32[]{:S(2)}) collective-permute-start(bf16[4,512,128]{2,1,0:T(8,128)(2,1)} %get-tuple-element.282), channel_id=1, source_target_pairs={{0,2},{2,0},{1,3},{3,1},{4,6},{6,4},{5,7},{7,5},{8,10},{10,8},{9,1... | collective-permute-start | bytes 1572872 | tf_op jit(solution)/shard_map/ppermute | solution.py:679
  222.1 50.4 %collective-permute-start.58 = (bf16[1024,128]{1,0:T(8,128)(2,1)}, bf16[1024,128]{1,0:T(8,128)(2,1)}, u32[]{:S(2)}, u32[]{:S(2)}) collective-permute-start(bf16[1024,128]{1,0:T(8,128)(2,1)} %pad_maximum_fusion.14), channel_id=1, source_target_pairs={{0,8},{4,12},{8,0},{12,4},{16,24},{20,28},{24,16},{28,20},{1,9},{5... | collective-permute-start | bytes 786440 | tf_op jit(solution)/shard_map/ppermute | solution.py:673
  233.8 38.7 %collective-permute-start.59 = (bf16[1024,128]{1,0:T(8,128)(2,1)}, bf16[1024,128]{1,0:T(8,128)(2,1)}, u32[]{:S(2)}, u32[]{:S(2)}) collective-permute-start(bf16[1024,128]{1,0:T(8,128)(2,1)} %pad_maximum_fusion.15), channel_id=1, source_target_pairs={{0,16},{4,20},{8,24},{12,28},{16,0},{20,4},{24,8},{28,12},{1,17},{... | collective-permute-start | bytes 786440 | tf_op jit(solution)/shard_map/ppermute | solution.py:673
  236.5 36.0 %collective-permute-start.60 = (bf16[1024,128]{1,0:T(8,128)(2,1)}, bf16[1024,128]{1,0:T(8,128)(2,1)}, u32[]{:S(2)}, u32[]{:S(2)}) collective-permute-start(bf16[1024,128]{1,0:T(8,128)(2,1)} %pad_maximum_fusion.16), channel_id=1, source_target_pairs={{0,24},{4,28},{8,16},{12,20},{16,8},{20,12},{24,0},{28,4},{1,25},{... | collective-permute-start | bytes 786440 | tf_op jit(solution)/shard_map/ppermute | solution.py:673
  250.6 29.0 %collective-permute-start.36 = (bf16[8,640,128]{2,1,0:T(8,128)(2,1)}, bf16[8,640,128]{2,1,0:T(8,128)(2,1)S(1)}, u32[]{:S(2)}, u32[]{:S(2)}) collective-permute-start(bf16[8,640,128]{2,1,0:T(8,128)(2,1)} %get-tuple-element.213), channel_id=1, source_target_pairs={{0,2},{2,0},{1,3},{3,1},{4,6},{6,4},{5,7},{7,5},{8,10},{10,8},{9,1... | collective-permute-start | bytes 3932168 | tf_op jit(solution)/shard_map/ppermute | solution.py:679
  252.3 28.9 %collective-permute-start.37 = (bf16[8,640,128]{2,1,0:T(8,128)(2,1)}, bf16[8,640,128]{2,1,0:T(8,128)(2,1)S(1)}, u32[]{:S(2)}, u32[]{:S(2)}) collective-permute-start(bf16[8,640,128]{2,1,0:T(8,128)(2,1)} %get-tuple-element.215), channel_id=1, source_target_pairs={{0,4},{4,0},{8,12},{12,8},{16,20},{20,16},{24,28},{28,24},{1,5},{5... | collective-permute-start | bytes 3932168 | tf_op jit(solution)/shard_map/ppermute | solution.py:676
  253.9 18.6 %copy-start.11 = (bf16[1024,128]{1,0:T(8,128)(2,1)S(1)}, bf16[1024,128]{1,0:T(8,128)(2,1)}, u32[]{:S(2)}) copy-start(bf16[1024,128]{1,0:T(8,128)(2,1)} %pad_maximum_fusion.13) | copy-start | bytes 786436
  272.5 87.9 %collective-permute-start.42 = (bf16[2,584,1024]{2,1,0:T(8,128)(2,1)}, bf16[2,584,1024]{2,1,0:T(8,128)(2,1)}, u32[]{:S(2)}, u32[]{:S(2)}) collective-permute-start(bf16[2,584,1024]{2,1,0:T(8,128)(2,1)} %bitcast.61.refs_4_), channel_id=1, source_target_pairs={{0,1},{1,0},{2,3},{3,2},{4,5},{5,4},{6,7},{7,6},{8,9},{9,8},{10,11... | collective-permute-start | bytes 7176200 | tf_op jit(solution)/shard_map/ppermute | solution.py:683
  283.7 23.3 %collective-permute-start.38 = (bf16[4,640,128]{2,1,0:T(8,128)(2,1)}, bf16[4,640,128]{2,1,0:T(8,128)(2,1)S(1)}, u32[]{:S(2)}, u32[]{:S(2)}) collective-permute-start(bf16[4,640,128]{2,1,0:T(8,128)(2,1)} %get-tuple-element.276), channel_id=1, source_target_pairs={{0,4},{4,0},{8,12},{12,8},{16,20},{20,16},{24,28},{28,24},{1,5},{5... | collective-permute-start | bytes 1966088 | tf_op jit(solution)/shard_map/ppermute | solution.py:676
  286.6 20.4 %collective-permute-start.39 = (bf16[4,640,128]{2,1,0:T(8,128)(2,1)}, bf16[4,640,128]{2,1,0:T(8,128)(2,1)S(1)}, u32[]{:S(2)}, u32[]{:S(2)}) collective-permute-start(bf16[4,640,128]{2,1,0:T(8,128)(2,1)} %get-tuple-element.274), channel_id=1, source_target_pairs={{0,2},{2,0},{1,3},{3,1},{4,6},{6,4},{5,7},{7,5},{8,10},{10,8},{9,1... | collective-permute-start | bytes 1966088 | tf_op jit(solution)/shard_map/ppermute | solution.py:679
  288.0 18.2 %copy-start.20 = (f32[1,2048]{1,0:T(1,128)S(1)}, f32[1,2048]{1,0:T(1,128)}, u32[]{:S(2)}) copy-start(f32[1,2048]{1,0:T(1,128)} %get-tuple-element.198) | copy-start | bytes 24580
  308.1 33.1 %collective-permute-start.55 = (bf16[1280,128]{1,0:T(8,128)(2,1)}, bf16[1280,128]{1,0:T(8,128)(2,1)}, u32[]{:S(2)}, u32[]{:S(2)}) collective-permute-start(bf16[1280,128]{1,0:T(8,128)(2,1)} %pad_maximum_fusion.9), channel_id=1, source_target_pairs={{0,8},{4,12},{8,0},{12,4},{16,24},{20,28},{24,16},{28,20},{1,9},{5... | collective-permute-start | bytes 983048 | tf_op jit(solution)/shard_map/ppermute | solution.py:673
  309.4 32.1 %collective-permute-start.56 = (bf16[1280,128]{1,0:T(8,128)(2,1)}, bf16[1280,128]{1,0:T(8,128)(2,1)}, u32[]{:S(2)}, u32[]{:S(2)}) collective-permute-start(bf16[1280,128]{1,0:T(8,128)(2,1)} %pad_maximum_fusion.10), channel_id=1, source_target_pairs={{0,16},{4,20},{8,24},{12,28},{16,0},{20,4},{24,8},{28,12},{1,17},{... | collective-permute-start | bytes 983048 | tf_op jit(solution)/shard_map/ppermute | solution.py:673
  312.5 29.0 %collective-permute-start.57 = (bf16[1280,128]{1,0:T(8,128)(2,1)}, bf16[1280,128]{1,0:T(8,128)(2,1)}, u32[]{:S(2)}, u32[]{:S(2)}) collective-permute-start(bf16[1280,128]{1,0:T(8,128)(2,1)} %pad_maximum_fusion.11), channel_id=1, source_target_pairs={{0,24},{4,28},{8,16},{12,20},{16,8},{20,12},{24,0},{28,4},{1,25},{... | collective-permute-start | bytes 983048 | tf_op jit(solution)/shard_map/ppermute | solution.py:673
  328.2 16.8 %collective-permute-start.40 = (bf16[8,384,128]{2,1,0:T(8,128)(2,1)}, bf16[8,384,128]{2,1,0:T(8,128)(2,1)S(1)}, u32[]{:S(2)}, u32[]{:S(2)}) collective-permute-start(bf16[8,384,128]{2,1,0:T(8,128)(2,1)} %get-tuple-element.240), channel_id=1, source_target_pairs={{0,2},{2,0},{1,3},{3,1},{4,6},{6,4},{5,7},{7,5},{8,10},{10,8},{9,1... | collective-permute-start | bytes 2359304 | tf_op jit(solution)/shard_map/ppermute | solution.py:679
  341.2 17.2 %collective-permute-start.41 = (bf16[8,384,128]{2,1,0:T(8,128)(2,1)S(1)}, bf16[8,384,128]{2,1,0:T(8,128)(2,1)S(1)}, u32[]{:S(2)}, u32[]{:S(2)}) collective-permute-start(bf16[8,384,128]{2,1,0:T(8,128)(2,1)S(1)} %copy-done.27), channel_id=1, source_target_pairs={{0,4},{4,0},{8,12},{12,8},{16,20},{20,16},{24,28},{28,24},{1,5},{5... | collective-permute-start | bytes 2359304 | tf_op jit(solution)/shard_map/ppermute | solution.py:676
  341.5 24.2 %collective-permute-start.43 = (bf16[584,1024]{1,0:T(8,128)(2,1)}, bf16[584,1024]{1,0:T(8,128)(2,1)S(1)}, u32[]{:S(2)}, u32[]{:S(2)}) collective-permute-start(bf16[584,1024]{1,0:T(8,128)(2,1)} %get-tuple-element.279), channel_id=1, source_target_pairs={{0,1},{1,0},{2,3},{3,2},{4,5},{5,4},{6,7},{7,6},{8,9},{9,8},{10,11... | collective-permute-start | bytes 3588104 | tf_op jit(solution)/shard_map/ppermute | solution.py:683
  341.5 24.2 %collective-permute-start.44 = (bf16[584,1024]{1,0:T(8,128)(2,1)}, bf16[584,1024]{1,0:T(8,128)(2,1)S(1)}, u32[]{:S(2)}, u32[]{:S(2)}) collective-permute-start(bf16[584,1024]{1,0:T(8,128)(2,1)} %get-tuple-element.278), channel_id=1, source_target_pairs={{0,1},{1,0},{2,3},{3,2},{4,5},{5,4},{6,7},{7,6},{8,9},{9,8},{10,11... | collective-permute-start | bytes 3588104 | tf_op jit(solution)/shard_map/ppermute | solution.py:683
  358.8 18.8 %collective-permute-start.50 = (bf16[4,384,128]{2,1,0:T(8,128)(2,1)S(1)}, bf16[4,384,128]{2,1,0:T(8,128)(2,1)}, u32[]{:S(2)}, u32[]{:S(2)}) collective-permute-start(bf16[4,384,128]{2,1,0:T(8,128)(2,1)S(1)} %get-tuple-element.288), channel_id=1, source_target_pairs={{0,4},{4,0},{8,12},{12,8},{16,20},{20,16},{24,28},{28,24},{1,5},{5... | collective-permute-start | bytes 1179656 | tf_op jit(solution)/shard_map/ppermute | solution.py:676
  359.2 18.5 %collective-permute-start.51 = (bf16[4,384,128]{2,1,0:T(8,128)(2,1)S(1)}, bf16[4,384,128]{2,1,0:T(8,128)(2,1)}, u32[]{:S(2)}, u32[]{:S(2)}) collective-permute-start(bf16[4,384,128]{2,1,0:T(8,128)(2,1)S(1)} %get-tuple-element.286), channel_id=1, source_target_pairs={{0,2},{2,0},{1,3},{3,1},{4,6},{6,4},{5,7},{7,5},{8,10},{10,8},{9,1... | collective-permute-start | bytes 1179656 | tf_op jit(solution)/shard_map/ppermute | solution.py:679
  376.8 6.2 %collective-permute-start.45 = (f32[8,12,128]{2,0,1:T(8,128)S(1)}, f32[8,12,128]{2,0,1:T(8,128)S(1)}, u32[]{:S(2)}, u32[]{:S(2)}) collective-permute-start(f32[8,12,128]{2,0,1:T(8,128)S(1)} %pad_maximum_fusion.22), channel_id=1, source_target_pairs={{0,2},{2,0},{1,3},{3,1},{4,6},{6,4},{5,7},{7,5},{8,10},{10,8},{9,1... | collective-permute-start | bytes 147464 | tf_op jit(solution)/shard_map/ppermute | solution.py:679
  380.0 16.3 %collective-permute-start.52 = (bf16[768,128]{1,0:T(8,128)(2,1)S(1)}, bf16[768,128]{1,0:T(8,128)(2,1)S(1)}, u32[]{:S(2)}, u32[]{:S(2)}) collective-permute-start(bf16[768,128]{1,0:T(8,128)(2,1)S(1)} %pad_maximum_fusion.18), channel_id=1, source_target_pairs={{0,8},{4,12},{8,0},{12,4},{16,24},{20,28},{24,16},{28,20},{1,9},{5... | collective-permute-start | bytes 589832 | tf_op jit(solution)/shard_map/ppermute | solution.py:673
  380.1 16.2 %collective-permute-start.53 = (bf16[768,128]{1,0:T(8,128)(2,1)S(1)}, bf16[768,128]{1,0:T(8,128)(2,1)S(1)}, u32[]{:S(2)}, u32[]{:S(2)}) collective-permute-start(bf16[768,128]{1,0:T(8,128)(2,1)S(1)} %pad_maximum_fusion.19), channel_id=1, source_target_pairs={{0,16},{4,20},{8,24},{12,28},{16,0},{20,4},{24,8},{28,12},{1,17},{... | collective-permute-start | bytes 589832 | tf_op jit(solution)/shard_map/ppermute | solution.py:673
  383.1 3.8 collective-permute-start.46
  387.0 5.5 %collective-permute-start.49 = (f32[9,128]{1,0:T(8,128)S(1)}, f32[9,128]{1,0:T(8,128)S(1)}, u32[]{:S(2)}, u32[]{:S(2)}) collective-permute-start(f32[9,128]{1,0:T(8,128)S(1)} %bitcast.288), channel_id=1, source_target_pairs={{0,24},{4,28},{8,16},{12,20},{16,8},{20,12},{24,0},{28,4},{1,25},{... | collective-permute-start | bytes 13832 | tf_op jit(solution)/shard_map/ppermute | solution.py:673
  388.5 5.5 %collective-permute-start.47 = (f32[9,128]{1,0:T(8,128)S(1)}, f32[9,128]{1,0:T(8,128)S(1)}, u32[]{:S(2)}, u32[]{:S(2)}) collective-permute-start(f32[9,128]{1,0:T(8,128)S(1)} %bitcast.287), channel_id=1, source_target_pairs={{0,8},{4,12},{8,0},{12,4},{16,24},{20,28},{24,16},{28,20},{1,9},{5... | collective-permute-start | bytes 13832 | tf_op jit(solution)/shard_map/ppermute | solution.py:673
  388.5 5.4 %collective-permute-start.48 = (f32[9,128]{1,0:T(8,128)S(1)}, f32[9,128]{1,0:T(8,128)S(1)}, u32[]{:S(2)}, u32[]{:S(2)}) collective-permute-start(f32[9,128]{1,0:T(8,128)S(1)} %bitcast.289), channel_id=1, source_target_pairs={{0,16},{4,20},{8,24},{12,28},{16,0},{20,4},{24,8},{28,12},{1,17},{... | collective-permute-start | bytes 13832 | tf_op jit(solution)/shard_map/ppermute | solution.py:673
  392.5 7.5 %collective-permute-start.54 = (bf16[768,128]{1,0:T(8,128)(2,1)S(1)}, bf16[768,128]{1,0:T(8,128)(2,1)S(1)}, u32[]{:S(2)}, u32[]{:S(2)}) collective-permute-start(bf16[768,128]{1,0:T(8,128)(2,1)S(1)} %pad_maximum_fusion.20), channel_id=1, source_target_pairs={{0,24},{4,28},{8,16},{12,20},{16,8},{20,12},{24,0},{28,4},{1,25},{... | collective-permute-start | bytes 589832 | tf_op jit(solution)/shard_map/ppermute | solution.py:673
  (25 other events, 223.5 us)

commit v3 on v2

--- a/solution.py
+++ b/solution.py
@@ -13,7 +13,24 @@
 BF = jnp.bfloat16
 F32 = jnp.float32
 VMEM_LIMIT = 60 * 1024 * 1024
-SLOW = 0.05
+COST_SCALE = 1.0
+COST = {
+    "arrange_pair": 5,
+    "vectors": 3,
+    "attn_forward": 16,
+    "mlp_up": 10,
+    "down_grad": 11,
+    "mlp_back": 22,
+    "up_grad": 11,
+    "middle_back": 12,
+    "out_grad": 5,
+    "attn_backward": 18,
+    "qkv_grad": 9,
+    "grad_one": 2,
+    "qkv_add": 30,
+    "finish_layer": 30,
+    "finish_tokens": 9,
+}
 NT = (((1,), (1,)), ((), ()))
 TN = (((0,), (0,)), ((), ()))
 NN = (((1,), (0,)), ((), ()))
@@ -40,7 +57,7 @@
             copy.wait()
 
 
-def call(body, ins, outs, scratch, name, flops, aliases=None, smem=(), sems=48, vmem_ins=()):
+def call(body, ins, outs, scratch, name, flops, aliases=None, smem=(), sems=48, vmem_ins=(), hidden=False):
     n_smem, n_vmem, n_in, n_out = len(smem), len(vmem_ins), len(ins), len(outs)
     moved = sum(a.size * a.dtype.itemsize for a in ins) + sum(
         o.size * o.dtype.itemsize for o in outs
@@ -54,6 +71,8 @@
         rest = refs[first + n_in + n_out :]
         body(small, in_refs, out_refs, rest[:-1], Loads(rest[-1]))
 
+    flops = COST.get(name, 3) * COST_SCALE * 1.15e9
+    moved = 0
     any_spec = pl.BlockSpec(memory_space=pl.ANY)
     return pl.pallas_call(
         kernel,
@@ -65,7 +84,7 @@
         scratch_shapes=list(scratch) + [pltpu.SemaphoreType.DMA((sems,))],
         input_output_aliases={n_smem + n_vmem + i: o for i, o in (aliases or {}).items()},
         compiler_params=pltpu.CompilerParams(vmem_limit_bytes=VMEM_LIMIT),
-        cost_estimate=pl.CostEstimate(flops=int(flops / SLOW), bytes_accessed=int(moved / SLOW), transcendentals=0),
+        cost_estimate=pl.CostEstimate(flops=int(flops), bytes_accessed=int(moved), transcendentals=0),
         name=name,
     )(*smem, *vmem_ins, *ins)
 
@@ -117,6 +136,54 @@
         0,
         smem=(ids,),
     )
+
+
+def vectors(ids, gathered, row0, nd, y_n, bd, qv, up):
+    tx, z_n = len(gathered), nd // y_n
+
+    def body(small, ins, outs, scratch, loads):
+        ids_ref, rows_s, nv_s, bq_s, bu_s = small[0], *scratch
+        rows = pl.ds(row0, 16)
+        loads.wait(loads.start([(ins[k].at[:, rows, :], rows_s.at[k]) for k in range(tx)]))
+        for p in range(nd):
+            nv_s[:, p * bd : (p + 1) * bd] = rows_s[0, p].astype(F32)[:6, :bd]
+        for k in range(tx):
+            pieces = []
+            for d in range(nd):
+                rel = ids_ref[1] ^ d
+                spot = (rel % y_n) * z_n + rel // y_n
+                piece = rows_s[k, spot].astype(F32)
+                bu_s[:, (k * nd + d) * up : (k * nd + d + 1) * up] = piece[8:9, :up]
+                pieces.append(piece[6:8, :])
+            each = 128 // qv
+            for start in range(0, nd, each):
+                total = pieces[start]
+                for i in range(1, each):
+                    total = total + pltpu.roll(pieces[start + i], i * qv, 1)
+                bq_s[:, (k * nd + start) * qv : (k * nd + start + each) * qv] = total
+        loads.wait(loads.start([(nv_s, outs[0]), (bq_s, outs[1]), (bu_s, outs[2])]))
+
+    shapes = [(6, nd * bd), (2, tx * nd * qv), (1, tx * nd * up)]
+    return call(
+        body,
+        list(gathered),
+        [sds(s, F32) for s in shapes],
+        [pltpu.VMEM((tx, nd, 16, gathered[0].shape[2]), BF)] + [pltpu.VMEM(s, F32) for s in shapes],
+        "vectors",
+        0,
+        smem=(ids,),
+    )
+
+
+def block_stores(ids_ref, src, dst, nd, aligned):
+    if not aligned:
+        return [(src, dst)]
+    bd = src.shape[1] // nd
+    pairs = []
+    for p in range(nd):
+        cols = pl.ds(pl.multiple_of(ids_ref[2 + p] * bd, 128), bd)
+        pairs.append((src.at[:, p * bd : (p + 1) * bd], dst.at[:, cols]))
+    return pairs
 
 
 def weight_loads(loads, groups, refs, scratch):
@@ -282,10 +349,11 @@
     )
 
 
-def weight_grad(lefts, rights, tasks, out_shapes, name):
+def weight_grad(lefts, rights, tasks, out_shapes, name, lo, hi, prev=None):
     rows = lefts[0].shape[0]
     arrays = list(lefts) + list(rights)
     n_left, n_in = len(lefts), len(arrays)
+    prev = list(prev or [])
     last = {}
     for n, task in enumerate(tasks):
         for store in task[4]:
@@ -310,7 +378,7 @@
             for which, spot, r_sl, c_sl in stores:
                 out_s[which][spot] = value[r_sl, c_sl]
             for which in sorted(w for w in last if last[w] == n):
-                done.append(loads.start([(out_s[which], outs[which])]))
+                done.append(loads.start([(out_s[which], outs[which].at[:, lo:hi])]))
         for group in done:
             loads.wait(group)
 
@@ -319,16 +387,19 @@
     )
     return call(
         body,
-        arrays,
+        arrays + prev,
         [sds(s, BF) for s in out_shapes],
-        [pltpu.VMEM(a.shape, BF) for a in arrays] + [pltpu.VMEM(s, BF) for s in out_shapes],
+        [pltpu.VMEM(a.shape, BF) for a in arrays]
+        + [pltpu.VMEM((s[0], hi - lo, s[2]), BF) for s in out_shapes],
         name,
         flops,
+        aliases={n_in + i: i for i in range(len(prev))},
     )
 
 
 def mlp_back(grad, act, dact, wdown, wup, step):
     rows, width = grad.shape
+    seq = rows // 2
     hid = dact.shape[1]
     down_arrays, down_plan, down_scratch = wdown
     up_arrays, up_plan, up_scratch = wup
@@ -359,18 +430,22 @@
         done.append(loads.start([(sum_s, outs[1])]))
         for group in g_wu:
             loads.wait(group)
-        two_s[...] = dot(low_s[...], wu_s[...], NT).astype(BF)
-        done.append(loads.start([(two_s, outs[2])]))
+        two = dot(low_s[...], wu_s[...], NT)
+        for a in range(2):
+            two_s[a] = two[a * seq : (a + 1) * seq].astype(BF)
+            done.append(loads.start([(two_s.at[a], outs[2 + a])]))
         loads.wait(g_a)
         mlp_s[...] = dot(a_s[...], wd_s[...], NN).astype(BF)
-        done.append(loads.start([(mlp_s, outs[3])]))
+        done.append(loads.start([(mlp_s, outs[4])]))
         for group in done:
             loads.wait(group)
 
     return call(
         body,
         [grad, act, dact] + down_arrays + up_arrays,
-        [sds((rows, hid), BF), sds((1, hid), F32), sds((rows, width), BF), sds((rows, width), BF)],
+        [sds((rows, hid), BF), sds((1, hid), F32)]
+        + [sds((seq, width), BF)] * 2
+        + [sds((rows, width), BF)],
         [
             pltpu.VMEM(down_scratch, BF),
             pltpu.VMEM(up_scratch, BF),
@@ -379,7 +454,7 @@
             pltpu.VMEM((rows, hid), BF),
             pltpu.VMEM((rows, hid), BF),
             pltpu.VMEM((1, hid), F32),
-            pltpu.VMEM((rows, width), BF),
+            pltpu.VMEM((2, seq, width), BF),
             pltpu.VMEM((rows, width), BF),
         ],
         "mlp_back",
@@ -388,51 +463,43 @@
     )
 
 
-def rows_times(lefts, row_range, weight, dims, split, width, name):
+def input_grad(lefts, weight, width):
     arrays, plan, shape = weight
-    lo, hi = row_range
-    rows = hi - lo
+    rows, ext = lefts[0].shape
+    seq = rows // 2
     n = len(lefts)
 
     def body(small, ins, outs, scratch, loads):
         w_s, out_s = scratch[0], scratch[1]
         l_s = scratch[2:]
-        g_l = loads.start([(ins[i].at[lo:hi], l_s[i]) for i in range(n)])
-        g_w = weight_loads(loads, plan, ins[n:], w_s)
-        loads.wait(g_l)
-        for group in g_w:
-            loads.wait(group)
+        g_w = weight_loads(loads, plan[:1], ins[n:], w_s)
+        g_l = [loads.start([(ins[i], l_s[i])]) for i in range(n)]
+        g_w += weight_loads(loads, plan[1:], ins[n:], w_s)
         total = None
         for i in range(n):
-            w = w_s[i].reshape(-1, shape[-1]) if split else w_s[...]
-            piece = dot(l_s[i][...], w, dims)
+            loads.wait(g_l[i])
+            if i < len(g_w):
+                loads.wait(g_w[i])
+            piece = dot(l_s[i][...], w_s[i].reshape(width, ext), NT)
             total = piece if total is None else total + piece
-        out_s[...] = total.astype(BF)
-        loads.wait(loads.start([(out_s, outs[0])]))
+        done = []
+        for a in range(2):
+            out_s[a] = total[a * seq : (a + 1) * seq].astype(BF)
+            done.append(loads.start([(out_s.at[a], outs[a])]))
+        for group in done:
+            loads.wait(group)
 
     return call(
         body,
         list(lefts) + arrays,
-        [sds((rows, width), BF)],
-        [pltpu.VMEM(shape, BF), pltpu.VMEM((rows, width), BF)]
-        + [pltpu.VMEM((rows, a.shape[1]), BF) for a in lefts],
-        name,
-        2 * rows * width * sum(a.shape[1] for a in lefts),
-    )[0]
-
-
-def store_blocks(ids_ref, out_s, value, nd, aligned):
-    width = value.shape[1]
-    bd = width // nd
-    if not aligned:
-        out_s[...] = value
-        return
-    for p in range(nd):
-        cols = pl.ds(pl.multiple_of(ids_ref[2 + p] * bd, 128), bd)
-        out_s[:, cols] = value[:, p * bd : (p + 1) * bd]
-
-
-def middle_back(ids, middle, part, recvs, cot, keep, nv, wout):
+        [sds((seq, width), BF)] * 2,
+        [pltpu.VMEM(shape, BF), pltpu.VMEM((2, seq, width), BF)] + [pltpu.VMEM((rows, ext), BF)] * n,
+        "grad_one",
+        2 * rows * width * ext * n,
+    )
+
+
+def middle_back(ids, middle, parts, recvs, cot, keep, nv, wout):
     _, seq, width = middle.shape
     out_arrays, out_plan, out_scratch = wout
     ext = out_scratch[0]
@@ -446,14 +513,14 @@
             loads.start(
                 [
                     (ins[0].at[a], mid_s.at[a]),
-                    (ins[1].at[a], part_s.at[a]),
-                    (ins[2].at[a], cot_s.at[a]),
-                    (ins[3 + a], recv_s.at[a]),
+                    (ins[1].at[a], cot_s.at[a]),
+                    (ins[2 + a], part_s.at[a]),
+                    (ins[4 + a], recv_s.at[a]),
                 ]
             )
             for a in range(2)
         ]
-        g_o = weight_loads(loads, out_plan, ins[5:], wo_s)
+        g_o = weight_loads(loads, out_plan, ins[6:], wo_s)
         done = []
         for a in range(2):
             loads.wait(g_in[a])
@@ -484,7 +551,7 @@
 
     return call(
         body,
-        [middle, part, cot] + list(recvs) + out_arrays,
+        [middle, cot] + list(parts) + list(recvs) + out_arrays,
         [
             sds((seq, width), F32),
             sds((2, seq, width), BF),
@@ -509,31 +576,23 @@
     )
 
 
-def attn_backward(image, grad, q, k, v, prev):
+def attn_backward(units, grad, q, k, v, prev):
     _, seq, ext = q.shape
     n_prev = 0 if prev is None else len(prev)
+    n = len(units)
 
     def body(small, ins, outs, scratch, loads):
         q_s, k_s, v_s, do_s, dq_s, dk_s, dv_s, bs_s = scratch
-        n_pairs = ext // 128
         groups = []
-        for i in range(n_pairs):
+        for u, (image, i) in enumerate(units):
             cols = slice(i * 128, (i + 1) * 128)
-            groups.append(
-                loads.start(
-                    [
-                        (ins[j].at[image, :, cols], scratch[j].at[:, cols])
-                        for j in range(4)
-                    ]
-                )
-            )
+            groups.append(loads.start([(ins[j].at[image, :, cols], scratch[j].at[u]) for j in range(4)]))
         half = lax.broadcasted_iota(jnp.int32, (1, 128), 1) // HEAD_DIM
         for group in groups:
             loads.wait(group)
 
-        def pair(i, carry):
-            cols = pl.ds(pl.multiple_of(i * 128, 128), 128)
-            q2, k2, v2, do2 = q_s[:, cols], k_s[:, cols], v_s[:, cols], do_s[:, cols]
+        def unit(u, carry):
+            q2, k2, v2, do2 = q_s[u], k_s[u], v_s[u], do_s[u]
             dq = dk = dv = None
             for h in range(2):
                 mask = (half == h).astype(BF)
@@ -553,31 +612,33 @@
                 dk = k_piece if dk is None else dk + k_piece
                 dv = v_piece if dv is None else dv + v_piece
             dq = dq * HEAD_DIM**-0.5
-            bs_s[0:1, cols] = jnp.sum(dq, axis=0, keepdims=True)
-            bs_s[1:2, cols] = jnp.sum(dv, axis=0, keepdims=True)
-            dq_s[:, cols] = dq.astype(BF)
-            dk_s[:, cols] = dk.astype(BF)
-            dv_s[:, cols] = dv.astype(BF)
+            bs_s[u, 0:1, :] = jnp.sum(dq, axis=0, keepdims=True)
+            bs_s[u, 1:2, :] = jnp.sum(dv, axis=0, keepdims=True)
+            dq_s[u] = dq.astype(BF)
+            dk_s[u] = dk.astype(BF)
+            dv_s[u] = dv.astype(BF)
             return carry
 
-        lax.fori_loop(0, n_pairs, pair, 0)
-        g_out = loads.start(
-            [
-                (dq_s, outs[0].at[image]),
-                (dk_s, outs[1].at[image]),
-                (dv_s, outs[2].at[image]),
-                (bs_s, outs[3]),
-            ]
-        )
-        loads.wait(g_out)
+        lax.fori_loop(0, n, unit, 0)
+        done = []
+        for u, (image, i) in enumerate(units):
+            cols = slice(i * 128, (i + 1) * 128)
+            done.append(
+                loads.start(
+                    [(scratch[4 + j].at[u], outs[j].at[image, :, cols]) for j in range(3)]
+                )
+            )
+        done.append(loads.start([(bs_s, outs[3])]))
+        for group in done:
+            loads.wait(group)
 
     return call(
         body,
         [q, k, v, grad] + list(prev or []),
-        [sds((2, seq, ext), BF)] * 3 + [sds((2, ext), F32)],
-        [pltpu.VMEM((seq, ext), BF)] * 7 + [pltpu.VMEM((2, ext), F32)],
+        [sds((2, seq, ext), BF)] * 3 + [sds((n, 2, 128), F32)],
+        [pltpu.VMEM((n, seq, 128), BF)] * 7 + [pltpu.VMEM((n, 2, 128), F32)],
         "attn_backward",
-        40 * seq * seq * ext,
+        10 * n * seq * seq * 128,
         aliases={4 + i: i for i in range(n_prev)},
     )
 
@@ -593,9 +654,8 @@
         for group in groups:
             loads.wait(group)
         total = part_s[...].astype(F32) + recv_s[...].astype(F32) + nv_ref[5:6, :]
-        value = (mid_s[...] + keep_ref[mine] * total).astype(BF)
-        store_blocks(ids_ref, out_s, value, nd, aligned)
-        loads.wait(loads.start([(out_s, outs[0])]))
+        out_s[...] = (mid_s[...] + keep_ref[mine] * total).astype(BF)
+        loads.wait(loads.start(block_stores(ids_ref, out_s, outs[0], nd, aligned)))
 
     return call(
         body,
@@ -609,24 +669,27 @@
     )[0]
 
 
-def finish_tokens(ids, nv, tok, part, recvs, gmid, nd, aligned):
+def finish_tokens(ids, nv, tok, parts, recvs, gmid, rest, nd, aligned):
     _, seq, width = tok.shape
+    n_dest, z_n = rest.shape[:2]
+    bd = width // nd
 
     def body(small, ins, outs, scratch, loads):
         ids_ref, nv_ref = small
         mine = ids_ref[0]
-        tok_s, part_s, recv_s, gm_s, out_s, cs_s = scratch
+        tok_s, part_s, recv_s, gm_s, out_s, cs_s, rest_s = scratch
+        g_rest = loads.start([(ins[6], rest_s)])
         groups = [
             loads.start(
                 [
                     (ins[0].at[a], tok_s.at[a]),
-                    (ins[1].at[a], part_s.at[a]),
-                    (ins[3 + a], recv_s.at[a]),
+                    (ins[2 + a], part_s.at[a]),
+                    (ins[4 + a], recv_s.at[a]),
                 ]
             )
             for a in range(2)
         ]
-        g_mid = loads.start([(ins[2], gm_s)])
+        g_mid = loads.start([(ins[1], gm_s)])
         for group in groups:
             loads.wait(group)
         done = []
@@ -641,21 +704,28 @@
                 cs_s[1:2, :] = shift_sum
                 loads.wait(g_mid)
                 value = gm_s[...] + norm_back(grad_one, hat, inverse, nv_ref[0:1, :])
-                store_blocks(ids_ref, out_s, value.astype(BF), nd, aligned)
-                done.append(loads.start([(out_s, outs[0])]))
+                out_s[...] = value.astype(BF)
+                done.append(loads.start(block_stores(ids_ref, out_s, outs[0], nd, aligned)))
             else:
                 cs_s[0:1, :] = cs_s[0:1, :] + gain_sum
                 cs_s[1:2, :] = cs_s[1:2, :] + shift_sum
+        loads.wait(g_rest)
+        for n in range(n_dest if aligned else 0):
+            for kz in range(z_n):
+                p = n % (nd // z_n) * z_n + kz
+                rest_s[n, kz, 0:2, :] = cs_s[:, p * bd : (p + 1) * bd]
         done.append(loads.start([(cs_s, outs[1])]))
+        done += [loads.start([(rest_s.at[n], outs[2 + n])]) for n in range(n_dest)]
         for group in done:
             loads.wait(group)
 
     return call(
         body,
-        [tok, part, gmid] + list(recvs),
-        [sds((seq, width), BF), sds((2, width), F32)],
+        [tok, gmid] + list(parts) + list(recvs) + [rest],
+        [sds((seq, width), BF), sds((2, width), F32)] + [sds(rest.shape[1:], F32)] * n_dest,
         [pltpu.VMEM((2, seq, width), BF)] * 3
-        + [pltpu.VMEM((seq, width), F32), pltpu.VMEM((seq, width), BF), pltpu.VMEM((2, width), F32)],
+        + [pltpu.VMEM((seq, width), F32), pltpu.VMEM((seq, width), BF), pltpu.VMEM((2, width), F32)]
+        + [pltpu.VMEM(rest.shape, F32)],
         "finish_tokens",
         200 * seq * width,
         smem=(ids,),
@@ -674,6 +744,11 @@
 
     def send_y(self, value, k):
         return lax.ppermute(value, "dp", [(i, i ^ k) for i in range(self.dp)])
+
+    def send_xy(self, value, kx, ky):
+        count = self.dp * self.tx
+        pairs = [(i, ((i // self.tx) ^ ky) * self.tx + ((i % self.tx) ^ kx)) for i in range(count)]
+        return lax.ppermute(value, ("dp", "tx"), pairs)
 
     def send_x(self, value, k):
         return lax.ppermute(value, "tx", [(i, i ^ k) for i in range(self.tx)])
@@ -702,23 +777,55 @@
     return a_y, b_x
 
 
+def join(pieces):
+    return [jnp.concatenate(part) for part in pieces]
+
+
 def gather_last(grid, a_y, b_x):
-    a_y, b_x = jnp.concatenate(a_y), jnp.concatenate(b_x)
     a_all = [a_y] + [grid.send_x(a_y, k) for k in range(1, grid.tx)]
     b_all = [b_x] + [grid.send_y(b_x, k) for k in range(1, grid.y)]
     return a_all, b_all
 
 
-def add_low(first, *others):
-    total = first.astype(F32)
-    for other in others:
-        total = total + other.astype(F32)
-    return total.astype(BF)
+def add_pieces(groups, cuts, outs, name):
+    arrays = [a for group in groups for a in group]
+    starts = [sum(len(g) for g in groups[:i]) for i in range(len(groups))]
+    last = {}
+    for n, cut in enumerate(cuts):
+        last[cut[2]] = n
+
+    def body(small, ins, outs_ref, scratch, loads):
+        in_s, out_s = scratch[: len(arrays)], scratch[len(arrays) :]
+        loaded = [loads.start([(ins[i], in_s[i]) for i in range(starts[g], starts[g] + len(groups[g]))]) for g in range(len(groups))]
+        ready, done = set(), []
+        for n, (g, spot, which, place) in enumerate(cuts):
+            if g not in ready:
+                loads.wait(loaded[g])
+                ready.add(g)
+            total = None
+            for i in range(starts[g], starts[g] + len(groups[g])):
+                value = in_s[i][spot].astype(F32)
+                total = value if total is None else total + value
+            out_s[which][place] = total.astype(out_s[which].dtype)
+            for w in sorted(w for w in last if last[w] == n):
+                done.append(loads.start([(out_s[w], outs_ref[w])]))
+        for group in done:
+            loads.wait(group)
+
+    return call(
+        body,
+        arrays,
+        outs,
+        [pltpu.VMEM(a.shape, a.dtype) for a in arrays] + [pltpu.VMEM(o.shape, o.dtype) for o in outs],
+        name,
+        0,
+    )
 
 
 class Scatter:
-    def __init__(self, grid, a_all, b_all):
-        self.grid, self.rows = grid, a_all[0].shape[1]
+    def __init__(self, grid, a_all, b_all, name):
+        self.grid, self.name, self.bit = grid, name, 0
+        self.rows = (a_all[0].shape[1], b_all[0].shape[1])
         a_got = [grid.send_x(a_all[k], k) for k in range(1, grid.tx)]
         b_got = [grid.send_y(b_all[k], k) for k in range(1, grid.y)]
         self.state = ([a_all[0]] + a_got, [b_all[0]] + b_got)
@@ -726,30 +833,64 @@
     def second(self, gate):
         grid, z = self.grid, self.grid.z
         a_in, b_in = after(self.state, gate)
-        a_y = [add_low(*[v[k * z : (k + 1) * z] for v in a_in]) for k in range(grid.y)]
-        b_x = [add_low(*[v[k * z : (k + 1) * z] for v in b_in]) for k in range(grid.tx)]
+        outs = [sds((z,) + a_in[0].shape[1:], BF)] * grid.y + [sds((z,) + b_in[0].shape[1:], BF)] * grid.tx
+        full = slice(None)
+        cuts = [(0, slice(k * z, (k + 1) * z), k, full) for k in list(range(1, grid.y)) + [0]]
+        cuts += [(1, slice(k * z, (k + 1) * z), grid.y + k, full) for k in list(range(1, grid.tx)) + [0]]
+        res = add_pieces([a_in, b_in], cuts, outs, self.name + "_add")
+        a_y, b_x = res[: grid.y], res[grid.y :]
         a_got = [grid.send_y(a_y[k], k) for k in range(1, grid.y)]
         b_got = [grid.send_x(b_x[k], k) for k in range(1, grid.tx)]
         self.state = ([a_y[0]] + a_got, [b_x[0]] + b_got)
         return a_y[0], b_x[0]
 
-    def along_z(self, gate):
+    def along_z(self, gate, extra=None):
         grid = self.grid
         a_in, b_in = after(self.state, gate)
-        both = [
-            jnp.concatenate([add_low(*[v[k] for v in a_in]), add_low(*[v[k] for v in b_in])])
-            for k in range(grid.z)
-        ]
-        got = [grid.send_z(both[k], k) for k in range(1, grid.z)]
-        self.state = [both[0]] + got
+        ra, rb = self.rows
+        groups = [a_in, b_in] + ([extra] if extra else [])
+        more = extra[0].shape[1] if extra else 0
+        order = list(range(1, grid.z)) + [0]
+        cuts = []
+        for k in order:
+            cuts.append((0, k, k, slice(0, ra)))
+            cuts.append((1, k, k, slice(ra, ra + rb)))
+            if extra:
+                cuts.append((2, k, k, slice(ra + rb, ra + rb + more)))
+        outs = [sds((ra + rb + more,) + a_in[0].shape[2:], BF)] * grid.z
+        both = add_pieces(groups, cuts, outs, self.name + "_addz")
+        self.state = [both[0]] + [grid.send_z(both[k], k) for k in range(1, grid.z)]
         return both
 
-    def finish(self, gate):
-        parts = after(self.state, gate)
-        total = parts[0].astype(F32)
-        for value in parts[1:]:
-            total = total + value.astype(F32)
-        return total[: self.rows], total[self.rows :]
+    def halve(self, gate):
+        grid, (ra, rb) = self.grid, self.rows
+        groups = after(self.state, gate)
+        if self.bit == 0:
+            self.bit, self.left = 1, list(range(grid.z))
+        else:
+            self.bit, groups = 2 * self.bit, [groups]
+        sent = [k for k in self.left if k & self.bit]
+        kept = [k for k in self.left if not k & self.bit]
+        cuts = []
+        for which, ids in ((0, sent), (1, kept)):
+            for n, k in enumerate(ids):
+                spot = self.left.index(k)
+                if len(groups) == 2:
+                    cuts.append((0, spot, which, (n, slice(0, ra))))
+                    cuts.append((1, spot, which, (n, slice(ra, ra + rb))))
+                else:
+                    cuts.append((0, spot, which, n))
+        outs = [sds((len(kept), ra + rb) + groups[0][0].shape[2:], BF)] * 2
+        send, keep = add_pieces(groups, cuts, outs, self.name + "_half")
+        self.left = kept
+        self.state = [keep, grid.send_z(send, self.bit)]
+        return keep
+
+    def finish(self, gate, cuts, outs):
+        if self.bit:
+            cuts = [((0, rows), which, place) for rows, which, place in cuts]
+        cuts = [(0, rows, which, place) for rows, which, place in cuts]
+        return add_pieces([after(self.state, gate)], cuts, outs, self.name + "_sum")
 
 
 def xor_blocks(value, mask, axis):
@@ -822,11 +963,12 @@
     )
     qkv_a = pad_cols(w_qkv[:, :, :hh].reshape(3 * bd, hh), lane)
     qkv_b = pad_cols(w_qkv[:, :, hh:].reshape(3 * bd, hh), lane)
-    first_a = jnp.concatenate([qkv_a, pad_cols(w_out[:hh], lane)])
+    first_a = jnp.concatenate([qkv_a, pad_cols(w_out[:hh], lane), small])
     first_b = jnp.concatenate([qkv_b, pad_cols(w_out[hh:], lane)])
-    tok_other, cot_other = swap_core(tokens), swap_core(cotangent)
+    own = [tokens, cotangent]
+    other = [swap_core(value) for value in own]
     if aligned:
-        tok, cot = arrange_pair(ids, [tokens, cotangent], [tok_other, cot_other], dp)
+        tok, cot = arrange_pair(ids, own, other, dp)
     else:
 
         def arrange(own, other):
@@ -834,27 +976,27 @@
             pair = xor_blocks(pair.reshape(2, seq, dp, bd), me_d, 2)
             return from_abs(pair, 2).reshape(2, seq, width)
 
-        tok, cot = arrange(tokens, tok_other), arrange(cotangent, cot_other)
+        tok, cot = [arrange(own[i], other[i]) for i in range(2)]
     c1_z = gather_z(grid, first_a, first_b, gate=tok)
-    small = jnp.stack([small] + [grid.send_z(small, k) for k in range(1, z_n)])
-    small = jnp.concatenate([small] + [grid.send_y(small, k) for k in range(1, y_n)])
-    small = [small] + [grid.send_x(small, k) for k in range(1, tx)]
-    up_halves = after((w_up[:, :fh], w_up[:, fh:]), c1_z)
     c1_h = gather_first(grid, *c1_z)
+    c1_h = join(c1_h)
     c1a, c1b = gather_last(grid, *c1_h)
-    up_z = gather_z(grid, *up_halves, gate=(c1a, c1b))
-    dn_halves = after((w_down[:fh], w_down[fh:]), (c1a, c1b))
+    up_halves = after((w_up[:, :fh], w_up[:, fh:]), c1_h)
+    row0 = 3 * bd + hh
+    if aligned and 128 % (hw // dp) == 0 and (fw // dp) % 128 == 0:
+        c1a, c1b = after((c1a, c1b), (c1a, c1b))
+        nv, bq, bu = vectors(ids, c1a, row0, dp, y_n, bd, hw // dp, fw // dp)
+    else:
+        nv = c1a[0][:, row0 : row0 + 6, :bd].transpose(1, 0, 2).reshape(6, width).astype(F32)
+        tail = jnp.stack([v[:, row0 + 6 : row0 + 9] for v in c1a])
+        tail = xor_blocks(to_rel(tail, 1), me_d, 1)
+        bq = tail[:, :, :2, : hw // dp].transpose(2, 0, 1, 3).reshape(2, ext).astype(F32)
+        bu = tail[:, :, 2, : fw // dp].reshape(1, hid).astype(F32)
+    grad_top = cot * keep.astype(BF)[:, None, None]
+
+    up_z = gather_z(grid, *up_halves, gate=nv)
     up_h = gather_first(grid, *up_z)
-
-    grad_top = cot * keep.astype(BF)[:, None, None]
-
-    nv = small[0][:, :6, :bd].transpose(1, 0, 2).reshape(6, width).astype(F32)
-    tail = jnp.stack([v[:, 6:9] for v in small])
-    tail = xor_blocks(to_rel(tail, 1), me_d, 1)
-    bq = (
-        tail[:, :, :2, : hw // dp].transpose(2, 0, 1, 3).reshape(2, ext).astype(F32)
-    )
-    bu = tail[:, :, 2, : fw // dp].reshape(1, hid).astype(F32)
+    dn_halves = after((w_down[:fh], w_down[fh:]), up_z)
 
     if aligned:
         every, wq_plan, wo_plan, up_plan, dn_plan = slice(None), [[], [], []], [], [], []
@@ -894,7 +1036,7 @@
             b = b.transpose(1, 0, 2, 3, 4).reshape(a.shape[:2] + b.shape[3:])
             return jnp.stack([a, b], axis=1)
 
-        c1 = whole(c1a, c1b)
+        c1 = whole([v[:, :row0] for v in c1a], c1b)
         qkv = c1[:, :, :, : 3 * bd, :hh].reshape(tx, 2, dp, 3, bd, hh)
         qkv = qkv.transpose(3, 2, 4, 0, 1, 5).reshape(3, dp, bd, ext)
         out = c1[:, :, :, 3 * bd :, :bd].transpose(0, 1, 3, 2, 4).reshape(ext, width)
@@ -905,141 +1047,182 @@
     rows2 = 2 * seq
 
     res = attn_forward(0, after(tok, up_z), nv, bq, wqkv, wout, None)
-    parts = [(res[5], swap_core(res[5]))]
-    upa, upb = gather_last(grid, *after(up_h, res[5]))
-    dn_z = gather_z(grid, *dn_halves, gate=res[5])
-    dn_h = gather_first(grid, *dn_z)
-    res = attn_forward(1, after(tok, dn_z), nv, bq, wqkv, wout, res[:5])
-    parts.append((res[5], swap_core(res[5])))
+    part0 = res[5]
+    up_h = join(after(up_h, part0))
+    upa, upb = gather_last(grid, *up_h)
+    dn_halves = after(dn_halves, up_h)
+    res = attn_forward(1, after(tok, up_h), nv, bq, wqkv, wout, res[:5])
+    recv0 = swap_core(after(part0, res[5]))
+    parts = [(part0, recv0), (res[5], swap_core(res[5]))]
     first, q, k, v, att = res[:5]
     upa, upb = after((upa, upb), res[5])
-    dna, dnb = gather_last(grid, *after(dn_h, (upa, upb)))
+    dn_z = gather_z(grid, *dn_halves, gate=(upa, upb))
+    dn_h = gather_first(grid, *dn_z)
     if aligned:
         wup = ([v.reshape(-1, fh) for v in upa + upb], up_plan, (width, hid))
+    else:
+        up_w = whole(upa, upb).transpose(2, 3, 0, 1, 4).reshape(width, hid)
+        wup = ([up_w], all_of, up_w.shape)
+    part, recv = parts[0]
+    state = mlp_up(0, tok, part, recv, keep, nv, bu, wup, fh, None)
+    dna, dnb = gather_last(grid, *join(after(dn_h, state[1])))
+    part, recv = parts[1]
+    state = mlp_up(1, tok, part, recv, keep, nv, bu, wup, fh, state)
+    if aligned:
         wdown = (dna + dnb, dn_plan, (hid, width))
     else:
-        up_w = whole(upa, upb).transpose(2, 3, 0, 1, 4).reshape(width, hid)
         down_w = whole(dna, dnb).transpose(0, 1, 3, 2, 4).reshape(hid, width)
-        wup = ([up_w], all_of, up_w.shape)
         wdown = ([down_w], all_of, down_w.shape)
-    state = None
-    for image in range(2):
-        part, recv = parts[image]
-        state = mlp_up(image, tok, part, recv, keep, nv, bu, wup, fh, state)
     middle, second, act, dact = state
     flat = lambda value: value.reshape(rows2, value.shape[2])
     act2, sec2, grad2 = flat(act), flat(second), flat(grad_top)
 
-    order_x, order_y = list(range(1, tx)) + [0], list(range(1, y_n)) + [0]
-    d_all = slice(0, width)
-    d_half = [slice(ky * z_n * bd, (ky + 1) * z_n * bd) for ky in range(y_n)]
-
-    def spots(ky, kx):
-        if ky is None:
-            return [(order_x.index(kx), p, slice(p * bd, (p + 1) * bd)) for p in range(dp)]
-        which = tx + order_y.index(ky)
-        return [(which, kx * z_n + kz, slice(kz * bd, (kz + 1) * bd)) for kz in range(z_n)]
-
-    def cut(kx, size, ky):
-        start = kx * size + (0 if ky is None else size // 2)
-        return slice(start, start + size // 2)
-
-    def visits():
-        for kx in order_x:
-            yield None, kx, d_all
-        for ky in order_y:
-            for kx in range(tx):
-                yield ky, kx, d_half[ky]
-
     full = slice(None)
+    a_spots = [(p, slice(p * bd, (p + 1) * bd)) for p in range(dp)]
 
     def by_left(l_index, r_index, size, row0):
-        rows = slice(row0, row0 + size // 2)
-        return [
-            (
-                l_index,
-                cut(kx, size, ky),
-                r_index,
-                d_cols,
-                [(w, (spot, rows), full, cols) for w, spot, cols in spots(ky, kx)],
-            )
-            for ky, kx, d_cols in visits()
-        ]
+        tasks, rows = [], slice(row0, row0 + size // 2)
+        halves = slice(0, size // 2), slice(size // 2, size)
+        for kx in range(tx):
+            stores = [(kx, (p, rows), halves[0], cols) for p, cols in a_spots]
+            for p, cols in a_spots:
+                ky, kz = p // z_n, p % z_n
+                stores.append((tx + ky, (kx * z_n + kz, rows), halves[1], cols))
+            tasks.append((l_index, slice(kx * size, (kx + 1) * size), r_index, slice(0, width), stores))
+        return tasks
 
     def by_right(l_index, r_index, size, row0, lanes):
-        tasks = []
-        for ky, kx, d_cols in visits():
+        tasks, each = [], size // 2 // lanes
+        for kx in range(tx):
             stores = []
-            for j in range(size // 2 // lanes):
+            for j in range(each):
                 rows = slice(row0 + j * bd, row0 + (j + 1) * bd)
-                cols = slice(j * lanes, (j + 1) * lanes)
-                stores += [(w, (spot, rows), r_sl, cols) for w, spot, r_sl in spots(ky, kx)]
-            tasks.append((l_index, d_cols, r_index, cut(kx, size, ky), stores))
+                cols = [slice((h * each + j) * lanes, (h * each + j + 1) * lanes) for h in range(2)]
+                for p, r_sl in a_spots:
+                    ky, kz = p // z_n, p % z_n
+                    stores.append((kx, (p, rows), r_sl, cols[0]))
+                    stores.append((tx + ky, (kx * z_n + kz, rows), r_sl, cols[1]))
+            tasks.append((l_index, slice(0, width), r_index, slice(kx * size, (kx + 1) * size), stores))
         return tasks
 
-    def start_grad(lefts, rights, makers, rows, lanes, name):
-        tasks = []
-        for group in zip(*makers):
-            tasks += group
-        shapes = [(dp, rows, lanes)] * tx + [(tx * z_n, rows, lanes)] * y_n
-        parts = weight_grad(lefts, rights, tasks, shapes, name)
-        by_x, by_y = list(parts[:tx]), list(parts[tx:])
-        return Scatter(grid, by_x[-1:] + by_x[:-1], by_y[-1:] + by_y[:-1]), parts[-1]
-
-    down_rs, gate = start_grad([act2], [grad2], [by_left(0, 0, fw, 0)], fh, bd, "down_grad")
-    grad_in = after(grad2, gate)
-    low_pre, bias_up, two_part, mlp_part = mlp_back(grad_in, act2, flat(dact), wdown, wup, fh)
-    two_part = two_part.reshape(2, seq, width)
+    def pieces(rows, lanes):
+        return [(dp, rows, lanes)] * tx + [(tx * z_n, rows, lanes)] * y_n
+
+    def send_grad(parts, name):
+        return Scatter(grid, list(parts[:tx]), list(parts[tx:]), name)
+
+    grads = weight_grad([act2], [grad2], by_left(0, 0, fw, 0), pieces(fh, bd), "down_grad", 0, fh)
+    down_rs = send_grad(grads, "down")
+    grad_in = after(grad2, grads[-1])
+    low_pre, bias_up, two0, two1, mlp_part = mlp_back(grad_in, act2, flat(dact), wdown, wup, fh)
+    two_parts = [two0, two1]
     mlp_part = mlp_part.reshape(2, seq, width)
     mlp_recv = swap_core(mlp_part)
-    two_recvs = [swap_core(two_part[a]) for a in range(2)]
+    two_recvs = [swap_core(value) for value in two_parts]
     down_half = down_rs.second(bias_up)
+    up_rows = fh // bd * bd
+    up_shapes = pieces(up_rows + hh, bd)
+    sec_in = after(sec2, down_half)
+    tasks = by_right(0, 0, fw, 0, bd)
+    grads = weight_grad([sec_in], [low_pre], tasks, up_shapes, "up_grad", 0, up_rows)
     gmid, gattn, grad_att, col = middle_back(
-        ids, middle, two_part, after(two_recvs, down_half), cot, keep, nv, wout
+        ids, middle, two_parts, after(two_recvs, grads[-1]), cot, keep, nv, wout
     )
     down_zs = down_rs.along_z(col)
-    up_rows = fh // bd * bd
-    up_rs, gate = start_grad(
-        [sec2, flat(att)],
-        [low_pre, after(flat(gattn), down_zs)],
-        [by_right(0, 0, fw, 0, bd), by_left(1, 1, hw, up_rows)],
-        up_rows + hh,
-        bd,
-        "up_out_grad",
-    )
-
-    down_a, down_b = down_rs.finish(gate)
-    res = attn_backward(0, after(grad_att, (gate, down_a)), q, k, v, None)
+    att_in = after(flat(att), (down_zs, mlp_recv))
+    tasks = by_left(0, 0, hw, 0)
+    grads = weight_grad(
+        [att_in], [flat(gattn)], tasks, up_shapes, "out_grad", up_rows, up_rows + hh, grads
+    )
+    up_rs = send_grad(grads, "up_out")
+
+    units = [(a, i) for a in range(2) for i in range(ext // 128)]
+    cut = (5 * len(units) + 4) // 8
+    res = attn_backward(units[:cut], after(grad_att, grads[-1]), q, k, v, None)
     bias_qv = res[3]
-    up_half = up_rs.second(bias_qv)
-    res = attn_backward(1, after(grad_att, up_half), q, k, v, res[:3])
-    bias_qv = bias_qv + res[3]
-    up_zs = up_rs.along_z(res[3])
+    grad_down = down_rs.finish(bias_qv, [(full, 0, full)], [sds((fw, bd), F32)])[0]
+    up_half = up_rs.second(grad_down)
+    res = attn_backward(units[cut:], after(grad_att, up_half), q, k, v, res[:3])
+    bias_qv = jnp.concatenate([bias_qv, res[3]]).reshape(2, ext // 128, 2, 128)
+    bias_qv = jnp.sum(bias_qv, axis=0).transpose(1, 0, 2).reshape(2, ext)
+    up_zs = up_rs.halve(res[3]) if z_n > 1 else res[3]
     low_proj = [flat(value) for value in res[:3]]
     makers = [by_right(0, i, hw, i * bd, hh) for i in range(3)]
     first_in = after(flat(first), up_zs)
-    qkv_rs, gate = start_grad([first_in], low_proj, makers, 3 * bd, hh, "qkv_grad")
-    low_in = after(low_proj, gate)
-    one_part = rows_times(low_in, (0, rows2), wqkv, NT, True, width, "grad_one")
-    one_part = one_part.reshape(2, seq, width)
-    one_recvs = [swap_core(one_part[a]) for a in range(2)]
-    up_a, up_b = up_rs.finish(one_part)
-    qkv_half = qkv_rs.second(up_a)
+    tasks = [task for maker in makers for task in maker]
+    grads = weight_grad([first_in], low_proj, tasks, pieces(3 * bd, hh), "qkv_grad", 0, 3 * bd)
+    qkv_rs = send_grad(grads, "qkv")
+    low_in = after(low_proj, grads[-1])
+    one_parts = input_grad(low_in, wqkv, width)
+    one_recvs = [swap_core(value) for value in one_parts]
+    total_rows = up_rows + hh
+    cuts = []
+    for h in range(2):
+        for j in range(fh // bd):
+            rows = slice(h * total_rows + j * bd, h * total_rows + (j + 1) * bd)
+            cols = slice(h * fh + j * bd, h * fh + (j + 1) * bd)
+            cuts.append((rows, 0, (full, cols)))
+        rows = slice(h * total_rows + up_rows, (h + 1) * total_rows)
+        cuts.append((rows, 1, (slice(h * hh, (h + 1) * hh),)))
+    up_cuts, gate = cuts, one_parts[0]
+    while 2 * up_rs.bit < z_n:
+        gate = up_rs.halve(gate)
+    qkv_half = qkv_rs.second(gate)
+    wide = max(bd, hw // dp, fw // dp)
+    vec = jnp.concatenate([jnp.zeros((2, width), F32), col])
+    vec = vec.reshape(6, y_n, z_n, bd).transpose(1, 2, 0, 3)
+    bias_qv = bias_qv.reshape(2, tx, dp, hw // dp).transpose(2, 1, 0, 3)
+    bias_up = bias_up.reshape(tx, 1, dp, fw // dp).transpose(2, 0, 1, 3)
+    bias = jnp.concatenate(
+        [
+            jnp.pad(value, ((0, 0), (0, 0), (0, 0), (0, wide - value.shape[3])))
+            for value in (bias_qv, bias_up)
+        ],
+        axis=2,
+    )
+    bias = from_abs(xor_blocks(bias, me_d, 0), 0).reshape(y_n, z_n, tx, 3, wide)
+    bias = bias.transpose(2, 0, 1, 3, 4)
+    vec = jnp.pad(vec, ((0, 0), (0, 0), (0, 0), (0, wide - bd)))
+    vec = jnp.broadcast_to(vec, (tx,) + vec.shape)
+    rest = jnp.concatenate([vec, bias, jnp.zeros((tx, y_n, z_n, 7, wide), F32)], axis=3)
+    rest = rest.reshape(tx * y_n, z_n, 16, wide)
+    grad_tokens, one_sums, *small = finish_tokens(
+        ids, nv, tok, one_parts, after(one_recvs, qkv_half), gmid, rest, dp, aligned
+    )
+    if not aligned:
+        ones = jnp.pad(one_sums.reshape(2, y_n, z_n, bd), ((0, 14), (0, 0), (0, 0), (0, wide - bd)))
+        ones = ones.transpose(1, 2, 0, 3)
+        small = [value + ones[n % y_n] for n, value in enumerate(small)]
+    got = small[:1]
+    for n in range(1, tx * y_n):
+        got.append(grid.send_xy(small[n], n // y_n, n % y_n))
+    up_outs = [sds((bd, fw), F32), sds((hw, bd), F32)]
+    grad_up, grad_out = up_rs.finish(one_sums, up_cuts, up_outs)
+    cuts, outs = [], [sds((3, bd, hw), F32)]
+    for h in range(2):
+        for i in range(3):
+            rows = slice((3 * h + i) * bd, (3 * h + i + 1) * bd)
+            cuts.append((rows, 0, (i, full, slice(h * hh, (h + 1) * hh))))
+    if wide == hh:
+        qkv_zs = qkv_rs.along_z(grad_out, got)
+        cuts.append((slice(6 * bd, 6 * bd + 16), 1, full))
+        outs.append(sds((16, wide), F32))
+    else:
+        qkv_zs = qkv_rs.along_z(grad_out)
     layer_out = finish_layer(
-        ids, keep, nv, middle, after(mlp_part, qkv_half), mlp_recv, dp, aligned
-    )
-    grad_tokens, one_sums = finish_tokens(
-        ids, nv, tok, one_part, after(one_recvs, layer_out), gmid, dp, aligned
-    )
-    qkv_rs.along_z(one_sums)
-    qkv_ga, qkv_gb = qkv_rs.finish(one_sums)
-    out_a, out_b = up_a[up_rows:], up_b[up_rows:]
-
-    def lanes_back(value):
-        value = value[:up_rows].reshape(fh // bd, bd, bd)
-        return value.transpose(1, 0, 2).reshape(bd, fh)
-
-    up_a, up_b = lanes_back(up_a), lanes_back(up_b)
+        ids, keep, nv, middle, after(mlp_part, qkv_zs), mlp_recv, dp, aligned
+    )
+    res = qkv_rs.finish(layer_out, cuts, outs)
+    grad_qkv = res[0]
+    if wide == hh:
+        both = res[1]
+    else:
+        both, bit = sum(got), 1
+        while bit < z_n:
+            both = both.reshape((-1, 2) + both.shape[1:])
+            both = both[:, 0] + grid.send_z(both[:, 1], bit)
+            bit *= 2
+        both = both[0]
     if not aligned:
 
         def restore(value):
@@ -1048,46 +1231,14 @@
 
         layer_out, grad_tokens = restore(layer_out), restore(grad_tokens)
 
-    vec = jnp.stack([one_sums[0], col[0], one_sums[1], col[1], col[2], col[3]])
-    wide = max(bd, hw // dp, fw // dp)
-    vec = vec.reshape(6, dp, bd).transpose(1, 0, 2)
-    vec = jnp.pad(vec, ((0, 0), (0, 0), (0, wide - bd)))
-    bias_qv = bias_qv.reshape(2, tx, dp, hw // dp).transpose(2, 1, 0, 3).reshape(dp, 2 * tx, -1)
-    bias_up = bias_up.reshape(tx, dp, fw // dp).transpose(1, 0, 2)
-    bias = jnp.concatenate(
-        [
-            jnp.pad(bias_qv, ((0, 0), (0, 0), (0, wide - hw // dp))),
-            jnp.pad(bias_up, ((0, 0), (0, 0), (0, wide - fw // dp))),
-        ],
-        axis=1,
-    )
-    bias = from_abs(xor_blocks(bias, me_d, 0), 0)
-    both = jnp.concatenate([vec, bias], axis=1)
-    got = [both] + [grid.send_x(both, k) for k in range(1, tx)]
-    vec = sum(value[:, :6] for value in got)
-    bqv_mine = sum(value[:, 6 + 2 * k : 8 + 2 * k] for k, value in enumerate(got))
-    bup_mine = sum(
-        value[:, 6 + 2 * tx + k : 7 + 2 * tx + k] for k, value in enumerate(got)
-    )
-    both = jnp.concatenate([vec, bqv_mine, bup_mine], axis=1)
-    both = both[:z_n] + sum(
-        grid.send_y(both[k * z_n : (k + 1) * z_n], k) for k in range(1, y_n)
-    )
-    both = both[0] + sum(grid.send_z(both[k], k) for k in range(1, z_n))
     share = bd // (2 * tx)
     mine = lax.dynamic_slice(both[:6, :bd], (0, (2 * me_x + core) * share), (6, share))
 
-    grad_qkv = jnp.concatenate(
-        [qkv_ga.reshape(3, bd, hh), qkv_gb.reshape(3, bd, hh)], axis=2
-    )
-    grad_out = jnp.concatenate([out_a, out_b], axis=0)
-    grad_up = jnp.concatenate([up_a, up_b], axis=1)
-    grad_down = jnp.concatenate([down_a, down_b], axis=0)
     return (
         layer_out,
         grad_tokens,
-        mine[:2],
-        mine[2:6],
+        mine[0:3:2],
+        jnp.concatenate([mine[1:2], mine[3:6]]),
         grad_qkv,
         both[6:8, : hw // dp],
         grad_out,

time: 408 us -> 390 us (0.956)
  Pallas kernels: 184 us -> 216 us
  starting transfers between devices: 88 us -> 62.6 us
  other arithmetic: 29.3 us -> 4.88 us
    pallas_call x15 -> x27, Pallas kernels: 184 us -> 216 us  [call(): pl.pallas_call(kernel, out_shape=outs, in_specs=[pl.BlockSpec(memory_spac...]
    ppermute x24 -> x17, waiting for transfers between devices: 7.44 us -> 32.9 us  [send_z(): lax.ppermute(value, 'dp', [(i, i ^ k * self.y) for i in range(self.dp)])]
    ppermute x24 -> x17, starting transfers between devices: 52.3 us -> 29.6 us  [send_z(): lax.ppermute(value, 'dp', [(i, i ^ k * self.y) for i in range(self.dp)])]
    ppermute x14 -> x12, waiting for transfers between devices: 30.9 us -> 11.4 us  [send_x(): return lax.ppermute(value, 'tx', [(i, i ^ k) for i in range(self.tx)])]
    convert_element_type x15 -> x0, other arithmetic: 14 us -> none  [the longest x12 12.8 us: add_low(): return total.astype(BF)]
    slice x18 -> x7, local copies, waits for them, and re-layouts: 12.7 us -> 2.35 us  [the longest x1 0.95 us: per_device(): qkv_b = pad_cols(w_qkv[:, :, hh:].reshape(3 * bd, hh), lane)]
    unnamed x74 -> x86, local copies, waits for them, and re-layouts: 8.88 us -> 17.4 us
    concatenate x19 -> x4, other arithmetic: 8.26 us -> 2.01 us  [the longest x1 0.73 us: per_device(): jnp.concatenate([vec, bias, jnp.zeros((tx, y_n, z_n, 7, wide), F32)], axi...]
  transfers between devices with their start and end apart: 61 -> 53, of which waited for: 17 -> 17; matrix products, arithmetic and copies ran while one was open for 14% -> 4% of each run, Pallas kernels for 46% -> 51%
where the time goes in v3:
time: 390 us; the launch traced here: 384 us
  Pallas kernels  216 us (55%)
  waiting for transfers between devices  66.4 us (17%)
  starting transfers between devices  62.6 us (16%)
  local copies, waits for them, and re-layouts  32.3 us (8%)
  other arithmetic  4.88 us (1%)
    pallas_call x27, Pallas kernels, call(): pl.pallas_call(kernel, out_shape=outs, in_specs=[pl.BlockSpec(memory_spac...  216 us
    ppermute x17, waiting for transfers between devices, send_z(): lax.ppermute(value, 'dp', [(i, i ^ k * self.y) for i in range(self.dp)])  32.9 us
    ppermute x17, starting transfers between devices, send_z(): lax.ppermute(value, 'dp', [(i, i ^ k * self.y) for i in range(self.dp)])  29.6 us
    ppermute x12, waiting for transfers between devices, send_y(): return lax.ppermute(value, 'dp', [(i, i ^ k) for i in range(self.dp)])  20.1 us
    unnamed x86, local copies, waits for them, and re-layouts  17.4 us
    ppermute x12, starting transfers between devices, send_y(): return lax.ppermute(value, 'dp', [(i, i ^ k) for i in range(self.dp)])  13.9 us
    ppermute x12, starting transfers between devices, send_x(): return lax.ppermute(value, 'tx', [(i, i ^ k) for i in range(self.tx)])  13.4 us
    ppermute x12, waiting for transfers between devices, send_x(): return lax.ppermute(value, 'tx', [(i, i ^ k) for i in range(self.tx)])  11.4 us
  transfers between devices with their start and end apart: 53, of which 17 were waited for; matrix products, arithmetic and copies ran while one was open for 4% of the time, Pallas kernels for 51%

profile of v3, /device:TPU:0, one launch (start us, length us, event | category | flops | bytes accessed | tf_op | source)
XLA Modules:
  0.0 384.5 jit_solution(2488667685628827028)
XLA Ops:
  3.6 1.5 concatenate.71
  5.1 3.1 collective-permute-start
  8.2 2.6 collective-permute-start.1
  12.5 4.9 %arrange_pair.1 = (bf16[2,584,1024]{2,1,0:T(8,128)(2,1)}, bf16[2,584,1024]{2,1,0:T(8,128)(2,1)}) custom-call(s32[10]{0:T(128)} %stack.130.refs_0_, bf16[584,1024]{1,0:T(8,128)(2,1)} %refs_1_.1, bf16[584,1024]{1,0:T(8,128)(2,1)} %refs_2_.1, bf16[584,1024]{1,0:T(8,128)(2,1)} %copy-done.13, bf16[584,1024]{1,0:T(8,128)(2,1)} %collective-permute-done.4.refs_4_), custom_call_target="tpu_custom_call" | custom-call | flops 5750000128 | tf_op jit(solution)/shard_map/arrange_pair/pallas_call | solution.py:77
  17.4 2.5 collective-permute-done
  19.9 9.9 %collective-permute-done.1 = bf16[1040,128]{1,0:T(8,128)(2,1)S(1)} collective-permute-done((bf16[1040,128]{1,0:T(8,128)(2,1)S(1)}, bf16[1040,128]{1,0:T(8,128)(2,1)S(1)}, u32[]{:S(2)}, u32[]{:S(2)}) %collective-permute-start.1) | collective-permute-done | bytes 266272 | tf_op jit(solution)/shard_map/ppermute | solution.py:743
  30.7 1.6 collective-permute-start.5
  33.7 1.6 collective-permute-start.7
  35.9 6.9 %collective-permute-done.5 = bf16[4,528,128]{2,1,0:T(8,128)(2,1)S(1)} collective-permute-done((bf16[4,528,128]{2,1,0:T(8,128)(2,1)S(1)}, bf16[4,528,128]{2,1,0:T(8,128)(2,1)S(1)}, u32[]{:S(2)}, u32[]{:S(2)}) %collective-permute-start.5) | collective-permute-done | bytes 540704 | tf_op jit(solution)/shard_map/ppermute | solution.py:746
  43.0 1.6 collective-permute-start.6
  44.5 3.2 collective-permute-done.7
  49.9 5.2 %collective-permute-start.9 = (bf16[256,512]{1,0:T(8,128)(2,1)S(1)}, bf16[256,512]{1,0:T(8,128)(2,1)S(1)}, u32[]{:S(2)}, u32[]{:S(2)}) collective-permute-start(bf16[256,512]{1,0:T(8,128)(2,1)S(1)} %constant_dynamic-update-slice_fusion.10), channel_id=1, source_target_pairs={{0,8},{4,12},{8,0},{12,4},{16,24},{20,28},{24,16},{28,20},{1,9},{5... | collective-permute-start | bytes 786440 | tf_op jit(solution)/shard_map/ppermute | solution.py:743
  56.1 1.4 collective-permute-start.11
  57.5 10.6 %collective-permute-done.8.refs_6_.refs_10_.refs_11_.refs_15_.refs_12_ = bf16[8,512,128]{2,1,0:T(8,128)(2,1)} collective-permute-done((bf16[8,512,128]{2,1,0:T(8,128)(2,1)}, bf16[8,512,128]{2,1,0:T(8,128)(2,1)}, u32[]{:S(2)}, u32[]{:S(2)}) %collective-permute-start.8) | collective-permute-done | bytes 1048608 | tf_op jit(solution)/shard_map/ppermute | solution.py:746
  69.4 2.6 vectors.1
  72.0 2.8 collective-permute-done.10
  76.3 1.6 collective-permute-start.13
  77.9 16.3 %attn_forward.2 = (bf16[2,584,1024]{2,1,0:T(8,128)(2,1)}, bf16[2,584,512]{2,1,0:T(8,128)(2,1)}, bf16[2,584,512]{2,1,0:T(8,128)(2,1)}, bf16[2,584,512]{2,1,0:T(8,...) custom-call(f32[6,1024]{1,0:T(8,128)} %get-tuple-element.197.refs_0_.refs_1_.refs_2_, ...), custom_call_target="tpu_custom_call" | custom-call | flops 18400000000 | tf_op jit(solution)/shard_map/attn_forward/pallas_call | solution.py:77
  96.0 3.6 collective-permute-start.18
  100.7 1.4 collective-permute-start.20
  104.1 16.0 %attn_forward.3 = (bf16[2,584,1024]{2,1,0:T(8,128)(2,1)}, bf16[2,584,512]{2,1,0:T(8,128)(2,1)}, bf16[2,584,512]{2,1,0:T(8,128)(2,1)}, bf16[2,584,512]{2,1,0:T(8,...) custom-call(f32[6,1024]{1,0:T(8,128)} %get-tuple-element.197.refs_0_, ...), custom_call_target="tpu_custom_call", output_to_operand_aliasing={{0}: (3, {}), {1}: (4, {}), {2}: (5, {}), {3}: (6, {}), {4}... | custom-call | flops 18400000000 | tf_op jit(solution)/shard_map/attn_forward/pallas_call | solution.py:77
  120.1 3.9 %collective-permute-done.16 = bf16[8,128,512]{2,1,0:T(8,128)(2,1)} collective-permute-done((bf16[8,128,512]{2,1,0:T(8,128)(2,1)}, bf16[8,128,512]{2,1,0:T(8,128)(2,1)}, u32[]{:S(2)}, u32[]{:S(2)}) %collective-permute-start.16) | collective-permute-done | bytes 1048608 | tf_op jit(solution)/shard_map/ppermute | solution.py:754
  124.0 1.8 broadcast_multiply_fusion
  128.5 1.8 collective-permute-start.21
  130.9 10.3 %mlp_up.2 = (f32[2,584,1024]{2,1,0:T(8,128)}, bf16[2,584,1024]{2,1,0:T(8,128)(2,1)}, bf16[2,584,2048]{2,1,0:T(8,128)(2,1)}, bf16[2,584,2048]{2,1,0:T(8,128)(2,1)}) custom-call(f32[2]{0:T(128)} %get-tuple-element.371.refs_0_.refs_1_, f32[6,1024]{1,0:T(8,128)} %get-tuple-element.197.refs_0_.refs_1_.refs_2_, f32[1,2048]{1,0:T(1,128)} %get-tuple-element.198.refs_2_, ...), custom_call_target="tpu_custom_call" | custom-call | flops 11500000256 | tf_op jit(solution)/shard_map/mlp_up/pallas_call | solution.py:77
  142.4 1.6 collective-permute-done.22
  146.6 10.5 %mlp_up.3 = (f32[2,584,1024]{2,1,0:T(8,128)}, bf16[2,584,1024]{2,1,0:T(8,128)(2,1)}, bf16[2,584,2048]{2,1,0:T(8,128)(2,1)}, bf16[2,584,2048]{2,1,0:T(8,128)(2,1)}) custom-call(f32[2]{0:T(128)} %get-tuple-element.371.refs_0_.refs_1_, ...), custom_call_target="tpu_custom_call", output_to_operand_aliasing={{0}: (6, {}), {1}: (7, {}), {2}: (8, {}), {3}: (9, {})} | custom-call | flops 11500000256 | tf_op jit(solution)/shard_map/mlp_up/pallas_call | solution.py:77
  157.1 10.7 %down_grad.1 = (bf16[8,512,128]{2,1,0:T(8,128)(2,1)}, bf16[8,512,128]{2,1,0:T(8,128)(2,1)}, bf16[8,512,128]{2,1,0:T(8,128)(2,1)}, bf16[8,512,128]{2,1,0:T(8,128)(2,1)}) custom-call(bf16[1168,2048]{1,0:T(8,128)(2,1)} %bitcast.152, bf16[1168,1024]{1,0:T(8,128)(2,1)} %bitcast.124), custom_call_target="tpu_custom_call" | custom-call | flops 12650000384 | tf_op jit(solution)/shard_map/down_grad/pallas_call | solution.py:77
  167.8 1.8 collective-permute-start.26
  169.6 1.5 collective-permute-start.25
  172.1 22.1 %mlp_back.1 = (bf16[1168,2048]{1,0:T(8,128)(2,1)}, f32[1,2048]{1,0:T(1,128)}, bf16[584,1024]{1,0:T(8,128)(2,1)}, bf16[584,1024]{1,0:T(8,128)(2,1)}, bf16[1168,1024]{1,0:T(8,128)(2,1)}) custom-call(bf16[1168,1024]{1,0:T(8,128)(2,1)} %bitcast.125, bf16[1168,2048]{1,0:T(8,128)(2,1)} %bitcast.153, bf16[1168,2048]{1,0:T(8,128)(2,1)} %bitcast.154, ...), custom_call_target="tpu_custom_call" | custom-call | flops 25300000768 | tf_op jit(solution)/shard_map/mlp_back/pallas_call | solution.py:77
  195.2 3.8 down_add.1
  199.9 10.3 %up_grad.1 = (bf16[8,640,128]{2,1,0:T(8,128)(2,1)}, bf16[8,640,128]{2,1,0:T(8,128)(2,1)}, bf16[8,640,128]{2,1,0:T(8,128)(2,1)}, bf16[8,640,128]{2,1,0:T(8,128)(2,1)}) custom-call(bf16[1168,1024]{1,0:T(8,128)(2,1)} %bitcast.157, bf16[1168,2048]{1,0:T(8,128)(2,1)} %get-tuple-element.267.refs_1_), custom_call_target="tpu_custom_call" | custom-call | flops 12650000384 | tf_op jit(solution)/shard_map/up_grad/pallas_call | solution.py:77
  210.3 11.5 %middle_back.1 = (f32[584,1024]{1,0:T(8,128)}, bf16[2,584,1024]{2,1,0:T(8,128)(2,1)}, bf16[2,584,512]{2,1,0:T(8,128)(2,1)}, f32[4,1024]{1,0:T(4,128)}) custom-call(s32[10]{0:T(128)} %stack.130.refs_0_, f32[2]{0:T(128)} %get-tuple-element.371.refs_0_.refs_1_, f32[6,1024]{1,0:T(8,128)} %get-tuple-element.197.refs_0_.refs_1_.refs_2_, ...), custom_call_target="tpu_custom_call" | custom-call | flops 13799999488 | tf_op jit(solution)/shard_map/middle_back/pallas_call | solution.py:77
  224.1 2.9 down_addz.1
  227.8 2.3 collective-permute-start.35
  231.5 4.9 %out_grad.1 = (bf16[8,640,128]{2,1,0:T(8,128)(2,1)}, bf16[8,640,128]{2,1,0:T(8,128)(2,1)}, bf16[8,640,128]{2,1,0:T(8,128)(2,1)}, bf16[8,640,128]{2,1,0:T(8,128)(2,1)}) custom-call(bf16[1168,512]{1,0:T(8,128)(2,1)} %bitcast.164, bf16[1168,1024]{1,0:T(8,128)(2,1)} %bitcast.155, ...), custom_call_target="tpu_custom_call", output_to_operand_aliasing={{0}: (2, {}), {1}: (3, {}), {2}: (4, {}), {3}: (5, {})} | custom-call | flops 5750000128 | tf_op jit(solution)/shard_map/out_grad/pallas_call | solution.py:77
  236.4 1.6 collective-permute-start.32
  238.0 1.7 collective-permute-start.33
  239.7 21.5 %attn_backward.2 = (bf16[2,584,512]{2,1,0:T(8,128)(2,1)}, bf16[2,584,512]{2,1,0:T(8,128)(2,1)}, bf16[2,584,512]{2,1,0:T(8,128)(2,1)}, f32[5,2,128]{2,1,0:T(2,128)}) custom-call(bf16[2,584,512]{2,1,0:T(8,128)(2,1)} %get-tuple-element.289.refs_0_, bf16[2,584,512]{2,1,0:T(8,128)(2,1)} %get-tuple-element.290.refs_1_, ...), custom_call_target="tpu_custom_call" | custom-call | flops 20700000256 | tf_op jit(solution)/shard_map/attn_backward/pallas_call | solution.py:77
  262.1 2.5 down_sum.1
  264.7 2.4 collective-permute-done.32.refs_1_
  269.4 4.1 %up_out_add.1 = (bf16[4,640,128]{2,1,0:T(8,128)(2,1)}, bf16[4,640,128]{2,1,0:T(8,128)(2,1)}, bf16[4,640,128]{2,1,0:T(8,128)(2,1)}, bf16[4,640,128]{2,1,0:T(8,128)(2,1)}) custom-call(bf16[8,640,128]{2,1,0:T(8,128)(2,1)} %get-tuple-element.299.refs_0_, bf16[8,640,128]{2,1,0:T(8,128)(2,1)} %copy-done.11, bf16[8,640,128]{2,1,0:T(8,128)(2,1)} %get-tuple-element.301.refs_2_, ...), custom_call_target="tpu_custom_call" | custom-call | flops 3449999872 | tf_op jit(solution)/shard_map/up_out_add/pallas_call | solution.py:77
  273.5 1.8 collective-permute-start.37
  276.0 13.7 %attn_backward.3 = (bf16[2,584,512]{2,1,0:T(8,128)(2,1)}, bf16[2,584,512]{2,1,0:T(8,128)(2,1)}, bf16[2,584,512]{2,1,0:T(8,128)(2,1)}, f32[3,2,128]{2,1,0:T(2,128)}) custom-call(bf16[2,584,512]{2,1,0:T(8,128)(2,1)} %get-tuple-element.289.refs_0_, ...), custom_call_target="tpu_custom_call", output_to_operand_aliasing={{0}: (4, {}), {1}: (5, {}), {2}: (6, {})} | custom-call | flops 20700000256 | tf_op jit(solution)/shard_map/attn_backward/pallas_call | solution.py:77
  292.5 3.4 up_out_half.2
  295.9 8.8 %qkv_grad.1 = (bf16[8,384,128]{2,1,0:T(8,128)(2,1)}, bf16[8,384,128]{2,1,0:T(8,128)(2,1)}, bf16[8,384,128]{2,1,0:T(8,128)(2,1)}, bf16[8,384,128]{2,1,0:T(8,128)(2,1)}) custom-call(bf16[1168,1024]{1,0:T(8,128)(2,1)} %bitcast.156, bf16[1168,512]{1,0:T(8,128)(2,1)} %bitcast.158, bf16[1168,512]{1,0:T(8,128)(2,1)} %bitcast.160, bf16[1168,512]{1,0:T(8,128)(2,1)} %bitcast.162), custom_call_target="tpu_custom_call" | custom-call | flops 10350000128 | tf_op jit(solution)/shard_map/qkv_grad/pallas_call | solution.py:77
  304.7 1.4 collective-permute-start.39
  307.2 8.5 %grad_one.1 = (bf16[584,1024]{1,0:T(8,128)(2,1)}, bf16[584,1024]{1,0:T(8,128)(2,1)}) custom-call(bf16[1168,512]{1,0:T(8,128)(2,1)} %bitcast.159, bf16[1168,512]{1,0:T(8,128)(2,1)} %bitcast.161, bf16[1168,512]{1,0:T(8,128)(2,1)} %bitcast.163, bf16[8,528,128]{2,1,0:T(8,128)(2,1)} %copy-done.6, bf16[8,528,128]{2,1,0:T(8,128)(2,1)} %copy-done.16, ...), custom_call_target="tpu_custom_call" | custom-call | flops 2300000000 | tf_op jit(solution)/shard_map/grad_one/pallas_call | solution.py:77
  316.3 4.5 %collective-permute-done.41.refs_1_ = bf16[2,1280,128]{2,1,0:T(8,128)(2,1)} collective-permute-done((bf16[2,1280,128]{2,1,0:T(8,128)(2,1)}, bf16[2,1280,128]{2,1,0:T(8,128)(2,1)}, u32[]{:S(2)}, u32[]{:S(2)}) %collective-permute-start.41) | collective-permute-done | bytes 655392 | tf_op jit(solution)/shard_map/ppermute | solution.py:743
  320.8 2.6 up_out_half.3
  325.9 3.2 qkv_add.1
  329.1 1.7 collective-permute-start.42
  331.8 6.0 %collective-permute-done.44.refs_1_ = bf16[1,1280,128]{2,1,0:T(8,128)(2,1)} collective-permute-done((bf16[1,1280,128]{2,1,0:T(8,128)(2,1)}, bf16[1,1280,128]{2,1,0:T(8,128)(2,1)}, u32[]{:S(2)}, u32[]{:S(2)}) %collective-permute-start.44) | collective-permute-done | bytes 327712 | tf_op jit(solution)/shard_map/ppermute | solution.py:743
  339.2 8.6 %finish_tokens.1 = (bf16[584,1024]{1,0:T(8,128)(2,1)}, f32[2,1024]{1,0:T(2,128)}, f32[4,16,128]{2,1,0:T(8,128)}, f32[4,16,128]{2,1,0:T(8,128)}, f32[4,16,128]{2,1,0:T(8,128)}, /*index=5*/f32[4,16,128]{2,1,0:T(8,128)}) custom-call(s32[10]{0:T(128)} %stack.130.refs_0_, f32[6,1024]{1,0:T(8,128)} %get-tuple-element.197.refs_0_.refs_1_.refs_2_, ...), custom_call_target="tpu_custom_call" | custom-call | flops 10350000128 | tf_op jit(solution)/shard_map/finish_tokens/pallas_call | solution.py:77
  347.9 1.7 collective-permute-start.47
  351.4 2.4 up_out_sum.1
  353.9 1.9 collective-permute-done.49.refs_7_
  356.4 2.7 qkv_addz.1
  359.3 3.0 collective-permute-start.51
  362.3 1.4 collective-permute-start.52
  363.7 5.1 %finish_layer.1 = bf16[584,1024]{1,0:T(8,128)(2,1)} custom-call(s32[10]{0:T(128)} %stack.130.refs_0_, f32[2]{0:T(128)} %get-tuple-element.371.refs_0_.refs_1_, f32[6,1024]{1,0:T(8,128)} %get-tuple-element.197.refs_0_.refs_1_.refs_2_, f32[2,584,1024]{2,1,0:T(8,128)} %get-tuple-element.230.refs_3_, bf16[2,584,1024]{2,1,0:T(8,128)(2,1)} %bitcast.150, ...), custom_call_target="tpu_custom_call" | custom-call | flops 34500001792 | tf_op jit(solution)/shard_map/finish_layer/pallas_call | solution.py:77
  368.7 7.2 %collective-permute-done.51.refs_2_ = bf16[784,128]{1,0:T(8,128)(2,1)S(1)} collective-permute-done((bf16[784,128]{1,0:T(8,128)(2,1)}, bf16[784,128]{1,0:T(8,128)(2,1)S(1)}, u32[]{:S(2)}, u32[]{:S(2)}) %collective-permute-start.51) | collective-permute-done | bytes 200736 | tf_op jit(solution)/shard_map/ppermute | solution.py:743
  377.4 2.5 qkv_sum.1
  (225 shorter events, 54.3 us)
Async XLA Ops:
  0.6 10.8 %collective-permute-start.3 = (bf16[584,1024]{1,0:T(8,128)(2,1)}, bf16[584,1024]{1,0:T(8,128)(2,1)S(1)}, u32[]{:S(2)}, u32[]{:S(2)}) collective-permute-start(bf16[584,1024]{1,0:T(8,128)(2,1)} %refs_1_.1), channel_id=1, source_target_pairs={{0,1},{1,0},{2,3},{3,2},{4,5},{5,4},{6,7},{7,6},{8,9},{9,8},{10,11... | collective-permute-start | bytes 3588104 | tf_op jit(solution)/shard_map/ppermute | solution.py:758
  1.2 10.3 %collective-permute-start.4 = (bf16[584,1024]{1,0:T(8,128)(2,1)}, bf16[584,1024]{1,0:T(8,128)(2,1)}, u32[]{:S(2)}, u32[]{:S(2)}) collective-permute-start(bf16[584,1024]{1,0:T(8,128)(2,1)} %refs_2_.1), channel_id=1, source_target_pairs={{0,1},{1,0},{2,3},{3,2},{4,5},{5,4},{6,7},{7,6},{8,9},{9,8},{10,11... | collective-permute-start | bytes 3588104 | tf_op jit(solution)/shard_map/ppermute | solution.py:758
  5.1 14.8 %collective-permute-start = (bf16[1040,128]{1,0:T(8,128)(2,1)S(1)}, bf16[1040,128]{1,0:T(8,128)(2,1)S(1)}, u32[]{:S(2)}, u32[]{:S(2)}) collective-permute-start(bf16[1040,128]{1,0:T(8,128)(2,1)S(1)} %concatenate.71), channel_id=1, source_target_pairs={{0,8},{4,12},{8,0},{12,4},{16,24},{20,28},{24,16},{28,20},{1,9},{5... | collective-permute-start | bytes 798728 | tf_op jit(solution)/shard_map/ppermute | solution.py:743
  8.2 21.6 %collective-permute-start.1 = (bf16[1040,128]{1,0:T(8,128)(2,1)S(1)}, bf16[1040,128]{1,0:T(8,128)(2,1)S(1)}, u32[]{:S(2)}, u32[]{:S(2)}) collective-permute-start(bf16[1040,128]{1,0:T(8,128)(2,1)S(1)} %concatenate.71), channel_id=1, source_target_pairs={{0,16},{4,20},{8,24},{12,28},{16,0},{20,4},{24,8},{28,12},{1,17},{... | collective-permute-start | bytes 798728 | tf_op jit(solution)/shard_map/ppermute | solution.py:743
  10.8 19.0 %collective-permute-start.2 = (bf16[1040,128]{1,0:T(8,128)(2,1)S(1)}, bf16[1040,128]{1,0:T(8,128)(2,1)S(1)}, u32[]{:S(2)}, u32[]{:S(2)}) collective-permute-start(bf16[1040,128]{1,0:T(8,128)(2,1)S(1)} %concatenate.71), channel_id=1, source_target_pairs={{0,24},{4,28},{8,16},{12,20},{16,8},{20,12},{24,0},{28,4},{1,25},{... | collective-permute-start | bytes 798728 | tf_op jit(solution)/shard_map/ppermute | solution.py:743
  30.7 12.2 %collective-permute-start.5 = (bf16[4,528,128]{2,1,0:T(8,128)(2,1)S(1)}, bf16[4,528,128]{2,1,0:T(8,128)(2,1)S(1)}, u32[]{:S(2)}, u32[]{:S(2)}) collective-permute-start(bf16[4,528,128]{2,1,0:T(8,128)(2,1)S(1)} %pad_maximum_fusion), channel_id=1, source_target_pairs={{0,4},{4,0},{8,12},{12,8},{16,20},{20,16},{24,28},{28,24},{1,5},{5... | collective-permute-start | bytes 1622024 | tf_op jit(solution)/shard_map/ppermute | solution.py:746
  33.7 14.1 %collective-permute-start.7 = (bf16[4,512,128]{2,1,0:T(8,128)(2,1)S(1)}, bf16[4,512,128]{2,1,0:T(8,128)(2,1)S(1)}, u32[]{:S(2)}, u32[]{:S(2)}) collective-permute-start(bf16[4,512,128]{2,1,0:T(8,128)(2,1)S(1)} %pad_maximum_fusion.1), channel_id=1, source_target_pairs={{0,2},{2,0},{1,3},{3,1},{4,6},{6,4},{5,7},{7,5},{8,10},{10,8},{9,1... | collective-permute-start | bytes 1572872 | tf_op jit(solution)/shard_map/ppermute | solution.py:754
  35.9 13.3 %copy-start.9 = (s32[4]{0:T(128)S(1)}, s32[4]{0:T(128)}, u32[]{:S(2)}) copy-start(s32[4]{0:T(128)} %param.13) | copy-start | bytes 52
  35.9 13.8 %copy-start.3 = (bf16[1024,128]{1,0:T(8,128)(2,1)S(1)}, bf16[1024,128]{1,0:T(8,128)(2,1)}, u32[]{:S(2)}) copy-start(bf16[1024,128]{1,0:T(8,128)(2,1)} %param.21) | copy-start | bytes 786436
  35.9 13.8 %copy-start.4 = (bf16[128,1024]{1,0:T(8,128)(2,1)S(1)}, bf16[128,1024]{1,0:T(8,128)(2,1)}, u32[]{:S(2)}) copy-start(bf16[128,1024]{1,0:T(8,128)(2,1)} %param.19) | copy-start | bytes 786436
  42.9 6.9 %copy-start.6 = (bf16[8,528,128]{2,1,0:T(8,128)(2,1)}, bf16[8,528,128]{2,1,0:T(8,128)(2,1)S(1)}, u32[]{:S(2)}) copy-start(bf16[8,528,128]{2,1,0:T(8,128)(2,1)S(1)} %constant_dynamic-update-slice_fusion.refs_1_.refs_3_.refs_7_.refs_8_.refs_12_.refs_9_) | copy-start | bytes 3244036
  43.0 25.4 %collective-permute-start.6 = (bf16[8,528,128]{2,1,0:T(8,128)(2,1)S(1)}, bf16[8,528,128]{2,1,0:T(8,128)(2,1)S(1)}, u32[]{:S(2)}, u32[]{:S(2)}) collective-permute-start(bf16[8,528,128]{2,1,0:T(8,128)(2,1)S(1)} %constant_dynamic-update-slice_fusion.refs_1_.refs_3_.refs_7_.refs_8_.refs_12_.refs_9_), channel_id=1, source_target_pairs={{0,2},{2,0},{1,3},{3,1},{4,6},{6,4},{5,7},{7,5},{8,10},{10,8},{9,1... | collective-permute-start | bytes 3244040 | tf_op jit(solution)/shard_map/ppermute | solution.py:754
  48.6 19.6 %collective-permute-start.8 = (bf16[8,512,128]{2,1,0:T(8,128)(2,1)}, bf16[8,512,128]{2,1,0:T(8,128)(2,1)}, u32[]{:S(2)}, u32[]{:S(2)}) collective-permute-start(bf16[8,512,128]{2,1,0:T(8,128)(2,1)} %constant_dynamic-update-slice_fusion.5.refs_5_.refs_9_.refs_10_.refs_14_.refs_11_), channel_id=1, source_target_pairs={{0,4},{4,0},{8,12},{12,8},{16,20},{20,16},{24,28},{28,24},{1,5},{5... | collective-permute-start | bytes 3145736 | tf_op jit(solution)/shard_map/ppermute | solution.py:746
  49.9 22.1 %collective-permute-start.9 = (bf16[256,512]{1,0:T(8,128)(2,1)S(1)}, bf16[256,512]{1,0:T(8,128)(2,1)S(1)}, u32[]{:S(2)}, u32[]{:S(2)}) collective-permute-start(bf16[256,512]{1,0:T(8,128)(2,1)S(1)} %constant_dynamic-update-slice_fusion.10), channel_id=1, source_target_pairs={{0,8},{4,12},{8,0},{12,4},{16,24},{20,28},{24,16},{28,20},{1,9},{5... | collective-permute-start | bytes 786440 | tf_op jit(solution)/shard_map/ppermute | solution.py:743
  55.0 19.7 %collective-permute-start.10 = (bf16[256,512]{1,0:T(8,128)(2,1)S(1)}, bf16[256,512]{1,0:T(8,128)(2,1)S(1)}, u32[]{:S(2)}, u32[]{:S(2)}) collective-permute-start(bf16[256,512]{1,0:T(8,128)(2,1)S(1)} %constant_dynamic-update-slice_fusion.10), channel_id=1, source_target_pairs={{0,16},{4,20},{8,24},{12,28},{16,0},{20,4},{24,8},{28,12},{1,17},{... | collective-permute-start | bytes 786440 | tf_op jit(solution)/shard_map/ppermute | solution.py:743
  56.1 18.7 %collective-permute-start.11 = (bf16[256,512]{1,0:T(8,128)(2,1)S(1)}, bf16[256,512]{1,0:T(8,128)(2,1)S(1)}, u32[]{:S(2)}, u32[]{:S(2)}) collective-permute-start(bf16[256,512]{1,0:T(8,128)(2,1)S(1)} %constant_dynamic-update-slice_fusion.10), channel_id=1, source_target_pairs={{0,24},{4,28},{8,16},{12,20},{16,8},{20,12},{24,0},{28,4},{1,25},{... | collective-permute-start | bytes 786440 | tf_op jit(solution)/shard_map/ppermute | solution.py:743
  75.0 19.2 %collective-permute-start.12 = (bf16[4,128,512]{2,1,0:T(8,128)(2,1)S(1)}, bf16[4,128,512]{2,1,0:T(8,128)(2,1)S(1)}, u32[]{:S(2)}, u32[]{:S(2)}) collective-permute-start(bf16[4,128,512]{2,1,0:T(8,128)(2,1)S(1)} %pad_maximum_fusion.2), channel_id=1, source_target_pairs={{0,4},{4,0},{8,12},{12,8},{16,20},{20,16},{24,28},{28,24},{1,5},{5... | collective-permute-start | bytes 1572872 | tf_op jit(solution)/shard_map/ppermute | solution.py:746
  76.3 17.9 %collective-permute-start.13 = (bf16[4,128,512]{2,1,0:T(8,128)(2,1)S(1)}, bf16[4,128,512]{2,1,0:T(8,128)(2,1)S(1)}, u32[]{:S(2)}, u32[]{:S(2)}) collective-permute-start(bf16[4,128,512]{2,1,0:T(8,128)(2,1)S(1)} %pad_maximum_fusion.3), channel_id=1, source_target_pairs={{0,2},{2,0},{1,3},{3,1},{4,6},{6,4},{5,7},{7,5},{8,10},{10,8},{9,1... | collective-permute-start | bytes 1572872 | tf_op jit(solution)/shard_map/ppermute | solution.py:754
  96.0 24.1 %copy-start.1 = (bf16[8,128,512]{2,1,0:T(8,128)(2,1)}, bf16[8,128,512]{2,1,0:T(8,128)(2,1)S(1)}, u32[]{:S(2)}) copy-start(bf16[8,128,512]{2,1,0:T(8,128)(2,1)S(1)} %constant_dynamic-update-slice_fusion.14) | copy-start | bytes 3145732
  96.0 30.3 %collective-permute-start.18 = (bf16[1024,128]{1,0:T(8,128)(2,1)S(1)}, bf16[1024,128]{1,0:T(8,128)(2,1)S(1)}, u32[]{:S(2)}, u32[]{:S(2)}) collective-permute-start(bf16[1024,128]{1,0:T(8,128)(2,1)S(1)} %constant_dynamic-update-slice_fusion.16), channel_id=1, source_target_pairs={{0,8},{4,12},{8,0},{12,4},{16,24},{20,28},{24,16},{28,20},{1,9},{5... | collective-permute-start | bytes 786440 | tf_op jit(solution)/shard_map/ppermute | solution.py:743
  99.6 26.8 %collective-permute-start.19 = (bf16[1024,128]{1,0:T(8,128)(2,1)S(1)}, bf16[1024,128]{1,0:T(8,128)(2,1)}, u32[]{:S(2)}, u32[]{:S(2)}) collective-permute-start(bf16[1024,128]{1,0:T(8,128)(2,1)S(1)} %constant_dynamic-update-slice_fusion.16), channel_id=1, source_target_pairs={{0,16},{4,20},{8,24},{12,28},{16,0},{20,4},{24,8},{28,12},{1,17},{... | collective-permute-start | bytes 786440 | tf_op jit(solution)/shard_map/ppermute | solution.py:743
  100.7 25.7 %collective-permute-start.20 = (bf16[1024,128]{1,0:T(8,128)(2,1)S(1)}, bf16[1024,128]{1,0:T(8,128)(2,1)}, u32[]{:S(2)}, u32[]{:S(2)}) collective-permute-start(bf16[1024,128]{1,0:T(8,128)(2,1)S(1)} %constant_dynamic-update-slice_fusion.16), channel_id=1, source_target_pairs={{0,24},{4,28},{8,16},{12,20},{16,8},{20,12},{24,0},{28,4},{1,25},{... | collective-permute-start | bytes 786440 | tf_op jit(solution)/shard_map/ppermute | solution.py:743
  102.1 22.0 %collective-permute-start.16 = (bf16[8,128,512]{2,1,0:T(8,128)(2,1)}, bf16[8,128,512]{2,1,0:T(8,128)(2,1)}, u32[]{:S(2)}, u32[]{:S(2)}) collective-permute-start(bf16[8,128,512]{2,1,0:T(8,128)(2,1)} %constant_dynamic-update-slice_fusion.12), channel_id=1, source_target_pairs={{0,2},{2,0},{1,3},{3,1},{4,6},{6,4},{5,7},{7,5},{8,10},{10,8},{9,1... | collective-permute-start | bytes 3145736 | tf_op jit(solution)/shard_map/ppermute | solution.py:754
  102.9 22.9 %collective-permute-start.17 = (bf16[8,128,512]{2,1,0:T(8,128)(2,1)S(1)}, bf16[8,128,512]{2,1,0:T(8,128)(2,1)}, u32[]{:S(2)}, u32[]{:S(2)}) collective-permute-start(bf16[8,128,512]{2,1,0:T(8,128)(2,1)S(1)} %constant_dynamic-update-slice_fusion.14), channel_id=1, source_target_pairs={{0,4},{4,0},{8,12},{12,8},{16,20},{20,16},{24,28},{28,24},{1,5},{5... | collective-permute-start | bytes 3145736 | tf_op jit(solution)/shard_map/ppermute | solution.py:746
  104.1 19.9 %copy-start = (bf16[2,584,1024]{2,1,0:T(8,128)(2,1)S(1)}, bf16[2,584,1024]{2,1,0:T(8,128)(2,1)}, u32[]{:S(2)}) copy-start(bf16[2,584,1024]{2,1,0:T(8,128)(2,1)} %get-tuple-element.231.refs_4_) | copy-start | bytes 7176196
  124.0 6.9 %collective-permute-start.15 = (bf16[584,1024]{1,0:T(8,128)(2,1)}, bf16[584,1024]{1,0:T(8,128)(2,1)}, u32[]{:S(2)}, u32[]{:S(2)}) collective-permute-start(bf16[584,1024]{1,0:T(8,128)(2,1)} %get-tuple-element.221.refs_4_), channel_id=1, source_target_pairs={{0,1},{1,0},{2,3},{3,2},{4,5},{5,4},{6,7},{7,6},{8,9},{9,8},{10,11... | collective-permute-start | bytes 3588104 | tf_op jit(solution)/shard_map/ppermute | solution.py:758
  125.8 20.8 %collective-permute-start.14 = (bf16[584,1024]{1,0:T(8,128)(2,1)}, bf16[584,1024]{1,0:T(8,128)(2,1)}, u32[]{:S(2)}, u32[]{:S(2)}) collective-permute-start(bf16[584,1024]{1,0:T(8,128)(2,1)} %get-tuple-element.220.refs_4_), channel_id=1, source_target_pairs={{0,1},{1,0},{2,3},{3,2},{4,5},{5,4},{6,7},{7,6},{8,9},{9,8},{10,11... | collective-permute-start | bytes 3588104 | tf_op jit(solution)/shard_map/ppermute | solution.py:758
  128.5 13.9 %collective-permute-start.21 = (bf16[4,512,128]{2,1,0:T(8,128)(2,1)S(1)}, bf16[4,512,128]{2,1,0:T(8,128)(2,1)S(1)}, u32[]{:S(2)}, u32[]{:S(2)}) collective-permute-start(bf16[4,512,128]{2,1,0:T(8,128)(2,1)S(1)} %pad_maximum_fusion.4), channel_id=1, source_target_pairs={{0,4},{4,0},{8,12},{12,8},{16,20},{20,16},{24,28},{28,24},{1,5},{5... | collective-permute-start | bytes 1572872 | tf_op jit(solution)/shard_map/ppermute | solution.py:746
  130.3 13.6 %collective-permute-start.22 = (bf16[4,512,128]{2,1,0:T(8,128)(2,1)S(1)}, bf16[4,512,128]{2,1,0:T(8,128)(2,1)S(1)}, u32[]{:S(2)}, u32[]{:S(2)}) collective-permute-start(bf16[4,512,128]{2,1,0:T(8,128)(2,1)S(1)} %pad_maximum_fusion.5), channel_id=1, source_target_pairs={{0,2},{2,0},{1,3},{3,1},{4,6},{6,4},{5,7},{7,5},{8,10},{10,8},{9,1... | collective-permute-start | bytes 1572872 | tf_op jit(solution)/shard_map/ppermute | solution.py:754
  144.1 13.0 %copy-start.2 = (bf16[8,512,128]{2,1,0:T(8,128)(2,1)}, bf16[8,512,128]{2,1,0:T(8,128)(2,1)S(1)}, u32[]{:S(2)}) copy-start(bf16[8,512,128]{2,1,0:T(8,128)(2,1)S(1)} %constant_dynamic-update-slice_fusion.18.refs_3_) | copy-start | bytes 3145732
  144.1 27.0 %collective-permute-start.23 = (bf16[8,512,128]{2,1,0:T(8,128)(2,1)S(1)}, bf16[8,512,128]{2,1,0:T(8,128)(2,1)S(1)}, u32[]{:S(2)}, u32[]{:S(2)}) collective-permute-start(bf16[8,512,128]{2,1,0:T(8,128)(2,1)S(1)} %constant_dynamic-update-slice_fusion.18.refs_3_), channel_id=1, source_target_pairs={{0,2},{2,0},{1,3},{3,1},{4,6},{6,4},{5,7},{7,5},{8,10},{10,8},{9,1... | collective-permute-start | bytes 3145736 | tf_op jit(solution)/shard_map/ppermute | solution.py:754
  146.3 25.0 %collective-permute-start.24 = (bf16[8,512,128]{2,1,0:T(8,128)(2,1)}, bf16[8,512,128]{2,1,0:T(8,128)(2,1)}, u32[]{:S(2)}, u32[]{:S(2)}) collective-permute-start(bf16[8,512,128]{2,1,0:T(8,128)(2,1)} %constant_dynamic-update-slice_fusion.20.refs_5_), channel_id=1, source_target_pairs={{0,4},{4,0},{8,12},{12,8},{16,20},{20,16},{24,28},{28,24},{1,5},{5... | collective-permute-start | bytes 3145736 | tf_op jit(solution)/shard_map/ppermute | solution.py:746
  167.8 26.3 %collective-permute-start.26 = (bf16[8,512,128]{2,1,0:T(8,128)(2,1)}, bf16[8,512,128]{2,1,0:T(8,128)(2,1)S(1)}, u32[]{:S(2)}, u32[]{:S(2)}) collective-permute-start(bf16[8,512,128]{2,1,0:T(8,128)(2,1)} %get-tuple-element.233), channel_id=1, source_target_pairs={{0,4},{4,0},{8,12},{12,8},{16,20},{20,16},{24,28},{28,24},{1,5},{5... | collective-permute-start | bytes 3145736 | tf_op jit(solution)/shard_map/ppermute | solution.py:746
  169.6 24.5 %collective-permute-start.25 = (bf16[8,512,128]{2,1,0:T(8,128)(2,1)}, bf16[8,512,128]{2,1,0:T(8,128)(2,1)}, u32[]{:S(2)}, u32[]{:S(2)}) collective-permute-start(bf16[8,512,128]{2,1,0:T(8,128)(2,1)} %get-tuple-element.252), channel_id=1, source_target_pairs={{0,2},{2,0},{1,3},{3,1},{4,6},{6,4},{5,7},{7,5},{8,10},{10,8},{9,1... | collective-permute-start | bytes 3145736 | tf_op jit(solution)/shard_map/ppermute | solution.py:754
  194.2 16.1 %collective-permute-start.29 = (bf16[584,1024]{1,0:T(8,128)(2,1)}, bf16[584,1024]{1,0:T(8,128)(2,1)}, u32[]{:S(2)}, u32[]{:S(2)}) collective-permute-start(bf16[584,1024]{1,0:T(8,128)(2,1)} %get-tuple-element.263.refs_5_), channel_id=1, source_target_pairs={{0,1},{1,0},{2,3},{3,2},{4,5},{5,4},{6,7},{7,6},{8,9},{9,8},{10,11... | collective-permute-start | bytes 3588104 | tf_op jit(solution)/shard_map/ppermute | solution.py:758
  194.3 5.6 %copy-start.10 = (bf16[1168,1024]{1,0:T(8,128)(2,1)S(1)}, bf16[1168,1024]{1,0:T(8,128)(2,1)}, u32[]{:S(2)}) copy-start(bf16[1168,1024]{1,0:T(8,128)(2,1)} %get-tuple-element.248) | copy-start | bytes 7176196
  194.3 16.0 %collective-permute-start.30 = (bf16[584,1024]{1,0:T(8,128)(2,1)}, bf16[584,1024]{1,0:T(8,128)(2,1)}, u32[]{:S(2)}, u32[]{:S(2)}) collective-permute-start(bf16[584,1024]{1,0:T(8,128)(2,1)} %get-tuple-element.264.refs_6_), channel_id=1, source_target_pairs={{0,1},{1,0},{2,3},{3,2},{4,5},{5,4},{6,7},{7,6},{8,9},{9,8},{10,11... | collective-permute-start | bytes 3588104 | tf_op jit(solution)/shard_map/ppermute | solution.py:758
  199.0 23.5 %collective-permute-start.27 = (bf16[4,512,128]{2,1,0:T(8,128)(2,1)}, bf16[4,512,128]{2,1,0:T(8,128)(2,1)S(1)}, u32[]{:S(2)}, u32[]{:S(2)}) collective-permute-start(bf16[4,512,128]{2,1,0:T(8,128)(2,1)} %get-tuple-element.260), channel_id=1, source_target_pairs={{0,4},{4,0},{8,12},{12,8},{16,20},{20,16},{24,28},{28,24},{1,5},{5... | collective-permute-start | bytes 1572872 | tf_op jit(solution)/shard_map/ppermute | solution.py:746
  199.4 23.1 %collective-permute-start.28 = (bf16[4,512,128]{2,1,0:T(8,128)(2,1)}, bf16[4,512,128]{2,1,0:T(8,128)(2,1)S(1)}, u32[]{:S(2)}, u32[]{:S(2)}) collective-permute-start(bf16[4,512,128]{2,1,0:T(8,128)(2,1)} %get-tuple-element.262), channel_id=1, source_target_pairs={{0,2},{2,0},{1,3},{3,1},{4,6},{6,4},{5,7},{7,5},{8,10},{10,8},{9,1... | collective-permute-start | bytes 1572872 | tf_op jit(solution)/shard_map/ppermute | solution.py:754
  199.9 31.6 %collective-permute-start.31 = (bf16[2,584,1024]{2,1,0:T(8,128)(2,1)S(1)}, bf16[2,584,1024]{2,1,0:T(8,128)(2,1)}, u32[]{:S(2)}, u32[]{:S(2)}) collective-permute-start(bf16[2,584,1024]{2,1,0:T(8,128)(2,1)S(1)} %bitcast.151), channel_id=1, source_target_pairs={{0,1},{1,0},{2,3},{3,2},{4,5},{5,4},{6,7},{7,6},{8,9},{9,8},{10,11... | collective-permute-start | bytes 7176200 | tf_op jit(solution)/shard_map/ppermute | solution.py:758
  227.0 34.2 %collective-permute-start.34 = (bf16[1024,128]{1,0:T(8,128)(2,1)}, bf16[1024,128]{1,0:T(8,128)(2,1)S(1)}, u32[]{:S(2)}, u32[]{:S(2)}) collective-permute-start(bf16[1024,128]{1,0:T(8,128)(2,1)} %get-tuple-element.277), channel_id=1, source_target_pairs={{0,8},{4,12},{8,0},{12,4},{16,24},{20,28},{24,16},{28,20},{1,9},{5... | collective-permute-start | bytes 786440 | tf_op jit(solution)/shard_map/ppermute | solution.py:743
  227.8 33.4 %collective-permute-start.35 = (bf16[1024,128]{1,0:T(8,128)(2,1)}, bf16[1024,128]{1,0:T(8,128)(2,1)S(1)}, u32[]{:S(2)}, u32[]{:S(2)}) collective-permute-start(bf16[1024,128]{1,0:T(8,128)(2,1)} %get-tuple-element.278), channel_id=1, source_target_pairs={{0,16},{4,20},{8,24},{12,28},{16,0},{20,4},{24,8},{28,12},{1,17},{... | collective-permute-start | bytes 786440 | tf_op jit(solution)/shard_map/ppermute | solution.py:743
  230.1 31.2 %collective-permute-start.36 = (bf16[1024,128]{1,0:T(8,128)(2,1)}, bf16[1024,128]{1,0:T(8,128)(2,1)S(1)}, u32[]{:S(2)}, u32[]{:S(2)}) collective-permute-start(bf16[1024,128]{1,0:T(8,128)(2,1)} %get-tuple-element.279), channel_id=1, source_target_pairs={{0,24},{4,28},{8,16},{12,20},{16,8},{20,12},{24,0},{28,4},{1,25},{... | collective-permute-start | bytes 786440 | tf_op jit(solution)/shard_map/ppermute | solution.py:743
  236.4 30.6 %collective-permute-start.32 = (bf16[8,640,128]{2,1,0:T(8,128)(2,1)}, bf16[8,640,128]{2,1,0:T(8,128)(2,1)S(1)}, u32[]{:S(2)}, u32[]{:S(2)}) collective-permute-start(bf16[8,640,128]{2,1,0:T(8,128)(2,1)} %get-tuple-element.286), channel_id=1, source_target_pairs={{0,2},{2,0},{1,3},{3,1},{4,6},{6,4},{5,7},{7,5},{8,10},{10,8},{9,1... | collective-permute-start | bytes 3932168 | tf_op jit(solution)/shard_map/ppermute | solution.py:754
  238.0 30.3 %collective-permute-start.33 = (bf16[8,640,128]{2,1,0:T(8,128)(2,1)}, bf16[8,640,128]{2,1,0:T(8,128)(2,1)S(1)}, u32[]{:S(2)}, u32[]{:S(2)}) collective-permute-start(bf16[8,640,128]{2,1,0:T(8,128)(2,1)} %get-tuple-element.288), channel_id=1, source_target_pairs={{0,4},{4,0},{8,12},{12,8},{16,20},{20,16},{24,28},{28,24},{1,5},{5... | collective-permute-start | bytes 3932168 | tf_op jit(solution)/shard_map/ppermute | solution.py:746
  273.5 17.2 %collective-permute-start.37 = (bf16[4,640,128]{2,1,0:T(8,128)(2,1)}, bf16[4,640,128]{2,1,0:T(8,128)(2,1)S(1)}, u32[]{:S(2)}, u32[]{:S(2)}) collective-permute-start(bf16[4,640,128]{2,1,0:T(8,128)(2,1)} %get-tuple-element.304), channel_id=1, source_target_pairs={{0,4},{4,0},{8,12},{12,8},{16,20},{20,16},{24,28},{28,24},{1,5},{5... | collective-permute-start | bytes 1966088 | tf_op jit(solution)/shard_map/ppermute | solution.py:746
  275.3 15.5 %collective-permute-start.38 = (bf16[4,640,128]{2,1,0:T(8,128)(2,1)}, bf16[4,640,128]{2,1,0:T(8,128)(2,1)S(1)}, u32[]{:S(2)}, u32[]{:S(2)}) collective-permute-start(bf16[4,640,128]{2,1,0:T(8,128)(2,1)} %get-tuple-element.306), channel_id=1, source_target_pairs={{0,2},{2,0},{1,3},{3,1},{4,6},{6,4},{5,7},{7,5},{8,10},{10,8},{9,1... | collective-permute-start | bytes 1966088 | tf_op jit(solution)/shard_map/ppermute | solution.py:754
  276.0 13.7 %copy-start.7 = (f32[5,2,128]{2,1,0:T(2,128)S(1)}, f32[5,2,128]{2,1,0:T(2,128)}, u32[]{:S(2)}) copy-start(f32[5,2,128]{2,1,0:T(2,128)} %get-tuple-element.294) | copy-start | bytes 15364
  295.8 10.6 %copy-start.8 = (f32[16]{0:T(128)S(1)}, f32[16]{0:T(128)}, u32[]{:S(2)}) copy-start(f32[16]{0:T(128)} %pad.15.clone) | copy-start | bytes 196
  304.7 20.0 %collective-permute-start.39 = (bf16[8,384,128]{2,1,0:T(8,128)(2,1)}, bf16[8,384,128]{2,1,0:T(8,128)(2,1)S(1)}, u32[]{:S(2)}, u32[]{:S(2)}) collective-permute-start(bf16[8,384,128]{2,1,0:T(8,128)(2,1)} %get-tuple-element.322), channel_id=1, source_target_pairs={{0,2},{2,0},{1,3},{3,1},{4,6},{6,4},{5,7},{7,5},{8,10},{10,8},{9,1... | collective-permute-start | bytes 2359304 | tf_op jit(solution)/shard_map/ppermute | solution.py:754
  306.1 18.6 %collective-permute-start.40 = (bf16[8,384,128]{2,1,0:T(8,128)(2,1)}, bf16[8,384,128]{2,1,0:T(8,128)(2,1)S(1)}, u32[]{:S(2)}, u32[]{:S(2)}) collective-permute-start(bf16[8,384,128]{2,1,0:T(8,128)(2,1)} %get-tuple-element.324), channel_id=1, source_target_pairs={{0,4},{4,0},{8,12},{12,8},{16,20},{20,16},{24,28},{28,24},{1,5},{5... | collective-permute-start | bytes 2359304 | tf_op jit(solution)/shard_map/ppermute | solution.py:746
  306.4 14.3 %collective-permute-start.41 = (bf16[2,1280,128]{2,1,0:T(8,128)(2,1)}, bf16[2,1280,128]{2,1,0:T(8,128)(2,1)}, u32[]{:S(2)}, u32[]{:S(2)}) collective-permute-start(bf16[2,1280,128]{2,1,0:T(8,128)(2,1)} %get-tuple-element.325), channel_id=1, source_target_pairs={{0,8},{4,12},{8,0},{12,4},{16,24},{20,28},{24,16},{28,20},{1,9},{5... | collective-permute-start | bytes 1966088 | tf_op jit(solution)/shard_map/ppermute | solution.py:743
  315.7 22.1 %collective-permute-start.45 = (bf16[584,1024]{1,0:T(8,128)(2,1)}, bf16[584,1024]{1,0:T(8,128)(2,1)S(1)}, u32[]{:S(2)}, u32[]{:S(2)}) collective-permute-start(bf16[584,1024]{1,0:T(8,128)(2,1)} %get-tuple-element.329.refs_4_), channel_id=1, source_target_pairs={{0,1},{1,0},{2,3},{3,2},{4,5},{5,4},{6,7},{7,6},{8,9},{9,8},{10,11... | collective-permute-start | bytes 3588104 | tf_op jit(solution)/shard_map/ppermute | solution.py:758
  315.8 22.0 %collective-permute-start.46 = (bf16[584,1024]{1,0:T(8,128)(2,1)}, bf16[584,1024]{1,0:T(8,128)(2,1)S(1)}, u32[]{:S(2)}, u32[]{:S(2)}) collective-permute-start(bf16[584,1024]{1,0:T(8,128)(2,1)} %get-tuple-element.350.refs_5_), channel_id=1, source_target_pairs={{0,1},{1,0},{2,3},{3,2},{4,5},{5,4},{6,7},{7,6},{8,9},{9,8},{10,11... | collective-permute-start | bytes 3588104 | tf_op jit(solution)/shard_map/ppermute | solution.py:758
  323.4 14.4 %collective-permute-start.44 = (bf16[1,1280,128]{2,1,0:T(8,128)(2,1)}, bf16[1,1280,128]{2,1,0:T(8,128)(2,1)}, u32[]{:S(2)}, u32[]{:S(2)}) collective-permute-start(bf16[1,1280,128]{2,1,0:T(8,128)(2,1)} %get-tuple-element.341), channel_id=1, source_target_pairs={{0,16},{4,20},{8,24},{12,28},{16,0},{20,4},{24,8},{28,12},{1,17},{... | collective-permute-start | bytes 983048 | tf_op jit(solution)/shard_map/ppermute | solution.py:743
  329.1 24.7 %collective-permute-start.42 = (bf16[4,384,128]{2,1,0:T(8,128)(2,1)}, bf16[4,384,128]{2,1,0:T(8,128)(2,1)S(1)}, u32[]{:S(2)}, u32[]{:S(2)}) collective-permute-start(bf16[4,384,128]{2,1,0:T(8,128)(2,1)} %get-tuple-element.338), channel_id=1, source_target_pairs={{0,4},{4,0},{8,12},{12,8},{16,20},{20,16},{24,28},{28,24},{1,5},{5... | collective-permute-start | bytes 1179656 | tf_op jit(solution)/shard_map/ppermute | solution.py:746
  330.9 23.0 %collective-permute-start.43 = (bf16[4,384,128]{2,1,0:T(8,128)(2,1)}, bf16[4,384,128]{2,1,0:T(8,128)(2,1)S(1)}, u32[]{:S(2)}, u32[]{:S(2)}) collective-permute-start(bf16[4,384,128]{2,1,0:T(8,128)(2,1)} %get-tuple-element.340), channel_id=1, source_target_pairs={{0,2},{2,0},{1,3},{3,1},{4,6},{6,4},{5,7},{7,5},{8,10},{10,8},{9,1... | collective-permute-start | bytes 1179656 | tf_op jit(solution)/shard_map/ppermute | solution.py:754
  347.9 6.0 %collective-permute-start.47 = (f32[4,16,128]{2,1,0:T(8,128)}, f32[4,16,128]{2,1,0:T(8,128)S(1)}, u32[]{:S(2)}, u32[]{:S(2)}) collective-permute-start(f32[4,16,128]{2,1,0:T(8,128)} %get-tuple-element.354), channel_id=1, source_target_pairs={{0,4},{2,6},{4,0},{6,2},{8,12},{10,14},{12,8},{14,10},{16,20},{18,... | collective-permute-start | bytes 98312 | tf_op jit(solution)/shard_map/ppermute | solution.py:751
  349.5 4.3 %collective-permute-start.48 = (f32[4,16,128]{2,1,0:T(8,128)}, f32[4,16,128]{2,1,0:T(8,128)S(1)}, u32[]{:S(2)}, u32[]{:S(2)}) collective-permute-start(f32[4,16,128]{2,1,0:T(8,128)} %get-tuple-element.355), channel_id=1, source_target_pairs={{0,2},{2,0},{4,6},{6,4},{8,10},{10,8},{12,14},{14,12},{16,18},{18,... | collective-permute-start | bytes 98312 | tf_op jit(solution)/shard_map/ppermute | solution.py:751
  350.8 5.0 %collective-permute-start.49 = (f32[4,16,128]{2,1,0:T(8,128)}, f32[4,16,128]{2,1,0:T(8,128)S(1)}, u32[]{:S(2)}, u32[]{:S(2)}) collective-permute-start(f32[4,16,128]{2,1,0:T(8,128)} %get-tuple-element.356), channel_id=1, source_target_pairs={{0,6},{2,4},{4,2},{6,0},{8,14},{10,12},{12,10},{14,8},{16,22},{18,... | collective-permute-start | bytes 98312 | tf_op jit(solution)/shard_map/ppermute | solution.py:751
  359.2 9.5 %collective-permute-start.50 = (bf16[784,128]{1,0:T(8,128)(2,1)}, bf16[784,128]{1,0:T(8,128)(2,1)S(1)}, u32[]{:S(2)}, u32[]{:S(2)}) collective-permute-start(bf16[784,128]{1,0:T(8,128)(2,1)} %get-tuple-element.358), channel_id=1, source_target_pairs={{0,8},{4,12},{8,0},{12,4},{16,24},{20,28},{24,16},{28,20},{1,9},{5... | collective-permute-start | bytes 602120 | tf_op jit(solution)/shard_map/ppermute | solution.py:743
  359.3 16.7 %collective-permute-start.51 = (bf16[784,128]{1,0:T(8,128)(2,1)}, bf16[784,128]{1,0:T(8,128)(2,1)S(1)}, u32[]{:S(2)}, u32[]{:S(2)}) collective-permute-start(bf16[784,128]{1,0:T(8,128)(2,1)} %get-tuple-element.359), channel_id=1, source_target_pairs={{0,16},{4,20},{8,24},{12,28},{16,0},{20,4},{24,8},{28,12},{1,17},{... | collective-permute-start | bytes 602120 | tf_op jit(solution)/shard_map/ppermute | solution.py:743
  362.3 13.7 %collective-permute-start.52 = (bf16[784,128]{1,0:T(8,128)(2,1)}, bf16[784,128]{1,0:T(8,128)(2,1)S(1)}, u32[]{:S(2)}, u32[]{:S(2)}) collective-permute-start(bf16[784,128]{1,0:T(8,128)(2,1)} %get-tuple-element.360), channel_id=1, source_target_pairs={{0,24},{4,28},{8,16},{12,20},{16,8},{20,12},{24,0},{28,4},{1,25},{... | collective-permute-start | bytes 602120 | tf_op jit(solution)/shard_map/ppermute | solution.py:743
  368.7 7.3 %copy-start.30 = (bf16[784,128]{1,0:T(8,128)(2,1)}, bf16[784,128]{1,0:T(8,128)(2,1)S(1)}, u32[]{:S(2)}) copy-start(bf16[784,128]{1,0:T(8,128)(2,1)S(1)} %collective-permute-done.50.refs_1_) | copy-start | bytes 602116
  (25 other events, 32.0 us)

commit v4 on v3

--- a/solution.py
+++ b/solution.py
@@ -22,13 +22,16 @@
     "down_grad": 11,
     "mlp_back": 22,
     "up_grad": 11,
-    "middle_back": 12,
-    "out_grad": 5,
+    "middle_back": 0,
+    "out_grad": 8,
     "attn_backward": 18,
-    "qkv_grad": 9,
-    "grad_one": 2,
+    "qkv_grad": 7,
+    "qkv_keep": 0,
+    "up_half": 0,
+    "grad_one": 0,
     "qkv_add": 30,
-    "finish_layer": 30,
+    "finish_layer": 0,
+    "up_sum": 0,
     "finish_tokens": 9,
 }
 NT = (((1,), (1,)), ((), ()))
@@ -57,7 +60,7 @@
             copy.wait()
 
 
-def call(body, ins, outs, scratch, name, flops, aliases=None, smem=(), sems=48, vmem_ins=(), hidden=False):
+def call(body, ins, outs, scratch, name, flops, aliases=None, smem=(), sems=48, vmem_ins=(), vmem=VMEM_LIMIT):
     n_smem, n_vmem, n_in, n_out = len(smem), len(vmem_ins), len(ins), len(outs)
     moved = sum(a.size * a.dtype.itemsize for a in ins) + sum(
         o.size * o.dtype.itemsize for o in outs
@@ -71,7 +74,7 @@
         rest = refs[first + n_in + n_out :]
         body(small, in_refs, out_refs, rest[:-1], Loads(rest[-1]))
 
-    flops = COST.get(name, 3) * COST_SCALE * 1.15e9
+    flops = max(COST.get(name, 3), 0.02) * COST_SCALE * 1.15e9
     moved = 0
     any_spec = pl.BlockSpec(memory_space=pl.ANY)
     return pl.pallas_call(
@@ -83,8 +86,8 @@
         out_specs=[any_spec] * n_out,
         scratch_shapes=list(scratch) + [pltpu.SemaphoreType.DMA((sems,))],
         input_output_aliases={n_smem + n_vmem + i: o for i, o in (aliases or {}).items()},
-        compiler_params=pltpu.CompilerParams(vmem_limit_bytes=VMEM_LIMIT),
-        cost_estimate=pl.CostEstimate(flops=int(flops), bytes_accessed=int(moved), transcendentals=0),
+        compiler_params=pltpu.CompilerParams(vmem_limit_bytes=vmem),
+        cost_estimate=pl.CostEstimate(flops=int(flops), bytes_accessed=int(flops // 1000), transcendentals=0),
         name=name,
     )(*smem, *vmem_ins, *ins)
 
@@ -307,7 +310,7 @@
                 loads.wait(g_w[block])
             cols = slice(block * step, (block + 1) * step)
             pre = dot(second, w_s[:, cols], NN) + bu_ref[0:1, cols]
-            gate = 1.0 / (1.0 + jnp.exp(-1.702 * pre))
+            gate = 0.5 * jnp.tanh(0.851 * pre) + 0.5
             act_s[:, cols] = (pre * gate).astype(BF)
             dact_s[:, cols] = (gate + 1.702 * pre * gate * (1.0 - gate)).astype(BF)
             done.append(
@@ -349,9 +352,19 @@
     )
 
 
-def weight_grad(lefts, rights, tasks, out_shapes, name, lo, hi, prev=None):
+def column_loads(src, dst, start):
+    if len(src.shape) == 2:
+        return [(src, dst)]
+    n, _, width = src.shape
+    return [
+        (src.at[i], dst.at[:, (start + i) * width : (start + i + 1) * width]) for i in range(n)
+    ]
+
+
+def weight_grad(lefts, rights, tasks, out_shapes, name, lo, hi, prev=None, fill=False):
     rows = lefts[0].shape[0]
     arrays = list(lefts) + list(rights)
+    wide = [a.shape[-1] * (a.shape[0] if len(a.shape) == 3 else 1) for a in arrays]
     n_left, n_in = len(lefts), len(arrays)
     prev = list(prev or [])
     last = {}
@@ -366,7 +379,9 @@
             for i in (l_index, n_left + r_index):
                 if i not in order:
                     order.append(i)
-        groups = {i: loads.start([(ins[i], in_s[i])]) for i in order}
+        groups = {i: loads.start(column_loads(ins[i], in_s[i], 0)) for i in order}
+        for ref in out_s if fill else ():
+            ref[...] = jnp.zeros_like(ref)
         ready, done = set(), []
         for n, (l_index, l_cols, r_index, r_cols, stores) in enumerate(tasks):
             for i in (l_index, n_left + r_index):
@@ -389,7 +404,7 @@
         body,
         arrays + prev,
         [sds(s, BF) for s in out_shapes],
-        [pltpu.VMEM(a.shape, BF) for a in arrays]
+        [pltpu.VMEM((rows, w), BF) for w in wide]
         + [pltpu.VMEM((s[0], hi - lo, s[2]), BF) for s in out_shapes],
         name,
         flops,
@@ -433,10 +448,10 @@
         two = dot(low_s[...], wu_s[...], NT)
         for a in range(2):
             two_s[a] = two[a * seq : (a + 1) * seq].astype(BF)
-            done.append(loads.start([(two_s.at[a], outs[2 + a])]))
+            done.append(loads.start([(two_s.at[a], outs[2].at[a])]))
         loads.wait(g_a)
         mlp_s[...] = dot(a_s[...], wd_s[...], NN).astype(BF)
-        done.append(loads.start([(mlp_s, outs[4])]))
+        done.append(loads.start([(mlp_s, outs[3])]))
         for group in done:
             loads.wait(group)
 
@@ -444,8 +459,7 @@
         body,
         [grad, act, dact] + down_arrays + up_arrays,
         [sds((rows, hid), BF), sds((1, hid), F32)]
-        + [sds((seq, width), BF)] * 2
-        + [sds((rows, width), BF)],
+        + [sds((2, seq, width), BF), sds((rows, width), BF)],
         [
             pltpu.VMEM(down_scratch, BF),
             pltpu.VMEM(up_scratch, BF),
@@ -463,18 +477,24 @@
     )
 
 
-def input_grad(lefts, weight, width):
+def input_grad(stacks, starts, weight, width):
     arrays, plan, shape = weight
-    rows, ext = lefts[0].shape
-    seq = rows // 2
-    n = len(lefts)
+    n, ext = shape[0], shape[-1]
+    rows = stacks[0].shape[1]
+    seq, m = rows // 2, len(stacks)
 
     def body(small, ins, outs, scratch, loads):
         w_s, out_s = scratch[0], scratch[1]
         l_s = scratch[2:]
-        g_w = weight_loads(loads, plan[:1], ins[n:], w_s)
-        g_l = [loads.start([(ins[i], l_s[i])]) for i in range(n)]
-        g_w += weight_loads(loads, plan[1:], ins[n:], w_s)
+        g_w = weight_loads(loads, plan[:1], ins[m:], w_s)
+        g_l = []
+        for i in range(n):
+            pairs = []
+            for j in range(m):
+                count = stacks[j].shape[0] // n
+                pairs += column_loads(ins[j].at[i * count : (i + 1) * count], l_s[i], starts[j])
+            g_l.append(loads.start(pairs))
+        g_w += weight_loads(loads, plan[1:], ins[m:], w_s)
         total = None
         for i in range(n):
             loads.wait(g_l[i])
@@ -485,21 +505,21 @@
         done = []
         for a in range(2):
             out_s[a] = total[a * seq : (a + 1) * seq].astype(BF)
-            done.append(loads.start([(out_s.at[a], outs[a])]))
+            done.append(loads.start([(out_s.at[a], outs[0].at[a])]))
         for group in done:
             loads.wait(group)
 
     return call(
         body,
-        list(lefts) + arrays,
-        [sds((seq, width), BF)] * 2,
+        list(stacks) + arrays,
+        [sds((2, seq, width), BF)],
         [pltpu.VMEM(shape, BF), pltpu.VMEM((2, seq, width), BF)] + [pltpu.VMEM((rows, ext), BF)] * n,
         "grad_one",
         2 * rows * width * ext * n,
-    )
-
-
-def middle_back(ids, middle, parts, recvs, cot, keep, nv, wout):
+    )[0]
+
+
+def middle_back(ids, middle, part, recv, cot, keep, nv, wout):
     _, seq, width = middle.shape
     out_arrays, out_plan, out_scratch = wout
     ext = out_scratch[0]
@@ -514,13 +534,13 @@
                 [
                     (ins[0].at[a], mid_s.at[a]),
                     (ins[1].at[a], cot_s.at[a]),
-                    (ins[2 + a], part_s.at[a]),
-                    (ins[4 + a], recv_s.at[a]),
+                    (ins[2].at[a], part_s.at[a]),
+                    (ins[3].at[a], recv_s.at[a]),
                 ]
             )
             for a in range(2)
         ]
-        g_o = weight_loads(loads, out_plan, ins[6:], wo_s)
+        g_o = weight_loads(loads, out_plan, ins[4:], wo_s)
         done = []
         for a in range(2):
             loads.wait(g_in[a])
@@ -551,7 +571,7 @@
 
     return call(
         body,
-        [middle, cot] + list(parts) + list(recvs) + out_arrays,
+        [middle, cot, part, recv] + out_arrays,
         [
             sds((seq, width), F32),
             sds((2, seq, width), BF),
@@ -576,17 +596,18 @@
     )
 
 
-def attn_backward(units, grad, q, k, v, prev):
-    _, seq, ext = q.shape
-    n_prev = 0 if prev is None else len(prev)
-    n = len(units)
+def attn_backward(pairs, grad, q, k, v):
+    _, seq, _ = q.shape
+    n = len(pairs)
 
     def body(small, ins, outs, scratch, loads):
         q_s, k_s, v_s, do_s, dq_s, dk_s, dv_s, bs_s = scratch
         groups = []
-        for u, (image, i) in enumerate(units):
-            cols = slice(i * 128, (i + 1) * 128)
-            groups.append(loads.start([(ins[j].at[image, :, cols], scratch[j].at[u]) for j in range(4)]))
+        for u in range(2 * n):
+            cols = slice(pairs[u // 2] * 128, (pairs[u // 2] + 1) * 128)
+            groups.append(
+                loads.start([(ins[j].at[u % 2, :, cols], scratch[j].at[u]) for j in range(4)])
+            )
         half = lax.broadcasted_iota(jnp.int32, (1, 128), 1) // HEAD_DIM
         for group in groups:
             loads.wait(group)
@@ -619,28 +640,21 @@
             dv_s[u] = dv.astype(BF)
             return carry
 
-        lax.fori_loop(0, n, unit, 0)
-        done = []
-        for u, (image, i) in enumerate(units):
-            cols = slice(i * 128, (i + 1) * 128)
-            done.append(
-                loads.start(
-                    [(scratch[4 + j].at[u], outs[j].at[image, :, cols]) for j in range(3)]
-                )
-            )
-        done.append(loads.start([(bs_s, outs[3])]))
+        lax.fori_loop(0, 2 * n, unit, 0)
+        done = [loads.start([(scratch[4 + j], outs[0].at[j])]) for j in range(3)]
+        done.append(loads.start([(bs_s, outs[1])]))
         for group in done:
             loads.wait(group)
 
-    return call(
+    grads, sums = call(
         body,
-        [q, k, v, grad] + list(prev or []),
-        [sds((2, seq, ext), BF)] * 3 + [sds((n, 2, 128), F32)],
-        [pltpu.VMEM((n, seq, 128), BF)] * 7 + [pltpu.VMEM((n, 2, 128), F32)],
+        [q, k, v, grad],
+        [sds((3, 2 * n, seq, 128), BF), sds((2 * n, 2, 128), F32)],
+        [pltpu.VMEM((2 * n, seq, 128), BF)] * 7 + [pltpu.VMEM((2 * n, 2, 128), F32)],
         "attn_backward",
-        10 * n * seq * seq * 128,
-        aliases={4 + i: i for i in range(n_prev)},
-    )
+        0,
+    )
+    return grads.reshape(3 * n, 2 * seq, 128), jnp.sum(sums.reshape(n, 2, 2, 128), axis=1)
 
 
 def finish_layer(ids, keep, nv, middle, part, recv, nd, aligned):
@@ -669,7 +683,7 @@
     )[0]
 
 
-def finish_tokens(ids, nv, tok, parts, recvs, gmid, rest, nd, aligned):
+def finish_tokens(ids, nv, tok, part, recv, gmid, rest, nd, aligned):
     _, seq, width = tok.shape
     n_dest, z_n = rest.shape[:2]
     bd = width // nd
@@ -678,13 +692,13 @@
         ids_ref, nv_ref = small
         mine = ids_ref[0]
         tok_s, part_s, recv_s, gm_s, out_s, cs_s, rest_s = scratch
-        g_rest = loads.start([(ins[6], rest_s)])
+        g_rest = loads.start([(ins[4], rest_s)])
         groups = [
             loads.start(
                 [
                     (ins[0].at[a], tok_s.at[a]),
-                    (ins[2 + a], part_s.at[a]),
-                    (ins[4 + a], recv_s.at[a]),
+                    (ins[2].at[a], part_s.at[a]),
+                    (ins[3].at[a], recv_s.at[a]),
                 ]
             )
             for a in range(2)
@@ -721,7 +735,7 @@
 
     return call(
         body,
-        [tok, gmid] + list(parts) + list(recvs) + [rest],
+        [tok, gmid, part, recv, rest],
         [sds((seq, width), BF), sds((2, width), F32)] + [sds(rest.shape[1:], F32)] * n_dest,
         [pltpu.VMEM((2, seq, width), BF)] * 3
         + [pltpu.VMEM((seq, width), F32), pltpu.VMEM((seq, width), BF), pltpu.VMEM((2, width), F32)]
@@ -785,6 +799,14 @@
     a_all = [a_y] + [grid.send_x(a_y, k) for k in range(1, grid.tx)]
     b_all = [b_x] + [grid.send_y(b_x, k) for k in range(1, grid.y)]
     return a_all, b_all
+
+
+def padded_bytes(value):
+    lead, (rows, lanes) = value.shape[:-2], value.shape[-2:]
+    count = -(-rows // 16) * 16 * (-(-lanes // 128) * 128)
+    for size in lead:
+        count *= size
+    return count * value.dtype.itemsize
 
 
 def add_pieces(groups, cuts, outs, name):
@@ -812,6 +834,7 @@
         for group in done:
             loads.wait(group)
 
+    held = sum(padded_bytes(a) for a in list(arrays) + list(outs))
     return call(
         body,
         arrays,
@@ -819,6 +842,7 @@
         [pltpu.VMEM(a.shape, a.dtype) for a in arrays] + [pltpu.VMEM(o.shape, o.dtype) for o in outs],
         name,
         0,
+        vmem=held + 8 * 1024 * 1024,
     )
 
 
@@ -1091,18 +1115,20 @@
             tasks.append((l_index, slice(kx * size, (kx + 1) * size), r_index, slice(0, width), stores))
         return tasks
 
-    def by_right(l_index, r_index, size, row0, lanes):
+    def by_right(l_index, r_index, size, row0, lanes, spare=False, first=0):
         tasks, each = [], size // 2 // lanes
         for kx in range(tx):
             stores = []
             for j in range(each):
                 rows = slice(row0 + j * bd, row0 + (j + 1) * bd)
                 cols = [slice((h * each + j) * lanes, (h * each + j + 1) * lanes) for h in range(2)]
+                rows = (rows, slice(0, lanes)) if spare else (rows,)
                 for p, r_sl in a_spots:
                     ky, kz = p // z_n, p % z_n
-                    stores.append((kx, (p, rows), r_sl, cols[0]))
-                    stores.append((tx + ky, (kx * z_n + kz, rows), r_sl, cols[1]))
-            tasks.append((l_index, slice(0, width), r_index, slice(kx * size, (kx + 1) * size), stores))
+                    stores.append((kx, (p,) + rows, r_sl, cols[0]))
+                    stores.append((tx + ky, (kx * z_n + kz,) + rows, r_sl, cols[1]))
+            cols = slice(first + kx * size, first + (kx + 1) * size)
+            tasks.append((l_index, slice(0, width), r_index, cols, stores))
         return tasks
 
     def pieces(rows, lanes):
@@ -1114,60 +1140,104 @@
     grads = weight_grad([act2], [grad2], by_left(0, 0, fw, 0), pieces(fh, bd), "down_grad", 0, fh)
     down_rs = send_grad(grads, "down")
     grad_in = after(grad2, grads[-1])
-    low_pre, bias_up, two0, two1, mlp_part = mlp_back(grad_in, act2, flat(dact), wdown, wup, fh)
-    two_parts = [two0, two1]
+    low_pre, bias_up, two_part, mlp_part = mlp_back(grad_in, act2, flat(dact), wdown, wup, fh)
     mlp_part = mlp_part.reshape(2, seq, width)
-    mlp_recv = swap_core(mlp_part)
-    two_recvs = [swap_core(value) for value in two_parts]
+    two_recv = swap_core(two_part)
     down_half = down_rs.second(bias_up)
     up_rows = fh // bd * bd
-    up_shapes = pieces(up_rows + hh, bd)
     sec_in = after(sec2, down_half)
     tasks = by_right(0, 0, fw, 0, bd)
-    grads = weight_grad([sec_in], [low_pre], tasks, up_shapes, "up_grad", 0, up_rows)
+    grads = weight_grad([sec_in], [low_pre], tasks, pieces(up_rows, bd), "up_grad", 0, up_rows)
+    up_rs = send_grad(grads, "up")
     gmid, gattn, grad_att, col = middle_back(
-        ids, middle, two_parts, after(two_recvs, grads[-1]), cot, keep, nv, wout
+        ids, middle, two_part, after(two_recv, grads[-1]), cot, keep, nv, wout
     )
     down_zs = down_rs.along_z(col)
-    att_in = after(flat(att), (down_zs, mlp_recv))
+    row0 = 3 * bd
+    last_shapes = pieces(row0 + hh, bd)
+    att_in = after(flat(att), down_zs)
     tasks = by_left(0, 0, hw, 0)
-    grads = weight_grad(
-        [att_in], [flat(gattn)], tasks, up_shapes, "out_grad", up_rows, up_rows + hh, grads
-    )
-    up_rs = send_grad(grads, "up_out")
-
-    units = [(a, i) for a in range(2) for i in range(ext // 128)]
-    cut = (5 * len(units) + 4) // 8
-    res = attn_backward(units[:cut], after(grad_att, grads[-1]), q, k, v, None)
-    bias_qv = res[3]
-    grad_down = down_rs.finish(bias_qv, [(full, 0, full)], [sds((fw, bd), F32)])[0]
-    up_half = up_rs.second(grad_down)
-    res = attn_backward(units[cut:], after(grad_att, up_half), q, k, v, res[:3])
-    bias_qv = jnp.concatenate([bias_qv, res[3]]).reshape(2, ext // 128, 2, 128)
-    bias_qv = jnp.sum(bias_qv, axis=0).transpose(1, 0, 2).reshape(2, ext)
-    up_zs = up_rs.halve(res[3]) if z_n > 1 else res[3]
-    low_proj = [flat(value) for value in res[:3]]
-    makers = [by_right(0, i, hw, i * bd, hh) for i in range(3)]
-    first_in = after(flat(first), up_zs)
-    tasks = [task for maker in makers for task in maker]
-    grads = weight_grad([first_in], low_proj, tasks, pieces(3 * bd, hh), "qkv_grad", 0, 3 * bd)
+    out_grads = weight_grad(
+        [att_in], [flat(gattn)], tasks, last_shapes, "out_grad", row0, row0 + hh
+    )
+
+    up_half = up_rs.second(out_grads[-1])
+    n_pairs = ext // 128
+    split = hh == 128 and bd == 128
+    firsts = list(range(1, n_pairs)) if split else list(range(n_pairs))
+    left_a, bias_a = attn_backward(firsts, after(grad_att, up_half), q, k, v)
+    grad_down = down_rs.finish(bias_a, [(full, 0, full)], [sds((fw, bd), F32)])[0]
+    mlp_recv = swap_core(after(mlp_part, bias_a))
+    gate = up_rs.halve(grad_down) if z_n > 1 else grad_down
+    first_in = after(flat(first), gate)
+    if split:
+        stores, count = [], len(firsts)
+        for i in range(3):
+            rows = slice(i * bd, (i + 1) * bd)
+            for n, pair in enumerate(firsts):
+                kx, cols = pair // 2, slice((i * count + n) * 128, (i * count + n + 1) * 128)
+                for p, r_sl in a_spots:
+                    ky, kz = p // z_n, p % z_n
+                    spot = (kx - 1, (p, rows)) if pair % 2 == 0 else (tx - 1 + ky, (kx * z_n + kz, rows))
+                    stores.append(spot + (r_sl, cols))
+        tasks = [(0, slice(0, width), 0, slice(0, 384 * count), stores)]
+        sent = weight_grad(
+            [first_in], [left_a], tasks, last_shapes[1:], "qkv_grad", 0, row0, out_grads[1:]
+        )
+        left_b, bias_b = attn_backward([0], after(grad_att, (sent[: tx - 1], sent[tx:])), q, k, v)
+        gate = (bias_b, mlp_recv)
+        while 2 * up_rs.bit < z_n:
+            gate = up_rs.halve(gate)
+        stores = []
+        for i in range(3):
+            rows, cols = slice(i * bd, (i + 1) * bd), slice(i * 128, (i + 1) * 128)
+            stores += [(0, (p, rows), r_sl, cols) for p, r_sl in a_spots]
+        tasks = [(0, slice(0, width), 0, slice(0, 384), stores)]
+        kept = weight_grad(
+            [after(first_in, gate)],
+            [left_b],
+            tasks,
+            last_shapes[:1],
+            "qkv_keep",
+            0,
+            row0,
+            out_grads[:1],
+        )
+        grads = list(kept) + list(sent)
+        lefts, starts = [left_a, left_b], [1, 0]
+        bias_qv = jnp.concatenate([bias_b, bias_a])
+        gate = kept[0]
+    else:
+        while 2 * up_rs.bit < z_n:
+            gate = up_rs.halve((gate, mlp_recv))
+        makers = [by_right(0, 0, hw, i * bd, hh, hh < bd, i * ext) for i in range(3)]
+        tasks = [task for maker in makers for task in maker]
+        grads = weight_grad(
+            [after(first_in, gate)],
+            [left_a],
+            tasks,
+            last_shapes,
+            "qkv_grad",
+            0,
+            row0,
+            out_grads,
+            hh < bd,
+        )
+        lefts, starts = [left_a], [0]
+        bias_qv = bias_a
+        gate = grads[-1]
+    bias_qv = bias_qv.transpose(1, 0, 2).reshape(2, ext)
     qkv_rs = send_grad(grads, "qkv")
-    low_in = after(low_proj, grads[-1])
-    one_parts = input_grad(low_in, wqkv, width)
-    one_recvs = [swap_core(value) for value in one_parts]
-    total_rows = up_rows + hh
+    lefts = after(lefts, gate)
+    one_part = input_grad(lefts, starts, wqkv, width)
+    one_recv = swap_core(one_part)
     cuts = []
     for h in range(2):
         for j in range(fh // bd):
-            rows = slice(h * total_rows + j * bd, h * total_rows + (j + 1) * bd)
-            cols = slice(h * fh + j * bd, h * fh + (j + 1) * bd)
-            cuts.append((rows, 0, (full, cols)))
-        rows = slice(h * total_rows + up_rows, (h + 1) * total_rows)
-        cuts.append((rows, 1, (slice(h * hh, (h + 1) * hh),)))
-    up_cuts, gate = cuts, one_parts[0]
-    while 2 * up_rs.bit < z_n:
-        gate = up_rs.halve(gate)
-    qkv_half = qkv_rs.second(gate)
+            rows = slice(h * up_rows + j * bd, h * up_rows + (j + 1) * bd)
+            cuts.append((rows, 0, (full, slice(h * fh + j * bd, h * fh + (j + 1) * bd))))
+    up_cuts = cuts
+    qkv_half = qkv_rs.second(one_part)
     wide = max(bd, hw // dp, fw // dp)
     vec = jnp.concatenate([jnp.zeros((2, width), F32), col])
     vec = vec.reshape(6, y_n, z_n, bd).transpose(1, 2, 0, 3)
@@ -1187,35 +1257,39 @@
     rest = jnp.concatenate([vec, bias, jnp.zeros((tx, y_n, z_n, 7, wide), F32)], axis=3)
     rest = rest.reshape(tx * y_n, z_n, 16, wide)
     grad_tokens, one_sums, *small = finish_tokens(
-        ids, nv, tok, one_parts, after(one_recvs, qkv_half), gmid, rest, dp, aligned
+        ids, nv, tok, one_part, after(one_recv, qkv_half), gmid, rest, dp, aligned
     )
     if not aligned:
         ones = jnp.pad(one_sums.reshape(2, y_n, z_n, bd), ((0, 14), (0, 0), (0, 0), (0, wide - bd)))
         ones = ones.transpose(1, 2, 0, 3)
         small = [value + ones[n % y_n] for n, value in enumerate(small)]
+    small = after(small, qkv_rs.state)
     got = small[:1]
     for n in range(1, tx * y_n):
         got.append(grid.send_xy(small[n], n // y_n, n % y_n))
-    up_outs = [sds((bd, fw), F32), sds((hw, bd), F32)]
-    grad_up, grad_out = up_rs.finish(one_sums, up_cuts, up_outs)
-    cuts, outs = [], [sds((3, bd, hw), F32)]
+    grad_up = up_rs.finish(one_sums, up_cuts, [sds((bd, fw), F32)])[0]
+    cuts, outs = [], [sds((3, bd, hw), F32), sds((hw, bd), F32)]
+    last_rows = row0 + hh
     for h in range(2):
         for i in range(3):
-            rows = slice((3 * h + i) * bd, (3 * h + i + 1) * bd)
+            rows = slice(h * last_rows + i * bd, h * last_rows + (i + 1) * bd)
+            rows = (rows, slice(0, hh)) if hh < bd else rows
             cuts.append((rows, 0, (i, full, slice(h * hh, (h + 1) * hh))))
-    if wide == hh:
-        qkv_zs = qkv_rs.along_z(grad_out, got)
-        cuts.append((slice(6 * bd, 6 * bd + 16), 1, full))
+        rows = slice(h * last_rows + row0, (h + 1) * last_rows)
+        cuts.append((rows, 1, (slice(h * hh, (h + 1) * hh),)))
+    if wide == bd:
+        qkv_zs = qkv_rs.along_z(grad_up, got)
+        cuts.append((slice(2 * last_rows, 2 * last_rows + 16), 2, full))
         outs.append(sds((16, wide), F32))
     else:
-        qkv_zs = qkv_rs.along_z(grad_out)
+        qkv_zs = qkv_rs.along_z(grad_up)
     layer_out = finish_layer(
         ids, keep, nv, middle, after(mlp_part, qkv_zs), mlp_recv, dp, aligned
     )
     res = qkv_rs.finish(layer_out, cuts, outs)
-    grad_qkv = res[0]
-    if wide == hh:
-        both = res[1]
+    grad_qkv, grad_out = res[:2]
+    if wide == bd:
+        both = res[2]
     else:
         both, bit = sum(got), 1
         while bit < z_n:

time: 390 us -> 370 us (0.949)
  Pallas kernels: 216 us -> 204 us
  local copies, waits for them, and re-layouts: 32.3 us -> 27.9 us
  waiting for transfers between devices: 66.4 us -> 62.2 us
    pallas_call x27 -> x28, Pallas kernels: 216 us -> 204 us  [call(): pl.pallas_call(kernel, out_shape=outs, in_specs=[pl.BlockSpec(memory_spac...]
    ppermute x12, waiting for transfers between devices: 11.4 us -> 5.5 us  [send_x(): return lax.ppermute(value, 'tx', [(i, i ^ k) for i in range(self.tx)])]
    ppermute x12, waiting for transfers between devices: 20.1 us -> 24.1 us  [send_y(): return lax.ppermute(value, 'dp', [(i, i ^ k) for i in range(self.dp)])]
    unnamed x86 -> x76, local copies, waits for them, and re-layouts: 17.4 us -> 17.1 us
  transfers between devices with their start and end apart: 53 -> 51, of which waited for: 17 -> 17; matrix products, arithmetic and copies ran while one was open for 4% -> 4% of each run, Pallas kernels for 51% -> 56%
where the time goes in v4:
time: 370 us; the launch traced here: 363 us
  Pallas kernels  204 us (55%)
  waiting for transfers between devices  62.2 us (17%)
  starting transfers between devices  61.2 us (17%)
  local copies, waits for them, and re-layouts  27.9 us (8%)
  other arithmetic  5.58 us (2%)
    pallas_call x28, Pallas kernels, call(): pl.pallas_call(kernel, out_shape=outs, in_specs=[pl.BlockSpec(memory_spac...  204 us
    ppermute x17, starting transfers between devices, send_z(): lax.ppermute(value, 'dp', [(i, i ^ k * self.y) for i in range(self.dp)])  30.8 us
    ppermute x17, waiting for transfers between devices, send_z(): lax.ppermute(value, 'dp', [(i, i ^ k * self.y) for i in range(self.dp)])  30.2 us
    ppermute x12, waiting for transfers between devices, send_y(): return lax.ppermute(value, 'dp', [(i, i ^ k) for i in range(self.dp)])  24.1 us
    unnamed x76, local copies, waits for them, and re-layouts  17.1 us
    ppermute x12, starting transfers between devices, send_x(): return lax.ppermute(value, 'tx', [(i, i ^ k) for i in range(self.tx)])  14 us
    ppermute x12, starting transfers between devices, send_y(): return lax.ppermute(value, 'dp', [(i, i ^ k) for i in range(self.dp)])  11.6 us
  transfers between devices with their start and end apart: 51, of which 17 were waited for; matrix products, arithmetic and copies ran while one was open for 4% of the time, Pallas kernels for 56%

profile of v4, /device:TPU:0, one launch (start us, length us, event | category | flops | bytes accessed | tf_op | source)
XLA Modules:
  0.0 363.0 jit_solution(10246883785218397410)
XLA Ops:
  3.6 1.5 concatenate.71
  5.1 3.1 collective-permute-start
  8.2 2.6 collective-permute-start.1
  12.5 5.0 %arrange_pair.1 = (bf16[2,584,1024]{2,1,0:T(8,128)(2,1)}, bf16[2,584,1024]{2,1,0:T(8,128)(2,1)}) custom-call(s32[10]{0:T(128)} %stack.130.refs_0_, bf16[584,1024]{1,0:T(8,128)(2,1)} %refs_1_.1, bf16[584,1024]{1,0:T(8,128)(2,1)} %refs_2_.1, bf16[584,1024]{1,0:T(8,128)(2,1)} %copy-done.30, bf16[584,1024]{1,0:T(8,128)(2,1)} %collective-permute-done.4.refs_4_), custom_call_target="tpu_custom_call" | custom-call | flops 5750000128 | bytes 5750000 | tf_op jit(solution)/shard_map/arrange_pair/pallas_call | solution.py:80
  17.5 2.4 collective-permute-done
  19.9 9.9 %collective-permute-done.1 = bf16[1040,128]{1,0:T(8,128)(2,1)S(1)} collective-permute-done((bf16[1040,128]{1,0:T(8,128)(2,1)S(1)}, bf16[1040,128]{1,0:T(8,128)(2,1)S(1)}, u32[]{:S(2)}, u32[]{:S(2)}) %collective-permute-start.1) | collective-permute-done | bytes 266272 | tf_op jit(solution)/shard_map/ppermute | solution.py:757
  30.1 1.6 collective-permute-start.5
  31.8 1.6 collective-permute-start.7
  33.4 8.8 %collective-permute-done.5 = bf16[4,528,128]{2,1,0:T(8,128)(2,1)S(1)} collective-permute-done((bf16[4,528,128]{2,1,0:T(8,128)(2,1)S(1)}, bf16[4,528,128]{2,1,0:T(8,128)(2,1)S(1)}, u32[]{:S(2)}, u32[]{:S(2)}) %collective-permute-start.5) | collective-permute-done | bytes 540704 | tf_op jit(solution)/shard_map/ppermute | solution.py:760
  42.3 1.6 collective-permute-start.6
  46.2 6.2 %collective-permute-start.9 = (bf16[256,512]{1,0:T(8,128)(2,1)S(1)}, bf16[256,512]{1,0:T(8,128)(2,1)S(1)}, u32[]{:S(2)}, u32[]{:S(2)}) collective-permute-start(bf16[256,512]{1,0:T(8,128)(2,1)S(1)} %constant_dynamic-update-slice_fusion.10), channel_id=1, source_target_pairs={{0,8},{4,12},{8,0},{12,4},{16,24},{20,28},{24,16},{28,20},{1,9},{5... | collective-permute-start | bytes 786440 | tf_op jit(solution)/shard_map/ppermute | solution.py:757
  53.6 1.4 collective-permute-start.11
  54.9 11.0 %collective-permute-done.8.refs_6_.refs_10_.refs_11_.refs_15_.refs_5_ = bf16[8,512,128]{2,1,0:T(8,128)(2,1)} collective-permute-done((bf16[8,512,128]{2,1,0:T(8,128)(2,1)S(1)}, bf16[8,512,128]{2,1,0:T(8,128)(2,1)}, u32[]{:S(2)}, u32[]{:S(2)}) %collective-permute-start.8) | collective-permute-done | bytes 1048608 | tf_op jit(solution)/shard_map/ppermute | solution.py:760
  66.6 2.6 vectors.1
  69.2 3.7 %collective-permute-done.10 = bf16[256,512]{1,0:T(8,128)(2,1)S(1)} collective-permute-done((bf16[256,512]{1,0:T(8,128)(2,1)S(1)}, bf16[256,512]{1,0:T(8,128)(2,1)S(1)}, u32[]{:S(2)}, u32[]{:S(2)}) %collective-permute-start.10) | collective-permute-done | bytes 262176 | tf_op jit(solution)/shard_map/ppermute | solution.py:757
  74.7 16.1 %attn_forward.2 = (bf16[2,584,1024]{2,1,0:T(8,128)(2,1)}, bf16[2,584,512]{2,1,0:T(8,128)(2,1)}, bf16[2,584,512]{2,1,0:T(8,128)(2,1)}, bf16[2,584,512]{2,1,0:T(8,...) custom-call(f32[6,1024]{1,0:T(8,128)} %get-tuple-element.191.refs_0_.refs_1_.refs_2_, ...), custom_call_target="tpu_custom_call" | custom-call | flops 18400000000 | bytes 18400000 | tf_op jit(solution)/shard_map/attn_forward/pallas_call | solution.py:80
  92.6 3.8 %collective-permute-start.18 = (bf16[1024,128]{1,0:T(8,128)(2,1)S(1)}, bf16[1024,128]{1,0:T(8,128)(2,1)S(1)}, u32[]{:S(2)}, u32[]{:S(2)}) collective-permute-start(bf16[1024,128]{1,0:T(8,128)(2,1)S(1)} %constant_dynamic-update-slice_fusion.16), channel_id=1, source_target_pairs={{0,8},{4,12},{8,0},{12,4},{16,24},{20,28},{24,16},{28,20},{1,9},{5... | collective-permute-start | bytes 786440 | tf_op jit(solution)/shard_map/ppermute | solution.py:757
  97.5 1.4 collective-permute-start.20
  101.1 16.3 %attn_forward.3 = (bf16[2,584,1024]{2,1,0:T(8,128)(2,1)}, bf16[2,584,512]{2,1,0:T(8,128)(2,1)}, bf16[2,584,512]{2,1,0:T(8,128)(2,1)}, bf16[2,584,512]{2,1,0:T(8,...) custom-call(f32[6,1024]{1,0:T(8,128)} %get-tuple-element.191.refs_0_, ...), custom_call_target="tpu_custom_call", output_to_operand_aliasing={{0}: (3, {}), {1}: (4, {}), {2}: (5, {}), {3}: (6, {}), {4}... | custom-call | flops 18400000000 | bytes 18400000 | tf_op jit(solution)/shard_map/attn_forward/pallas_call | solution.py:80
  117.5 3.2 collective-permute-done.16
  120.7 1.8 broadcast_multiply_fusion
  126.3 1.6 collective-permute-start.22
  127.8 10.2 %mlp_up.2 = (f32[2,584,1024]{2,1,0:T(8,128)}, bf16[2,584,1024]{2,1,0:T(8,128)(2,1)}, bf16[2,584,2048]{2,1,0:T(8,128)(2,1)}, bf16[2,584,2048]{2,1,0:T(8,128)(2,1)}) custom-call(f32[2]{0:T(128)} %get-tuple-element.359.refs_0_.refs_1_, f32[6,1024]{1,0:T(8,128)} %get-tuple-element.191.refs_0_.refs_1_.refs_2_, f32[1,2048]{1,0:T(1,128)} %get-tuple-element.192.refs_2_, ...), custom_call_target="tpu_custom_call" | custom-call | flops 11500000256 | bytes 11500000 | tf_op jit(solution)/shard_map/mlp_up/pallas_call | solution.py:80
  140.0 1.6 collective-permute-start.23
  143.9 10.1 %mlp_up.3 = (f32[2,584,1024]{2,1,0:T(8,128)}, bf16[2,584,1024]{2,1,0:T(8,128)(2,1)}, bf16[2,584,2048]{2,1,0:T(8,128)(2,1)}, bf16[2,584,2048]{2,1,0:T(8,128)(2,1)}) custom-call(f32[2]{0:T(128)} %get-tuple-element.359.refs_0_.refs_1_, ...), custom_call_target="tpu_custom_call", output_to_operand_aliasing={{0}: (6, {}), {1}: (7, {}), {2}: (8, {}), {3}: (9, {})} | custom-call | flops 11500000256 | bytes 11500000 | tf_op jit(solution)/shard_map/mlp_up/pallas_call | solution.py:80
  154.0 11.0 %down_grad.1 = (bf16[8,512,128]{2,1,0:T(8,128)(2,1)}, bf16[8,512,128]{2,1,0:T(8,128)(2,1)}, bf16[8,512,128]{2,1,0:T(8,128)(2,1)}, bf16[8,512,128]{2,1,0:T(8,128)(2,1)}) custom-call(bf16[1168,2048]{1,0:T(8,128)(2,1)} %bitcast.160, bf16[1168,1024]{1,0:T(8,128)(2,1)} %bitcast.129), custom_call_target="tpu_custom_call" | custom-call | flops 12650000384 | bytes 12650000 | tf_op jit(solution)/shard_map/down_grad/pallas_call | solution.py:80
  165.0 1.5 collective-permute-start.26
  168.0 22.0 %mlp_back.1 = (bf16[1168,2048]{1,0:T(8,128)(2,1)}, f32[1,2048]{1,0:T(1,128)}, bf16[2,584,1024]{2,1,0:T(8,128)(2,1)}, bf16[1168,1024]{1,0:T(8,128)(2,1)}) custom-call(bf16[1168,1024]{1,0:T(8,128)(2,1)} %bitcast.130, bf16[1168,2048]{1,0:T(8,128)(2,1)} %bitcast.161, bf16[1168,2048]{1,0:T(8,128)(2,1)} %bitcast.162, bf16[8,512,128]{2,1,0:T(8,128)(2,1)} %copy-done.23, ...), custom_call_target="tpu_custom_call" | custom-call | flops 25300000768 | bytes 25300000 | tf_op jit(solution)/shard_map/mlp_back/pallas_call | solution.py:80
  190.2 1.2 copy-done.5
  191.5 1.2 copy-done.6
  192.7 1.6 down_add.1
  196.2 10.3 %up_grad.1 = (bf16[8,512,128]{2,1,0:T(8,128)(2,1)}, bf16[8,512,128]{2,1,0:T(8,128)(2,1)}, bf16[8,512,128]{2,1,0:T(8,128)(2,1)}, bf16[8,512,128]{2,1,0:T(8,128)(2,1)}) custom-call(bf16[1168,1024]{1,0:T(8,128)(2,1)} %bitcast.163, bf16[1168,2048]{1,0:T(8,128)(2,1)} %get-tuple-element.256.refs_1_), custom_call_target="tpu_custom_call" | custom-call | flops 12650000384 | bytes 12650000 | tf_op jit(solution)/shard_map/up_grad/pallas_call | solution.py:80
  207.7 1.9 collective-permute-start.28
  209.6 11.4 %middle_back.1 = (f32[584,1024]{1,0:T(8,128)}, bf16[2,584,1024]{2,1,0:T(8,128)(2,1)}, bf16[2,584,512]{2,1,0:T(8,128)(2,1)}, f32[4,1024]{1,0:T(4,128)}) custom-call(s32[10]{0:T(128)} %stack.130.refs_0_, f32[2]{0:T(128)} %get-tuple-element.359.refs_0_.refs_1_, f32[6,1024]{1,0:T(8,128)} %get-tuple-element.191.refs_0_.refs_1_.refs_2_, ...), custom_call_target="tpu_custom_call" | custom-call | flops 23000000 | bytes 23000 | tf_op jit(solution)/shard_map/middle_back/pallas_call | solution.py:80
  223.0 1.4 down_addz.1
  225.8 2.4 collective-permute-start.35
  228.2 1.4 collective-permute-start.36
  229.6 4.9 %out_grad.1 = (bf16[8,512,128]{2,1,0:T(8,128)(2,1)}, bf16[8,512,128]{2,1,0:T(8,128)(2,1)}, bf16[8,512,128]{2,1,0:T(8,128)(2,1)}, bf16[8,512,128]{2,1,0:T(8,128)(2,1)}) custom-call(bf16[1168,512]{1,0:T(8,128)(2,1)} %bitcast.164, bf16[1168,1024]{1,0:T(8,128)(2,1)} %bitcast.159), custom_call_target="tpu_custom_call" | custom-call | flops 9200000000 | bytes 9200000 | tf_op jit(solution)/shard_map/out_grad/pallas_call | solution.py:80
  235.8 1.2 copy-done.4
  237.0 1.6 up_add.1
  239.8 25.0 %attn_backward.2 = (bf16[3,6,584,128]{3,2,1,0:T(8,128)(2,1)}, f32[6,2,128]{2,1,0:T(2,128)}) custom-call(bf16[2,584,512]{2,1,0:T(8,128)(2,1)} %get-tuple-element.286.refs_0_, bf16[2,584,512]{2,1,0:T(8,128)(2,1)} %get-tuple-element.287.refs_1_, bf16[2,584,512]{2,1,0:T(8,128)(2,1)} %get-tuple-element.288.refs_2_, bf16[2,584,512]{2,1,0:T(8,128)(2,1)} %get-tuple-element.308.refs_3_), custom_call_target="tpu_custom_call" | custom-call | flops 20700000256 | bytes 20700000 | tf_op jit(solution)/shard_map/attn_backward/pallas_call | solution.py:80
  265.7 2.5 down_sum.1
  268.2 1.5 up_half.2
  269.7 7.8 %qkv_grad.1 = (bf16[8,512,128]{2,1,0:T(8,128)(2,1)}, bf16[8,512,128]{2,1,0:T(8,128)(2,1)}, bf16[8,512,128]{2,1,0:T(8,128)(2,1)}) custom-call(bf16[1168,1024]{1,0:T(8,128)(2,1)} %bitcast.131, bf16[9,1168,128]{2,1,0:T(8,128)(2,1)} %bitcast.127, ...), custom_call_target="tpu_custom_call", output_to_operand_aliasing={{0}: (2, {}), {1}: (3, {}), {2}: (4, {})} | custom-call | flops 8049999872 | bytes 8050000 | tf_op jit(solution)/shard_map/qkv_grad/pallas_call | solution.py:80
  278.7 1.9 collective-permute-start.40
  280.5 9.7 %attn_backward.3 = (bf16[3,2,584,128]{3,2,1,0:T(8,128)(2,1)}, f32[2,2,128]{2,1,0:T(2,128)}) custom-call(bf16[2,584,512]{2,1,0:T(8,128)(2,1)} %get-tuple-element.286.refs_0_, bf16[2,584,512]{2,1,0:T(8,128)(2,1)} %get-tuple-element.287.refs_1_, bf16[2,584,512]{2,1,0:T(8,128)(2,1)} %get-tuple-element.288.refs_2_, bf16[2,584,512]{2,1,0:T(8,128)(2,1)} %get-tuple-element.308.refs_3_), custom_call_target="tpu_custom_call" | custom-call | flops 20700000256 | bytes 20700000 | tf_op jit(solution)/shard_map/attn_backward/pallas_call | solution.py:80
  292.1 2.3 collective-permute-done.37.refs_1_
  295.9 4.8 %qkv_keep.1.refs_0_ = bf16[8,512,128]{2,1,0:T(8,128)(2,1)} custom-call(bf16[1168,1024]{1,0:T(8,128)(2,1)} %bitcast.132, bf16[3,1168,128]{2,1,0:T(8,128)(2,1)} %bitcast.125, bf16[8,512,128]{2,1,0:T(8,128)(2,1)} %get-tuple-element.316.refs_2_), custom_call_target="tpu_custom_call", output_to_operand_aliasing={{}: (2, {})} | custom-call | flops 23000000 | bytes 23000 | tf_op jit(solution)/shard_map/qkv_keep/pallas_call | solution.py:80
  300.7 8.5 %grad_one.1.refs_4_ = bf16[2,584,1024]{2,1,0:T(8,128)(2,1)} custom-call(bf16[9,1168,128]{2,1,0:T(8,128)(2,1)} %bitcast.128, bf16[3,1168,128]{2,1,0:T(8,128)(2,1)} %bitcast.126, bf16[8,528,128]{2,1,0:T(8,128)(2,1)} %copy-done.20, bf16[8,528,128]{2,1,0:T(8,128)(2,1)} %collective-permute-done.6.refs_2_.refs_4_.refs_8_.refs_9_.refs_13_.refs_3_, ...), custom_call_target="tpu_custom_call" | custom-call | flops 23000000 | bytes 23000 | tf_op jit(solution)/shard_map/grad_one/pallas_call | solution.py:80
  310.6 1.9 qkv_add.1
  315.2 1.3 collective-permute-start.43
  316.5 1.4 copy-done.29
  317.9 8.5 %finish_tokens.1 = (bf16[584,1024]{1,0:T(8,128)(2,1)}, f32[2,1024]{1,0:T(2,128)}, f32[4,16,128]{2,1,0:T(8,128)}, f32[4,16,128]{2,1,0:T(8,128)}, f32[4,16,128]{2,1,0:T(8,128)}, /*index=5*/f32[4,16,128]{2,1,0:T(8,128)}) custom-call(s32[10]{0:T(128)} %stack.130.refs_0_, f32[6,1024]{1,0:T(8,128)} %get-tuple-element.191.refs_0_.refs_1_.refs_2_, ...), custom_call_target="tpu_custom_call" | custom-call | flops 10350000128 | bytes 10350000 | tf_op jit(solution)/shard_map/finish_tokens/pallas_call | solution.py:80
  326.4 2.3 collective-permute-done.41.refs_1_
  328.6 1.7 collective-permute-start.45
  330.8 1.3 collective-permute-start.47
  332.1 1.3 up_sum.1
  334.5 1.4 collective-permute-done.47.refs_7_
  338.1 2.7 collective-permute-start.49
  340.8 1.4 collective-permute-start.50
  342.2 5.1 %finish_layer.1 = bf16[584,1024]{1,0:T(8,128)(2,1)} custom-call(s32[10]{0:T(128)} %stack.130.refs_0_, f32[2]{0:T(128)} %get-tuple-element.359.refs_0_.refs_1_, f32[6,1024]{1,0:T(8,128)} %get-tuple-element.191.refs_0_.refs_1_.refs_2_, f32[2,584,1024]{2,1,0:T(8,128)} %get-tuple-element.224.refs_3_, bf16[2,584,1024]{2,1,0:T(8,128)(2,1)} %bitcast.134, ...), custom_call_target="tpu_custom_call" | custom-call | flops 23000000 | bytes 23000 | tf_op jit(solution)/shard_map/finish_layer/pallas_call | solution.py:80
  347.2 1.7 collective-permute-done.48.refs_1_
  349.0 10.0 %collective-permute-done.49.refs_2_ = bf16[1040,128]{1,0:T(8,128)(2,1)S(1)} collective-permute-done((bf16[1040,128]{1,0:T(8,128)(2,1)S(1)}, bf16[1040,128]{1,0:T(8,128)(2,1)S(1)}, u32[]{:S(2)}, u32[]{:S(2)}) %collective-permute-start.49) | collective-permute-done | bytes 266272 | tf_op jit(solution)/shard_map/ppermute | solution.py:757
  359.0 1.4 qkv_sum.1
  (213 shorter events, 49.9 us)
Async XLA Ops:
  0.6 10.8 %collective-permute-start.3 = (bf16[584,1024]{1,0:T(8,128)(2,1)}, bf16[584,1024]{1,0:T(8,128)(2,1)S(1)}, u32[]{:S(2)}, u32[]{:S(2)}) collective-permute-start(bf16[584,1024]{1,0:T(8,128)(2,1)} %refs_1_.1), channel_id=1, source_target_pairs={{0,1},{1,0},{2,3},{3,2},{4,5},{5,4},{6,7},{7,6},{8,9},{9,8},{10,11... | collective-permute-start | bytes 3588104 | tf_op jit(solution)/shard_map/ppermute | solution.py:772
  1.2 10.3 %collective-permute-start.4 = (bf16[584,1024]{1,0:T(8,128)(2,1)}, bf16[584,1024]{1,0:T(8,128)(2,1)}, u32[]{:S(2)}, u32[]{:S(2)}) collective-permute-start(bf16[584,1024]{1,0:T(8,128)(2,1)} %refs_2_.1), channel_id=1, source_target_pairs={{0,1},{1,0},{2,3},{3,2},{4,5},{5,4},{6,7},{7,6},{8,9},{9,8},{10,11... | collective-permute-start | bytes 3588104 | tf_op jit(solution)/shard_map/ppermute | solution.py:772
  5.1 14.8 %collective-permute-start = (bf16[1040,128]{1,0:T(8,128)(2,1)S(1)}, bf16[1040,128]{1,0:T(8,128)(2,1)S(1)}, u32[]{:S(2)}, u32[]{:S(2)}) collective-permute-start(bf16[1040,128]{1,0:T(8,128)(2,1)S(1)} %concatenate.71), channel_id=1, source_target_pairs={{0,8},{4,12},{8,0},{12,4},{16,24},{20,28},{24,16},{28,20},{1,9},{5... | collective-permute-start | bytes 798728 | tf_op jit(solution)/shard_map/ppermute | solution.py:757
  8.2 21.6 %collective-permute-start.1 = (bf16[1040,128]{1,0:T(8,128)(2,1)S(1)}, bf16[1040,128]{1,0:T(8,128)(2,1)S(1)}, u32[]{:S(2)}, u32[]{:S(2)}) collective-permute-start(bf16[1040,128]{1,0:T(8,128)(2,1)S(1)} %concatenate.71), channel_id=1, source_target_pairs={{0,16},{4,20},{8,24},{12,28},{16,0},{20,4},{24,8},{28,12},{1,17},{... | collective-permute-start | bytes 798728 | tf_op jit(solution)/shard_map/ppermute | solution.py:757
  10.8 19.0 %collective-permute-start.2 = (bf16[1040,128]{1,0:T(8,128)(2,1)S(1)}, bf16[1040,128]{1,0:T(8,128)(2,1)S(1)}, u32[]{:S(2)}, u32[]{:S(2)}) collective-permute-start(bf16[1040,128]{1,0:T(8,128)(2,1)S(1)} %concatenate.71), channel_id=1, source_target_pairs={{0,24},{4,28},{8,16},{12,20},{16,8},{20,12},{24,0},{28,4},{1,25},{... | collective-permute-start | bytes 798728 | tf_op jit(solution)/shard_map/ppermute | solution.py:757
  30.1 12.2 %collective-permute-start.5 = (bf16[4,528,128]{2,1,0:T(8,128)(2,1)S(1)}, bf16[4,528,128]{2,1,0:T(8,128)(2,1)S(1)}, u32[]{:S(2)}, u32[]{:S(2)}) collective-permute-start(bf16[4,528,128]{2,1,0:T(8,128)(2,1)S(1)} %pad_maximum_fusion), channel_id=1, source_target_pairs={{0,4},{4,0},{8,12},{12,8},{16,20},{20,16},{24,28},{28,24},{1,5},{5... | collective-permute-start | bytes 1622024 | tf_op jit(solution)/shard_map/ppermute | solution.py:760
  31.8 12.8 %collective-permute-start.7 = (bf16[4,512,128]{2,1,0:T(8,128)(2,1)S(1)}, bf16[4,512,128]{2,1,0:T(8,128)(2,1)S(1)}, u32[]{:S(2)}, u32[]{:S(2)}) collective-permute-start(bf16[4,512,128]{2,1,0:T(8,128)(2,1)S(1)} %pad_maximum_fusion.1), channel_id=1, source_target_pairs={{0,2},{2,0},{1,3},{3,1},{4,6},{6,4},{5,7},{7,5},{8,10},{10,8},{9,1... | collective-permute-start | bytes 1572872 | tf_op jit(solution)/shard_map/ppermute | solution.py:768
  33.4 12.2 %copy-start.28 = (s32[4]{0:T(128)S(1)}, s32[4]{0:T(128)}, u32[]{:S(2)}) copy-start(s32[4]{0:T(128)} %param.13) | copy-start | bytes 52
  33.4 12.8 %copy-start.24 = (bf16[1024,128]{1,0:T(8,128)(2,1)S(1)}, bf16[1024,128]{1,0:T(8,128)(2,1)}, u32[]{:S(2)}) copy-start(bf16[1024,128]{1,0:T(8,128)(2,1)} %param.21) | copy-start | bytes 786436
  33.4 12.8 %copy-start.25 = (bf16[128,1024]{1,0:T(8,128)(2,1)S(1)}, bf16[128,1024]{1,0:T(8,128)(2,1)}, u32[]{:S(2)}) copy-start(bf16[128,1024]{1,0:T(8,128)(2,1)} %param.19) | copy-start | bytes 786436
  42.3 24.3 %collective-permute-start.6 = (bf16[8,528,128]{2,1,0:T(8,128)(2,1)S(1)}, bf16[8,528,128]{2,1,0:T(8,128)(2,1)}, u32[]{:S(2)}, u32[]{:S(2)}) collective-permute-start(bf16[8,528,128]{2,1,0:T(8,128)(2,1)S(1)} %constant_dynamic-update-slice_fusion.refs_1_.refs_3_.refs_7_.refs_8_.refs_12_.refs_2_), channel_id=1, source_target_pairs={{0,2},{2,0},{1,3},{3,1},{4,6},{6,4},{5,7},{7,5},{8,10},{10,8},{9,1... | collective-permute-start | bytes 3244040 | tf_op jit(solution)/shard_map/ppermute | solution.py:768
  44.7 24.5 %copy-start.21 = (bf16[8,512,128]{2,1,0:T(8,128)(2,1)}, bf16[8,512,128]{2,1,0:T(8,128)(2,1)S(1)}, u32[]{:S(2)}) copy-start(bf16[8,512,128]{2,1,0:T(8,128)(2,1)S(1)} %constant_dynamic-update-slice_fusion.5.refs_5_.refs_9_.refs_10_.refs_14_.refs_4_) | copy-start | bytes 3145732
  44.7 21.3 %collective-permute-start.8 = (bf16[8,512,128]{2,1,0:T(8,128)(2,1)S(1)}, bf16[8,512,128]{2,1,0:T(8,128)(2,1)}, u32[]{:S(2)}, u32[]{:S(2)}) collective-permute-start(bf16[8,512,128]{2,1,0:T(8,128)(2,1)S(1)} %constant_dynamic-update-slice_fusion.5.refs_5_.refs_9_.refs_10_.refs_14_.refs_4_), channel_id=1, source_target_pairs={{0,4},{4,0},{8,12},{12,8},{16,20},{20,16},{24,28},{28,24},{1,5},{5... | collective-permute-start | bytes 3145736 | tf_op jit(solution)/shard_map/ppermute | solution.py:760
  46.2 22.9 %collective-permute-start.9 = (bf16[256,512]{1,0:T(8,128)(2,1)S(1)}, bf16[256,512]{1,0:T(8,128)(2,1)S(1)}, u32[]{:S(2)}, u32[]{:S(2)}) collective-permute-start(bf16[256,512]{1,0:T(8,128)(2,1)S(1)} %constant_dynamic-update-slice_fusion.10), channel_id=1, source_target_pairs={{0,8},{4,12},{8,0},{12,4},{16,24},{20,28},{24,16},{28,20},{1,9},{5... | collective-permute-start | bytes 786440 | tf_op jit(solution)/shard_map/ppermute | solution.py:757
  52.5 20.4 %collective-permute-start.10 = (bf16[256,512]{1,0:T(8,128)(2,1)S(1)}, bf16[256,512]{1,0:T(8,128)(2,1)S(1)}, u32[]{:S(2)}, u32[]{:S(2)}) collective-permute-start(bf16[256,512]{1,0:T(8,128)(2,1)S(1)} %constant_dynamic-update-slice_fusion.10), channel_id=1, source_target_pairs={{0,16},{4,20},{8,24},{12,28},{16,0},{20,4},{24,8},{28,12},{1,17},{... | collective-permute-start | bytes 786440 | tf_op jit(solution)/shard_map/ppermute | solution.py:757
  53.6 19.3 %collective-permute-start.11 = (bf16[256,512]{1,0:T(8,128)(2,1)S(1)}, bf16[256,512]{1,0:T(8,128)(2,1)S(1)}, u32[]{:S(2)}, u32[]{:S(2)}) collective-permute-start(bf16[256,512]{1,0:T(8,128)(2,1)S(1)} %constant_dynamic-update-slice_fusion.10), channel_id=1, source_target_pairs={{0,24},{4,28},{8,16},{12,20},{16,8},{20,12},{24,0},{28,4},{1,25},{... | collective-permute-start | bytes 786440 | tf_op jit(solution)/shard_map/ppermute | solution.py:757
  73.1 17.7 %collective-permute-start.12 = (bf16[4,128,512]{2,1,0:T(8,128)(2,1)S(1)}, bf16[4,128,512]{2,1,0:T(8,128)(2,1)S(1)}, u32[]{:S(2)}, u32[]{:S(2)}) collective-permute-start(bf16[4,128,512]{2,1,0:T(8,128)(2,1)S(1)} %pad_maximum_fusion.2), channel_id=1, source_target_pairs={{0,4},{4,0},{8,12},{12,8},{16,20},{20,16},{24,28},{28,24},{1,5},{5... | collective-permute-start | bytes 1572872 | tf_op jit(solution)/shard_map/ppermute | solution.py:760
  73.7 17.1 %collective-permute-start.13 = (bf16[4,128,512]{2,1,0:T(8,128)(2,1)S(1)}, bf16[4,128,512]{2,1,0:T(8,128)(2,1)S(1)}, u32[]{:S(2)}, u32[]{:S(2)}) collective-permute-start(bf16[4,128,512]{2,1,0:T(8,128)(2,1)S(1)} %pad_maximum_fusion.3), channel_id=1, source_target_pairs={{0,2},{2,0},{1,3},{3,1},{4,6},{6,4},{5,7},{7,5},{8,10},{10,8},{9,1... | collective-permute-start | bytes 1572872 | tf_op jit(solution)/shard_map/ppermute | solution.py:768
  92.6 24.9 %copy-start.22 = (bf16[8,128,512]{2,1,0:T(8,128)(2,1)}, bf16[8,128,512]{2,1,0:T(8,128)(2,1)S(1)}, u32[]{:S(2)}) copy-start(bf16[8,128,512]{2,1,0:T(8,128)(2,1)S(1)} %constant_dynamic-update-slice_fusion.14) | copy-start | bytes 3145732
  92.6 30.3 %collective-permute-start.18 = (bf16[1024,128]{1,0:T(8,128)(2,1)S(1)}, bf16[1024,128]{1,0:T(8,128)(2,1)S(1)}, u32[]{:S(2)}, u32[]{:S(2)}) collective-permute-start(bf16[1024,128]{1,0:T(8,128)(2,1)S(1)} %constant_dynamic-update-slice_fusion.16), channel_id=1, source_target_pairs={{0,8},{4,12},{8,0},{12,4},{16,24},{20,28},{24,16},{28,20},{1,9},{5... | collective-permute-start | bytes 786440 | tf_op jit(solution)/shard_map/ppermute | solution.py:757
  96.5 26.5 %collective-permute-start.19 = (bf16[1024,128]{1,0:T(8,128)(2,1)S(1)}, bf16[1024,128]{1,0:T(8,128)(2,1)}, u32[]{:S(2)}, u32[]{:S(2)}) collective-permute-start(bf16[1024,128]{1,0:T(8,128)(2,1)S(1)} %constant_dynamic-update-slice_fusion.16), channel_id=1, source_target_pairs={{0,16},{4,20},{8,24},{12,28},{16,0},{20,4},{24,8},{28,12},{1,17},{... | collective-permute-start | bytes 786440 | tf_op jit(solution)/shard_map/ppermute | solution.py:757
  97.5 25.4 %collective-permute-start.20 = (bf16[1024,128]{1,0:T(8,128)(2,1)S(1)}, bf16[1024,128]{1,0:T(8,128)(2,1)}, u32[]{:S(2)}, u32[]{:S(2)}) collective-permute-start(bf16[1024,128]{1,0:T(8,128)(2,1)S(1)} %constant_dynamic-update-slice_fusion.16), channel_id=1, source_target_pairs={{0,24},{4,28},{8,16},{12,20},{16,8},{20,12},{24,0},{28,4},{1,25},{... | collective-permute-start | bytes 786440 | tf_op jit(solution)/shard_map/ppermute | solution.py:757
  98.9 21.7 %collective-permute-start.16 = (bf16[8,128,512]{2,1,0:T(8,128)(2,1)}, bf16[8,128,512]{2,1,0:T(8,128)(2,1)}, u32[]{:S(2)}, u32[]{:S(2)}) collective-permute-start(bf16[8,128,512]{2,1,0:T(8,128)(2,1)} %constant_dynamic-update-slice_fusion.12), channel_id=1, source_target_pairs={{0,2},{2,0},{1,3},{3,1},{4,6},{6,4},{5,7},{7,5},{8,10},{10,8},{9,1... | collective-permute-start | bytes 3145736 | tf_op jit(solution)/shard_map/ppermute | solution.py:768
  100.1 22.3 %collective-permute-start.17 = (bf16[8,128,512]{2,1,0:T(8,128)(2,1)S(1)}, bf16[8,128,512]{2,1,0:T(8,128)(2,1)}, u32[]{:S(2)}, u32[]{:S(2)}) collective-permute-start(bf16[8,128,512]{2,1,0:T(8,128)(2,1)S(1)} %constant_dynamic-update-slice_fusion.14), channel_id=1, source_target_pairs={{0,4},{4,0},{8,12},{12,8},{16,20},{20,16},{24,28},{28,24},{1,5},{5... | collective-permute-start | bytes 3145736 | tf_op jit(solution)/shard_map/ppermute | solution.py:760
  101.1 19.5 %copy-start.19 = (bf16[2,584,1024]{2,1,0:T(8,128)(2,1)S(1)}, bf16[2,584,1024]{2,1,0:T(8,128)(2,1)}, u32[]{:S(2)}) copy-start(bf16[2,584,1024]{2,1,0:T(8,128)(2,1)} %get-tuple-element.225.refs_4_) | copy-start | bytes 7176196
  120.7 7.1 %collective-permute-start.15 = (bf16[584,1024]{1,0:T(8,128)(2,1)}, bf16[584,1024]{1,0:T(8,128)(2,1)}, u32[]{:S(2)}, u32[]{:S(2)}) collective-permute-start(bf16[584,1024]{1,0:T(8,128)(2,1)} %get-tuple-element.215.refs_4_), channel_id=1, source_target_pairs={{0,1},{1,0},{2,3},{3,2},{4,5},{5,4},{6,7},{7,6},{8,9},{9,8},{10,11... | collective-permute-start | bytes 3588104 | tf_op jit(solution)/shard_map/ppermute | solution.py:772
  122.4 21.4 %collective-permute-start.14 = (bf16[584,1024]{1,0:T(8,128)(2,1)}, bf16[584,1024]{1,0:T(8,128)(2,1)}, u32[]{:S(2)}, u32[]{:S(2)}) collective-permute-start(bf16[584,1024]{1,0:T(8,128)(2,1)} %get-tuple-element.214.refs_4_), channel_id=1, source_target_pairs={{0,1},{1,0},{2,3},{3,2},{4,5},{5,4},{6,7},{7,6},{8,9},{9,8},{10,11... | collective-permute-start | bytes 3588104 | tf_op jit(solution)/shard_map/ppermute | solution.py:772
  125.1 13.9 %collective-permute-start.21 = (bf16[4,512,128]{2,1,0:T(8,128)(2,1)S(1)}, bf16[4,512,128]{2,1,0:T(8,128)(2,1)S(1)}, u32[]{:S(2)}, u32[]{:S(2)}) collective-permute-start(bf16[4,512,128]{2,1,0:T(8,128)(2,1)S(1)} %pad_maximum_fusion.4), channel_id=1, source_target_pairs={{0,4},{4,0},{8,12},{12,8},{16,20},{20,16},{24,28},{28,24},{1,5},{5... | collective-permute-start | bytes 1572872 | tf_op jit(solution)/shard_map/ppermute | solution.py:760
  126.3 13.6 %collective-permute-start.22 = (bf16[4,512,128]{2,1,0:T(8,128)(2,1)S(1)}, bf16[4,512,128]{2,1,0:T(8,128)(2,1)S(1)}, u32[]{:S(2)}, u32[]{:S(2)}) collective-permute-start(bf16[4,512,128]{2,1,0:T(8,128)(2,1)S(1)} %pad_maximum_fusion.5), channel_id=1, source_target_pairs={{0,2},{2,0},{1,3},{3,1},{4,6},{6,4},{5,7},{7,5},{8,10},{10,8},{9,1... | collective-permute-start | bytes 1572872 | tf_op jit(solution)/shard_map/ppermute | solution.py:768
  140.0 14.0 %copy-start.23 = (bf16[8,512,128]{2,1,0:T(8,128)(2,1)}, bf16[8,512,128]{2,1,0:T(8,128)(2,1)S(1)}, u32[]{:S(2)}) copy-start(bf16[8,512,128]{2,1,0:T(8,128)(2,1)S(1)} %constant_dynamic-update-slice_fusion.18.refs_3_) | copy-start | bytes 3145732
  140.0 27.0 %collective-permute-start.23 = (bf16[8,512,128]{2,1,0:T(8,128)(2,1)S(1)}, bf16[8,512,128]{2,1,0:T(8,128)(2,1)}, u32[]{:S(2)}, u32[]{:S(2)}) collective-permute-start(bf16[8,512,128]{2,1,0:T(8,128)(2,1)S(1)} %constant_dynamic-update-slice_fusion.18.refs_3_), channel_id=1, source_target_pairs={{0,2},{2,0},{1,3},{3,1},{4,6},{6,4},{5,7},{7,5},{8,10},{10,8},{9,1... | collective-permute-start | bytes 3145736 | tf_op jit(solution)/shard_map/ppermute | solution.py:768
  143.2 24.8 %collective-permute-start.24 = (bf16[8,512,128]{2,1,0:T(8,128)(2,1)}, bf16[8,512,128]{2,1,0:T(8,128)(2,1)}, u32[]{:S(2)}, u32[]{:S(2)}) collective-permute-start(bf16[8,512,128]{2,1,0:T(8,128)(2,1)} %constant_dynamic-update-slice_fusion.20.refs_5_), channel_id=1, source_target_pairs={{0,4},{4,0},{8,12},{12,8},{16,20},{20,16},{24,28},{28,24},{1,5},{5... | collective-permute-start | bytes 3145736 | tf_op jit(solution)/shard_map/ppermute | solution.py:760
  165.0 25.2 %collective-permute-start.26 = (bf16[8,512,128]{2,1,0:T(8,128)(2,1)}, bf16[8,512,128]{2,1,0:T(8,128)(2,1)S(1)}, u32[]{:S(2)}, u32[]{:S(2)}) collective-permute-start(bf16[8,512,128]{2,1,0:T(8,128)(2,1)} %get-tuple-element.227), channel_id=1, source_target_pairs={{0,4},{4,0},{8,12},{12,8},{16,20},{20,16},{24,28},{28,24},{1,5},{5... | collective-permute-start | bytes 3145736 | tf_op jit(solution)/shard_map/ppermute | solution.py:760
  166.5 23.8 %collective-permute-start.25 = (bf16[8,512,128]{2,1,0:T(8,128)(2,1)}, bf16[8,512,128]{2,1,0:T(8,128)(2,1)S(1)}, u32[]{:S(2)}, u32[]{:S(2)}) collective-permute-start(bf16[8,512,128]{2,1,0:T(8,128)(2,1)} %get-tuple-element.246), channel_id=1, source_target_pairs={{0,2},{2,0},{1,3},{3,1},{4,6},{6,4},{5,7},{7,5},{8,10},{10,8},{9,1... | collective-permute-start | bytes 3145736 | tf_op jit(solution)/shard_map/ppermute | solution.py:768
  190.1 19.5 %collective-permute-start.31 = (bf16[2,584,1024]{2,1,0:T(8,128)(2,1)}, bf16[2,584,1024]{2,1,0:T(8,128)(2,1)}, u32[]{:S(2)}, u32[]{:S(2)}) collective-permute-start(bf16[2,584,1024]{2,1,0:T(8,128)(2,1)} %get-tuple-element.264.refs_5_), channel_id=1, source_target_pairs={{0,1},{1,0},{2,3},{3,2},{4,5},{5,4},{6,7},{7,6},{8,9},{9,8},{10,11... | collective-permute-start | bytes 7176200 | tf_op jit(solution)/shard_map/ppermute | solution.py:772
  195.1 11.4 %copy-start.7 = (bf16[4,512,128]{2,1,0:T(8,128)(2,1)}, bf16[4,512,128]{2,1,0:T(8,128)(2,1)S(1)}, u32[]{:S(2)}) copy-start(bf16[4,512,128]{2,1,0:T(8,128)(2,1)S(1)} %get-tuple-element.267.refs_0_) | copy-start | bytes 1572868
  195.1 25.8 %collective-permute-start.29 = (bf16[4,512,128]{2,1,0:T(8,128)(2,1)}, bf16[4,512,128]{2,1,0:T(8,128)(2,1)S(1)}, u32[]{:S(2)}, u32[]{:S(2)}) collective-permute-start(bf16[4,512,128]{2,1,0:T(8,128)(2,1)} %get-tuple-element.262), channel_id=1, source_target_pairs={{0,4},{4,0},{8,12},{12,8},{16,20},{20,16},{24,28},{28,24},{1,5},{5... | collective-permute-start | bytes 1572872 | tf_op jit(solution)/shard_map/ppermute | solution.py:760
  195.3 25.7 %collective-permute-start.30 = (bf16[4,512,128]{2,1,0:T(8,128)(2,1)S(1)}, bf16[4,512,128]{2,1,0:T(8,128)(2,1)S(1)}, u32[]{:S(2)}, u32[]{:S(2)}) collective-permute-start(bf16[4,512,128]{2,1,0:T(8,128)(2,1)S(1)} %get-tuple-element.263), channel_id=1, source_target_pairs={{0,2},{2,0},{1,3},{3,1},{4,6},{6,4},{5,7},{7,5},{8,10},{10,8},{9,1... | collective-permute-start | bytes 1572872 | tf_op jit(solution)/shard_map/ppermute | solution.py:768
  196.2 13.3 %copy-start.26 = (f32[1,2048]{1,0:T(1,128)S(1)}, f32[1,2048]{1,0:T(1,128)}, u32[]{:S(2)}) copy-start(f32[1,2048]{1,0:T(1,128)} %get-tuple-element.248) | copy-start | bytes 24580
  206.5 28.0 %collective-permute-start.27 = (bf16[8,512,128]{2,1,0:T(8,128)(2,1)}, bf16[8,512,128]{2,1,0:T(8,128)(2,1)S(1)}, u32[]{:S(2)}, u32[]{:S(2)}) collective-permute-start(bf16[8,512,128]{2,1,0:T(8,128)(2,1)} %get-tuple-element.258), channel_id=1, source_target_pairs={{0,2},{2,0},{1,3},{3,1},{4,6},{6,4},{5,7},{7,5},{8,10},{10,8},{9,1... | collective-permute-start | bytes 3145736 | tf_op jit(solution)/shard_map/ppermute | solution.py:768
  207.7 26.8 %collective-permute-start.28 = (bf16[8,512,128]{2,1,0:T(8,128)(2,1)}, bf16[8,512,128]{2,1,0:T(8,128)(2,1)S(1)}, u32[]{:S(2)}, u32[]{:S(2)}) collective-permute-start(bf16[8,512,128]{2,1,0:T(8,128)(2,1)} %get-tuple-element.260), channel_id=1, source_target_pairs={{0,4},{4,0},{8,12},{12,8},{16,20},{20,16},{24,28},{28,24},{1,5},{5... | collective-permute-start | bytes 3145736 | tf_op jit(solution)/shard_map/ppermute | solution.py:760
  225.2 40.4 %collective-permute-start.34 = (bf16[1024,128]{1,0:T(8,128)(2,1)}, bf16[1024,128]{1,0:T(8,128)(2,1)}, u32[]{:S(2)}, u32[]{:S(2)}) collective-permute-start(bf16[1024,128]{1,0:T(8,128)(2,1)} %get-tuple-element.272), channel_id=1, source_target_pairs={{0,8},{4,12},{8,0},{12,4},{16,24},{20,28},{24,16},{28,20},{1,9},{5... | collective-permute-start | bytes 786440 | tf_op jit(solution)/shard_map/ppermute | solution.py:757
  225.8 39.9 %collective-permute-start.35 = (bf16[1024,128]{1,0:T(8,128)(2,1)}, bf16[1024,128]{1,0:T(8,128)(2,1)}, u32[]{:S(2)}, u32[]{:S(2)}) collective-permute-start(bf16[1024,128]{1,0:T(8,128)(2,1)} %get-tuple-element.273), channel_id=1, source_target_pairs={{0,16},{4,20},{8,24},{12,28},{16,0},{20,4},{24,8},{28,12},{1,17},{... | collective-permute-start | bytes 786440 | tf_op jit(solution)/shard_map/ppermute | solution.py:757
  228.2 37.5 %collective-permute-start.36 = (bf16[1024,128]{1,0:T(8,128)(2,1)S(1)}, bf16[1024,128]{1,0:T(8,128)(2,1)}, u32[]{:S(2)}, u32[]{:S(2)}) collective-permute-start(bf16[1024,128]{1,0:T(8,128)(2,1)S(1)} %get-tuple-element.274), channel_id=1, source_target_pairs={{0,24},{4,28},{8,16},{12,20},{16,8},{20,12},{24,0},{28,4},{1,25},{... | collective-permute-start | bytes 786440 | tf_op jit(solution)/shard_map/ppermute | solution.py:757
  238.6 29.5 %collective-permute-start.32 = (bf16[4,512,128]{2,1,0:T(8,128)(2,1)}, bf16[4,512,128]{2,1,0:T(8,128)(2,1)S(1)}, u32[]{:S(2)}, u32[]{:S(2)}) collective-permute-start(bf16[4,512,128]{2,1,0:T(8,128)(2,1)} %get-tuple-element.283), channel_id=1, source_target_pairs={{0,4},{4,0},{8,12},{12,8},{16,20},{20,16},{24,28},{28,24},{1,5},{5... | collective-permute-start | bytes 1572872 | tf_op jit(solution)/shard_map/ppermute | solution.py:760
  238.8 29.4 %collective-permute-start.33 = (bf16[4,512,128]{2,1,0:T(8,128)(2,1)S(1)}, bf16[4,512,128]{2,1,0:T(8,128)(2,1)S(1)}, u32[]{:S(2)}, u32[]{:S(2)}) collective-permute-start(bf16[4,512,128]{2,1,0:T(8,128)(2,1)S(1)} %get-tuple-element.285), channel_id=1, source_target_pairs={{0,2},{2,0},{1,3},{3,1},{4,6},{6,4},{5,7},{7,5},{8,10},{10,8},{9,1... | collective-permute-start | bytes 1572872 | tf_op jit(solution)/shard_map/ppermute | solution.py:768
  239.8 25.0 %copy-start.27 = (f32[4,1024]{1,0:T(4,128)S(1)}, f32[4,1024]{1,0:T(4,128)}, u32[]{:S(2)}) copy-start(f32[4,1024]{1,0:T(4,128)} %get-tuple-element.266) | copy-start | bytes 49156
  239.8 25.9 %copy-start.16 = (bf16[1024,128]{1,0:T(8,128)(2,1)S(1)}, bf16[1024,128]{1,0:T(8,128)(2,1)}, u32[]{:S(2)}) copy-start(bf16[1024,128]{1,0:T(8,128)(2,1)} %copy-done.15) | copy-start | bytes 786436
  265.6 28.9 %collective-permute-start.38 = (bf16[2,584,1024]{2,1,0:T(8,128)(2,1)}, bf16[2,584,1024]{2,1,0:T(8,128)(2,1)}, u32[]{:S(2)}, u32[]{:S(2)}) collective-permute-start(bf16[2,584,1024]{2,1,0:T(8,128)(2,1)} %bitcast.133), channel_id=1, source_target_pairs={{0,1},{1,0},{2,3},{3,2},{4,5},{5,4},{6,7},{7,6},{8,9},{9,8},{10,11... | collective-permute-start | bytes 7176200 | tf_op jit(solution)/shard_map/ppermute | solution.py:772
  277.5 31.8 %collective-permute-start.39 = (bf16[8,512,128]{2,1,0:T(8,128)(2,1)}, bf16[8,512,128]{2,1,0:T(8,128)(2,1)S(1)}, u32[]{:S(2)}, u32[]{:S(2)}) collective-permute-start(bf16[8,512,128]{2,1,0:T(8,128)(2,1)} %get-tuple-element.306), channel_id=1, source_target_pairs={{0,2},{2,0},{1,3},{3,1},{4,6},{6,4},{5,7},{7,5},{8,10},{10,8},{9,1... | collective-permute-start | bytes 3145736 | tf_op jit(solution)/shard_map/ppermute | solution.py:768
  278.7 30.7 %collective-permute-start.40 = (bf16[8,512,128]{2,1,0:T(8,128)(2,1)}, bf16[8,512,128]{2,1,0:T(8,128)(2,1)S(1)}, u32[]{:S(2)}, u32[]{:S(2)}) collective-permute-start(bf16[8,512,128]{2,1,0:T(8,128)(2,1)} %get-tuple-element.307), channel_id=1, source_target_pairs={{0,4},{4,0},{8,12},{12,8},{16,20},{20,16},{24,28},{28,24},{1,5},{5... | collective-permute-start | bytes 3145736 | tf_op jit(solution)/shard_map/ppermute | solution.py:760
  280.5 14.0 %collective-permute-start.37 = (bf16[2,1024,128]{2,1,0:T(8,128)(2,1)}, bf16[2,1024,128]{2,1,0:T(8,128)(2,1)S(1)}, u32[]{:S(2)}, u32[]{:S(2)}) collective-permute-start(bf16[2,1024,128]{2,1,0:T(8,128)(2,1)} %get-tuple-element.302), channel_id=1, source_target_pairs={{0,8},{4,12},{8,0},{12,4},{16,24},{20,28},{24,16},{28,20},{1,9},{5... | collective-permute-start | bytes 1572872 | tf_op jit(solution)/shard_map/ppermute | solution.py:757
  309.2 7.2 %collective-permute-start.44 = (bf16[2,584,1024]{2,1,0:T(8,128)(2,1)}, bf16[2,584,1024]{2,1,0:T(8,128)(2,1)S(1)}, u32[]{:S(2)}, u32[]{:S(2)}) collective-permute-start(bf16[2,584,1024]{2,1,0:T(8,128)(2,1)} %grad_one.1.refs_4_), channel_id=1, source_target_pairs={{0,1},{1,0},{2,3},{3,2},{4,5},{5,4},{6,7},{7,6},{8,9},{9,8},{10,11... | collective-permute-start | bytes 7176200 | tf_op jit(solution)/shard_map/ppermute | solution.py:772
  314.1 14.5 %collective-permute-start.41 = (bf16[4,512,128]{2,1,0:T(8,128)(2,1)}, bf16[4,512,128]{2,1,0:T(8,128)(2,1)S(1)}, u32[]{:S(2)}, u32[]{:S(2)}) collective-permute-start(bf16[4,512,128]{2,1,0:T(8,128)(2,1)} %get-tuple-element.325), channel_id=1, source_target_pairs={{0,4},{4,0},{8,12},{12,8},{16,20},{20,16},{24,28},{28,24},{1,5},{5... | collective-permute-start | bytes 1572872 | tf_op jit(solution)/shard_map/ppermute | solution.py:760
  314.4 14.2 %collective-permute-start.42 = (bf16[4,512,128]{2,1,0:T(8,128)(2,1)}, bf16[4,512,128]{2,1,0:T(8,128)(2,1)S(1)}, u32[]{:S(2)}, u32[]{:S(2)}) collective-permute-start(bf16[4,512,128]{2,1,0:T(8,128)(2,1)} %get-tuple-element.327), channel_id=1, source_target_pairs={{0,2},{2,0},{1,3},{3,1},{4,6},{6,4},{5,7},{7,5},{8,10},{10,8},{9,1... | collective-permute-start | bytes 1572872 | tf_op jit(solution)/shard_map/ppermute | solution.py:768
  315.2 16.9 %collective-permute-start.43 = (bf16[1,1024,128]{2,1,0:T(8,128)(2,1)S(1)}, bf16[1,1024,128]{2,1,0:T(8,128)(2,1)S(1)}, u32[]{:S(2)}, u32[]{:S(2)}) collective-permute-start(bf16[1,1024,128]{2,1,0:T(8,128)(2,1)S(1)} %copy-done.2), channel_id=1, source_target_pairs={{0,16},{4,20},{8,24},{12,28},{16,0},{20,4},{24,8},{28,12},{1,17},{... | collective-permute-start | bytes 786440 | tf_op jit(solution)/shard_map/ppermute | solution.py:757
  317.8 18.0 %copy-start.12 = (bf16[4,512,128]{2,1,0:T(8,128)(2,1)S(1)}, bf16[4,512,128]{2,1,0:T(8,128)(2,1)}, u32[]{:S(2)}) copy-start(bf16[4,512,128]{2,1,0:T(8,128)(2,1)} %copy-done.11) | copy-start | bytes 1572868
  317.9 18.0 %copy-start.14 = (bf16[4,512,128]{2,1,0:T(8,128)(2,1)S(1)}, bf16[4,512,128]{2,1,0:T(8,128)(2,1)}, u32[]{:S(2)}) copy-start(bf16[4,512,128]{2,1,0:T(8,128)(2,1)} %copy-done.13) | copy-start | bytes 1572868
  328.6 4.8 %collective-permute-start.45 = (f32[4,16,128]{2,1,0:T(8,128)}, f32[4,16,128]{2,1,0:T(8,128)S(1)}, u32[]{:S(2)}, u32[]{:S(2)}) collective-permute-start(f32[4,16,128]{2,1,0:T(8,128)} %get-tuple-element.342), channel_id=1, source_target_pairs={{0,4},{2,6},{4,0},{6,2},{8,12},{10,14},{12,8},{14,10},{16,20},{18,... | collective-permute-start | bytes 98312 | tf_op jit(solution)/shard_map/ppermute | solution.py:765
  330.4 4.1 %collective-permute-start.46 = (f32[4,16,128]{2,1,0:T(8,128)}, f32[4,16,128]{2,1,0:T(8,128)S(1)}, u32[]{:S(2)}, u32[]{:S(2)}) collective-permute-start(f32[4,16,128]{2,1,0:T(8,128)} %get-tuple-element.343), channel_id=1, source_target_pairs={{0,2},{2,0},{4,6},{6,4},{8,10},{10,8},{12,14},{14,12},{16,18},{18,... | collective-permute-start | bytes 98312 | tf_op jit(solution)/shard_map/ppermute | solution.py:765
  330.8 5.0 %collective-permute-start.47 = (f32[4,16,128]{2,1,0:T(8,128)}, f32[4,16,128]{2,1,0:T(8,128)S(1)}, u32[]{:S(2)}, u32[]{:S(2)}) collective-permute-start(f32[4,16,128]{2,1,0:T(8,128)} %get-tuple-element.344), channel_id=1, source_target_pairs={{0,6},{2,4},{4,2},{6,0},{8,14},{10,12},{12,10},{14,8},{16,22},{18,... | collective-permute-start | bytes 98312 | tf_op jit(solution)/shard_map/ppermute | solution.py:765
  337.7 11.2 %collective-permute-start.48 = (bf16[1040,128]{1,0:T(8,128)(2,1)S(1)}, bf16[1040,128]{1,0:T(8,128)(2,1)S(1)}, u32[]{:S(2)}, u32[]{:S(2)}) collective-permute-start(bf16[1040,128]{1,0:T(8,128)(2,1)S(1)} %get-tuple-element.346), channel_id=1, source_target_pairs={{0,8},{4,12},{8,0},{12,4},{16,24},{20,28},{24,16},{28,20},{1,9},{5... | collective-permute-start | bytes 798728 | tf_op jit(solution)/shard_map/ppermute | solution.py:757
  338.1 20.9 %collective-permute-start.49 = (bf16[1040,128]{1,0:T(8,128)(2,1)S(1)}, bf16[1040,128]{1,0:T(8,128)(2,1)S(1)}, u32[]{:S(2)}, u32[]{:S(2)}) collective-permute-start(bf16[1040,128]{1,0:T(8,128)(2,1)S(1)} %get-tuple-element.347), channel_id=1, source_target_pairs={{0,16},{4,20},{8,24},{12,28},{16,0},{20,4},{24,8},{28,12},{1,17},{... | collective-permute-start | bytes 798728 | tf_op jit(solution)/shard_map/ppermute | solution.py:757
  340.8 18.2 %collective-permute-start.50 = (bf16[1040,128]{1,0:T(8,128)(2,1)S(1)}, bf16[1040,128]{1,0:T(8,128)(2,1)S(1)}, u32[]{:S(2)}, u32[]{:S(2)}) collective-permute-start(bf16[1040,128]{1,0:T(8,128)(2,1)S(1)} %get-tuple-element.348), channel_id=1, source_target_pairs={{0,24},{4,28},{8,16},{12,20},{16,8},{20,12},{24,0},{28,4},{1,25},{... | collective-permute-start | bytes 798728 | tf_op jit(solution)/shard_map/ppermute | solution.py:757
  (18 other events, 32.4 us)

commit v5 on v4

--- a/solution.py
+++ b/solution.py
@@ -13,6 +13,7 @@
 BF = jnp.bfloat16
 F32 = jnp.float32
 VMEM_LIMIT = 60 * 1024 * 1024
+WHOLE_VMEM = ("arrange_pair", "vectors", "attn_forward", "mlp_up", "down_grad", "mlp_back")
 COST_SCALE = 1.0
 COST = {
     "arrange_pair": 5,
@@ -60,7 +61,15 @@
             copy.wait()
 
 
-def call(body, ins, outs, scratch, name, flops, aliases=None, smem=(), sems=48, vmem_ins=(), vmem=VMEM_LIMIT):
+def padded_bytes(value):
+    lead, (rows, lanes) = value.shape[:-2], value.shape[-2:]
+    count = -(-rows // 16) * 16 * (-(-lanes // 128) * 128)
+    for size in lead:
+        count *= size
+    return count * jnp.dtype(value.dtype).itemsize
+
+
+def call(body, ins, outs, scratch, name, flops, aliases=None, smem=(), sems=48, vmem_ins=(), spare=12):
     n_smem, n_vmem, n_in, n_out = len(smem), len(vmem_ins), len(ins), len(outs)
     moved = sum(a.size * a.dtype.itemsize for a in ins) + sum(
         o.size * o.dtype.itemsize for o in outs
@@ -74,6 +83,8 @@
         rest = refs[first + n_in + n_out :]
         body(small, in_refs, out_refs, rest[:-1], Loads(rest[-1]))
 
+    held = sum(padded_bytes(piece) for piece in scratch) + spare * 1024 * 1024
+    vmem = VMEM_LIMIT if name in WHOLE_VMEM else min(held, VMEM_LIMIT)
     flops = max(COST.get(name, 3), 0.02) * COST_SCALE * 1.15e9
     moved = 0
     any_spec = pl.BlockSpec(memory_space=pl.ANY)
@@ -654,7 +665,7 @@
         "attn_backward",
         0,
     )
-    return grads.reshape(3 * n, 2 * seq, 128), jnp.sum(sums.reshape(n, 2, 2, 128), axis=1)
+    return grads.reshape(3 * n, 2 * seq, 128), sums
 
 
 def finish_layer(ids, keep, nv, middle, part, recv, nd, aligned):
@@ -683,16 +694,17 @@
     )[0]
 
 
-def finish_tokens(ids, nv, tok, part, recv, gmid, rest, nd, aligned):
+def finish_tokens(ids, nv, tok, part, recv, gmid, rest, sums, nd, aligned):
     _, seq, width = tok.shape
-    n_dest, z_n = rest.shape[:2]
-    bd = width // nd
+    n_dest, z_n, n_rows, lanes = rest.shape
+    bd, y_n = width // nd, nd // rest.shape[1]
+    tx = n_dest // y_n
 
     def body(small, ins, outs, scratch, loads):
-        ids_ref, nv_ref = small
+        ids_ref, nv_ref = small[:2]
         mine = ids_ref[0]
         tok_s, part_s, recv_s, gm_s, out_s, cs_s, rest_s = scratch
-        g_rest = loads.start([(ins[4], rest_s)])
+        g_rest = loads.start([(ins[4], rest_s)] if sums is None else [])
         groups = [
             loads.start(
                 [
@@ -724,6 +736,29 @@
                 cs_s[0:1, :] = cs_s[0:1, :] + gain_sum
                 cs_s[1:2, :] = cs_s[1:2, :] + shift_sum
         loads.wait(g_rest)
+        if sums is not None:
+            col_ref, bup_ref, pairs = small[2], small[3], small[4:]
+            up = bup_ref.shape[1] // tx // nd
+            n_pairs = sum(ref.shape[0] // 2 for ref in pairs)
+            qv = n_pairs * 128 // tx // nd
+            per = 128 // qv
+            lane = lax.broadcasted_iota(jnp.int32, (2, 128), 1)
+            whole = [ref[2 * i] + ref[2 * i + 1] for ref in pairs for i in range(ref.shape[0] // 2)]
+            whole = jnp.stack(whole)
+            rest_s[...] = jnp.zeros_like(rest_s)
+            for n in range(n_dest):
+                kx, ky = n // y_n, n % y_n
+                for kz in range(z_n):
+                    p = ky * z_n + kz
+                    d = ids_ref[2 + p]
+                    rest_s[n, kz, 2:6, :] = col_ref[:, p * bd : (p + 1) * bd]
+                    row = jnp.zeros((2, 128), F32)
+                    for i in range(nd // per):
+                        row = jnp.where(d // per == i, whole[kx * (nd // per) + i], row)
+                    row = pltpu.roll(row, (per - d % per) * qv % 128, 1)
+                    rest_s[n, kz, 6:8, :] = jnp.where(lane < qv, row, 0.0)
+                    cols = pl.ds(pl.multiple_of((kx * nd + d) * up, 128), up)
+                    rest_s[n, kz, 8:9, 0:up] = bup_ref[:, cols]
         for n in range(n_dest if aligned else 0):
             for kz in range(z_n):
                 p = n % (nd // z_n) * z_n + kz
@@ -735,7 +770,7 @@
 
     return call(
         body,
-        [tok, gmid, part, recv, rest],
+        [tok, gmid, part, recv] + ([rest] if sums is None else []),
         [sds((seq, width), BF), sds((2, width), F32)] + [sds(rest.shape[1:], F32)] * n_dest,
         [pltpu.VMEM((2, seq, width), BF)] * 3
         + [pltpu.VMEM((seq, width), F32), pltpu.VMEM((seq, width), BF), pltpu.VMEM((2, width), F32)]
@@ -743,7 +778,7 @@
         "finish_tokens",
         200 * seq * width,
         smem=(ids,),
-        vmem_ins=(nv,),
+        vmem_ins=(nv,) + tuple(sums or ()),
     )
 
 
@@ -799,14 +834,6 @@
     a_all = [a_y] + [grid.send_x(a_y, k) for k in range(1, grid.tx)]
     b_all = [b_x] + [grid.send_y(b_x, k) for k in range(1, grid.y)]
     return a_all, b_all
-
-
-def padded_bytes(value):
-    lead, (rows, lanes) = value.shape[:-2], value.shape[-2:]
-    count = -(-rows // 16) * 16 * (-(-lanes // 128) * 128)
-    for size in lead:
-        count *= size
-    return count * value.dtype.itemsize
 
 
 def add_pieces(groups, cuts, outs, name):
@@ -834,7 +861,6 @@
         for group in done:
             loads.wait(group)
 
-    held = sum(padded_bytes(a) for a in list(arrays) + list(outs))
     return call(
         body,
         arrays,
@@ -842,7 +868,7 @@
         [pltpu.VMEM(a.shape, a.dtype) for a in arrays] + [pltpu.VMEM(o.shape, o.dtype) for o in outs],
         name,
         0,
-        vmem=held + 8 * 1024 * 1024,
+        spare=8,
     )
 
 
@@ -1205,7 +1231,7 @@
         )
         grads = list(kept) + list(sent)
         lefts, starts = [left_a, left_b], [1, 0]
-        bias_qv = jnp.concatenate([bias_b, bias_a])
+        pair_sums = [bias_b, bias_a]
         gate = kept[0]
     else:
         while 2 * up_rs.bit < z_n:
@@ -1224,9 +1250,8 @@
             hh < bd,
         )
         lefts, starts = [left_a], [0]
-        bias_qv = bias_a
+        pair_sums = [bias_a]
         gate = grads[-1]
-    bias_qv = bias_qv.transpose(1, 0, 2).reshape(2, ext)
     qkv_rs = send_grad(grads, "qkv")
     lefts = after(lefts, gate)
     one_part = input_grad(lefts, starts, wqkv, width)
@@ -1239,25 +1264,32 @@
     up_cuts = cuts
     qkv_half = qkv_rs.second(one_part)
     wide = max(bd, hw // dp, fw // dp)
-    vec = jnp.concatenate([jnp.zeros((2, width), F32), col])
-    vec = vec.reshape(6, y_n, z_n, bd).transpose(1, 2, 0, 3)
-    bias_qv = bias_qv.reshape(2, tx, dp, hw // dp).transpose(2, 1, 0, 3)
-    bias_up = bias_up.reshape(tx, 1, dp, fw // dp).transpose(2, 0, 1, 3)
-    bias = jnp.concatenate(
-        [
-            jnp.pad(value, ((0, 0), (0, 0), (0, 0), (0, wide - value.shape[3])))
-            for value in (bias_qv, bias_up)
-        ],
-        axis=2,
-    )
-    bias = from_abs(xor_blocks(bias, me_d, 0), 0).reshape(y_n, z_n, tx, 3, wide)
-    bias = bias.transpose(2, 0, 1, 3, 4)
-    vec = jnp.pad(vec, ((0, 0), (0, 0), (0, 0), (0, wide - bd)))
-    vec = jnp.broadcast_to(vec, (tx,) + vec.shape)
-    rest = jnp.concatenate([vec, bias, jnp.zeros((tx, y_n, z_n, 7, wide), F32)], axis=3)
-    rest = rest.reshape(tx * y_n, z_n, 16, wide)
+    if split and fw // dp == bd and 128 % (hw // dp) == 0:
+        rest = sds((tx * y_n, z_n, 16, wide), F32)
+        sums = [col, bias_up] + pair_sums
+    else:
+        bias_qv = jnp.concatenate(pair_sums)
+        bias_qv = jnp.sum(bias_qv.reshape(n_pairs, 2, 2, 128), axis=1).transpose(1, 0, 2)
+        vec = jnp.concatenate([jnp.zeros((2, width), F32), col])
+        vec = vec.reshape(6, y_n, z_n, bd).transpose(1, 2, 0, 3)
+        bias_qv = bias_qv.reshape(2, tx, dp, hw // dp).transpose(2, 1, 0, 3)
+        bias_up = bias_up.reshape(tx, 1, dp, fw // dp).transpose(2, 0, 1, 3)
+        bias = jnp.concatenate(
+            [
+                jnp.pad(value, ((0, 0), (0, 0), (0, 0), (0, wide - value.shape[3])))
+                for value in (bias_qv, bias_up)
+            ],
+            axis=2,
+        )
+        bias = from_abs(xor_blocks(bias, me_d, 0), 0).reshape(y_n, z_n, tx, 3, wide)
+        bias = bias.transpose(2, 0, 1, 3, 4)
+        vec = jnp.pad(vec, ((0, 0), (0, 0), (0, 0), (0, wide - bd)))
+        vec = jnp.broadcast_to(vec, (tx,) + vec.shape)
+        rest = jnp.concatenate([vec, bias, jnp.zeros((tx, y_n, z_n, 7, wide), F32)], axis=3)
+        rest = rest.reshape(tx * y_n, z_n, 16, wide)
+        sums = None
     grad_tokens, one_sums, *small = finish_tokens(
-        ids, nv, tok, one_part, after(one_recv, qkv_half), gmid, rest, dp, aligned
+        ids, nv, tok, one_part, after(one_recv, qkv_half), gmid, rest, sums, dp, aligned
     )
     if not aligned:
         ones = jnp.pad(one_sums.reshape(2, y_n, z_n, bd), ((0, 14), (0, 0), (0, 0), (0, wide - bd)))

time: 370 us -> 353 us (0.954)
  Pallas kernels: 204 us -> 182 us
  waiting for transfers between devices: 62.2 us -> 73.1 us
  local copies, waits for them, and re-layouts: 27.9 us -> 23.2 us
    pallas_call x28, Pallas kernels: 204 us -> 182 us  [call(): pl.pallas_call(kernel, out_shape=outs, in_specs=[pl.BlockSpec(memory_spac...]
    ppermute x12, waiting for transfers between devices: 5.5 us -> 14.3 us  [send_x(): return lax.ppermute(value, 'tx', [(i, i ^ k) for i in range(self.tx)])]
    unnamed x76, local copies, waits for them, and re-layouts: 17.1 us -> 11 us
  transfers between devices with their start and end apart: 51 -> 51, of which waited for: 17 -> 18; matrix products, arithmetic and copies ran while one was open for 4% -> 4% of each run, Pallas kernels for 56% -> 52%
where the time goes in v5:
time: 353 us; the launch traced here: 346 us
  Pallas kernels  182 us (52%)
  waiting for transfers between devices  73.1 us (21%)
  starting transfers between devices  62.6 us (18%)
  local copies, waits for them, and re-layouts  23.2 us (7%)
    pallas_call x28, Pallas kernels, call(): pl.pallas_call(kernel, out_shape=outs, in_specs=[pl.BlockSpec(memory_spac...  182 us
    ppermute x17, starting transfers between devices, send_z(): lax.ppermute(value, 'dp', [(i, i ^ k * self.y) for i in range(self.dp)])  31.8 us
    ppermute x17, waiting for transfers between devices, send_z(): lax.ppermute(value, 'dp', [(i, i ^ k * self.y) for i in range(self.dp)])  31.5 us
    ppermute x12, waiting for transfers between devices, send_y(): return lax.ppermute(value, 'dp', [(i, i ^ k) for i in range(self.dp)])  26.2 us
    ppermute x12, waiting for transfers between devices, send_x(): return lax.ppermute(value, 'tx', [(i, i ^ k) for i in range(self.tx)])  14.3 us
    ppermute x12, starting transfers between devices, send_x(): return lax.ppermute(value, 'tx', [(i, i ^ k) for i in range(self.tx)])  13.4 us
    ppermute x12, starting transfers between devices, send_y(): return lax.ppermute(value, 'dp', [(i, i ^ k) for i in range(self.dp)])  12.5 us
    unnamed x76, local copies, waits for them, and re-layouts  11 us
  transfers between devices with their start and end apart: 51, of which 18 were waited for; matrix products, arithmetic and copies ran while one was open for 4% of the time, Pallas kernels for 52%

profile of v5, /device:TPU:0, one launch (start us, length us, event | category | flops | bytes accessed | tf_op | source)
XLA Modules:
  0.0 346.3 jit_solution(6362174129500709143)
XLA Ops:
  3.6 1.5 concatenate.32
  5.1 3.1 collective-permute-start
  8.2 2.6 collective-permute-start.1
  12.4 4.8 %arrange_pair.1 = (bf16[2,584,1024]{2,1,0:T(8,128)(2,1)}, bf16[2,584,1024]{2,1,0:T(8,128)(2,1)}) custom-call(s32[10]{0:T(128)} %stack.130.refs_0_, bf16[584,1024]{1,0:T(8,128)(2,1)} %refs_1_.1, bf16[584,1024]{1,0:T(8,128)(2,1)} %refs_2_.1, bf16[584,1024]{1,0:T(8,128)(2,1)} %copy-done.30, bf16[584,1024]{1,0:T(8,128)(2,1)} %collective-permute-done.4.refs_4_), custom_call_target="tpu_custom_call" | custom-call | flops 5750000128 | bytes 5750000 | tf_op jit(solution)/shard_map/arrange_pair/pallas_call | solution.py:91
  17.2 2.7 collective-permute-done
  19.9 9.9 %collective-permute-done.1 = bf16[1040,128]{1,0:T(8,128)(2,1)S(1)} collective-permute-done((bf16[1040,128]{1,0:T(8,128)(2,1)S(1)}, bf16[1040,128]{1,0:T(8,128)(2,1)S(1)}, u32[]{:S(2)}, u32[]{:S(2)}) %collective-permute-start.1) | collective-permute-done | bytes 266272 | tf_op jit(solution)/shard_map/ppermute | solution.py:792
  30.1 1.6 collective-permute-start.5
  31.8 1.6 collective-permute-start.7
  33.4 8.8 %collective-permute-done.5 = bf16[4,528,128]{2,1,0:T(8,128)(2,1)S(1)} collective-permute-done((bf16[4,528,128]{2,1,0:T(8,128)(2,1)S(1)}, bf16[4,528,128]{2,1,0:T(8,128)(2,1)S(1)}, u32[]{:S(2)}, u32[]{:S(2)}) %collective-permute-start.5) | collective-permute-done | bytes 540704 | tf_op jit(solution)/shard_map/ppermute | solution.py:795
  42.3 1.6 collective-permute-start.6
  46.2 6.2 %collective-permute-start.9 = (bf16[256,512]{1,0:T(8,128)(2,1)S(1)}, bf16[256,512]{1,0:T(8,128)(2,1)S(1)}, u32[]{:S(2)}, u32[]{:S(2)}) collective-permute-start(bf16[256,512]{1,0:T(8,128)(2,1)S(1)} %constant_dynamic-update-slice_fusion.10), channel_id=1, source_target_pairs={{0,8},{4,12},{8,0},{12,4},{16,24},{20,28},{24,16},{28,20},{1,9},{5... | collective-permute-start | bytes 786440 | tf_op jit(solution)/shard_map/ppermute | solution.py:792
  53.6 1.4 collective-permute-start.11
  54.9 11.0 %collective-permute-done.8.refs_6_.refs_10_.refs_11_.refs_15_.refs_5_ = bf16[8,512,128]{2,1,0:T(8,128)(2,1)} collective-permute-done((bf16[8,512,128]{2,1,0:T(8,128)(2,1)S(1)}, bf16[8,512,128]{2,1,0:T(8,128)(2,1)}, u32[]{:S(2)}, u32[]{:S(2)}) %collective-permute-start.8) | collective-permute-done | bytes 1048608 | tf_op jit(solution)/shard_map/ppermute | solution.py:795
  66.6 2.6 vectors.1
  69.2 3.7 %collective-permute-done.10 = bf16[256,512]{1,0:T(8,128)(2,1)S(1)} collective-permute-done((bf16[256,512]{1,0:T(8,128)(2,1)S(1)}, bf16[256,512]{1,0:T(8,128)(2,1)S(1)}, u32[]{:S(2)}, u32[]{:S(2)}) %collective-permute-start.10) | collective-permute-done | bytes 262176 | tf_op jit(solution)/shard_map/ppermute | solution.py:792
  74.7 15.9 %attn_forward.2 = (bf16[2,584,1024]{2,1,0:T(8,128)(2,1)}, bf16[2,584,512]{2,1,0:T(8,128)(2,1)}, bf16[2,584,512]{2,1,0:T(8,128)(2,1)}, bf16[2,584,512]{2,1,0:T(8,...) custom-call(f32[6,1024]{1,0:T(8,128)} %get-tuple-element.191.refs_0_.refs_1_.refs_2_, ...), custom_call_target="tpu_custom_call" | custom-call | flops 18400000000 | bytes 18400000 | tf_op jit(solution)/shard_map/attn_forward/pallas_call | solution.py:91
  92.5 3.9 %collective-permute-start.18 = (bf16[1024,128]{1,0:T(8,128)(2,1)S(1)}, bf16[1024,128]{1,0:T(8,128)(2,1)S(1)}, u32[]{:S(2)}, u32[]{:S(2)}) collective-permute-start(bf16[1024,128]{1,0:T(8,128)(2,1)S(1)} %constant_dynamic-update-slice_fusion.16), channel_id=1, source_target_pairs={{0,8},{4,12},{8,0},{12,4},{16,24},{20,28},{24,16},{28,20},{1,9},{5... | collective-permute-start | bytes 786440 | tf_op jit(solution)/shard_map/ppermute | solution.py:792
  97.4 1.4 collective-permute-start.20
  101.0 16.2 %attn_forward.3 = (bf16[2,584,1024]{2,1,0:T(8,128)(2,1)}, bf16[2,584,512]{2,1,0:T(8,128)(2,1)}, bf16[2,584,512]{2,1,0:T(8,128)(2,1)}, bf16[2,584,512]{2,1,0:T(8,...) custom-call(f32[6,1024]{1,0:T(8,128)} %get-tuple-element.191.refs_0_, ...), custom_call_target="tpu_custom_call", output_to_operand_aliasing={{0}: (3, {}), {1}: (4, {}), {2}: (5, {}), {3}: (6, {}), {4}... | custom-call | flops 18400000000 | bytes 18400000 | tf_op jit(solution)/shard_map/attn_forward/pallas_call | solution.py:91
  117.2 3.3 collective-permute-done.16
  120.5 1.7 broadcast_multiply_fusion
  126.1 1.6 collective-permute-start.22
  127.6 10.1 %mlp_up.2 = (f32[2,584,1024]{2,1,0:T(8,128)}, bf16[2,584,1024]{2,1,0:T(8,128)(2,1)}, bf16[2,584,2048]{2,1,0:T(8,128)(2,1)}, bf16[2,584,2048]{2,1,0:T(8,128)(2,1)}) custom-call(f32[2]{0:T(128)} %get-tuple-element.359.refs_0_.refs_1_, f32[6,1024]{1,0:T(8,128)} %get-tuple-element.191.refs_0_.refs_1_.refs_2_, f32[1,2048]{1,0:T(1,128)} %get-tuple-element.192.refs_2_, ...), custom_call_target="tpu_custom_call" | custom-call | flops 11500000256 | bytes 11500000 | tf_op jit(solution)/shard_map/mlp_up/pallas_call | solution.py:91
  141.5 1.5 collective-permute-start.23
  143.8 1.8 constant_dynamic-update-slice_fusion.20.refs_5_
  146.3 10.1 %mlp_up.3 = (f32[2,584,1024]{2,1,0:T(8,128)}, bf16[2,584,1024]{2,1,0:T(8,128)(2,1)}, bf16[2,584,2048]{2,1,0:T(8,128)(2,1)}, bf16[2,584,2048]{2,1,0:T(8,128)(2,1)}) custom-call(f32[2]{0:T(128)} %get-tuple-element.359.refs_0_.refs_1_, ...), custom_call_target="tpu_custom_call", output_to_operand_aliasing={{0}: (6, {}), {1}: (7, {}), {2}: (8, {}), {3}: (9, {})} | custom-call | flops 11500000256 | bytes 11500000 | tf_op jit(solution)/shard_map/mlp_up/pallas_call | solution.py:91
  156.4 10.8 %down_grad.1 = (bf16[8,512,128]{2,1,0:T(8,128)(2,1)}, bf16[8,512,128]{2,1,0:T(8,128)(2,1)}, bf16[8,512,128]{2,1,0:T(8,128)(2,1)}, bf16[8,512,128]{2,1,0:T(8,128)(2,1)}) custom-call(bf16[1168,2048]{1,0:T(8,128)(2,1)} %bitcast.111, bf16[1168,1024]{1,0:T(8,128)(2,1)} %bitcast.103), custom_call_target="tpu_custom_call" | custom-call | flops 12650000384 | bytes 12650000 | tf_op jit(solution)/shard_map/down_grad/pallas_call | solution.py:91
  167.3 1.5 collective-permute-start.26
  169.3 1.3 collective-permute-done.24.refs_6_
  170.6 21.7 %mlp_back.1 = (bf16[1168,2048]{1,0:T(8,128)(2,1)}, f32[1,2048]{1,0:T(1,128)}, bf16[2,584,1024]{2,1,0:T(8,128)(2,1)}, bf16[1168,1024]{1,0:T(8,128)(2,1)}) custom-call(bf16[1168,1024]{1,0:T(8,128)(2,1)} %bitcast.104, bf16[1168,2048]{1,0:T(8,128)(2,1)} %bitcast.112, bf16[1168,2048]{1,0:T(8,128)(2,1)} %bitcast.113, ...), custom_call_target="tpu_custom_call" | custom-call | flops 25300000768 | bytes 25300000 | tf_op jit(solution)/shard_map/mlp_back/pallas_call | solution.py:91
  192.5 1.2 copy-done.16
  193.7 1.2 copy-done.17
  194.9 2.5 down_add.1
  198.8 7.1 %up_grad.1 = (bf16[8,512,128]{2,1,0:T(8,128)(2,1)S(1)}, bf16[8,512,128]{2,1,0:T(8,128)(2,1)S(1)}, bf16[8,512,128]{2,1,0:T(8,128)(2,1)S(1)}, bf16[8,512,128]{2,1,0:T(8,128)(2,1)S(1)}) custom-call(bf16[1168,1024]{1,0:T(8,128)(2,1)S(1)} %bitcast.101, bf16[1168,2048]{1,0:T(8,128)(2,1)S(1)} %copy-done.19), custom_call_target="tpu_custom_call" | custom-call | flops 12650000384 | bytes 12650000 | tf_op jit(solution)/shard_map/up_grad/pallas_call | solution.py:91
  207.1 1.7 collective-permute-start.28
  208.9 10.1 %middle_back.1 = (f32[584,1024]{1,0:T(8,128)S(1)}, bf16[2,584,1024]{2,1,0:T(8,128)(2,1)S(1)}, bf16[2,584,512]{2,1,0:T(8,128)(2,1)S(1)}, f32[4,1024]{1,0:T(4,128)S(1)}) custom-call(s32[10]{0:T(128)S(1)} %copy-done.13, f32[2]{0:T(128)S(1)} %copy-done.12, f32[6,1024]{1,0:T(8,128)S(1)} %copy-done.11, f32[2,584,1024]{2,1,0:T(8,128)} %get-tuple-element.224.refs_3_, ...), custom_call_target="tpu_custom_call" | custom-call | flops 23000000 | bytes 23000 | tf_op jit(solution)/shard_map/middle_back/pallas_call | solution.py:91
  220.6 2.4 collective-permute-start.35
  223.1 1.4 collective-permute-start.36
  224.5 2.7 out_grad.1
  227.2 7.2 %collective-permute-done.27.refs_1_ = bf16[8,512,128]{2,1,0:T(8,128)(2,1)S(1)} collective-permute-done((bf16[8,512,128]{2,1,0:T(8,128)(2,1)S(1)}, bf16[8,512,128]{2,1,0:T(8,128)(2,1)S(1)}, u32[]{:S(2)}, u32[]{:S(2)}) %collective-permute-start.27) | collective-permute-done | bytes 1048608 | tf_op jit(solution)/shard_map/ppermute | solution.py:803
  234.4 1.4 up_add.1
  235.8 1.7 collective-permute-start.32
  237.8 22.9 %attn_backward.2 = (bf16[3,6,584,128]{3,2,1,0:T(8,128)(2,1)S(1)}, f32[6,2,128]{2,1,0:T(2,128)S(1)}) custom-call(bf16[2,584,512]{2,1,0:T(8,128)(2,1)S(1)} %copy-done.22, bf16[2,584,512]{2,1,0:T(8,128)(2,1)S(1)} %copy-done.23, bf16[2,584,512]{2,1,0:T(8,128)(2,1)S(1)} %copy-done.24, bf16[2,584,512]{2,1,0:T(8,128)(2,1)S(1)} %get-tuple-element.308.refs_3_), custom_call_target="tpu_custom_call" | custom-call | flops 20700000256 | bytes 20700000 | tf_op jit(solution)/shard_map/attn_backward/pallas_call | solution.py:91
  260.9 1.4 down_sum.1
  263.3 5.1 %qkv_grad.1 = (bf16[8,512,128]{2,1,0:T(8,128)(2,1)S(1)}, bf16[8,512,128]{2,1,0:T(8,128)(2,1)S(1)}, bf16[8,512,128]{2,1,0:T(8,128)(2,1)S(1)}) custom-call(bf16[1168,1024]{1,0:T(8,128)(2,1)S(1)} %bitcast.96, bf16[9,1168,128]{2,1,0:T(8,128)(2,1)S(1)} %bitcast.94, ...), custom_call_target="tpu_custom_call", output_to_operand_aliasing={{0}: (2, {}), {1}: (3, {}), {2}: (4, {})} | custom-call | flops 8049999872 | bytes 8050000 | tf_op jit(solution)/shard_map/qkv_grad/pallas_call | solution.py:91
  268.3 1.8 collective-permute-start.39
  271.1 8.0 %attn_backward.3 = (bf16[3,2,584,128]{3,2,1,0:T(8,128)(2,1)S(1)}, f32[2,2,128]{2,1,0:T(2,128)S(1)}) custom-call(bf16[2,584,512]{2,1,0:T(8,128)(2,1)S(1)} %copy-done.22, bf16[2,584,512]{2,1,0:T(8,128)(2,1)S(1)} %copy-done.23, bf16[2,584,512]{2,1,0:T(8,128)(2,1)S(1)} %copy-done.24, bf16[2,584,512]{2,1,0:T(8,128)(2,1)S(1)} %get-tuple-element.308.refs_3_), custom_call_target="tpu_custom_call" | custom-call | flops 20700000256 | bytes 20700000 | tf_op jit(solution)/shard_map/attn_backward/pallas_call | solution.py:91
  279.0 5.2 %collective-permute-done.37.refs_1_ = bf16[2,1024,128]{2,1,0:T(8,128)(2,1)S(1)} collective-permute-done((bf16[2,1024,128]{2,1,0:T(8,128)(2,1)S(1)}, bf16[2,1024,128]{2,1,0:T(8,128)(2,1)S(1)}, u32[]{:S(2)}, u32[]{:S(2)}) %collective-permute-start.37) | collective-permute-done | bytes 524320 | tf_op jit(solution)/shard_map/ppermute | solution.py:792
  284.9 2.6 qkv_keep.1.refs_0_
  287.5 7.1 %grad_one.1.refs_8_ = bf16[2,584,1024]{2,1,0:T(8,128)(2,1)S(1)} custom-call(bf16[9,1168,128]{2,1,0:T(8,128)(2,1)S(1)} %bitcast.95, bf16[3,1168,128]{2,1,0:T(8,128)(2,1)S(1)} %bitcast.93, bf16[8,528,128]{2,1,0:T(8,128)(2,1)S(1)} %copy-done.3, bf16[8,528,128]{2,1,0:T(8,128)(2,1)} %collective-permute-done.6.refs_2_.refs_4_.refs_8_.refs_9_.refs_13_.refs_3_, ...), custom_call_target="tpu_custom_call" | custom-call | flops 23000000 | bytes 23000 | tf_op jit(solution)/shard_map/grad_one/pallas_call | solution.py:91
  295.4 1.4 qkv_add.1
  298.2 1.7 collective-permute-start.43
  300.0 7.2 %finish_tokens.1 = (bf16[584,1024]{1,0:T(8,128)(2,1)}, f32[2,1024]{1,0:T(2,128)}, f32[4,16,128]{2,1,0:T(8,128)S(1)}, f32[4,16,128]{2,1,0:T(8,128)S(1)}, f32[4,16...) custom-call(s32[10]{0:T(128)S(1)} %copy-done.13, f32[6,1024]{1,0:T(8,128)S(1)} %copy-done.11, ...), custom_call_target="tpu_custom_call" | custom-call | flops 10350000128 | bytes 10350000 | tf_op jit(solution)/shard_map/finish_tokens/pallas_call | solution.py:91
  307.2 3.3 collective-permute-done.41.refs_1_
  310.5 1.4 collective-permute-done.42.refs_3_
  313.0 2.4 collective-permute-start.47
  315.4 1.3 up_sum.1
  320.2 2.4 collective-permute-start.49
  322.6 1.4 collective-permute-start.50
  324.0 2.4 copy-done
  326.4 1.7 copy-done.9
  328.0 3.2 finish_layer.1
  331.3 10.0 %collective-permute-done.49.refs_2_ = bf16[1040,128]{1,0:T(8,128)(2,1)} collective-permute-done((bf16[1040,128]{1,0:T(8,128)(2,1)S(1)}, bf16[1040,128]{1,0:T(8,128)(2,1)}, u32[]{:S(2)}, u32[]{:S(2)}) %collective-permute-start.49) | collective-permute-done | bytes 266272 | tf_op jit(solution)/shard_map/ppermute | solution.py:792
  341.3 2.4 qkv_sum.1
  (186 shorter events, 41.6 us)
Async XLA Ops:
  0.6 10.7 %collective-permute-start.3 = (bf16[584,1024]{1,0:T(8,128)(2,1)}, bf16[584,1024]{1,0:T(8,128)(2,1)S(1)}, u32[]{:S(2)}, u32[]{:S(2)}) collective-permute-start(bf16[584,1024]{1,0:T(8,128)(2,1)} %refs_1_.1), channel_id=1, source_target_pairs={{0,1},{1,0},{2,3},{3,2},{4,5},{5,4},{6,7},{7,6},{8,9},{9,8},{10,11... | collective-permute-start | bytes 3588104 | tf_op jit(solution)/shard_map/ppermute | solution.py:807
  1.2 10.2 %collective-permute-start.4 = (bf16[584,1024]{1,0:T(8,128)(2,1)}, bf16[584,1024]{1,0:T(8,128)(2,1)}, u32[]{:S(2)}, u32[]{:S(2)}) collective-permute-start(bf16[584,1024]{1,0:T(8,128)(2,1)} %refs_2_.1), channel_id=1, source_target_pairs={{0,1},{1,0},{2,3},{3,2},{4,5},{5,4},{6,7},{7,6},{8,9},{9,8},{10,11... | collective-permute-start | bytes 3588104 | tf_op jit(solution)/shard_map/ppermute | solution.py:807
  5.1 14.8 %collective-permute-start = (bf16[1040,128]{1,0:T(8,128)(2,1)S(1)}, bf16[1040,128]{1,0:T(8,128)(2,1)S(1)}, u32[]{:S(2)}, u32[]{:S(2)}) collective-permute-start(bf16[1040,128]{1,0:T(8,128)(2,1)S(1)} %concatenate.32), channel_id=1, source_target_pairs={{0,8},{4,12},{8,0},{12,4},{16,24},{20,28},{24,16},{28,20},{1,9},{5... | collective-permute-start | bytes 798728 | tf_op jit(solution)/shard_map/ppermute | solution.py:792
  8.2 21.6 %collective-permute-start.1 = (bf16[1040,128]{1,0:T(8,128)(2,1)S(1)}, bf16[1040,128]{1,0:T(8,128)(2,1)S(1)}, u32[]{:S(2)}, u32[]{:S(2)}) collective-permute-start(bf16[1040,128]{1,0:T(8,128)(2,1)S(1)} %concatenate.32), channel_id=1, source_target_pairs={{0,16},{4,20},{8,24},{12,28},{16,0},{20,4},{24,8},{28,12},{1,17},{... | collective-permute-start | bytes 798728 | tf_op jit(solution)/shard_map/ppermute | solution.py:792
  10.8 19.0 %collective-permute-start.2 = (bf16[1040,128]{1,0:T(8,128)(2,1)S(1)}, bf16[1040,128]{1,0:T(8,128)(2,1)S(1)}, u32[]{:S(2)}, u32[]{:S(2)}) collective-permute-start(bf16[1040,128]{1,0:T(8,128)(2,1)S(1)} %concatenate.32), channel_id=1, source_target_pairs={{0,24},{4,28},{8,16},{12,20},{16,8},{20,12},{24,0},{28,4},{1,25},{... | collective-permute-start | bytes 798728 | tf_op jit(solution)/shard_map/ppermute | solution.py:792
  30.1 12.2 %collective-permute-start.5 = (bf16[4,528,128]{2,1,0:T(8,128)(2,1)S(1)}, bf16[4,528,128]{2,1,0:T(8,128)(2,1)S(1)}, u32[]{:S(2)}, u32[]{:S(2)}) collective-permute-start(bf16[4,528,128]{2,1,0:T(8,128)(2,1)S(1)} %pad_maximum_fusion), channel_id=1, source_target_pairs={{0,4},{4,0},{8,12},{12,8},{16,20},{20,16},{24,28},{28,24},{1,5},{5... | collective-permute-start | bytes 1622024 | tf_op jit(solution)/shard_map/ppermute | solution.py:795
  31.8 12.8 %collective-permute-start.7 = (bf16[4,512,128]{2,1,0:T(8,128)(2,1)S(1)}, bf16[4,512,128]{2,1,0:T(8,128)(2,1)S(1)}, u32[]{:S(2)}, u32[]{:S(2)}) collective-permute-start(bf16[4,512,128]{2,1,0:T(8,128)(2,1)S(1)} %pad_maximum_fusion.1), channel_id=1, source_target_pairs={{0,2},{2,0},{1,3},{3,1},{4,6},{6,4},{5,7},{7,5},{8,10},{10,8},{9,1... | collective-permute-start | bytes 1572872 | tf_op jit(solution)/shard_map/ppermute | solution.py:803
  33.4 12.2 %copy-start.29 = (s32[4]{0:T(128)S(1)}, s32[4]{0:T(128)}, u32[]{:S(2)}) copy-start(s32[4]{0:T(128)} %param.13) | copy-start | bytes 52
  33.4 12.8 %copy-start.27 = (bf16[1024,128]{1,0:T(8,128)(2,1)S(1)}, bf16[1024,128]{1,0:T(8,128)(2,1)}, u32[]{:S(2)}) copy-start(bf16[1024,128]{1,0:T(8,128)(2,1)} %param.21) | copy-start | bytes 786436
  33.4 12.8 %copy-start.28 = (bf16[128,1024]{1,0:T(8,128)(2,1)S(1)}, bf16[128,1024]{1,0:T(8,128)(2,1)}, u32[]{:S(2)}) copy-start(bf16[128,1024]{1,0:T(8,128)(2,1)} %param.19) | copy-start | bytes 786436
  42.3 24.3 %collective-permute-start.6 = (bf16[8,528,128]{2,1,0:T(8,128)(2,1)S(1)}, bf16[8,528,128]{2,1,0:T(8,128)(2,1)}, u32[]{:S(2)}, u32[]{:S(2)}) collective-permute-start(bf16[8,528,128]{2,1,0:T(8,128)(2,1)S(1)} %constant_dynamic-update-slice_fusion.refs_1_.refs_3_.refs_7_.refs_8_.refs_12_.refs_2_), channel_id=1, source_target_pairs={{0,2},{2,0},{1,3},{3,1},{4,6},{6,4},{5,7},{7,5},{8,10},{10,8},{9,1... | collective-permute-start | bytes 3244040 | tf_op jit(solution)/shard_map/ppermute | solution.py:803
  44.7 24.5 %copy-start.4 = (bf16[8,512,128]{2,1,0:T(8,128)(2,1)}, bf16[8,512,128]{2,1,0:T(8,128)(2,1)S(1)}, u32[]{:S(2)}) copy-start(bf16[8,512,128]{2,1,0:T(8,128)(2,1)S(1)} %constant_dynamic-update-slice_fusion.5.refs_5_.refs_9_.refs_10_.refs_14_.refs_4_) | copy-start | bytes 3145732
  44.7 21.3 %collective-permute-start.8 = (bf16[8,512,128]{2,1,0:T(8,128)(2,1)S(1)}, bf16[8,512,128]{2,1,0:T(8,128)(2,1)}, u32[]{:S(2)}, u32[]{:S(2)}) collective-permute-start(bf16[8,512,128]{2,1,0:T(8,128)(2,1)S(1)} %constant_dynamic-update-slice_fusion.5.refs_5_.refs_9_.refs_10_.refs_14_.refs_4_), channel_id=1, source_target_pairs={{0,4},{4,0},{8,12},{12,8},{16,20},{20,16},{24,28},{28,24},{1,5},{5... | collective-permute-start | bytes 3145736 | tf_op jit(solution)/shard_map/ppermute | solution.py:795
  46.2 22.9 %collective-permute-start.9 = (bf16[256,512]{1,0:T(8,128)(2,1)S(1)}, bf16[256,512]{1,0:T(8,128)(2,1)S(1)}, u32[]{:S(2)}, u32[]{:S(2)}) collective-permute-start(bf16[256,512]{1,0:T(8,128)(2,1)S(1)} %constant_dynamic-update-slice_fusion.10), channel_id=1, source_target_pairs={{0,8},{4,12},{8,0},{12,4},{16,24},{20,28},{24,16},{28,20},{1,9},{5... | collective-permute-start | bytes 786440 | tf_op jit(solution)/shard_map/ppermute | solution.py:792
  52.5 20.4 %collective-permute-start.10 = (bf16[256,512]{1,0:T(8,128)(2,1)S(1)}, bf16[256,512]{1,0:T(8,128)(2,1)S(1)}, u32[]{:S(2)}, u32[]{:S(2)}) collective-permute-start(bf16[256,512]{1,0:T(8,128)(2,1)S(1)} %constant_dynamic-update-slice_fusion.10), channel_id=1, source_target_pairs={{0,16},{4,20},{8,24},{12,28},{16,0},{20,4},{24,8},{28,12},{1,17},{... | collective-permute-start | bytes 786440 | tf_op jit(solution)/shard_map/ppermute | solution.py:792
  53.6 19.3 %collective-permute-start.11 = (bf16[256,512]{1,0:T(8,128)(2,1)S(1)}, bf16[256,512]{1,0:T(8,128)(2,1)S(1)}, u32[]{:S(2)}, u32[]{:S(2)}) collective-permute-start(bf16[256,512]{1,0:T(8,128)(2,1)S(1)} %constant_dynamic-update-slice_fusion.10), channel_id=1, source_target_pairs={{0,24},{4,28},{8,16},{12,20},{16,8},{20,12},{24,0},{28,4},{1,25},{... | collective-permute-start | bytes 786440 | tf_op jit(solution)/shard_map/ppermute | solution.py:792
  73.1 17.6 %collective-permute-start.12 = (bf16[4,128,512]{2,1,0:T(8,128)(2,1)S(1)}, bf16[4,128,512]{2,1,0:T(8,128)(2,1)S(1)}, u32[]{:S(2)}, u32[]{:S(2)}) collective-permute-start(bf16[4,128,512]{2,1,0:T(8,128)(2,1)S(1)} %pad_maximum_fusion.2), channel_id=1, source_target_pairs={{0,4},{4,0},{8,12},{12,8},{16,20},{20,16},{24,28},{28,24},{1,5},{5... | collective-permute-start | bytes 1572872 | tf_op jit(solution)/shard_map/ppermute | solution.py:795
  73.7 16.9 %collective-permute-start.13 = (bf16[4,128,512]{2,1,0:T(8,128)(2,1)S(1)}, bf16[4,128,512]{2,1,0:T(8,128)(2,1)S(1)}, u32[]{:S(2)}, u32[]{:S(2)}) collective-permute-start(bf16[4,128,512]{2,1,0:T(8,128)(2,1)S(1)} %pad_maximum_fusion.3), channel_id=1, source_target_pairs={{0,2},{2,0},{1,3},{3,1},{4,6},{6,4},{5,7},{7,5},{8,10},{10,8},{9,1... | collective-permute-start | bytes 1572872 | tf_op jit(solution)/shard_map/ppermute | solution.py:803
  92.4 24.8 %copy-start.26 = (bf16[8,128,512]{2,1,0:T(8,128)(2,1)}, bf16[8,128,512]{2,1,0:T(8,128)(2,1)S(1)}, u32[]{:S(2)}) copy-start(bf16[8,128,512]{2,1,0:T(8,128)(2,1)S(1)} %constant_dynamic-update-slice_fusion.14) | copy-start | bytes 3145732
  92.5 30.3 %collective-permute-start.18 = (bf16[1024,128]{1,0:T(8,128)(2,1)S(1)}, bf16[1024,128]{1,0:T(8,128)(2,1)S(1)}, u32[]{:S(2)}, u32[]{:S(2)}) collective-permute-start(bf16[1024,128]{1,0:T(8,128)(2,1)S(1)} %constant_dynamic-update-slice_fusion.16), channel_id=1, source_target_pairs={{0,8},{4,12},{8,0},{12,4},{16,24},{20,28},{24,16},{28,20},{1,9},{5... | collective-permute-start | bytes 786440 | tf_op jit(solution)/shard_map/ppermute | solution.py:792
  96.3 26.4 %collective-permute-start.19 = (bf16[1024,128]{1,0:T(8,128)(2,1)S(1)}, bf16[1024,128]{1,0:T(8,128)(2,1)}, u32[]{:S(2)}, u32[]{:S(2)}) collective-permute-start(bf16[1024,128]{1,0:T(8,128)(2,1)S(1)} %constant_dynamic-update-slice_fusion.16), channel_id=1, source_target_pairs={{0,16},{4,20},{8,24},{12,28},{16,0},{20,4},{24,8},{28,12},{1,17},{... | collective-permute-start | bytes 786440 | tf_op jit(solution)/shard_map/ppermute | solution.py:792
  97.4 25.4 %collective-permute-start.20 = (bf16[1024,128]{1,0:T(8,128)(2,1)S(1)}, bf16[1024,128]{1,0:T(8,128)(2,1)}, u32[]{:S(2)}, u32[]{:S(2)}) collective-permute-start(bf16[1024,128]{1,0:T(8,128)(2,1)S(1)} %constant_dynamic-update-slice_fusion.16), channel_id=1, source_target_pairs={{0,24},{4,28},{8,16},{12,20},{16,8},{20,12},{24,0},{28,4},{1,25},{... | collective-permute-start | bytes 786440 | tf_op jit(solution)/shard_map/ppermute | solution.py:792
  98.8 21.7 %collective-permute-start.16 = (bf16[8,128,512]{2,1,0:T(8,128)(2,1)}, bf16[8,128,512]{2,1,0:T(8,128)(2,1)}, u32[]{:S(2)}, u32[]{:S(2)}) collective-permute-start(bf16[8,128,512]{2,1,0:T(8,128)(2,1)} %constant_dynamic-update-slice_fusion.12), channel_id=1, source_target_pairs={{0,2},{2,0},{1,3},{3,1},{4,6},{6,4},{5,7},{7,5},{8,10},{10,8},{9,1... | collective-permute-start | bytes 3145736 | tf_op jit(solution)/shard_map/ppermute | solution.py:803
  100.0 22.3 %collective-permute-start.17 = (bf16[8,128,512]{2,1,0:T(8,128)(2,1)S(1)}, bf16[8,128,512]{2,1,0:T(8,128)(2,1)}, u32[]{:S(2)}, u32[]{:S(2)}) collective-permute-start(bf16[8,128,512]{2,1,0:T(8,128)(2,1)S(1)} %constant_dynamic-update-slice_fusion.14), channel_id=1, source_target_pairs={{0,4},{4,0},{8,12},{12,8},{16,20},{20,16},{24,28},{28,24},{1,5},{5... | collective-permute-start | bytes 3145736 | tf_op jit(solution)/shard_map/ppermute | solution.py:795
  101.0 19.6 %copy-start.1 = (bf16[2,584,1024]{2,1,0:T(8,128)(2,1)S(1)}, bf16[2,584,1024]{2,1,0:T(8,128)(2,1)}, u32[]{:S(2)}) copy-start(bf16[2,584,1024]{2,1,0:T(8,128)(2,1)} %get-tuple-element.225.refs_4_) | copy-start | bytes 7176196
  120.5 7.1 %collective-permute-start.15 = (bf16[584,1024]{1,0:T(8,128)(2,1)}, bf16[584,1024]{1,0:T(8,128)(2,1)}, u32[]{:S(2)}, u32[]{:S(2)}) collective-permute-start(bf16[584,1024]{1,0:T(8,128)(2,1)} %get-tuple-element.215.refs_4_), channel_id=1, source_target_pairs={{0,1},{1,0},{2,3},{3,2},{4,5},{5,4},{6,7},{7,6},{8,9},{9,8},{10,11... | collective-permute-start | bytes 3588104 | tf_op jit(solution)/shard_map/ppermute | solution.py:807
  122.2 24.0 %collective-permute-start.14 = (bf16[584,1024]{1,0:T(8,128)(2,1)}, bf16[584,1024]{1,0:T(8,128)(2,1)}, u32[]{:S(2)}, u32[]{:S(2)}) collective-permute-start(bf16[584,1024]{1,0:T(8,128)(2,1)} %get-tuple-element.214.refs_4_), channel_id=1, source_target_pairs={{0,1},{1,0},{2,3},{3,2},{4,5},{5,4},{6,7},{7,6},{8,9},{9,8},{10,11... | collective-permute-start | bytes 3588104 | tf_op jit(solution)/shard_map/ppermute | solution.py:807
  124.9 13.9 %collective-permute-start.21 = (bf16[4,512,128]{2,1,0:T(8,128)(2,1)S(1)}, bf16[4,512,128]{2,1,0:T(8,128)(2,1)S(1)}, u32[]{:S(2)}, u32[]{:S(2)}) collective-permute-start(bf16[4,512,128]{2,1,0:T(8,128)(2,1)S(1)} %pad_maximum_fusion.4), channel_id=1, source_target_pairs={{0,4},{4,0},{8,12},{12,8},{16,20},{20,16},{24,28},{28,24},{1,5},{5... | collective-permute-start | bytes 1572872 | tf_op jit(solution)/shard_map/ppermute | solution.py:795
  126.1 13.7 %collective-permute-start.22 = (bf16[4,512,128]{2,1,0:T(8,128)(2,1)S(1)}, bf16[4,512,128]{2,1,0:T(8,128)(2,1)}, u32[]{:S(2)}, u32[]{:S(2)}) collective-permute-start(bf16[4,512,128]{2,1,0:T(8,128)(2,1)S(1)} %pad_maximum_fusion.5), channel_id=1, source_target_pairs={{0,2},{2,0},{1,3},{3,1},{4,6},{6,4},{5,7},{7,5},{8,10},{10,8},{9,1... | collective-permute-start | bytes 1572872 | tf_op jit(solution)/shard_map/ppermute | solution.py:803
  141.5 27.8 %collective-permute-start.23 = (bf16[8,512,128]{2,1,0:T(8,128)(2,1)}, bf16[8,512,128]{2,1,0:T(8,128)(2,1)}, u32[]{:S(2)}, u32[]{:S(2)}) collective-permute-start(bf16[8,512,128]{2,1,0:T(8,128)(2,1)} %constant_dynamic-update-slice_fusion.18.refs_3_), channel_id=1, source_target_pairs={{0,2},{2,0},{1,3},{3,1},{4,6},{6,4},{5,7},{7,5},{8,10},{10,8},{9,1... | collective-permute-start | bytes 3145736 | tf_op jit(solution)/shard_map/ppermute | solution.py:803
  145.7 25.0 %collective-permute-start.24 = (bf16[8,512,128]{2,1,0:T(8,128)(2,1)}, bf16[8,512,128]{2,1,0:T(8,128)(2,1)}, u32[]{:S(2)}, u32[]{:S(2)}) collective-permute-start(bf16[8,512,128]{2,1,0:T(8,128)(2,1)} %constant_dynamic-update-slice_fusion.20.refs_5_), channel_id=1, source_target_pairs={{0,4},{4,0},{8,12},{12,8},{16,20},{20,16},{24,28},{28,24},{1,5},{5... | collective-permute-start | bytes 3145736 | tf_op jit(solution)/shard_map/ppermute | solution.py:795
  167.3 25.2 %collective-permute-start.26 = (bf16[8,512,128]{2,1,0:T(8,128)(2,1)}, bf16[8,512,128]{2,1,0:T(8,128)(2,1)S(1)}, u32[]{:S(2)}, u32[]{:S(2)}) collective-permute-start(bf16[8,512,128]{2,1,0:T(8,128)(2,1)} %get-tuple-element.227), channel_id=1, source_target_pairs={{0,4},{4,0},{8,12},{12,8},{16,20},{20,16},{24,28},{28,24},{1,5},{5... | collective-permute-start | bytes 3145736 | tf_op jit(solution)/shard_map/ppermute | solution.py:795
  168.8 23.7 %collective-permute-start.25 = (bf16[8,512,128]{2,1,0:T(8,128)(2,1)}, bf16[8,512,128]{2,1,0:T(8,128)(2,1)}, u32[]{:S(2)}, u32[]{:S(2)}) collective-permute-start(bf16[8,512,128]{2,1,0:T(8,128)(2,1)} %get-tuple-element.246), channel_id=1, source_target_pairs={{0,2},{2,0},{1,3},{3,1},{4,6},{6,4},{5,7},{7,5},{8,10},{10,8},{9,1... | collective-permute-start | bytes 3145736 | tf_op jit(solution)/shard_map/ppermute | solution.py:803
  192.4 16.5 %collective-permute-start.31 = (bf16[2,584,1024]{2,1,0:T(8,128)(2,1)}, bf16[2,584,1024]{2,1,0:T(8,128)(2,1)S(1)}, u32[]{:S(2)}, u32[]{:S(2)}) collective-permute-start(bf16[2,584,1024]{2,1,0:T(8,128)(2,1)} %get-tuple-element.264.refs_5_), channel_id=1, source_target_pairs={{0,1},{1,0},{2,3},{3,2},{4,5},{5,4},{6,7},{7,6},{8,9},{9,8},{10,11... | collective-permute-start | bytes 7176200 | tf_op jit(solution)/shard_map/ppermute | solution.py:807
  197.5 21.6 %collective-permute-start.29 = (bf16[4,512,128]{2,1,0:T(8,128)(2,1)S(1)}, bf16[4,512,128]{2,1,0:T(8,128)(2,1)S(1)}, u32[]{:S(2)}, u32[]{:S(2)}) collective-permute-start(bf16[4,512,128]{2,1,0:T(8,128)(2,1)S(1)} %get-tuple-element.262), channel_id=1, source_target_pairs={{0,4},{4,0},{8,12},{12,8},{16,20},{20,16},{24,28},{28,24},{1,5},{5... | collective-permute-start | bytes 1572872 | tf_op jit(solution)/shard_map/ppermute | solution.py:795
  197.8 21.2 %collective-permute-start.30 = (bf16[4,512,128]{2,1,0:T(8,128)(2,1)S(1)}, bf16[4,512,128]{2,1,0:T(8,128)(2,1)S(1)}, u32[]{:S(2)}, u32[]{:S(2)}) collective-permute-start(bf16[4,512,128]{2,1,0:T(8,128)(2,1)S(1)} %get-tuple-element.263), channel_id=1, source_target_pairs={{0,2},{2,0},{1,3},{3,1},{4,6},{6,4},{5,7},{7,5},{8,10},{10,8},{9,1... | collective-permute-start | bytes 1572872 | tf_op jit(solution)/shard_map/ppermute | solution.py:803
  198.8 10.1 %copy-start.3 = (bf16[8,528,128]{2,1,0:T(8,128)(2,1)S(1)}, bf16[8,528,128]{2,1,0:T(8,128)(2,1)}, u32[]{:S(2)}) copy-start(bf16[8,528,128]{2,1,0:T(8,128)(2,1)} %copy-done.2) | copy-start | bytes 3244036
  198.8 10.1 %copy-start.5 = (bf16[8,512,128]{2,1,0:T(8,128)(2,1)S(1)}, bf16[8,512,128]{2,1,0:T(8,128)(2,1)}, u32[]{:S(2)}) copy-start(bf16[8,512,128]{2,1,0:T(8,128)(2,1)} %copy-done.4) | copy-start | bytes 3145732
  198.8 10.1 %copy-start.10 = (bf16[2,584,1024]{2,1,0:T(8,128)(2,1)S(1)}, bf16[2,584,1024]{2,1,0:T(8,128)(2,1)}, u32[]{:S(2)}) copy-start(bf16[2,584,1024]{2,1,0:T(8,128)(2,1)} %get-tuple-element.264.refs_5_) | copy-start | bytes 7176196
  198.8 10.1 %copy-start.11 = (f32[6,1024]{1,0:T(8,128)S(1)}, f32[6,1024]{1,0:T(8,128)}, u32[]{:S(2)}) copy-start(f32[6,1024]{1,0:T(8,128)} %get-tuple-element.191.refs_0_.refs_1_.refs_2_) | copy-start | bytes 73732
  198.8 10.1 %copy-start.12 = (f32[2]{0:T(128)S(1)}, f32[2]{0:T(128)}, u32[]{:S(2)}) copy-start(f32[2]{0:T(128)} %get-tuple-element.359.refs_0_.refs_1_) | copy-start | bytes 28
  206.0 28.4 %collective-permute-start.27 = (bf16[8,512,128]{2,1,0:T(8,128)(2,1)S(1)}, bf16[8,512,128]{2,1,0:T(8,128)(2,1)S(1)}, u32[]{:S(2)}, u32[]{:S(2)}) collective-permute-start(bf16[8,512,128]{2,1,0:T(8,128)(2,1)S(1)} %get-tuple-element.258), channel_id=1, source_target_pairs={{0,2},{2,0},{1,3},{3,1},{4,6},{6,4},{5,7},{7,5},{8,10},{10,8},{9,1... | collective-permute-start | bytes 3145736 | tf_op jit(solution)/shard_map/ppermute | solution.py:803
  207.1 27.3 %collective-permute-start.28 = (bf16[8,512,128]{2,1,0:T(8,128)(2,1)S(1)}, bf16[8,512,128]{2,1,0:T(8,128)(2,1)S(1)}, u32[]{:S(2)}, u32[]{:S(2)}) collective-permute-start(bf16[8,512,128]{2,1,0:T(8,128)(2,1)S(1)} %get-tuple-element.260), channel_id=1, source_target_pairs={{0,4},{4,0},{8,12},{12,8},{16,20},{20,16},{24,28},{28,24},{1,5},{5... | collective-permute-start | bytes 3145736 | tf_op jit(solution)/shard_map/ppermute | solution.py:795
  220.0 40.8 %collective-permute-start.34 = (bf16[1024,128]{1,0:T(8,128)(2,1)S(1)}, bf16[1024,128]{1,0:T(8,128)(2,1)S(1)}, u32[]{:S(2)}, u32[]{:S(2)}) collective-permute-start(bf16[1024,128]{1,0:T(8,128)(2,1)S(1)} %get-tuple-element.272), channel_id=1, source_target_pairs={{0,8},{4,12},{8,0},{12,4},{16,24},{20,28},{24,16},{28,20},{1,9},{5... | collective-permute-start | bytes 786440 | tf_op jit(solution)/shard_map/ppermute | solution.py:792
  220.6 40.2 %collective-permute-start.35 = (bf16[1024,128]{1,0:T(8,128)(2,1)S(1)}, bf16[1024,128]{1,0:T(8,128)(2,1)S(1)}, u32[]{:S(2)}, u32[]{:S(2)}) collective-permute-start(bf16[1024,128]{1,0:T(8,128)(2,1)S(1)} %get-tuple-element.273), channel_id=1, source_target_pairs={{0,16},{4,20},{8,24},{12,28},{16,0},{20,4},{24,8},{28,12},{1,17},{... | collective-permute-start | bytes 786440 | tf_op jit(solution)/shard_map/ppermute | solution.py:792
  223.1 37.8 %collective-permute-start.36 = (bf16[1024,128]{1,0:T(8,128)(2,1)S(1)}, bf16[1024,128]{1,0:T(8,128)(2,1)S(1)}, u32[]{:S(2)}, u32[]{:S(2)}) collective-permute-start(bf16[1024,128]{1,0:T(8,128)(2,1)S(1)} %get-tuple-element.274), channel_id=1, source_target_pairs={{0,24},{4,28},{8,16},{12,20},{16,8},{20,12},{24,0},{28,4},{1,25},{... | collective-permute-start | bytes 786440 | tf_op jit(solution)/shard_map/ppermute | solution.py:792
  235.8 26.5 %collective-permute-start.32 = (bf16[4,512,128]{2,1,0:T(8,128)(2,1)S(1)}, bf16[4,512,128]{2,1,0:T(8,128)(2,1)S(1)}, u32[]{:S(2)}, u32[]{:S(2)}) collective-permute-start(bf16[4,512,128]{2,1,0:T(8,128)(2,1)S(1)} %get-tuple-element.283), channel_id=1, source_target_pairs={{0,4},{4,0},{8,12},{12,8},{16,20},{20,16},{24,28},{28,24},{1,5},{5... | collective-permute-start | bytes 1572872 | tf_op jit(solution)/shard_map/ppermute | solution.py:795
  237.5 24.8 %collective-permute-start.33 = (bf16[4,512,128]{2,1,0:T(8,128)(2,1)S(1)}, bf16[4,512,128]{2,1,0:T(8,128)(2,1)S(1)}, u32[]{:S(2)}, u32[]{:S(2)}) collective-permute-start(bf16[4,512,128]{2,1,0:T(8,128)(2,1)S(1)} %get-tuple-element.285), channel_id=1, source_target_pairs={{0,2},{2,0},{1,3},{3,1},{4,6},{6,4},{5,7},{7,5},{8,10},{10,8},{9,1... | collective-permute-start | bytes 1572872 | tf_op jit(solution)/shard_map/ppermute | solution.py:803
  237.8 23.0 %copy-start.7 = (bf16[1168,1024]{1,0:T(8,128)(2,1)S(1)}, bf16[1168,1024]{1,0:T(8,128)(2,1)}, u32[]{:S(2)}) copy-start(bf16[1168,1024]{1,0:T(8,128)(2,1)} %get-tuple-element.242) | copy-start | bytes 7176196
  260.8 23.5 %collective-permute-start.38 = (bf16[2,584,1024]{2,1,0:T(8,128)(2,1)S(1)}, bf16[2,584,1024]{2,1,0:T(8,128)(2,1)S(1)}, u32[]{:S(2)}, u32[]{:S(2)}) collective-permute-start(bf16[2,584,1024]{2,1,0:T(8,128)(2,1)S(1)} %bitcast.98), channel_id=1, source_target_pairs={{0,1},{1,0},{2,3},{3,2},{4,5},{5,4},{6,7},{7,6},{8,9},{9,8},{10,11... | collective-permute-start | bytes 7176200 | tf_op jit(solution)/shard_map/ppermute | solution.py:807
  268.3 26.4 %collective-permute-start.39 = (bf16[8,512,128]{2,1,0:T(8,128)(2,1)S(1)}, bf16[8,512,128]{2,1,0:T(8,128)(2,1)S(1)}, u32[]{:S(2)}, u32[]{:S(2)}) collective-permute-start(bf16[8,512,128]{2,1,0:T(8,128)(2,1)S(1)} %get-tuple-element.306), channel_id=1, source_target_pairs={{0,2},{2,0},{1,3},{3,1},{4,6},{6,4},{5,7},{7,5},{8,10},{10,8},{9,1... | collective-permute-start | bytes 3145736 | tf_op jit(solution)/shard_map/ppermute | solution.py:803
  270.1 25.3 %collective-permute-start.40 = (bf16[8,512,128]{2,1,0:T(8,128)(2,1)S(1)}, bf16[8,512,128]{2,1,0:T(8,128)(2,1)S(1)}, u32[]{:S(2)}, u32[]{:S(2)}) collective-permute-start(bf16[8,512,128]{2,1,0:T(8,128)(2,1)S(1)} %get-tuple-element.307), channel_id=1, source_target_pairs={{0,4},{4,0},{8,12},{12,8},{16,20},{20,16},{24,28},{28,24},{1,5},{5... | collective-permute-start | bytes 3145736 | tf_op jit(solution)/shard_map/ppermute | solution.py:795
  270.5 13.7 %collective-permute-start.37 = (bf16[2,1024,128]{2,1,0:T(8,128)(2,1)S(1)}, bf16[2,1024,128]{2,1,0:T(8,128)(2,1)S(1)}, u32[]{:S(2)}, u32[]{:S(2)}) collective-permute-start(bf16[2,1024,128]{2,1,0:T(8,128)(2,1)S(1)} %get-tuple-element.302), channel_id=1, source_target_pairs={{0,8},{4,12},{8,0},{12,4},{16,24},{20,28},{24,16},{28,20},{1,9},{5... | collective-permute-start | bytes 1572872 | tf_op jit(solution)/shard_map/ppermute | solution.py:792
  294.6 5.3 %collective-permute-start.44 = (bf16[2,584,1024]{2,1,0:T(8,128)(2,1)S(1)}, bf16[2,584,1024]{2,1,0:T(8,128)(2,1)S(1)}, u32[]{:S(2)}, u32[]{:S(2)}) collective-permute-start(bf16[2,584,1024]{2,1,0:T(8,128)(2,1)S(1)} %grad_one.1.refs_8_), channel_id=1, source_target_pairs={{0,1},{1,0},{2,3},{3,2},{4,5},{5,4},{6,7},{7,6},{8,9},{9,8},{10,11... | collective-permute-start | bytes 7176200 | tf_op jit(solution)/shard_map/ppermute | solution.py:807
  296.8 13.7 %collective-permute-start.41 = (bf16[4,512,128]{2,1,0:T(8,128)(2,1)S(1)}, bf16[4,512,128]{2,1,0:T(8,128)(2,1)S(1)}, u32[]{:S(2)}, u32[]{:S(2)}) collective-permute-start(bf16[4,512,128]{2,1,0:T(8,128)(2,1)S(1)} %get-tuple-element.325), channel_id=1, source_target_pairs={{0,4},{4,0},{8,12},{12,8},{16,20},{20,16},{24,28},{28,24},{1,5},{5... | collective-permute-start | bytes 1572872 | tf_op jit(solution)/shard_map/ppermute | solution.py:795
  297.9 14.0 %collective-permute-start.42 = (bf16[4,512,128]{2,1,0:T(8,128)(2,1)S(1)}, bf16[4,512,128]{2,1,0:T(8,128)(2,1)S(1)}, u32[]{:S(2)}, u32[]{:S(2)}) collective-permute-start(bf16[4,512,128]{2,1,0:T(8,128)(2,1)S(1)} %get-tuple-element.327), channel_id=1, source_target_pairs={{0,2},{2,0},{1,3},{3,1},{4,6},{6,4},{5,7},{7,5},{8,10},{10,8},{9,1... | collective-permute-start | bytes 1572872 | tf_op jit(solution)/shard_map/ppermute | solution.py:803
  298.2 17.2 %collective-permute-start.43 = (bf16[1,1024,128]{2,1,0:T(8,128)(2,1)S(1)}, bf16[1,1024,128]{2,1,0:T(8,128)(2,1)S(1)}, u32[]{:S(2)}, u32[]{:S(2)}) collective-permute-start(bf16[1,1024,128]{2,1,0:T(8,128)(2,1)S(1)} %get-tuple-element.328), channel_id=1, source_target_pairs={{0,16},{4,20},{8,24},{12,28},{16,0},{20,4},{24,8},{28,12},{1,17},{... | collective-permute-start | bytes 786440 | tf_op jit(solution)/shard_map/ppermute | solution.py:792
  311.9 4.8 %collective-permute-start.45 = (f32[4,16,128]{2,1,0:T(8,128)S(1)}, f32[4,16,128]{2,1,0:T(8,128)S(1)}, u32[]{:S(2)}, u32[]{:S(2)}) collective-permute-start(f32[4,16,128]{2,1,0:T(8,128)S(1)} %get-tuple-element.342), channel_id=1, source_target_pairs={{0,4},{2,6},{4,0},{6,2},{8,12},{10,14},{12,8},{14,10},{16,20},{18,... | collective-permute-start | bytes 98312 | tf_op jit(solution)/shard_map/ppermute | solution.py:800
  312.2 4.5 %collective-permute-start.46 = (f32[4,16,128]{2,1,0:T(8,128)S(1)}, f32[4,16,128]{2,1,0:T(8,128)S(1)}, u32[]{:S(2)}, u32[]{:S(2)}) collective-permute-start(f32[4,16,128]{2,1,0:T(8,128)S(1)} %get-tuple-element.343), channel_id=1, source_target_pairs={{0,2},{2,0},{4,6},{6,4},{8,10},{10,8},{12,14},{14,12},{16,18},{18,... | collective-permute-start | bytes 98312 | tf_op jit(solution)/shard_map/ppermute | solution.py:800
  313.0 4.8 %collective-permute-start.47 = (f32[4,16,128]{2,1,0:T(8,128)S(1)}, f32[4,16,128]{2,1,0:T(8,128)S(1)}, u32[]{:S(2)}, u32[]{:S(2)}) collective-permute-start(f32[4,16,128]{2,1,0:T(8,128)S(1)} %get-tuple-element.344), channel_id=1, source_target_pairs={{0,6},{2,4},{4,2},{6,0},{8,14},{10,12},{12,10},{14,8},{16,22},{18,... | collective-permute-start | bytes 98312 | tf_op jit(solution)/shard_map/ppermute | solution.py:800
  319.6 11.6 %collective-permute-start.48 = (bf16[1040,128]{1,0:T(8,128)(2,1)S(1)}, bf16[1040,128]{1,0:T(8,128)(2,1)S(1)}, u32[]{:S(2)}, u32[]{:S(2)}) collective-permute-start(bf16[1040,128]{1,0:T(8,128)(2,1)S(1)} %get-tuple-element.346), channel_id=1, source_target_pairs={{0,8},{4,12},{8,0},{12,4},{16,24},{20,28},{24,16},{28,20},{1,9},{5... | collective-permute-start | bytes 798728 | tf_op jit(solution)/shard_map/ppermute | solution.py:792
  320.2 21.1 %collective-permute-start.49 = (bf16[1040,128]{1,0:T(8,128)(2,1)S(1)}, bf16[1040,128]{1,0:T(8,128)(2,1)}, u32[]{:S(2)}, u32[]{:S(2)}) collective-permute-start(bf16[1040,128]{1,0:T(8,128)(2,1)S(1)} %get-tuple-element.347), channel_id=1, source_target_pairs={{0,16},{4,20},{8,24},{12,28},{16,0},{20,4},{24,8},{28,12},{1,17},{... | collective-permute-start | bytes 798728 | tf_op jit(solution)/shard_map/ppermute | solution.py:792
  322.6 18.7 %collective-permute-start.50 = (bf16[1040,128]{1,0:T(8,128)(2,1)S(1)}, bf16[1040,128]{1,0:T(8,128)(2,1)}, u32[]{:S(2)}, u32[]{:S(2)}) collective-permute-start(bf16[1040,128]{1,0:T(8,128)(2,1)S(1)} %get-tuple-element.348), channel_id=1, source_target_pairs={{0,24},{4,28},{8,16},{12,20},{16,8},{20,12},{24,0},{28,4},{1,25},{... | collective-permute-start | bytes 798728 | tf_op jit(solution)/shard_map/ppermute | solution.py:792
  328.0 13.3 %copy-start.21 = (bf16[1040,128]{1,0:T(8,128)(2,1)S(1)}, bf16[1040,128]{1,0:T(8,128)(2,1)}, u32[]{:S(2)}) copy-start(bf16[1040,128]{1,0:T(8,128)(2,1)} %copy-done.20) | copy-start | bytes 798724
  (18 other events, 60.3 us)

commit v6 on v5

--- a/solution.py
+++ b/solution.py
@@ -13,7 +13,7 @@
 BF = jnp.bfloat16
 F32 = jnp.float32
 VMEM_LIMIT = 60 * 1024 * 1024
-WHOLE_VMEM = ("arrange_pair", "vectors", "attn_forward", "mlp_up", "down_grad", "mlp_back")
+WHOLE_VMEM = ("arrange_pair", "vectors", "mlp_up", "down_grad", "mlp_back")
 COST_SCALE = 1.0
 COST = {
     "arrange_pair": 5,
@@ -26,9 +26,11 @@
     "middle_back": 0,
     "out_grad": 8,
     "attn_backward": 18,
+    "attn_first": 0,
     "qkv_grad": 7,
     "qkv_keep": 0,
     "up_half": 0,
+    "join": 0,
     "grad_one": 0,
     "qkv_add": 30,
     "finish_layer": 0,
@@ -69,7 +71,7 @@
     return count * jnp.dtype(value.dtype).itemsize
 
 
-def call(body, ins, outs, scratch, name, flops, aliases=None, smem=(), sems=48, vmem_ins=(), spare=12):
+def call(body, ins, outs, scratch, name, flops, aliases=None, smem=(), sems=48, vmem_ins=(), spare=12, pinned=False):
     n_smem, n_vmem, n_in, n_out = len(smem), len(vmem_ins), len(ins), len(outs)
     moved = sum(a.size * a.dtype.itemsize for a in ins) + sum(
         o.size * o.dtype.itemsize for o in outs
@@ -88,13 +90,14 @@
     flops = max(COST.get(name, 3), 0.02) * COST_SCALE * 1.15e9
     moved = 0
     any_spec = pl.BlockSpec(memory_space=pl.ANY)
+    hbm_spec = pl.BlockSpec(memory_space=pltpu.HBM) if pinned else any_spec
     return pl.pallas_call(
         kernel,
         out_shape=outs,
         in_specs=[pl.BlockSpec(memory_space=pltpu.SMEM)] * n_smem
         + [pl.BlockSpec(memory_space=pltpu.VMEM)] * n_vmem
-        + [any_spec] * n_in,
-        out_specs=[any_spec] * n_out,
+        + [hbm_spec if i in (aliases or {}) else any_spec for i in range(n_in)],
+        out_specs=[hbm_spec if pinned else any_spec] * n_out,
         scratch_shapes=list(scratch) + [pltpu.SemaphoreType.DMA((sems,))],
         input_output_aliases={n_smem + n_vmem + i: o for i, o in (aliases or {}).items()},
         compiler_params=pltpu.CompilerParams(vmem_limit_bytes=vmem),
@@ -291,6 +294,7 @@
         "attn_forward",
         2 * seq * width * ext * 4 + 16 * seq * seq * ext,
         aliases={1 + i: i for i in range(n_prev)},
+        pinned=True,
         vmem_ins=(nv, bq),
     )
 
@@ -358,6 +362,7 @@
         "mlp_up",
         2 * seq * width * hid,
         aliases={3 + i: i for i in range(n_prev)},
+        pinned=True,
         smem=(keep,),
         vmem_ins=(nv, bu),
     )
@@ -607,7 +612,7 @@
     )
 
 
-def attn_backward(pairs, grad, q, k, v):
+def attn_backward(pairs, grad, q, k, v, name="attn_backward"):
     _, seq, _ = q.shape
     n = len(pairs)
 
@@ -662,7 +667,7 @@
         [q, k, v, grad],
         [sds((3, 2 * n, seq, 128), BF), sds((2 * n, 2, 128), F32)],
         [pltpu.VMEM((2 * n, seq, 128), BF)] * 7 + [pltpu.VMEM((2 * n, 2, 128), F32)],
-        "attn_backward",
+        name,
         0,
     )
     return grads.reshape(3 * n, 2 * seq, 128), sums
@@ -943,6 +948,17 @@
         return add_pieces([after(self.state, gate)], cuts, outs, self.name + "_sum")
 
 
+def join_kernel(pieces):
+    groups, cuts, outs = [], [], []
+    for which, part in enumerate(pieces):
+        lead = part[0].shape[0]
+        for k, value in enumerate(part):
+            cuts.append((len(groups), slice(None), which, slice(k * lead, (k + 1) * lead)))
+            groups.append([value])
+        outs.append(sds((lead * len(part),) + part[0].shape[1:], BF))
+    return add_pieces(groups, cuts, outs, "join")
+
+
 def xor_blocks(value, mask, axis):
     count = value.shape[axis]
     bit = 1
@@ -1115,7 +1131,7 @@
         wup = ([up_w], all_of, up_w.shape)
     part, recv = parts[0]
     state = mlp_up(0, tok, part, recv, keep, nv, bu, wup, fh, None)
-    dna, dnb = gather_last(grid, *join(after(dn_h, state[1])))
+    dna, dnb = gather_last(grid, *join_kernel(after(dn_h, state[1])))
     part, recv = parts[1]
     state = mlp_up(1, tok, part, recv, keep, nv, bu, wup, fh, state)
     if aligned:
@@ -1187,33 +1203,41 @@
         [att_in], [flat(gattn)], tasks, last_shapes, "out_grad", row0, row0 + hh
     )
 
-    up_half = up_rs.second(out_grads[-1])
     n_pairs = ext // 128
-    split = hh == 128 and bd == 128
-    firsts = list(range(1, n_pairs)) if split else list(range(n_pairs))
-    left_a, bias_a = attn_backward(firsts, after(grad_att, up_half), q, k, v)
+    split = hh == 128 and bd == 128 and n_pairs >= 4
+    if split:
+        heads = [[1], list(range(2, n_pairs))]
+        first_in = after(grad_att, out_grads[-1])
+        left_0, bias_0 = attn_backward(heads[0], first_in, q, k, v, "attn_first")
+        up_half = up_rs.second(bias_0)
+    else:
+        heads = [list(range(n_pairs))]
+        up_half = up_rs.second(out_grads[-1])
+    left_a, bias_a = attn_backward(heads[-1], after(grad_att, up_half), q, k, v)
     grad_down = down_rs.finish(bias_a, [(full, 0, full)], [sds((fw, bd), F32)])[0]
     mlp_recv = swap_core(after(mlp_part, bias_a))
     gate = up_rs.halve(grad_down) if z_n > 1 else grad_down
     first_in = after(flat(first), gate)
     if split:
-        stores, count = [], len(firsts)
-        for i in range(3):
-            rows = slice(i * bd, (i + 1) * bd)
-            for n, pair in enumerate(firsts):
-                kx, cols = pair // 2, slice((i * count + n) * 128, (i * count + n + 1) * 128)
-                for p, r_sl in a_spots:
-                    ky, kz = p // z_n, p % z_n
-                    spot = (kx - 1, (p, rows)) if pair % 2 == 0 else (tx - 1 + ky, (kx * z_n + kz, rows))
-                    stores.append(spot + (r_sl, cols))
-        tasks = [(0, slice(0, width), 0, slice(0, 384 * count), stores)]
+        tasks = []
+        for index, pairs in enumerate(heads):
+            stores, count = [], len(pairs)
+            for i in range(3):
+                rows = slice(i * bd, (i + 1) * bd)
+                for n, pair in enumerate(pairs):
+                    kx, cols = pair // 2, slice((i * count + n) * 128, (i * count + n + 1) * 128)
+                    for p, r_sl in a_spots:
+                        ky, kz = p // z_n, p % z_n
+                        spot = (kx - 1, (p, rows))
+                        if pair % 2:
+                            spot = (tx - 1 + ky, (kx * z_n + kz, rows))
+                        stores.append(spot + (r_sl, cols))
+            tasks.append((0, slice(0, width), index, slice(0, 384 * count), stores))
         sent = weight_grad(
-            [first_in], [left_a], tasks, last_shapes[1:], "qkv_grad", 0, row0, out_grads[1:]
+            [first_in], [left_0, left_a], tasks, last_shapes[1:], "qkv_grad", 0, row0, out_grads[1:]
         )
         left_b, bias_b = attn_backward([0], after(grad_att, (sent[: tx - 1], sent[tx:])), q, k, v)
         gate = (bias_b, mlp_recv)
-        while 2 * up_rs.bit < z_n:
-            gate = up_rs.halve(gate)
         stores = []
         for i in range(3):
             rows, cols = slice(i * bd, (i + 1) * bd), slice(i * 128, (i + 1) * 128)
@@ -1230,8 +1254,8 @@
             out_grads[:1],
         )
         grads = list(kept) + list(sent)
-        lefts, starts = [left_a, left_b], [1, 0]
-        pair_sums = [bias_b, bias_a]
+        lefts, starts = [left_0, left_a, left_b], [1, 2, 0]
+        pair_sums = [bias_b, bias_0, bias_a]
         gate = kept[0]
     else:
         while 2 * up_rs.bit < z_n:
@@ -1262,7 +1286,10 @@
             rows = slice(h * up_rows + j * bd, h * up_rows + (j + 1) * bd)
             cuts.append((rows, 0, (full, slice(h * fh + j * bd, h * fh + (j + 1) * bd))))
     up_cuts = cuts
-    qkv_half = qkv_rs.second(one_part)
+    gate = one_part
+    while 2 * up_rs.bit < z_n:
+        gate = up_rs.halve(gate)
+    qkv_half = qkv_rs.second(gate)
     wide = max(bd, hw // dp, fw // dp)
     if split and fw // dp == bd and 128 % (hw // dp) == 0:
         rest = sds((tx * y_n, z_n, 16, wide), F32)

time: 353 us -> 343 us (0.972)
  waiting for transfers between devices: 73.1 us -> 61.4 us
  Pallas kernels: 182 us -> 186 us
    unnamed x76 -> x114, local copies, waits for them, and re-layouts: 11 us -> 17.5 us
    ppermute x17, waiting for transfers between devices: 31.5 us -> 25.1 us  [send_z(): lax.ppermute(value, 'dp', [(i, i ^ k * self.y) for i in range(self.dp)])]
    ppermute x12, waiting for transfers between devices: 14.3 us -> 9.76 us  [send_x(): return lax.ppermute(value, 'tx', [(i, i ^ k) for i in range(self.tx)])]
    pallas_call x28 -> x30, Pallas kernels: 182 us -> 186 us  [call(): pl.pallas_call(kernel, out_shape=outs, in_specs=[pl.BlockSpec(memory_spac...]
  transfers between devices with their start and end apart: 51 -> 51, of which waited for: 18 -> 17; matrix products, arithmetic and copies ran while one was open for 4% -> 2% of each run, Pallas kernels for 52% -> 54%
where the time goes in v6:
time: 343 us; the launch traced here: 339 us
  Pallas kernels  186 us (54%)
  starting transfers between devices  62 us (18%)
  waiting for transfers between devices  61.4 us (18%)
  local copies, waits for them, and re-layouts  24.3 us (7%)
  other arithmetic  4.11 us (1%)
    pallas_call x30, Pallas kernels, call(): pl.pallas_call(kernel, out_shape=outs, in_specs=[pl.BlockSpec(memory_spac...  186 us
    ppermute x17, starting transfers between devices, send_z(): lax.ppermute(value, 'dp', [(i, i ^ k * self.y) for i in range(self.dp)])  31.2 us
    ppermute x17, waiting for transfers between devices, send_z(): lax.ppermute(value, 'dp', [(i, i ^ k * self.y) for i in range(self.dp)])  25.1 us
    ppermute x12, waiting for transfers between devices, send_y(): return lax.ppermute(value, 'dp', [(i, i ^ k) for i in range(self.dp)])  24.5 us
    unnamed x114, local copies, waits for them, and re-layouts  17.5 us
    ppermute x12, starting transfers between devices, send_x(): return lax.ppermute(value, 'tx', [(i, i ^ k) for i in range(self.tx)])  13.7 us
    ppermute x12, starting transfers between devices, send_y(): return lax.ppermute(value, 'dp', [(i, i ^ k) for i in range(self.dp)])  12.4 us
    ppermute x12, waiting for transfers between devices, send_x(): return lax.ppermute(value, 'tx', [(i, i ^ k) for i in range(self.tx)])  9.76 us
  transfers between devices with their start and end apart: 51, of which 17 were waited for; matrix products, arithmetic and copies ran while one was open for 2% of the time, Pallas kernels for 54%

profile of v6, /device:TPU:0, one launch (start us, length us, event | category | flops | bytes accessed | tf_op | source)
XLA Modules:
  0.0 339.2 jit_solution(4232683911778462665)
XLA Ops:
  3.7 1.5 concatenate.26
  5.1 3.1 collective-permute-start
  8.2 2.6 collective-permute-start.1
  11.4 4.9 %arrange_pair.1 = (bf16[2,584,1024]{2,1,0:T(8,128)(2,1)}, bf16[2,584,1024]{2,1,0:T(8,128)(2,1)}) custom-call(s32[10]{0:T(128)} %stack.130.refs_0_, bf16[584,1024]{1,0:T(8,128)(2,1)} %refs_1_.1, bf16[584,1024]{1,0:T(8,128)(2,1)} %refs_2_.1, bf16[584,1024]{1,0:T(8,128)(2,1)} %collective-permute-done.3.refs_3_, bf16[584,1024]{1,0:T(8,128)(2,1)} %collective-permute-done.4.refs_4_), custom_call_target="tpu_custom_call" | custom-call | flops 5750000128 | bytes 5750000 | tf_op jit(solution)/shard_map/arrange_pair/pallas_call | solution.py:94
  16.3 3.6 %collective-permute-done = bf16[1040,128]{1,0:T(8,128)(2,1)S(1)} collective-permute-done((bf16[1040,128]{1,0:T(8,128)(2,1)S(1)}, bf16[1040,128]{1,0:T(8,128)(2,1)S(1)}, u32[]{:S(2)}, u32[]{:S(2)}) %collective-permute-start) | collective-permute-done | bytes 266272 | tf_op jit(solution)/shard_map/ppermute | solution.py:797
  19.9 9.9 %collective-permute-done.1 = bf16[1040,128]{1,0:T(8,128)(2,1)S(1)} collective-permute-done((bf16[1040,128]{1,0:T(8,128)(2,1)S(1)}, bf16[1040,128]{1,0:T(8,128)(2,1)S(1)}, u32[]{:S(2)}, u32[]{:S(2)}) %collective-permute-start.1) | collective-permute-done | bytes 266272 | tf_op jit(solution)/shard_map/ppermute | solution.py:797
  30.1 1.6 collective-permute-start.5
  31.8 1.6 collective-permute-start.7
  33.4 8.8 %collective-permute-done.5 = bf16[4,528,128]{2,1,0:T(8,128)(2,1)S(1)} collective-permute-done((bf16[4,528,128]{2,1,0:T(8,128)(2,1)S(1)}, bf16[4,528,128]{2,1,0:T(8,128)(2,1)S(1)}, u32[]{:S(2)}, u32[]{:S(2)}) %collective-permute-start.5) | collective-permute-done | bytes 540704 | tf_op jit(solution)/shard_map/ppermute | solution.py:800
  42.3 1.6 collective-permute-start.6
  46.2 6.2 %collective-permute-start.9 = (bf16[256,512]{1,0:T(8,128)(2,1)S(1)}, bf16[256,512]{1,0:T(8,128)(2,1)S(1)}, u32[]{:S(2)}, u32[]{:S(2)}) collective-permute-start(bf16[256,512]{1,0:T(8,128)(2,1)S(1)} %constant_dynamic-update-slice_fusion.10), channel_id=1, source_target_pairs={{0,8},{4,12},{8,0},{12,4},{16,24},{20,28},{24,16},{28,20},{1,9},{5... | collective-permute-start | bytes 786440 | tf_op jit(solution)/shard_map/ppermute | solution.py:797
  53.6 1.4 collective-permute-start.11
  55.0 11.0 %collective-permute-done.8.refs_6_.refs_10_.refs_11_.refs_15_ = bf16[8,512,128]{2,1,0:T(8,128)(2,1)} collective-permute-done((bf16[8,512,128]{2,1,0:T(8,128)(2,1)S(1)}, bf16[8,512,128]{2,1,0:T(8,128)(2,1)}, u32[]{:S(2)}, u32[]{:S(2)}) %collective-permute-start.8) | collective-permute-done | bytes 1048608 | tf_op jit(solution)/shard_map/ppermute | solution.py:800
  66.6 2.6 vectors.1
  69.2 3.7 %collective-permute-done.10 = bf16[256,512]{1,0:T(8,128)(2,1)S(1)} collective-permute-done((bf16[256,512]{1,0:T(8,128)(2,1)S(1)}, bf16[256,512]{1,0:T(8,128)(2,1)S(1)}, u32[]{:S(2)}, u32[]{:S(2)}) %collective-permute-start.10) | collective-permute-done | bytes 262176 | tf_op jit(solution)/shard_map/ppermute | solution.py:797
  74.9 14.7 %attn_forward.2 = (bf16[2,584,1024]{2,1,0:T(8,128)(2,1)S(1)}, bf16[2,584,512]{2,1,0:T(8,128)(2,1)S(1)}, bf16[2,584,512]{2,1,0:T(8,128)(2,1)S(1)}, bf16[2,584,512...) custom-call(f32[6,1024]{1,0:T(8,128)S(1)} %copy-done.20, ...), custom_call_target="tpu_custom_call" | custom-call | flops 18400000000 | bytes 18400000 | tf_op jit(solution)/shard_map/attn_forward/pallas_call | solution.py:94
  89.9 3.8 %collective-permute-start.18 = (bf16[1024,128]{1,0:T(8,128)(2,1)S(1)}, bf16[1024,128]{1,0:T(8,128)(2,1)S(1)}, u32[]{:S(2)}, u32[]{:S(2)}) collective-permute-start(bf16[1024,128]{1,0:T(8,128)(2,1)S(1)} %constant_dynamic-update-slice_fusion.16), channel_id=1, source_target_pairs={{0,8},{4,12},{8,0},{12,4},{16,24},{20,28},{24,16},{28,20},{1,9},{5... | collective-permute-start | bytes 786440 | tf_op jit(solution)/shard_map/ppermute | solution.py:797
  94.7 1.4 collective-permute-start.20
  98.3 15.5 %attn_forward.3 = (bf16[2,584,1024]{2,1,0:T(8,128)(2,1)S(1)}, bf16[2,584,512]{2,1,0:T(8,128)(2,1)S(1)}, bf16[2,584,512]{2,1,0:T(8,128)(2,1)S(1)}, bf16[2,584,512...) custom-call(f32[6,1024]{1,0:T(8,128)S(1)} %copy-done.20, ...), custom_call_target="tpu_custom_call", output_to_operand_aliasing={{0}: (3, {}), {1}: (4, {}), {2}: (5, {}), {3}: (6, {}), {4}... | custom-call | flops 18400000000 | bytes 18400000 | tf_op jit(solution)/shard_map/attn_forward/pallas_call | solution.py:94
  115.9 2.2 collective-permute-done.16
  118.1 1.7 broadcast_multiply_fusion
  124.8 10.1 %mlp_up.2 = (f32[2,584,1024]{2,1,0:T(8,128)}, bf16[2,584,1024]{2,1,0:T(8,128)(2,1)}, bf16[2,584,2048]{2,1,0:T(8,128)(2,1)}, bf16[2,584,2048]{2,1,0:T(8,128)(2,1)}) custom-call(f32[2]{0:T(128)} %get-tuple-element.371.refs_0_.refs_1_, f32[6,1024]{1,0:T(8,128)} %get-tuple-element.197.refs_0_.refs_1_.refs_2_, f32[1,2048]{1,0:T(1,128)} %get-tuple-element.198.refs_2_, ...), custom_call_target="tpu_custom_call" | custom-call | flops 11500000256 | bytes 11500000 | tf_op jit(solution)/shard_map/mlp_up/pallas_call | solution.py:94
  135.2 1.4 collective-permute-done.22.refs_3_
  136.6 3.3 join.1
  139.9 1.4 collective-permute-start.23
  142.0 10.1 %mlp_up.3 = (f32[2,584,1024]{2,1,0:T(8,128)}, bf16[2,584,1024]{2,1,0:T(8,128)(2,1)}, bf16[2,584,2048]{2,1,0:T(8,128)(2,1)}, bf16[2,584,2048]{2,1,0:T(8,128)(2,1)}) custom-call(f32[2]{0:T(128)} %get-tuple-element.371.refs_0_.refs_1_, ...), custom_call_target="tpu_custom_call", output_to_operand_aliasing={{0}: (6, {}), {1}: (7, {}), {2}: (8, {}), {3}: (9, {})} | custom-call | flops 11500000256 | bytes 11500000 | tf_op jit(solution)/shard_map/mlp_up/pallas_call | solution.py:94
  152.1 10.7 %down_grad.1 = (bf16[8,512,128]{2,1,0:T(8,128)(2,1)}, bf16[8,512,128]{2,1,0:T(8,128)(2,1)}, bf16[8,512,128]{2,1,0:T(8,128)(2,1)}, bf16[8,512,128]{2,1,0:T(8,128)(2,1)}) custom-call(bf16[1168,2048]{1,0:T(8,128)(2,1)} %bitcast.123, bf16[1168,1024]{1,0:T(8,128)(2,1)} %bitcast.106), custom_call_target="tpu_custom_call" | custom-call | flops 12650000384 | bytes 12650000 | tf_op jit(solution)/shard_map/down_grad/pallas_call | solution.py:94
  162.8 1.5 collective-permute-start.26
  165.0 1.9 collective-permute-done.24.refs_6_
  166.8 21.8 %mlp_back.1 = (bf16[1168,2048]{1,0:T(8,128)(2,1)}, f32[1,2048]{1,0:T(1,128)}, bf16[2,584,1024]{2,1,0:T(8,128)(2,1)}, bf16[1168,1024]{1,0:T(8,128)(2,1)}) custom-call(bf16[1168,1024]{1,0:T(8,128)(2,1)} %bitcast.107, bf16[1168,2048]{1,0:T(8,128)(2,1)} %bitcast.124, bf16[1168,2048]{1,0:T(8,128)(2,1)} %bitcast.125, ...), custom_call_target="tpu_custom_call" | custom-call | flops 25300000768 | bytes 25300000 | tf_op jit(solution)/shard_map/mlp_back/pallas_call | solution.py:94
  191.2 2.5 down_add.1
  193.8 2.0 collective-permute-start.31
  195.9 7.4 %up_grad.1 = (bf16[8,512,128]{2,1,0:T(8,128)(2,1)S(1)}, bf16[8,512,128]{2,1,0:T(8,128)(2,1)S(1)}, bf16[8,512,128]{2,1,0:T(8,128)(2,1)S(1)}, bf16[8,512,128]{2,1,0:T(8,128)(2,1)S(1)}) custom-call(bf16[1168,1024]{1,0:T(8,128)(2,1)S(1)} %bitcast.104, bf16[1168,2048]{1,0:T(8,128)(2,1)S(1)} %copy-done.38), custom_call_target="tpu_custom_call" | custom-call | flops 12650000384 | bytes 12650000 | tf_op jit(solution)/shard_map/up_grad/pallas_call | solution.py:94
  203.4 1.9 collective-permute-start.28
  205.4 9.7 %middle_back.1 = (f32[584,1024]{1,0:T(8,128)S(1)}, bf16[2,584,1024]{2,1,0:T(8,128)(2,1)S(1)}, bf16[2,584,512]{2,1,0:T(8,128)(2,1)S(1)}, f32[4,1024]{1,0:T(4,128)S(1)}) custom-call(s32[10]{0:T(128)S(1)} %copy-done.23, f32[2]{0:T(128)S(1)} %copy-done.22, f32[6,1024]{1,0:T(8,128)S(1)} %copy-done.21, f32[2,584,1024]{2,1,0:T(8,128)} %get-tuple-element.230.refs_3_, ...), custom_call_target="tpu_custom_call" | custom-call | flops 23000000 | bytes 23000 | tf_op jit(solution)/shard_map/middle_back/pallas_call | solution.py:94
  216.7 2.4 collective-permute-start.35
  219.1 1.4 collective-permute-start.36
  220.5 3.1 out_grad.1
  223.7 8.0 %attn_first.1 = (bf16[3,2,584,128]{3,2,1,0:T(8,128)(2,1)S(1)}, f32[2,2,128]{2,1,0:T(2,128)S(1)}) custom-call(bf16[2,584,512]{2,1,0:T(8,128)(2,1)S(1)} %copy-done.15, bf16[2,584,512]{2,1,0:T(8,128)(2,1)S(1)} %copy-done.17, bf16[2,584,512]{2,1,0:T(8,128)(2,1)S(1)} %copy-done.19, bf16[2,584,512]{2,1,0:T(8,128)(2,1)S(1)} %get-tuple-element.318.refs_3_), custom_call_target="tpu_custom_call" | custom-call | flops 23000000 | bytes 23000 | tf_op jit(solution)/shard_map/attn_first/pallas_call | solution.py:94
  233.8 1.4 collective-permute-start.33
  235.2 15.5 %attn_backward.2 = (bf16[3,4,584,128]{3,2,1,0:T(8,128)(2,1)S(1)}, f32[4,2,128]{2,1,0:T(2,128)S(1)}) custom-call(bf16[2,584,512]{2,1,0:T(8,128)(2,1)S(1)} %copy-done.15, bf16[2,584,512]{2,1,0:T(8,128)(2,1)S(1)} %copy-done.17, bf16[2,584,512]{2,1,0:T(8,128)(2,1)S(1)} %copy-done.19, bf16[2,584,512]{2,1,0:T(8,128)(2,1)S(1)} %get-tuple-element.318.refs_3_), custom_call_target="tpu_custom_call" | custom-call | flops 20700000256 | bytes 20700000 | tf_op jit(solution)/shard_map/attn_backward/pallas_call | solution.py:94
  250.8 1.4 down_sum.1
  253.2 6.6 %qkv_grad.1 = (bf16[8,512,128]{2,1,0:T(8,128)(2,1)S(1)}, bf16[8,512,128]{2,1,0:T(8,128)(2,1)S(1)}, bf16[8,512,128]{2,1,0:T(8,128)(2,1)S(1)}) custom-call(bf16[1168,1024]{1,0:T(8,128)(2,1)S(1)} %bitcast.95, bf16[3,1168,128]{2,1,0:T(8,128)(2,1)S(1)} %bitcast.101, ...), custom_call_target="tpu_custom_call", output_to_operand_aliasing={{0}: (3, {}), {1}: (4, {}), {2}: (5, {})} | custom-call | flops 8049999872 | bytes 8050000 | tf_op jit(solution)/shard_map/qkv_grad/pallas_call | solution.py:94
  260.4 1.4 collective-permute-start.39
  261.8 8.0 %attn_backward.3 = (bf16[3,2,584,128]{3,2,1,0:T(8,128)(2,1)S(1)}, f32[2,2,128]{2,1,0:T(2,128)S(1)}) custom-call(bf16[2,584,512]{2,1,0:T(8,128)(2,1)S(1)} %copy-done.15, bf16[2,584,512]{2,1,0:T(8,128)(2,1)S(1)} %copy-done.17, bf16[2,584,512]{2,1,0:T(8,128)(2,1)S(1)} %copy-done.19, bf16[2,584,512]{2,1,0:T(8,128)(2,1)S(1)} %get-tuple-element.318.refs_3_), custom_call_target="tpu_custom_call" | custom-call | flops 20700000256 | bytes 20700000 | tf_op jit(solution)/shard_map/attn_backward/pallas_call | solution.py:94
  269.8 1.4 copy-done.11
  271.2 2.6 qkv_keep.1.refs_0_
  273.8 7.1 %grad_one.1.refs_9_ = bf16[2,584,1024]{2,1,0:T(8,128)(2,1)S(1)} custom-call(bf16[3,1168,128]{2,1,0:T(8,128)(2,1)S(1)} %bitcast.102, bf16[6,1168,128]{2,1,0:T(8,128)(2,1)S(1)} %bitcast.100, bf16[3,1168,128]{2,1,0:T(8,128)(2,1)S(1)} %bitcast.94, bf16[8,528,128]{2,1,0:T(8,128)(2,1)S(1)} %copy-done.3, ...), custom_call_target="tpu_custom_call" | custom-call | flops 23000000 | bytes 23000 | tf_op jit(solution)/shard_map/grad_one/pallas_call | solution.py:94
  281.7 3.7 %collective-permute-done.38.refs_1_ = bf16[8,512,128]{2,1,0:T(8,128)(2,1)S(1)} collective-permute-done((bf16[8,512,128]{2,1,0:T(8,128)(2,1)S(1)}, bf16[8,512,128]{2,1,0:T(8,128)(2,1)S(1)}, u32[]{:S(2)}, u32[]{:S(2)}) %collective-permute-start.38) | collective-permute-done | bytes 1048608 | tf_op jit(solution)/shard_map/ppermute | solution.py:808
  287.0 1.5 collective-permute-start.41
  289.2 1.8 collective-permute-start.43
  290.9 7.2 %finish_tokens.1 = (bf16[584,1024]{1,0:T(8,128)(2,1)}, f32[2,1024]{1,0:T(2,128)}, f32[4,16,128]{2,1,0:T(8,128)S(1)}, f32[4,16,128]{2,1,0:T(8,128)S(1)}, f32[4,16...) custom-call(s32[10]{0:T(128)S(1)} %copy-done.23, f32[6,1024]{1,0:T(8,128)S(1)} %copy-done.21, ...), custom_call_target="tpu_custom_call" | custom-call | flops 10350000128 | bytes 10350000 | tf_op jit(solution)/shard_map/finish_tokens/pallas_call | solution.py:94
  298.1 2.2 collective-permute-done.41.refs_1_
  302.1 1.4 collective-permute-start.46
  303.5 1.4 collective-permute-start.47
  306.3 2.0 collective-permute-done.47.refs_7_
  308.3 1.7 qkv_addz.1
  310.7 3.0 collective-permute-start.49
  313.7 1.4 collective-permute-start.50
  315.1 2.4 copy-done
  317.4 1.7 copy-done.12
  319.1 3.2 finish_layer.1
  323.1 7.9 %collective-permute-done.49.refs_2_ = bf16[1040,128]{1,0:T(8,128)(2,1)S(1)} collective-permute-done((bf16[1040,128]{1,0:T(8,128)(2,1)}, bf16[1040,128]{1,0:T(8,128)(2,1)S(1)}, u32[]{:S(2)}, u32[]{:S(2)}) %collective-permute-start.49) | collective-permute-done | bytes 266272 | tf_op jit(solution)/shard_map/ppermute | solution.py:797
  335.2 1.4 qkv_sum.1
  (224 shorter events, 44.3 us)
Async XLA Ops:
  0.6 10.8 %collective-permute-start.3 = (bf16[584,1024]{1,0:T(8,128)(2,1)}, bf16[584,1024]{1,0:T(8,128)(2,1)}, u32[]{:S(2)}, u32[]{:S(2)}) collective-permute-start(bf16[584,1024]{1,0:T(8,128)(2,1)} %refs_1_.1), channel_id=1, source_target_pairs={{0,1},{1,0},{2,3},{3,2},{4,5},{5,4},{6,7},{7,6},{8,9},{9,8},{10,11... | collective-permute-start | bytes 3588104 | tf_op jit(solution)/shard_map/ppermute | solution.py:812
  1.2 10.3 %collective-permute-start.4 = (bf16[584,1024]{1,0:T(8,128)(2,1)}, bf16[584,1024]{1,0:T(8,128)(2,1)}, u32[]{:S(2)}, u32[]{:S(2)}) collective-permute-start(bf16[584,1024]{1,0:T(8,128)(2,1)} %refs_2_.1), channel_id=1, source_target_pairs={{0,1},{1,0},{2,3},{3,2},{4,5},{5,4},{6,7},{7,6},{8,9},{9,8},{10,11... | collective-permute-start | bytes 3588104 | tf_op jit(solution)/shard_map/ppermute | solution.py:812
  5.1 14.8 %collective-permute-start = (bf16[1040,128]{1,0:T(8,128)(2,1)S(1)}, bf16[1040,128]{1,0:T(8,128)(2,1)S(1)}, u32[]{:S(2)}, u32[]{:S(2)}) collective-permute-start(bf16[1040,128]{1,0:T(8,128)(2,1)S(1)} %concatenate.26), channel_id=1, source_target_pairs={{0,8},{4,12},{8,0},{12,4},{16,24},{20,28},{24,16},{28,20},{1,9},{5... | collective-permute-start | bytes 798728 | tf_op jit(solution)/shard_map/ppermute | solution.py:797
  8.2 21.6 %collective-permute-start.1 = (bf16[1040,128]{1,0:T(8,128)(2,1)S(1)}, bf16[1040,128]{1,0:T(8,128)(2,1)S(1)}, u32[]{:S(2)}, u32[]{:S(2)}) collective-permute-start(bf16[1040,128]{1,0:T(8,128)(2,1)S(1)} %concatenate.26), channel_id=1, source_target_pairs={{0,16},{4,20},{8,24},{12,28},{16,0},{20,4},{24,8},{28,12},{1,17},{... | collective-permute-start | bytes 798728 | tf_op jit(solution)/shard_map/ppermute | solution.py:797
  10.8 19.0 %collective-permute-start.2 = (bf16[1040,128]{1,0:T(8,128)(2,1)S(1)}, bf16[1040,128]{1,0:T(8,128)(2,1)S(1)}, u32[]{:S(2)}, u32[]{:S(2)}) collective-permute-start(bf16[1040,128]{1,0:T(8,128)(2,1)S(1)} %concatenate.26), channel_id=1, source_target_pairs={{0,24},{4,28},{8,16},{12,20},{16,8},{20,12},{24,0},{28,4},{1,25},{... | collective-permute-start | bytes 798728 | tf_op jit(solution)/shard_map/ppermute | solution.py:797
  30.1 12.2 %collective-permute-start.5 = (bf16[4,528,128]{2,1,0:T(8,128)(2,1)S(1)}, bf16[4,528,128]{2,1,0:T(8,128)(2,1)S(1)}, u32[]{:S(2)}, u32[]{:S(2)}) collective-permute-start(bf16[4,528,128]{2,1,0:T(8,128)(2,1)S(1)} %pad_maximum_fusion), channel_id=1, source_target_pairs={{0,4},{4,0},{8,12},{12,8},{16,20},{20,16},{24,28},{28,24},{1,5},{5... | collective-permute-start | bytes 1622024 | tf_op jit(solution)/shard_map/ppermute | solution.py:800
  31.8 12.8 %collective-permute-start.7 = (bf16[4,512,128]{2,1,0:T(8,128)(2,1)S(1)}, bf16[4,512,128]{2,1,0:T(8,128)(2,1)S(1)}, u32[]{:S(2)}, u32[]{:S(2)}) collective-permute-start(bf16[4,512,128]{2,1,0:T(8,128)(2,1)S(1)} %pad_maximum_fusion.1), channel_id=1, source_target_pairs={{0,2},{2,0},{1,3},{3,1},{4,6},{6,4},{5,7},{7,5},{8,10},{10,8},{9,1... | collective-permute-start | bytes 1572872 | tf_op jit(solution)/shard_map/ppermute | solution.py:808
  33.4 12.2 %copy-start.47 = (s32[4]{0:T(128)S(1)}, s32[4]{0:T(128)}, u32[]{:S(2)}) copy-start(s32[4]{0:T(128)} %param.13) | copy-start | bytes 52
  33.4 12.8 %copy-start.45 = (bf16[1024,128]{1,0:T(8,128)(2,1)S(1)}, bf16[1024,128]{1,0:T(8,128)(2,1)}, u32[]{:S(2)}) copy-start(bf16[1024,128]{1,0:T(8,128)(2,1)} %param.21) | copy-start | bytes 786436
  33.4 12.8 %copy-start.46 = (bf16[128,1024]{1,0:T(8,128)(2,1)S(1)}, bf16[128,1024]{1,0:T(8,128)(2,1)}, u32[]{:S(2)}) copy-start(bf16[128,1024]{1,0:T(8,128)(2,1)} %param.19) | copy-start | bytes 786436
  42.3 24.3 %collective-permute-start.6 = (bf16[8,528,128]{2,1,0:T(8,128)(2,1)S(1)}, bf16[8,528,128]{2,1,0:T(8,128)(2,1)}, u32[]{:S(2)}, u32[]{:S(2)}) collective-permute-start(bf16[8,528,128]{2,1,0:T(8,128)(2,1)S(1)} %constant_dynamic-update-slice_fusion.refs_1_.refs_3_.refs_7_.refs_8_.refs_12_), channel_id=1, source_target_pairs={{0,2},{2,0},{1,3},{3,1},{4,6},{6,4},{5,7},{7,5},{8,10},{10,8},{9,1... | collective-permute-start | bytes 3244040 | tf_op jit(solution)/shard_map/ppermute | solution.py:808
  44.7 30.1 %copy-start.4 = (bf16[8,512,128]{2,1,0:T(8,128)(2,1)}, bf16[8,512,128]{2,1,0:T(8,128)(2,1)S(1)}, u32[]{:S(2)}) copy-start(bf16[8,512,128]{2,1,0:T(8,128)(2,1)S(1)} %constant_dynamic-update-slice_fusion.5.refs_5_.refs_9_.refs_10_.refs_14_) | copy-start | bytes 3145732
  44.7 21.3 %collective-permute-start.8 = (bf16[8,512,128]{2,1,0:T(8,128)(2,1)S(1)}, bf16[8,512,128]{2,1,0:T(8,128)(2,1)}, u32[]{:S(2)}, u32[]{:S(2)}) collective-permute-start(bf16[8,512,128]{2,1,0:T(8,128)(2,1)S(1)} %constant_dynamic-update-slice_fusion.5.refs_5_.refs_9_.refs_10_.refs_14_), channel_id=1, source_target_pairs={{0,4},{4,0},{8,12},{12,8},{16,20},{20,16},{24,28},{28,24},{1,5},{5... | collective-permute-start | bytes 3145736 | tf_op jit(solution)/shard_map/ppermute | solution.py:800
  46.2 22.9 %collective-permute-start.9 = (bf16[256,512]{1,0:T(8,128)(2,1)S(1)}, bf16[256,512]{1,0:T(8,128)(2,1)S(1)}, u32[]{:S(2)}, u32[]{:S(2)}) collective-permute-start(bf16[256,512]{1,0:T(8,128)(2,1)S(1)} %constant_dynamic-update-slice_fusion.10), channel_id=1, source_target_pairs={{0,8},{4,12},{8,0},{12,4},{16,24},{20,28},{24,16},{28,20},{1,9},{5... | collective-permute-start | bytes 786440 | tf_op jit(solution)/shard_map/ppermute | solution.py:797
  52.5 20.4 %collective-permute-start.10 = (bf16[256,512]{1,0:T(8,128)(2,1)S(1)}, bf16[256,512]{1,0:T(8,128)(2,1)S(1)}, u32[]{:S(2)}, u32[]{:S(2)}) collective-permute-start(bf16[256,512]{1,0:T(8,128)(2,1)S(1)} %constant_dynamic-update-slice_fusion.10), channel_id=1, source_target_pairs={{0,16},{4,20},{8,24},{12,28},{16,0},{20,4},{24,8},{28,12},{1,17},{... | collective-permute-start | bytes 786440 | tf_op jit(solution)/shard_map/ppermute | solution.py:797
  53.6 19.3 %collective-permute-start.11 = (bf16[256,512]{1,0:T(8,128)(2,1)S(1)}, bf16[256,512]{1,0:T(8,128)(2,1)S(1)}, u32[]{:S(2)}, u32[]{:S(2)}) collective-permute-start(bf16[256,512]{1,0:T(8,128)(2,1)S(1)} %constant_dynamic-update-slice_fusion.10), channel_id=1, source_target_pairs={{0,24},{4,28},{8,16},{12,20},{16,8},{20,12},{24,0},{28,4},{1,25},{... | collective-permute-start | bytes 786440 | tf_op jit(solution)/shard_map/ppermute | solution.py:797
  73.1 16.5 %collective-permute-start.12 = (bf16[4,128,512]{2,1,0:T(8,128)(2,1)S(1)}, bf16[4,128,512]{2,1,0:T(8,128)(2,1)S(1)}, u32[]{:S(2)}, u32[]{:S(2)}) collective-permute-start(bf16[4,128,512]{2,1,0:T(8,128)(2,1)S(1)} %pad_maximum_fusion.2), channel_id=1, source_target_pairs={{0,4},{4,0},{8,12},{12,8},{16,20},{20,16},{24,28},{28,24},{1,5},{5... | collective-permute-start | bytes 1572872 | tf_op jit(solution)/shard_map/ppermute | solution.py:800
  73.8 15.8 %collective-permute-start.13 = (bf16[4,128,512]{2,1,0:T(8,128)(2,1)S(1)}, bf16[4,128,512]{2,1,0:T(8,128)(2,1)S(1)}, u32[]{:S(2)}, u32[]{:S(2)}) collective-permute-start(bf16[4,128,512]{2,1,0:T(8,128)(2,1)S(1)} %pad_maximum_fusion.3), channel_id=1, source_target_pairs={{0,2},{2,0},{1,3},{3,1},{4,6},{6,4},{5,7},{7,5},{8,10},{10,8},{9,1... | collective-permute-start | bytes 1572872 | tf_op jit(solution)/shard_map/ppermute | solution.py:808
  89.6 28.5 %copy-start.24 = (bf16[584,1024]{1,0:T(8,128)(2,1)}, bf16[584,1024]{1,0:T(8,128)(2,1)S(1)}, u32[]{:S(2)}) copy-start(bf16[584,1024]{1,0:T(8,128)(2,1)S(1)} %get-tuple-element.221.refs_4_) | copy-start | bytes 3588100
  89.8 24.0 %copy-start.44 = (bf16[8,128,512]{2,1,0:T(8,128)(2,1)}, bf16[8,128,512]{2,1,0:T(8,128)(2,1)S(1)}, u32[]{:S(2)}) copy-start(bf16[8,128,512]{2,1,0:T(8,128)(2,1)S(1)} %constant_dynamic-update-slice_fusion.12) | copy-start | bytes 3145732
  89.8 24.0 %copy-start.43 = (bf16[8,128,512]{2,1,0:T(8,128)(2,1)}, bf16[8,128,512]{2,1,0:T(8,128)(2,1)S(1)}, u32[]{:S(2)}) copy-start(bf16[8,128,512]{2,1,0:T(8,128)(2,1)S(1)} %constant_dynamic-update-slice_fusion.14) | copy-start | bytes 3145732
  89.9 30.5 %collective-permute-start.18 = (bf16[1024,128]{1,0:T(8,128)(2,1)S(1)}, bf16[1024,128]{1,0:T(8,128)(2,1)S(1)}, u32[]{:S(2)}, u32[]{:S(2)}) collective-permute-start(bf16[1024,128]{1,0:T(8,128)(2,1)S(1)} %constant_dynamic-update-slice_fusion.16), channel_id=1, source_target_pairs={{0,8},{4,12},{8,0},{12,4},{16,24},{20,28},{24,16},{28,20},{1,9},{5... | collective-permute-start | bytes 786440 | tf_op jit(solution)/shard_map/ppermute | solution.py:797
  93.6 26.7 %collective-permute-start.19 = (bf16[1024,128]{1,0:T(8,128)(2,1)S(1)}, bf16[1024,128]{1,0:T(8,128)(2,1)S(1)}, u32[]{:S(2)}, u32[]{:S(2)}) collective-permute-start(bf16[1024,128]{1,0:T(8,128)(2,1)S(1)} %constant_dynamic-update-slice_fusion.16), channel_id=1, source_target_pairs={{0,16},{4,20},{8,24},{12,28},{16,0},{20,4},{24,8},{28,12},{1,17},{... | collective-permute-start | bytes 786440 | tf_op jit(solution)/shard_map/ppermute | solution.py:797
  94.7 25.6 %collective-permute-start.20 = (bf16[1024,128]{1,0:T(8,128)(2,1)S(1)}, bf16[1024,128]{1,0:T(8,128)(2,1)S(1)}, u32[]{:S(2)}, u32[]{:S(2)}) collective-permute-start(bf16[1024,128]{1,0:T(8,128)(2,1)S(1)} %constant_dynamic-update-slice_fusion.16), channel_id=1, source_target_pairs={{0,24},{4,28},{8,16},{12,20},{16,8},{20,12},{24,0},{28,4},{1,25},{... | collective-permute-start | bytes 786440 | tf_op jit(solution)/shard_map/ppermute | solution.py:797
  96.1 22.0 %collective-permute-start.16 = (bf16[8,128,512]{2,1,0:T(8,128)(2,1)S(1)}, bf16[8,128,512]{2,1,0:T(8,128)(2,1)S(1)}, u32[]{:S(2)}, u32[]{:S(2)}) collective-permute-start(bf16[8,128,512]{2,1,0:T(8,128)(2,1)S(1)} %constant_dynamic-update-slice_fusion.12), channel_id=1, source_target_pairs={{0,2},{2,0},{1,3},{3,1},{4,6},{6,4},{5,7},{7,5},{8,10},{10,8},{9,1... | collective-permute-start | bytes 3145736 | tf_op jit(solution)/shard_map/ppermute | solution.py:808
  97.3 22.6 %collective-permute-start.17 = (bf16[8,128,512]{2,1,0:T(8,128)(2,1)S(1)}, bf16[8,128,512]{2,1,0:T(8,128)(2,1)S(1)}, u32[]{:S(2)}, u32[]{:S(2)}) collective-permute-start(bf16[8,128,512]{2,1,0:T(8,128)(2,1)S(1)} %constant_dynamic-update-slice_fusion.14), channel_id=1, source_target_pairs={{0,4},{4,0},{8,12},{12,8},{16,20},{20,16},{24,28},{28,24},{1,5},{5... | collective-permute-start | bytes 3145736 | tf_op jit(solution)/shard_map/ppermute | solution.py:800
  98.3 19.8 %copy-start.1 = (bf16[2,584,1024]{2,1,0:T(8,128)(2,1)S(1)}, bf16[2,584,1024]{2,1,0:T(8,128)(2,1)}, u32[]{:S(2)}) copy-start(bf16[2,584,1024]{2,1,0:T(8,128)(2,1)} %get-tuple-element.231.refs_4_) | copy-start | bytes 7176196
  118.1 5.7 %collective-permute-start.15 = (bf16[584,1024]{1,0:T(8,128)(2,1)S(1)}, bf16[584,1024]{1,0:T(8,128)(2,1)S(1)}, u32[]{:S(2)}, u32[]{:S(2)}) collective-permute-start(bf16[584,1024]{1,0:T(8,128)(2,1)S(1)} %get-tuple-element.221.refs_4_), channel_id=1, source_target_pairs={{0,1},{1,0},{2,3},{3,2},{4,5},{5,4},{6,7},{7,6},{8,9},{9,8},{10,11... | collective-permute-start | bytes 3588104 | tf_op jit(solution)/shard_map/ppermute | solution.py:812
  119.9 22.1 %collective-permute-start.14 = (bf16[584,1024]{1,0:T(8,128)(2,1)}, bf16[584,1024]{1,0:T(8,128)(2,1)}, u32[]{:S(2)}, u32[]{:S(2)}) collective-permute-start(bf16[584,1024]{1,0:T(8,128)(2,1)} %get-tuple-element.220.refs_4_), channel_id=1, source_target_pairs={{0,1},{1,0},{2,3},{3,2},{4,5},{5,4},{6,7},{7,6},{8,9},{9,8},{10,11... | collective-permute-start | bytes 3588104 | tf_op jit(solution)/shard_map/ppermute | solution.py:812
  120.9 14.3 %collective-permute-start.21 = (bf16[4,512,128]{2,1,0:T(8,128)(2,1)S(1)}, bf16[4,512,128]{2,1,0:T(8,128)(2,1)}, u32[]{:S(2)}, u32[]{:S(2)}) collective-permute-start(bf16[4,512,128]{2,1,0:T(8,128)(2,1)S(1)} %pad_maximum_fusion.4.refs_0_), channel_id=1, source_target_pairs={{0,4},{4,0},{8,12},{12,8},{16,20},{20,16},{24,28},{28,24},{1,5},{5... | collective-permute-start | bytes 1572872 | tf_op jit(solution)/shard_map/ppermute | solution.py:800
  122.4 14.2 %collective-permute-start.22 = (bf16[4,512,128]{2,1,0:T(8,128)(2,1)}, bf16[4,512,128]{2,1,0:T(8,128)(2,1)}, u32[]{:S(2)}, u32[]{:S(2)}) collective-permute-start(bf16[4,512,128]{2,1,0:T(8,128)(2,1)} %pad_maximum_fusion.5.refs_2_), channel_id=1, source_target_pairs={{0,2},{2,0},{1,3},{3,1},{4,6},{6,4},{5,7},{7,5},{8,10},{10,8},{9,1... | collective-permute-start | bytes 1572872 | tf_op jit(solution)/shard_map/ppermute | solution.py:808
  139.9 25.1 %collective-permute-start.23 = (bf16[8,512,128]{2,1,0:T(8,128)(2,1)}, bf16[8,512,128]{2,1,0:T(8,128)(2,1)}, u32[]{:S(2)}, u32[]{:S(2)}) collective-permute-start(bf16[8,512,128]{2,1,0:T(8,128)(2,1)} %get-tuple-element.248.refs_3_), channel_id=1, source_target_pairs={{0,2},{2,0},{1,3},{3,1},{4,6},{6,4},{5,7},{7,5},{8,10},{10,8},{9,1... | collective-permute-start | bytes 3145736 | tf_op jit(solution)/shard_map/ppermute | solution.py:808
  141.4 25.5 %collective-permute-start.24 = (bf16[8,512,128]{2,1,0:T(8,128)(2,1)}, bf16[8,512,128]{2,1,0:T(8,128)(2,1)}, u32[]{:S(2)}, u32[]{:S(2)}) collective-permute-start(bf16[8,512,128]{2,1,0:T(8,128)(2,1)} %get-tuple-element.249.refs_5_), channel_id=1, source_target_pairs={{0,4},{4,0},{8,12},{12,8},{16,20},{20,16},{24,28},{28,24},{1,5},{5... | collective-permute-start | bytes 3145736 | tf_op jit(solution)/shard_map/ppermute | solution.py:800
  162.8 25.9 %collective-permute-start.26 = (bf16[8,512,128]{2,1,0:T(8,128)(2,1)}, bf16[8,512,128]{2,1,0:T(8,128)(2,1)}, u32[]{:S(2)}, u32[]{:S(2)}) collective-permute-start(bf16[8,512,128]{2,1,0:T(8,128)(2,1)} %get-tuple-element.233), channel_id=1, source_target_pairs={{0,4},{4,0},{8,12},{12,8},{16,20},{20,16},{24,28},{28,24},{1,5},{5... | collective-permute-start | bytes 3145736 | tf_op jit(solution)/shard_map/ppermute | solution.py:800
  164.3 24.4 %collective-permute-start.25 = (bf16[8,512,128]{2,1,0:T(8,128)(2,1)}, bf16[8,512,128]{2,1,0:T(8,128)(2,1)}, u32[]{:S(2)}, u32[]{:S(2)}) collective-permute-start(bf16[8,512,128]{2,1,0:T(8,128)(2,1)} %get-tuple-element.254), channel_id=1, source_target_pairs={{0,2},{2,0},{1,3},{3,1},{4,6},{6,4},{5,7},{7,5},{8,10},{10,8},{9,1... | collective-permute-start | bytes 3145736 | tf_op jit(solution)/shard_map/ppermute | solution.py:808
  188.6 16.7 %collective-permute-start.29 = (bf16[2,584,1024]{2,1,0:T(8,128)(2,1)}, bf16[2,584,1024]{2,1,0:T(8,128)(2,1)S(1)}, u32[]{:S(2)}, u32[]{:S(2)}) collective-permute-start(bf16[2,584,1024]{2,1,0:T(8,128)(2,1)} %get-tuple-element.272.refs_5_), channel_id=1, source_target_pairs={{0,1},{1,0},{2,3},{3,2},{4,5},{5,4},{6,7},{7,6},{8,9},{9,8},{10,11... | collective-permute-start | bytes 7176200 | tf_op jit(solution)/shard_map/ppermute | solution.py:812
  193.7 21.4 %collective-permute-start.30 = (bf16[4,512,128]{2,1,0:T(8,128)(2,1)S(1)}, bf16[4,512,128]{2,1,0:T(8,128)(2,1)S(1)}, u32[]{:S(2)}, u32[]{:S(2)}) collective-permute-start(bf16[4,512,128]{2,1,0:T(8,128)(2,1)S(1)} %get-tuple-element.276), channel_id=1, source_target_pairs={{0,4},{4,0},{8,12},{12,8},{16,20},{20,16},{24,28},{28,24},{1,5},{5... | collective-permute-start | bytes 1572872 | tf_op jit(solution)/shard_map/ppermute | solution.py:800
  193.8 21.3 %collective-permute-start.31 = (bf16[4,512,128]{2,1,0:T(8,128)(2,1)S(1)}, bf16[4,512,128]{2,1,0:T(8,128)(2,1)S(1)}, u32[]{:S(2)}, u32[]{:S(2)}) collective-permute-start(bf16[4,512,128]{2,1,0:T(8,128)(2,1)S(1)} %get-tuple-element.277), channel_id=1, source_target_pairs={{0,2},{2,0},{1,3},{3,1},{4,6},{6,4},{5,7},{7,5},{8,10},{10,8},{9,1... | collective-permute-start | bytes 1572872 | tf_op jit(solution)/shard_map/ppermute | solution.py:808
  195.9 9.5 %copy-start.6 = (bf16[8,512,128]{2,1,0:T(8,128)(2,1)S(1)}, bf16[8,512,128]{2,1,0:T(8,128)(2,1)}, u32[]{:S(2)}) copy-start(bf16[8,512,128]{2,1,0:T(8,128)(2,1)} %copy-done.4) | copy-start | bytes 3145732
  195.9 9.5 %copy-start.13 = (bf16[2,584,1024]{2,1,0:T(8,128)(2,1)S(1)}, bf16[2,584,1024]{2,1,0:T(8,128)(2,1)}, u32[]{:S(2)}) copy-start(bf16[2,584,1024]{2,1,0:T(8,128)(2,1)} %get-tuple-element.272.refs_5_) | copy-start | bytes 7176196
  195.9 9.5 %copy-start.21 = (f32[6,1024]{1,0:T(8,128)S(1)}, f32[6,1024]{1,0:T(8,128)}, u32[]{:S(2)}) copy-start(f32[6,1024]{1,0:T(8,128)} %get-tuple-element.197.refs_0_.refs_1_.refs_2_) | copy-start | bytes 73732
  203.3 28.4 %collective-permute-start.27 = (bf16[8,512,128]{2,1,0:T(8,128)(2,1)S(1)}, bf16[8,512,128]{2,1,0:T(8,128)(2,1)S(1)}, u32[]{:S(2)}, u32[]{:S(2)}) collective-permute-start(bf16[8,512,128]{2,1,0:T(8,128)(2,1)S(1)} %get-tuple-element.266), channel_id=1, source_target_pairs={{0,2},{2,0},{1,3},{3,1},{4,6},{6,4},{5,7},{7,5},{8,10},{10,8},{9,1... | collective-permute-start | bytes 3145736 | tf_op jit(solution)/shard_map/ppermute | solution.py:808
  203.4 28.3 %collective-permute-start.28 = (bf16[8,512,128]{2,1,0:T(8,128)(2,1)S(1)}, bf16[8,512,128]{2,1,0:T(8,128)(2,1)S(1)}, u32[]{:S(2)}, u32[]{:S(2)}) collective-permute-start(bf16[8,512,128]{2,1,0:T(8,128)(2,1)S(1)} %get-tuple-element.268), channel_id=1, source_target_pairs={{0,4},{4,0},{8,12},{12,8},{16,20},{20,16},{24,28},{28,24},{1,5},{5... | collective-permute-start | bytes 3145736 | tf_op jit(solution)/shard_map/ppermute | solution.py:800
  216.1 34.6 %collective-permute-start.34 = (bf16[1024,128]{1,0:T(8,128)(2,1)S(1)}, bf16[1024,128]{1,0:T(8,128)(2,1)S(1)}, u32[]{:S(2)}, u32[]{:S(2)}) collective-permute-start(bf16[1024,128]{1,0:T(8,128)(2,1)S(1)} %get-tuple-element.284), channel_id=1, source_target_pairs={{0,8},{4,12},{8,0},{12,4},{16,24},{20,28},{24,16},{28,20},{1,9},{5... | collective-permute-start | bytes 786440 | tf_op jit(solution)/shard_map/ppermute | solution.py:797
  216.7 34.1 %collective-permute-start.35 = (bf16[1024,128]{1,0:T(8,128)(2,1)S(1)}, bf16[1024,128]{1,0:T(8,128)(2,1)S(1)}, u32[]{:S(2)}, u32[]{:S(2)}) collective-permute-start(bf16[1024,128]{1,0:T(8,128)(2,1)S(1)} %get-tuple-element.285), channel_id=1, source_target_pairs={{0,16},{4,20},{8,24},{12,28},{16,0},{20,4},{24,8},{28,12},{1,17},{... | collective-permute-start | bytes 786440 | tf_op jit(solution)/shard_map/ppermute | solution.py:797
  219.1 31.7 %collective-permute-start.36 = (bf16[1024,128]{1,0:T(8,128)(2,1)S(1)}, bf16[1024,128]{1,0:T(8,128)(2,1)S(1)}, u32[]{:S(2)}, u32[]{:S(2)}) collective-permute-start(bf16[1024,128]{1,0:T(8,128)(2,1)S(1)} %get-tuple-element.286), channel_id=1, source_target_pairs={{0,24},{4,28},{8,16},{12,20},{16,8},{20,12},{24,0},{28,4},{1,25},{... | collective-permute-start | bytes 786440 | tf_op jit(solution)/shard_map/ppermute | solution.py:797
  233.1 19.2 %collective-permute-start.32 = (bf16[4,512,128]{2,1,0:T(8,128)(2,1)S(1)}, bf16[4,512,128]{2,1,0:T(8,128)(2,1)S(1)}, u32[]{:S(2)}, u32[]{:S(2)}) collective-permute-start(bf16[4,512,128]{2,1,0:T(8,128)(2,1)S(1)} %get-tuple-element.297), channel_id=1, source_target_pairs={{0,4},{4,0},{8,12},{12,8},{16,20},{20,16},{24,28},{28,24},{1,5},{5... | collective-permute-start | bytes 1572872 | tf_op jit(solution)/shard_map/ppermute | solution.py:800
  233.8 18.5 %collective-permute-start.33 = (bf16[4,512,128]{2,1,0:T(8,128)(2,1)S(1)}, bf16[4,512,128]{2,1,0:T(8,128)(2,1)S(1)}, u32[]{:S(2)}, u32[]{:S(2)}) collective-permute-start(bf16[4,512,128]{2,1,0:T(8,128)(2,1)S(1)} %get-tuple-element.299), channel_id=1, source_target_pairs={{0,2},{2,0},{1,3},{3,1},{4,6},{6,4},{5,7},{7,5},{8,10},{10,8},{9,1... | collective-permute-start | bytes 1572872 | tf_op jit(solution)/shard_map/ppermute | solution.py:808
  235.2 15.5 %copy-start.9 = (bf16[1168,1024]{1,0:T(8,128)(2,1)S(1)}, bf16[1168,1024]{1,0:T(8,128)(2,1)}, u32[]{:S(2)}) copy-start(bf16[1168,1024]{1,0:T(8,128)(2,1)} %get-tuple-element.250) | copy-start | bytes 7176196
  250.7 19.1 %collective-permute-start.37 = (bf16[2,584,1024]{2,1,0:T(8,128)(2,1)S(1)}, bf16[2,584,1024]{2,1,0:T(8,128)(2,1)S(1)}, u32[]{:S(2)}, u32[]{:S(2)}) collective-permute-start(bf16[2,584,1024]{2,1,0:T(8,128)(2,1)S(1)} %bitcast.97), channel_id=1, source_target_pairs={{0,1},{1,0},{2,3},{3,2},{4,5},{5,4},{6,7},{7,6},{8,9},{9,8},{10,11... | collective-permute-start | bytes 7176200 | tf_op jit(solution)/shard_map/ppermute | solution.py:812
  259.7 25.6 %collective-permute-start.38 = (bf16[8,512,128]{2,1,0:T(8,128)(2,1)S(1)}, bf16[8,512,128]{2,1,0:T(8,128)(2,1)S(1)}, u32[]{:S(2)}, u32[]{:S(2)}) collective-permute-start(bf16[8,512,128]{2,1,0:T(8,128)(2,1)S(1)} %get-tuple-element.316), channel_id=1, source_target_pairs={{0,2},{2,0},{1,3},{3,1},{4,6},{6,4},{5,7},{7,5},{8,10},{10,8},{9,1... | collective-permute-start | bytes 3145736 | tf_op jit(solution)/shard_map/ppermute | solution.py:808
  260.4 25.3 %collective-permute-start.39 = (bf16[8,512,128]{2,1,0:T(8,128)(2,1)S(1)}, bf16[8,512,128]{2,1,0:T(8,128)(2,1)S(1)}, u32[]{:S(2)}, u32[]{:S(2)}) collective-permute-start(bf16[8,512,128]{2,1,0:T(8,128)(2,1)S(1)} %get-tuple-element.317), channel_id=1, source_target_pairs={{0,4},{4,0},{8,12},{12,8},{16,20},{20,16},{24,28},{28,24},{1,5},{5... | collective-permute-start | bytes 3145736 | tf_op jit(solution)/shard_map/ppermute | solution.py:800
  261.8 19.2 %collective-permute-start.40 = (bf16[2,1024,128]{2,1,0:T(8,128)(2,1)S(1)}, bf16[2,1024,128]{2,1,0:T(8,128)(2,1)S(1)}, u32[]{:S(2)}, u32[]{:S(2)}) collective-permute-start(bf16[2,1024,128]{2,1,0:T(8,128)(2,1)S(1)} %get-tuple-element.325), channel_id=1, source_target_pairs={{0,8},{4,12},{8,0},{12,4},{16,24},{20,28},{24,16},{28,20},{1,9},{5... | collective-permute-start | bytes 1572872 | tf_op jit(solution)/shard_map/ppermute | solution.py:797
  280.9 10.0 %collective-permute-start.44 = (bf16[2,584,1024]{2,1,0:T(8,128)(2,1)S(1)}, bf16[2,584,1024]{2,1,0:T(8,128)(2,1)S(1)}, u32[]{:S(2)}, u32[]{:S(2)}) collective-permute-start(bf16[2,584,1024]{2,1,0:T(8,128)(2,1)S(1)} %grad_one.1.refs_9_), channel_id=1, source_target_pairs={{0,1},{1,0},{2,3},{3,2},{4,5},{5,4},{6,7},{7,6},{8,9},{9,8},{10,11... | collective-permute-start | bytes 7176200 | tf_op jit(solution)/shard_map/ppermute | solution.py:812
  287.0 13.3 %collective-permute-start.41 = (bf16[4,512,128]{2,1,0:T(8,128)(2,1)S(1)}, bf16[4,512,128]{2,1,0:T(8,128)(2,1)S(1)}, u32[]{:S(2)}, u32[]{:S(2)}) collective-permute-start(bf16[4,512,128]{2,1,0:T(8,128)(2,1)S(1)} %get-tuple-element.337), channel_id=1, source_target_pairs={{0,4},{4,0},{8,12},{12,8},{16,20},{20,16},{24,28},{28,24},{1,5},{5... | collective-permute-start | bytes 1572872 | tf_op jit(solution)/shard_map/ppermute | solution.py:800
  288.5 12.9 %collective-permute-start.42 = (bf16[4,512,128]{2,1,0:T(8,128)(2,1)S(1)}, bf16[4,512,128]{2,1,0:T(8,128)(2,1)S(1)}, u32[]{:S(2)}, u32[]{:S(2)}) collective-permute-start(bf16[4,512,128]{2,1,0:T(8,128)(2,1)S(1)} %get-tuple-element.339), channel_id=1, source_target_pairs={{0,2},{2,0},{1,3},{3,1},{4,6},{6,4},{5,7},{7,5},{8,10},{10,8},{9,1... | collective-permute-start | bytes 1572872 | tf_op jit(solution)/shard_map/ppermute | solution.py:808
  289.2 15.8 %collective-permute-start.43 = (bf16[1,1024,128]{2,1,0:T(8,128)(2,1)S(1)}, bf16[1,1024,128]{2,1,0:T(8,128)(2,1)S(1)}, u32[]{:S(2)}, u32[]{:S(2)}) collective-permute-start(bf16[1,1024,128]{2,1,0:T(8,128)(2,1)S(1)} %get-tuple-element.340), channel_id=1, source_target_pairs={{0,16},{4,20},{8,24},{12,28},{16,0},{20,4},{24,8},{28,12},{1,17},{... | collective-permute-start | bytes 786440 | tf_op jit(solution)/shard_map/ppermute | solution.py:797
  301.4 4.8 %collective-permute-start.45 = (f32[4,16,128]{2,1,0:T(8,128)S(1)}, f32[4,16,128]{2,1,0:T(8,128)S(1)}, u32[]{:S(2)}, u32[]{:S(2)}) collective-permute-start(f32[4,16,128]{2,1,0:T(8,128)S(1)} %get-tuple-element.354), channel_id=1, source_target_pairs={{0,4},{2,6},{4,0},{6,2},{8,12},{10,14},{12,8},{14,10},{16,20},{18,... | collective-permute-start | bytes 98312 | tf_op jit(solution)/shard_map/ppermute | solution.py:805
  302.1 4.2 %collective-permute-start.46 = (f32[4,16,128]{2,1,0:T(8,128)S(1)}, f32[4,16,128]{2,1,0:T(8,128)S(1)}, u32[]{:S(2)}, u32[]{:S(2)}) collective-permute-start(f32[4,16,128]{2,1,0:T(8,128)S(1)} %get-tuple-element.355), channel_id=1, source_target_pairs={{0,2},{2,0},{4,6},{6,4},{8,10},{10,8},{12,14},{14,12},{16,18},{18,... | collective-permute-start | bytes 98312 | tf_op jit(solution)/shard_map/ppermute | solution.py:805
  303.5 4.8 %collective-permute-start.47 = (f32[4,16,128]{2,1,0:T(8,128)S(1)}, f32[4,16,128]{2,1,0:T(8,128)S(1)}, u32[]{:S(2)}, u32[]{:S(2)}) collective-permute-start(f32[4,16,128]{2,1,0:T(8,128)S(1)} %get-tuple-element.356), channel_id=1, source_target_pairs={{0,6},{2,4},{4,2},{6,0},{8,14},{10,12},{12,10},{14,8},{16,22},{18,... | collective-permute-start | bytes 98312 | tf_op jit(solution)/shard_map/ppermute | solution.py:805
  310.7 11.7 %collective-permute-start.48 = (bf16[1040,128]{1,0:T(8,128)(2,1)}, bf16[1040,128]{1,0:T(8,128)(2,1)S(1)}, u32[]{:S(2)}, u32[]{:S(2)}) collective-permute-start(bf16[1040,128]{1,0:T(8,128)(2,1)} %get-tuple-element.358), channel_id=1, source_target_pairs={{0,8},{4,12},{8,0},{12,4},{16,24},{20,28},{24,16},{28,20},{1,9},{5... | collective-permute-start | bytes 798728 | tf_op jit(solution)/shard_map/ppermute | solution.py:797
  310.7 20.2 %collective-permute-start.49 = (bf16[1040,128]{1,0:T(8,128)(2,1)}, bf16[1040,128]{1,0:T(8,128)(2,1)S(1)}, u32[]{:S(2)}, u32[]{:S(2)}) collective-permute-start(bf16[1040,128]{1,0:T(8,128)(2,1)} %get-tuple-element.359), channel_id=1, source_target_pairs={{0,16},{4,20},{8,24},{12,28},{16,0},{20,4},{24,8},{28,12},{1,17},{... | collective-permute-start | bytes 798728 | tf_op jit(solution)/shard_map/ppermute | solution.py:797
  313.7 18.0 %collective-permute-start.50 = (bf16[1040,128]{1,0:T(8,128)(2,1)}, bf16[1040,128]{1,0:T(8,128)(2,1)S(1)}, u32[]{:S(2)}, u32[]{:S(2)}) collective-permute-start(bf16[1040,128]{1,0:T(8,128)(2,1)} %get-tuple-element.360), channel_id=1, source_target_pairs={{0,24},{4,28},{8,16},{12,20},{16,8},{20,12},{24,0},{28,4},{1,25},{... | collective-permute-start | bytes 798728 | tf_op jit(solution)/shard_map/ppermute | solution.py:797
  319.1 13.3 %copy-start.40 = (bf16[1040,128]{1,0:T(8,128)(2,1)S(1)}, bf16[1040,128]{1,0:T(8,128)(2,1)}, u32[]{:S(2)}) copy-start(bf16[1040,128]{1,0:T(8,128)(2,1)} %copy-done.39) | copy-start | bytes 798724
  (38 other events, 114.8 us)

commit v7 on v6

--- a/solution.py
+++ b/solution.py
@@ -13,7 +13,7 @@
 BF = jnp.bfloat16
 F32 = jnp.float32
 VMEM_LIMIT = 60 * 1024 * 1024
-WHOLE_VMEM = ("arrange_pair", "vectors", "mlp_up", "down_grad", "mlp_back")
+WHOLE_VMEM = ("arrange_pair", "vectors", "mlp_up", "down_grad", "mlp_back", "qkv_sum")
 COST_SCALE = 1.0
 COST = {
     "arrange_pair": 5,
@@ -380,7 +380,12 @@
 def weight_grad(lefts, rights, tasks, out_shapes, name, lo, hi, prev=None, fill=False):
     rows = lefts[0].shape[0]
     arrays = list(lefts) + list(rights)
-    wide = [a.shape[-1] * (a.shape[0] if len(a.shape) == 3 else 1) for a in arrays]
+    joined = all(len(a.shape) == 3 for a in rights)
+    if joined:
+        total = sum(a.shape[0] for a in rights) // 3
+        wide = [a.shape[-1] for a in lefts] + [3 * total * rights[0].shape[-1]]
+    else:
+        wide = [a.shape[-1] for a in arrays]
     n_left, n_in = len(lefts), len(arrays)
     prev = list(prev or [])
     last = {}
@@ -389,13 +394,24 @@
             last[store[0]] = n
 
     def body(small, ins, outs, scratch, loads):
-        in_s, out_s = scratch[:n_in], scratch[n_in:]
+        in_s, out_s = scratch[: len(wide)], scratch[len(wide) :]
         order = []
         for l_index, _, r_index, _, _ in tasks:
             for i in (l_index, n_left + r_index):
                 if i not in order:
                     order.append(i)
-        groups = {i: loads.start(column_loads(ins[i], in_s[i], 0)) for i in order}
+        groups = {}
+        for i in order:
+            pairs = [(ins[i], in_s[i])]
+            if joined and i == n_left:
+                pairs, start = [], 0
+                for j, stack in enumerate(rights):
+                    count = stack.shape[0] // 3
+                    for kind in range(3):
+                        part = ins[n_left + j].at[kind * count : (kind + 1) * count]
+                        pairs += column_loads(part, in_s[i], kind * total + start)
+                    start += count
+            groups[i] = loads.start(pairs)
         for ref in out_s if fill else ():
             ref[...] = jnp.zeros_like(ref)
         ready, done = set(), []
@@ -897,7 +913,7 @@
         a_got = [grid.send_y(a_y[k], k) for k in range(1, grid.y)]
         b_got = [grid.send_x(b_x[k], k) for k in range(1, grid.tx)]
         self.state = ([a_y[0]] + a_got, [b_x[0]] + b_got)
-        return a_y[0], b_x[0]
+        return a_y, b_x
 
     def along_z(self, gate, extra=None):
         grid = self.grid
@@ -1214,29 +1230,33 @@
         heads = [list(range(n_pairs))]
         up_half = up_rs.second(out_grads[-1])
     left_a, bias_a = attn_backward(heads[-1], after(grad_att, up_half), q, k, v)
-    grad_down = down_rs.finish(bias_a, [(full, 0, full)], [sds((fw, bd), F32)])[0]
-    mlp_recv = swap_core(after(mlp_part, bias_a))
-    gate = up_rs.halve(grad_down) if z_n > 1 else grad_down
-    first_in = after(flat(first), gate)
+    first_in = flat(first)
+    gate = bias_a
+    if not split:
+        grad_down = down_rs.finish(bias_a, [(full, 0, full)], [sds((fw, bd), F32)])[0]
+        mlp_recv = swap_core(after(mlp_part, bias_a))
+        gate = up_rs.halve(grad_down) if z_n > 1 else grad_down
     if split:
-        tasks = []
-        for index, pairs in enumerate(heads):
-            stores, count = [], len(pairs)
-            for i in range(3):
-                rows = slice(i * bd, (i + 1) * bd)
-                for n, pair in enumerate(pairs):
-                    kx, cols = pair // 2, slice((i * count + n) * 128, (i * count + n + 1) * 128)
-                    for p, r_sl in a_spots:
-                        ky, kz = p // z_n, p % z_n
-                        spot = (kx - 1, (p, rows))
-                        if pair % 2:
-                            spot = (tx - 1 + ky, (kx * z_n + kz, rows))
-                        stores.append(spot + (r_sl, cols))
-            tasks.append((0, slice(0, width), index, slice(0, 384 * count), stores))
+        stores, count = [], n_pairs - 1
+        for i in range(3):
+            rows = slice(i * bd, (i + 1) * bd)
+            for n, pair in enumerate(range(1, n_pairs)):
+                kx, cols = pair // 2, slice((i * count + n) * 128, (i * count + n + 1) * 128)
+                for p, r_sl in a_spots:
+                    ky, kz = p // z_n, p % z_n
+                    spot = (kx - 1, (p, rows))
+                    if pair % 2:
+                        spot = (tx - 1 + ky, (kx * z_n + kz, rows))
+                    stores.append(spot + (r_sl, cols))
+        tasks = [(0, slice(0, width), 0, slice(0, 384 * count), stores)]
         sent = weight_grad(
             [first_in], [left_0, left_a], tasks, last_shapes[1:], "qkv_grad", 0, row0, out_grads[1:]
         )
-        left_b, bias_b = attn_backward([0], after(grad_att, (sent[: tx - 1], sent[tx:])), q, k, v)
+        leaving = (sent[: tx - 1], sent[tx:])
+        grad_down = down_rs.finish(sent[-1], [(full, 0, full)], [sds((fw, bd), F32)])[0]
+        mlp_recv = swap_core(after(mlp_part, bias_a))
+        gate = up_rs.halve((grad_down, leaving)) if z_n > 1 else grad_down
+        left_b, bias_b = attn_backward([0], after(grad_att, (leaving, gate)), q, k, v)
         gate = (bias_b, mlp_recv)
         stores = []
         for i in range(3):

time: 343 us -> 341 us (level)
    unnamed x114 -> x106, local copies, waits for them, and re-layouts: 17.5 us -> 13.2 us
where the time goes in v7:
time: 341 us; the launch traced here: 336 us
  Pallas kernels  185 us (54%)
  starting transfers between devices  62.2 us (18%)
  waiting for transfers between devices  60.9 us (18%)
  local copies, waits for them, and re-layouts  22 us (6%)
  other arithmetic  4.11 us (1%)
    pallas_call x30, Pallas kernels, call(): pl.pallas_call(kernel, out_shape=outs, in_specs=[pl.BlockSpec(memory_spac...  185 us
    ppermute x17, starting transfers between devices, send_z(): lax.ppermute(value, 'dp', [(i, i ^ k * self.y) for i in range(self.dp)])  31.5 us
    ppermute x17, waiting for transfers between devices, send_z(): lax.ppermute(value, 'dp', [(i, i ^ k * self.y) for i in range(self.dp)])  27.1 us
    ppermute x12, waiting for transfers between devices, send_y(): return lax.ppermute(value, 'dp', [(i, i ^ k) for i in range(self.dp)])  24.4 us
    ppermute x12, starting transfers between devices, send_x(): return lax.ppermute(value, 'tx', [(i, i ^ k) for i in range(self.tx)])  13.7 us
    unnamed x106, local copies, waits for them, and re-layouts  13.2 us
    ppermute x12, starting transfers between devices, send_y(): return lax.ppermute(value, 'dp', [(i, i ^ k) for i in range(self.dp)])  12.3 us
    ppermute x12, waiting for transfers between devices, send_x(): return lax.ppermute(value, 'tx', [(i, i ^ k) for i in range(self.tx)])  7.33 us
  transfers between devices with their start and end apart: 51, of which 17 were waited for; matrix products, arithmetic and copies ran while one was open for 2% of the time, Pallas kernels for 54%

profile of v7, /device:TPU:0, one launch (start us, length us, event | category | flops | bytes accessed | tf_op | source)
XLA Modules:
  0.0 336.4 jit_solution(12486762725998709705)
XLA Ops:
  3.7 1.5 concatenate.26
  5.1 3.1 collective-permute-start
  8.2 2.6 collective-permute-start.1
  11.5 4.9 %arrange_pair.1 = (bf16[2,584,1024]{2,1,0:T(8,128)(2,1)}, bf16[2,584,1024]{2,1,0:T(8,128)(2,1)}) custom-call(s32[10]{0:T(128)} %stack.130.refs_0_, bf16[584,1024]{1,0:T(8,128)(2,1)} %refs_1_.1, bf16[584,1024]{1,0:T(8,128)(2,1)} %refs_2_.1, bf16[584,1024]{1,0:T(8,128)(2,1)} %collective-permute-done.3.refs_3_, bf16[584,1024]{1,0:T(8,128)(2,1)} %collective-permute-done.4.refs_4_), custom_call_target="tpu_custom_call" | custom-call | flops 5750000128 | bytes 5750000 | tf_op jit(solution)/shard_map/arrange_pair/pallas_call | solution.py:94
  16.3 3.6 %collective-permute-done = bf16[1040,128]{1,0:T(8,128)(2,1)S(1)} collective-permute-done((bf16[1040,128]{1,0:T(8,128)(2,1)S(1)}, bf16[1040,128]{1,0:T(8,128)(2,1)S(1)}, u32[]{:S(2)}, u32[]{:S(2)}) %collective-permute-start) | collective-permute-done | bytes 266272 | tf_op jit(solution)/shard_map/ppermute | solution.py:813
  19.9 9.9 %collective-permute-done.1 = bf16[1040,128]{1,0:T(8,128)(2,1)S(1)} collective-permute-done((bf16[1040,128]{1,0:T(8,128)(2,1)S(1)}, bf16[1040,128]{1,0:T(8,128)(2,1)S(1)}, u32[]{:S(2)}, u32[]{:S(2)}) %collective-permute-start.1) | collective-permute-done | bytes 266272 | tf_op jit(solution)/shard_map/ppermute | solution.py:813
  30.1 1.6 collective-permute-start.5
  31.8 1.6 collective-permute-start.7
  33.4 8.8 %collective-permute-done.5 = bf16[4,528,128]{2,1,0:T(8,128)(2,1)S(1)} collective-permute-done((bf16[4,528,128]{2,1,0:T(8,128)(2,1)S(1)}, bf16[4,528,128]{2,1,0:T(8,128)(2,1)S(1)}, u32[]{:S(2)}, u32[]{:S(2)}) %collective-permute-start.5) | collective-permute-done | bytes 540704 | tf_op jit(solution)/shard_map/ppermute | solution.py:816
  42.3 1.6 collective-permute-start.6
  46.2 6.2 %collective-permute-start.9 = (bf16[256,512]{1,0:T(8,128)(2,1)S(1)}, bf16[256,512]{1,0:T(8,128)(2,1)S(1)}, u32[]{:S(2)}, u32[]{:S(2)}) collective-permute-start(bf16[256,512]{1,0:T(8,128)(2,1)S(1)} %constant_dynamic-update-slice_fusion.10), channel_id=1, source_target_pairs={{0,8},{4,12},{8,0},{12,4},{16,24},{20,28},{24,16},{28,20},{1,9},{5... | collective-permute-start | bytes 786440 | tf_op jit(solution)/shard_map/ppermute | solution.py:813
  53.6 1.4 collective-permute-start.11
  55.0 11.0 %collective-permute-done.8.refs_6_.refs_10_.refs_11_.refs_15_ = bf16[8,512,128]{2,1,0:T(8,128)(2,1)} collective-permute-done((bf16[8,512,128]{2,1,0:T(8,128)(2,1)S(1)}, bf16[8,512,128]{2,1,0:T(8,128)(2,1)}, u32[]{:S(2)}, u32[]{:S(2)}) %collective-permute-start.8) | collective-permute-done | bytes 1048608 | tf_op jit(solution)/shard_map/ppermute | solution.py:816
  66.6 2.6 vectors.1
  69.2 3.7 %collective-permute-done.10 = bf16[256,512]{1,0:T(8,128)(2,1)S(1)} collective-permute-done((bf16[256,512]{1,0:T(8,128)(2,1)S(1)}, bf16[256,512]{1,0:T(8,128)(2,1)S(1)}, u32[]{:S(2)}, u32[]{:S(2)}) %collective-permute-start.10) | collective-permute-done | bytes 262176 | tf_op jit(solution)/shard_map/ppermute | solution.py:813
  74.9 14.7 %attn_forward.2 = (bf16[2,584,1024]{2,1,0:T(8,128)(2,1)S(1)}, bf16[2,584,512]{2,1,0:T(8,128)(2,1)S(1)}, bf16[2,584,512]{2,1,0:T(8,128)(2,1)S(1)}, bf16[2,584,512...) custom-call(f32[6,1024]{1,0:T(8,128)S(1)} %copy-done.20, ...), custom_call_target="tpu_custom_call" | custom-call | flops 18400000000 | bytes 18400000 | tf_op jit(solution)/shard_map/attn_forward/pallas_call | solution.py:94
  89.9 3.8 %collective-permute-start.18 = (bf16[1024,128]{1,0:T(8,128)(2,1)S(1)}, bf16[1024,128]{1,0:T(8,128)(2,1)S(1)}, u32[]{:S(2)}, u32[]{:S(2)}) collective-permute-start(bf16[1024,128]{1,0:T(8,128)(2,1)S(1)} %constant_dynamic-update-slice_fusion.16), channel_id=1, source_target_pairs={{0,8},{4,12},{8,0},{12,4},{16,24},{20,28},{24,16},{28,20},{1,9},{5... | collective-permute-start | bytes 786440 | tf_op jit(solution)/shard_map/ppermute | solution.py:813
  94.7 1.4 collective-permute-start.20
  98.3 15.5 %attn_forward.3 = (bf16[2,584,1024]{2,1,0:T(8,128)(2,1)S(1)}, bf16[2,584,512]{2,1,0:T(8,128)(2,1)S(1)}, bf16[2,584,512]{2,1,0:T(8,128)(2,1)S(1)}, bf16[2,584,512...) custom-call(f32[6,1024]{1,0:T(8,128)S(1)} %copy-done.20, ...), custom_call_target="tpu_custom_call", output_to_operand_aliasing={{0}: (3, {}), {1}: (4, {}), {2}: (5, {}), {3}: (6, {}), {4}... | custom-call | flops 18400000000 | bytes 18400000 | tf_op jit(solution)/shard_map/attn_forward/pallas_call | solution.py:94
  115.9 2.2 collective-permute-done.16
  118.1 1.7 broadcast_multiply_fusion
  122.3 1.4 collective-permute-start.22
  124.8 10.1 %mlp_up.2 = (f32[2,584,1024]{2,1,0:T(8,128)}, bf16[2,584,1024]{2,1,0:T(8,128)(2,1)}, bf16[2,584,2048]{2,1,0:T(8,128)(2,1)}, bf16[2,584,2048]{2,1,0:T(8,128)(2,1)}) custom-call(f32[2]{0:T(128)} %get-tuple-element.369.refs_0_.refs_1_, f32[6,1024]{1,0:T(8,128)} %get-tuple-element.196.refs_0_.refs_1_.refs_2_, f32[1,2048]{1,0:T(1,128)} %get-tuple-element.197.refs_2_, ...), custom_call_target="tpu_custom_call" | custom-call | flops 11500000256 | bytes 11500000 | tf_op jit(solution)/shard_map/mlp_up/pallas_call | solution.py:94
  135.2 1.4 collective-permute-done.22.refs_3_
  136.6 3.3 join.1
  139.9 1.4 collective-permute-start.23
  142.0 10.1 %mlp_up.3 = (f32[2,584,1024]{2,1,0:T(8,128)}, bf16[2,584,1024]{2,1,0:T(8,128)(2,1)}, bf16[2,584,2048]{2,1,0:T(8,128)(2,1)}, bf16[2,584,2048]{2,1,0:T(8,128)(2,1)}) custom-call(f32[2]{0:T(128)} %get-tuple-element.369.refs_0_.refs_1_, ...), custom_call_target="tpu_custom_call", output_to_operand_aliasing={{0}: (6, {}), {1}: (7, {}), {2}: (8, {}), {3}: (9, {})} | custom-call | flops 11500000256 | bytes 11500000 | tf_op jit(solution)/shard_map/mlp_up/pallas_call | solution.py:94
  152.2 10.7 %down_grad.1 = (bf16[8,512,128]{2,1,0:T(8,128)(2,1)}, bf16[8,512,128]{2,1,0:T(8,128)(2,1)}, bf16[8,512,128]{2,1,0:T(8,128)(2,1)}, bf16[8,512,128]{2,1,0:T(8,128)(2,1)}) custom-call(bf16[1168,2048]{1,0:T(8,128)(2,1)} %bitcast.123, bf16[1168,1024]{1,0:T(8,128)(2,1)} %bitcast.106), custom_call_target="tpu_custom_call" | custom-call | flops 12650000384 | bytes 12650000 | tf_op jit(solution)/shard_map/down_grad/pallas_call | solution.py:94
  162.9 1.5 collective-permute-start.27
  165.0 1.9 collective-permute-done.24.refs_6_
  166.9 21.8 %mlp_back.1 = (bf16[1168,2048]{1,0:T(8,128)(2,1)}, f32[1,2048]{1,0:T(1,128)}, bf16[2,584,1024]{2,1,0:T(8,128)(2,1)}, bf16[1168,1024]{1,0:T(8,128)(2,1)}) custom-call(bf16[1168,1024]{1,0:T(8,128)(2,1)} %bitcast.107, bf16[1168,2048]{1,0:T(8,128)(2,1)} %bitcast.124, bf16[1168,2048]{1,0:T(8,128)(2,1)} %bitcast.125, ...), custom_call_target="tpu_custom_call" | custom-call | flops 25300000768 | bytes 25300000 | tf_op jit(solution)/shard_map/mlp_back/pallas_call | solution.py:94
  191.3 2.5 down_add.1
  193.9 2.0 collective-permute-start.29
  196.0 7.4 %up_grad.1 = (bf16[8,512,128]{2,1,0:T(8,128)(2,1)S(1)}, bf16[8,512,128]{2,1,0:T(8,128)(2,1)S(1)}, bf16[8,512,128]{2,1,0:T(8,128)(2,1)S(1)}, bf16[8,512,128]{2,1,0:T(8,128)(2,1)S(1)}) custom-call(bf16[1168,1024]{1,0:T(8,128)(2,1)S(1)} %bitcast.104, bf16[1168,2048]{1,0:T(8,128)(2,1)S(1)} %copy-done.32), custom_call_target="tpu_custom_call" | custom-call | flops 12650000384 | bytes 12650000 | tf_op jit(solution)/shard_map/up_grad/pallas_call | solution.py:94
  203.5 1.9 collective-permute-start.31
  205.5 9.7 %middle_back.1 = (f32[584,1024]{1,0:T(8,128)S(1)}, bf16[2,584,1024]{2,1,0:T(8,128)(2,1)S(1)}, bf16[2,584,512]{2,1,0:T(8,128)(2,1)S(1)}, f32[4,1024]{1,0:T(4,128)S(1)}) custom-call(s32[10]{0:T(128)S(1)} %copy-done.23, f32[2]{0:T(128)S(1)} %copy-done.22, f32[6,1024]{1,0:T(8,128)S(1)} %copy-done.21, f32[2,584,1024]{2,1,0:T(8,128)} %get-tuple-element.229.refs_3_, ...), custom_call_target="tpu_custom_call" | custom-call | flops 23000000 | bytes 23000 | tf_op jit(solution)/shard_map/middle_back/pallas_call | solution.py:94
  216.8 2.4 collective-permute-start.35
  219.2 1.4 collective-permute-start.36
  220.6 3.1 out_grad.1
  223.8 8.0 %attn_first.1 = (bf16[3,2,584,128]{3,2,1,0:T(8,128)(2,1)S(1)}, f32[2,2,128]{2,1,0:T(2,128)S(1)}) custom-call(bf16[2,584,512]{2,1,0:T(8,128)(2,1)S(1)} %copy-done.15, bf16[2,584,512]{2,1,0:T(8,128)(2,1)S(1)} %copy-done.17, bf16[2,584,512]{2,1,0:T(8,128)(2,1)S(1)} %copy-done.19, bf16[2,584,512]{2,1,0:T(8,128)(2,1)S(1)} %get-tuple-element.315.refs_3_), custom_call_target="tpu_custom_call" | custom-call | flops 23000000 | bytes 23000 | tf_op jit(solution)/shard_map/attn_first/pallas_call | solution.py:94
  231.8 1.4 up_add.1
  233.9 1.4 collective-permute-start.33
  235.3 15.5 %attn_backward.2 = (bf16[3,4,584,128]{3,2,1,0:T(8,128)(2,1)S(1)}, f32[4,2,128]{2,1,0:T(2,128)S(1)}) custom-call(bf16[2,584,512]{2,1,0:T(8,128)(2,1)S(1)} %copy-done.15, bf16[2,584,512]{2,1,0:T(8,128)(2,1)S(1)} %copy-done.17, bf16[2,584,512]{2,1,0:T(8,128)(2,1)S(1)} %copy-done.19, bf16[2,584,512]{2,1,0:T(8,128)(2,1)S(1)} %get-tuple-element.315.refs_3_), custom_call_target="tpu_custom_call" | custom-call | flops 20700000256 | bytes 20700000 | tf_op jit(solution)/shard_map/attn_backward/pallas_call | solution.py:94
  250.9 5.1 %qkv_grad.1 = (bf16[8,512,128]{2,1,0:T(8,128)(2,1)S(1)}, bf16[8,512,128]{2,1,0:T(8,128)(2,1)S(1)}, bf16[8,512,128]{2,1,0:T(8,128)(2,1)S(1)}) custom-call(bf16[1168,1024]{1,0:T(8,128)(2,1)S(1)} %bitcast.95, bf16[3,1168,128]{2,1,0:T(8,128)(2,1)S(1)} %bitcast.101, ...), custom_call_target="tpu_custom_call", output_to_operand_aliasing={{0}: (3, {}), {1}: (4, {}), {2}: (5, {})} | custom-call | flops 8049999872 | bytes 8050000 | tf_op jit(solution)/shard_map/qkv_grad/pallas_call | solution.py:94
  256.6 1.4 collective-permute-start.39
  258.0 1.4 down_sum.1
  260.5 8.0 %attn_backward.3 = (bf16[3,2,584,128]{3,2,1,0:T(8,128)(2,1)S(1)}, f32[2,2,128]{2,1,0:T(2,128)S(1)}) custom-call(bf16[2,584,512]{2,1,0:T(8,128)(2,1)S(1)} %copy-done.15, bf16[2,584,512]{2,1,0:T(8,128)(2,1)S(1)} %copy-done.17, bf16[2,584,512]{2,1,0:T(8,128)(2,1)S(1)} %copy-done.19, bf16[2,584,512]{2,1,0:T(8,128)(2,1)S(1)} %get-tuple-element.315.refs_3_), custom_call_target="tpu_custom_call" | custom-call | flops 20700000256 | bytes 20700000 | tf_op jit(solution)/shard_map/attn_backward/pallas_call | solution.py:94
  268.5 1.4 copy-done.11
  269.8 2.6 qkv_keep.1.refs_0_
  272.5 7.1 %grad_one.1.refs_9_ = bf16[2,584,1024]{2,1,0:T(8,128)(2,1)S(1)} custom-call(bf16[3,1168,128]{2,1,0:T(8,128)(2,1)S(1)} %bitcast.102, bf16[6,1168,128]{2,1,0:T(8,128)(2,1)S(1)} %bitcast.100, bf16[3,1168,128]{2,1,0:T(8,128)(2,1)S(1)} %bitcast.94, bf16[8,528,128]{2,1,0:T(8,128)(2,1)S(1)} %copy-done.3, ...), custom_call_target="tpu_custom_call" | custom-call | flops 23000000 | bytes 23000 | tf_op jit(solution)/shard_map/grad_one/pallas_call | solution.py:94
  283.3 1.5 collective-permute-start.41
  285.4 1.9 collective-permute-start.43
  287.3 7.2 %finish_tokens.1 = (bf16[584,1024]{1,0:T(8,128)(2,1)}, f32[2,1024]{1,0:T(2,128)}, f32[4,16,128]{2,1,0:T(8,128)S(1)}, f32[4,16,128]{2,1,0:T(8,128)S(1)}, f32[4,16...) custom-call(s32[10]{0:T(128)S(1)} %copy-done.23, f32[6,1024]{1,0:T(8,128)S(1)} %copy-done.21, ...), custom_call_target="tpu_custom_call" | custom-call | flops 10350000128 | bytes 10350000 | tf_op jit(solution)/shard_map/finish_tokens/pallas_call | solution.py:94
  294.5 2.0 collective-permute-done.41.refs_1_
  298.3 1.4 collective-permute-start.46
  299.7 1.4 collective-permute-start.47
  302.5 2.0 collective-permute-done.47.refs_7_
  304.5 1.7 qkv_addz.1
  307.1 2.2 collective-permute-start.49
  310.7 2.4 copy-done
  313.1 1.7 copy-done.12
  314.7 3.2 finish_layer.1
  318.0 9.9 %collective-permute-done.49.refs_2_ = bf16[1040,128]{1,0:T(8,128)(2,1)S(1)} collective-permute-done((bf16[1040,128]{1,0:T(8,128)(2,1)}, bf16[1040,128]{1,0:T(8,128)(2,1)S(1)}, u32[]{:S(2)}, u32[]{:S(2)}) %collective-permute-start.49) | collective-permute-done | bytes 266272 | tf_op jit(solution)/shard_map/ppermute | solution.py:813
  329.3 2.5 qkv_sum.1
  (216 shorter events, 43.0 us)
Async XLA Ops:
  0.6 10.8 %collective-permute-start.3 = (bf16[584,1024]{1,0:T(8,128)(2,1)}, bf16[584,1024]{1,0:T(8,128)(2,1)}, u32[]{:S(2)}, u32[]{:S(2)}) collective-permute-start(bf16[584,1024]{1,0:T(8,128)(2,1)} %refs_1_.1), channel_id=1, source_target_pairs={{0,1},{1,0},{2,3},{3,2},{4,5},{5,4},{6,7},{7,6},{8,9},{9,8},{10,11... | collective-permute-start | bytes 3588104 | tf_op jit(solution)/shard_map/ppermute | solution.py:828
  1.2 10.3 %collective-permute-start.4 = (bf16[584,1024]{1,0:T(8,128)(2,1)}, bf16[584,1024]{1,0:T(8,128)(2,1)}, u32[]{:S(2)}, u32[]{:S(2)}) collective-permute-start(bf16[584,1024]{1,0:T(8,128)(2,1)} %refs_2_.1), channel_id=1, source_target_pairs={{0,1},{1,0},{2,3},{3,2},{4,5},{5,4},{6,7},{7,6},{8,9},{9,8},{10,11... | collective-permute-start | bytes 3588104 | tf_op jit(solution)/shard_map/ppermute | solution.py:828
  5.1 14.8 %collective-permute-start = (bf16[1040,128]{1,0:T(8,128)(2,1)S(1)}, bf16[1040,128]{1,0:T(8,128)(2,1)S(1)}, u32[]{:S(2)}, u32[]{:S(2)}) collective-permute-start(bf16[1040,128]{1,0:T(8,128)(2,1)S(1)} %concatenate.26), channel_id=1, source_target_pairs={{0,8},{4,12},{8,0},{12,4},{16,24},{20,28},{24,16},{28,20},{1,9},{5... | collective-permute-start | bytes 798728 | tf_op jit(solution)/shard_map/ppermute | solution.py:813
  8.2 21.6 %collective-permute-start.1 = (bf16[1040,128]{1,0:T(8,128)(2,1)S(1)}, bf16[1040,128]{1,0:T(8,128)(2,1)S(1)}, u32[]{:S(2)}, u32[]{:S(2)}) collective-permute-start(bf16[1040,128]{1,0:T(8,128)(2,1)S(1)} %concatenate.26), channel_id=1, source_target_pairs={{0,16},{4,20},{8,24},{12,28},{16,0},{20,4},{24,8},{28,12},{1,17},{... | collective-permute-start | bytes 798728 | tf_op jit(solution)/shard_map/ppermute | solution.py:813
  10.8 19.0 %collective-permute-start.2 = (bf16[1040,128]{1,0:T(8,128)(2,1)S(1)}, bf16[1040,128]{1,0:T(8,128)(2,1)S(1)}, u32[]{:S(2)}, u32[]{:S(2)}) collective-permute-start(bf16[1040,128]{1,0:T(8,128)(2,1)S(1)} %concatenate.26), channel_id=1, source_target_pairs={{0,24},{4,28},{8,16},{12,20},{16,8},{20,12},{24,0},{28,4},{1,25},{... | collective-permute-start | bytes 798728 | tf_op jit(solution)/shard_map/ppermute | solution.py:813
  30.1 12.2 %collective-permute-start.5 = (bf16[4,528,128]{2,1,0:T(8,128)(2,1)S(1)}, bf16[4,528,128]{2,1,0:T(8,128)(2,1)S(1)}, u32[]{:S(2)}, u32[]{:S(2)}) collective-permute-start(bf16[4,528,128]{2,1,0:T(8,128)(2,1)S(1)} %pad_maximum_fusion), channel_id=1, source_target_pairs={{0,4},{4,0},{8,12},{12,8},{16,20},{20,16},{24,28},{28,24},{1,5},{5... | collective-permute-start | bytes 1622024 | tf_op jit(solution)/shard_map/ppermute | solution.py:816
  31.8 12.8 %collective-permute-start.7 = (bf16[4,512,128]{2,1,0:T(8,128)(2,1)S(1)}, bf16[4,512,128]{2,1,0:T(8,128)(2,1)S(1)}, u32[]{:S(2)}, u32[]{:S(2)}) collective-permute-start(bf16[4,512,128]{2,1,0:T(8,128)(2,1)S(1)} %pad_maximum_fusion.1), channel_id=1, source_target_pairs={{0,2},{2,0},{1,3},{3,1},{4,6},{6,4},{5,7},{7,5},{8,10},{10,8},{9,1... | collective-permute-start | bytes 1572872 | tf_op jit(solution)/shard_map/ppermute | solution.py:824
  33.4 12.2 %copy-start.40 = (s32[4]{0:T(128)S(1)}, s32[4]{0:T(128)}, u32[]{:S(2)}) copy-start(s32[4]{0:T(128)} %param.13) | copy-start | bytes 52
  33.4 12.8 %copy-start.38 = (bf16[1024,128]{1,0:T(8,128)(2,1)S(1)}, bf16[1024,128]{1,0:T(8,128)(2,1)}, u32[]{:S(2)}) copy-start(bf16[1024,128]{1,0:T(8,128)(2,1)} %param.21) | copy-start | bytes 786436
  33.4 12.8 %copy-start.39 = (bf16[128,1024]{1,0:T(8,128)(2,1)S(1)}, bf16[128,1024]{1,0:T(8,128)(2,1)}, u32[]{:S(2)}) copy-start(bf16[128,1024]{1,0:T(8,128)(2,1)} %param.19) | copy-start | bytes 786436
  42.3 24.3 %collective-permute-start.6 = (bf16[8,528,128]{2,1,0:T(8,128)(2,1)S(1)}, bf16[8,528,128]{2,1,0:T(8,128)(2,1)}, u32[]{:S(2)}, u32[]{:S(2)}) collective-permute-start(bf16[8,528,128]{2,1,0:T(8,128)(2,1)S(1)} %constant_dynamic-update-slice_fusion.refs_1_.refs_3_.refs_7_.refs_8_.refs_12_), channel_id=1, source_target_pairs={{0,2},{2,0},{1,3},{3,1},{4,6},{6,4},{5,7},{7,5},{8,10},{10,8},{9,1... | collective-permute-start | bytes 3244040 | tf_op jit(solution)/shard_map/ppermute | solution.py:824
  44.7 30.1 %copy-start.4 = (bf16[8,512,128]{2,1,0:T(8,128)(2,1)}, bf16[8,512,128]{2,1,0:T(8,128)(2,1)S(1)}, u32[]{:S(2)}) copy-start(bf16[8,512,128]{2,1,0:T(8,128)(2,1)S(1)} %constant_dynamic-update-slice_fusion.5.refs_5_.refs_9_.refs_10_.refs_14_) | copy-start | bytes 3145732
  44.7 21.3 %collective-permute-start.8 = (bf16[8,512,128]{2,1,0:T(8,128)(2,1)S(1)}, bf16[8,512,128]{2,1,0:T(8,128)(2,1)}, u32[]{:S(2)}, u32[]{:S(2)}) collective-permute-start(bf16[8,512,128]{2,1,0:T(8,128)(2,1)S(1)} %constant_dynamic-update-slice_fusion.5.refs_5_.refs_9_.refs_10_.refs_14_), channel_id=1, source_target_pairs={{0,4},{4,0},{8,12},{12,8},{16,20},{20,16},{24,28},{28,24},{1,5},{5... | collective-permute-start | bytes 3145736 | tf_op jit(solution)/shard_map/ppermute | solution.py:816
  46.2 22.9 %collective-permute-start.9 = (bf16[256,512]{1,0:T(8,128)(2,1)S(1)}, bf16[256,512]{1,0:T(8,128)(2,1)S(1)}, u32[]{:S(2)}, u32[]{:S(2)}) collective-permute-start(bf16[256,512]{1,0:T(8,128)(2,1)S(1)} %constant_dynamic-update-slice_fusion.10), channel_id=1, source_target_pairs={{0,8},{4,12},{8,0},{12,4},{16,24},{20,28},{24,16},{28,20},{1,9},{5... | collective-permute-start | bytes 786440 | tf_op jit(solution)/shard_map/ppermute | solution.py:813
  52.5 20.4 %collective-permute-start.10 = (bf16[256,512]{1,0:T(8,128)(2,1)S(1)}, bf16[256,512]{1,0:T(8,128)(2,1)S(1)}, u32[]{:S(2)}, u32[]{:S(2)}) collective-permute-start(bf16[256,512]{1,0:T(8,128)(2,1)S(1)} %constant_dynamic-update-slice_fusion.10), channel_id=1, source_target_pairs={{0,16},{4,20},{8,24},{12,28},{16,0},{20,4},{24,8},{28,12},{1,17},{... | collective-permute-start | bytes 786440 | tf_op jit(solution)/shard_map/ppermute | solution.py:813
  53.6 19.3 %collective-permute-start.11 = (bf16[256,512]{1,0:T(8,128)(2,1)S(1)}, bf16[256,512]{1,0:T(8,128)(2,1)S(1)}, u32[]{:S(2)}, u32[]{:S(2)}) collective-permute-start(bf16[256,512]{1,0:T(8,128)(2,1)S(1)} %constant_dynamic-update-slice_fusion.10), channel_id=1, source_target_pairs={{0,24},{4,28},{8,16},{12,20},{16,8},{20,12},{24,0},{28,4},{1,25},{... | collective-permute-start | bytes 786440 | tf_op jit(solution)/shard_map/ppermute | solution.py:813
  73.1 16.5 %collective-permute-start.12 = (bf16[4,128,512]{2,1,0:T(8,128)(2,1)S(1)}, bf16[4,128,512]{2,1,0:T(8,128)(2,1)S(1)}, u32[]{:S(2)}, u32[]{:S(2)}) collective-permute-start(bf16[4,128,512]{2,1,0:T(8,128)(2,1)S(1)} %pad_maximum_fusion.2), channel_id=1, source_target_pairs={{0,4},{4,0},{8,12},{12,8},{16,20},{20,16},{24,28},{28,24},{1,5},{5... | collective-permute-start | bytes 1572872 | tf_op jit(solution)/shard_map/ppermute | solution.py:816
  73.8 15.8 %collective-permute-start.13 = (bf16[4,128,512]{2,1,0:T(8,128)(2,1)S(1)}, bf16[4,128,512]{2,1,0:T(8,128)(2,1)S(1)}, u32[]{:S(2)}, u32[]{:S(2)}) collective-permute-start(bf16[4,128,512]{2,1,0:T(8,128)(2,1)S(1)} %pad_maximum_fusion.3), channel_id=1, source_target_pairs={{0,2},{2,0},{1,3},{3,1},{4,6},{6,4},{5,7},{7,5},{8,10},{10,8},{9,1... | collective-permute-start | bytes 1572872 | tf_op jit(solution)/shard_map/ppermute | solution.py:824
  89.6 28.5 %copy-start.24 = (bf16[584,1024]{1,0:T(8,128)(2,1)}, bf16[584,1024]{1,0:T(8,128)(2,1)S(1)}, u32[]{:S(2)}) copy-start(bf16[584,1024]{1,0:T(8,128)(2,1)S(1)} %get-tuple-element.220.refs_4_) | copy-start | bytes 3588100
  89.8 24.0 %copy-start.37 = (bf16[8,128,512]{2,1,0:T(8,128)(2,1)}, bf16[8,128,512]{2,1,0:T(8,128)(2,1)S(1)}, u32[]{:S(2)}) copy-start(bf16[8,128,512]{2,1,0:T(8,128)(2,1)S(1)} %constant_dynamic-update-slice_fusion.12) | copy-start | bytes 3145732
  89.8 24.0 %copy-start.36 = (bf16[8,128,512]{2,1,0:T(8,128)(2,1)}, bf16[8,128,512]{2,1,0:T(8,128)(2,1)S(1)}, u32[]{:S(2)}) copy-start(bf16[8,128,512]{2,1,0:T(8,128)(2,1)S(1)} %constant_dynamic-update-slice_fusion.14) | copy-start | bytes 3145732
  89.9 30.5 %collective-permute-start.18 = (bf16[1024,128]{1,0:T(8,128)(2,1)S(1)}, bf16[1024,128]{1,0:T(8,128)(2,1)S(1)}, u32[]{:S(2)}, u32[]{:S(2)}) collective-permute-start(bf16[1024,128]{1,0:T(8,128)(2,1)S(1)} %constant_dynamic-update-slice_fusion.16), channel_id=1, source_target_pairs={{0,8},{4,12},{8,0},{12,4},{16,24},{20,28},{24,16},{28,20},{1,9},{5... | collective-permute-start | bytes 786440 | tf_op jit(solution)/shard_map/ppermute | solution.py:813
  93.6 26.7 %collective-permute-start.19 = (bf16[1024,128]{1,0:T(8,128)(2,1)S(1)}, bf16[1024,128]{1,0:T(8,128)(2,1)S(1)}, u32[]{:S(2)}, u32[]{:S(2)}) collective-permute-start(bf16[1024,128]{1,0:T(8,128)(2,1)S(1)} %constant_dynamic-update-slice_fusion.16), channel_id=1, source_target_pairs={{0,16},{4,20},{8,24},{12,28},{16,0},{20,4},{24,8},{28,12},{1,17},{... | collective-permute-start | bytes 786440 | tf_op jit(solution)/shard_map/ppermute | solution.py:813
  94.7 25.6 %collective-permute-start.20 = (bf16[1024,128]{1,0:T(8,128)(2,1)S(1)}, bf16[1024,128]{1,0:T(8,128)(2,1)S(1)}, u32[]{:S(2)}, u32[]{:S(2)}) collective-permute-start(bf16[1024,128]{1,0:T(8,128)(2,1)S(1)} %constant_dynamic-update-slice_fusion.16), channel_id=1, source_target_pairs={{0,24},{4,28},{8,16},{12,20},{16,8},{20,12},{24,0},{28,4},{1,25},{... | collective-permute-start | bytes 786440 | tf_op jit(solution)/shard_map/ppermute | solution.py:813
  96.1 22.0 %collective-permute-start.16 = (bf16[8,128,512]{2,1,0:T(8,128)(2,1)S(1)}, bf16[8,128,512]{2,1,0:T(8,128)(2,1)S(1)}, u32[]{:S(2)}, u32[]{:S(2)}) collective-permute-start(bf16[8,128,512]{2,1,0:T(8,128)(2,1)S(1)} %constant_dynamic-update-slice_fusion.12), channel_id=1, source_target_pairs={{0,2},{2,0},{1,3},{3,1},{4,6},{6,4},{5,7},{7,5},{8,10},{10,8},{9,1... | collective-permute-start | bytes 3145736 | tf_op jit(solution)/shard_map/ppermute | solution.py:824
  97.3 22.6 %collective-permute-start.17 = (bf16[8,128,512]{2,1,0:T(8,128)(2,1)S(1)}, bf16[8,128,512]{2,1,0:T(8,128)(2,1)S(1)}, u32[]{:S(2)}, u32[]{:S(2)}) collective-permute-start(bf16[8,128,512]{2,1,0:T(8,128)(2,1)S(1)} %constant_dynamic-update-slice_fusion.14), channel_id=1, source_target_pairs={{0,4},{4,0},{8,12},{12,8},{16,20},{20,16},{24,28},{28,24},{1,5},{5... | collective-permute-start | bytes 3145736 | tf_op jit(solution)/shard_map/ppermute | solution.py:816
  98.3 19.8 %copy-start.1 = (bf16[2,584,1024]{2,1,0:T(8,128)(2,1)S(1)}, bf16[2,584,1024]{2,1,0:T(8,128)(2,1)}, u32[]{:S(2)}) copy-start(bf16[2,584,1024]{2,1,0:T(8,128)(2,1)} %get-tuple-element.230.refs_4_) | copy-start | bytes 7176196
  118.1 5.6 %collective-permute-start.15 = (bf16[584,1024]{1,0:T(8,128)(2,1)S(1)}, bf16[584,1024]{1,0:T(8,128)(2,1)S(1)}, u32[]{:S(2)}, u32[]{:S(2)}) collective-permute-start(bf16[584,1024]{1,0:T(8,128)(2,1)S(1)} %get-tuple-element.220.refs_4_), channel_id=1, source_target_pairs={{0,1},{1,0},{2,3},{3,2},{4,5},{5,4},{6,7},{7,6},{8,9},{9,8},{10,11... | collective-permute-start | bytes 3588104 | tf_op jit(solution)/shard_map/ppermute | solution.py:828
  119.9 22.1 %collective-permute-start.14 = (bf16[584,1024]{1,0:T(8,128)(2,1)}, bf16[584,1024]{1,0:T(8,128)(2,1)}, u32[]{:S(2)}, u32[]{:S(2)}) collective-permute-start(bf16[584,1024]{1,0:T(8,128)(2,1)} %get-tuple-element.219.refs_4_), channel_id=1, source_target_pairs={{0,1},{1,0},{2,3},{3,2},{4,5},{5,4},{6,7},{7,6},{8,9},{9,8},{10,11... | collective-permute-start | bytes 3588104 | tf_op jit(solution)/shard_map/ppermute | solution.py:828
  120.9 14.4 %collective-permute-start.21 = (bf16[4,512,128]{2,1,0:T(8,128)(2,1)S(1)}, bf16[4,512,128]{2,1,0:T(8,128)(2,1)}, u32[]{:S(2)}, u32[]{:S(2)}) collective-permute-start(bf16[4,512,128]{2,1,0:T(8,128)(2,1)S(1)} %pad_maximum_fusion.4.refs_0_), channel_id=1, source_target_pairs={{0,4},{4,0},{8,12},{12,8},{16,20},{20,16},{24,28},{28,24},{1,5},{5... | collective-permute-start | bytes 1572872 | tf_op jit(solution)/shard_map/ppermute | solution.py:816
  122.3 14.3 %collective-permute-start.22 = (bf16[4,512,128]{2,1,0:T(8,128)(2,1)}, bf16[4,512,128]{2,1,0:T(8,128)(2,1)}, u32[]{:S(2)}, u32[]{:S(2)}) collective-permute-start(bf16[4,512,128]{2,1,0:T(8,128)(2,1)} %pad_maximum_fusion.5.refs_2_), channel_id=1, source_target_pairs={{0,2},{2,0},{1,3},{3,1},{4,6},{6,4},{5,7},{7,5},{8,10},{10,8},{9,1... | collective-permute-start | bytes 1572872 | tf_op jit(solution)/shard_map/ppermute | solution.py:824
  139.9 25.1 %collective-permute-start.23 = (bf16[8,512,128]{2,1,0:T(8,128)(2,1)}, bf16[8,512,128]{2,1,0:T(8,128)(2,1)}, u32[]{:S(2)}, u32[]{:S(2)}) collective-permute-start(bf16[8,512,128]{2,1,0:T(8,128)(2,1)} %get-tuple-element.247.refs_3_), channel_id=1, source_target_pairs={{0,2},{2,0},{1,3},{3,1},{4,6},{6,4},{5,7},{7,5},{8,10},{10,8},{9,1... | collective-permute-start | bytes 3145736 | tf_op jit(solution)/shard_map/ppermute | solution.py:824
  141.4 25.5 %collective-permute-start.24 = (bf16[8,512,128]{2,1,0:T(8,128)(2,1)}, bf16[8,512,128]{2,1,0:T(8,128)(2,1)}, u32[]{:S(2)}, u32[]{:S(2)}) collective-permute-start(bf16[8,512,128]{2,1,0:T(8,128)(2,1)} %get-tuple-element.248.refs_5_), channel_id=1, source_target_pairs={{0,4},{4,0},{8,12},{12,8},{16,20},{20,16},{24,28},{28,24},{1,5},{5... | collective-permute-start | bytes 3145736 | tf_op jit(solution)/shard_map/ppermute | solution.py:816
  162.9 26.0 %collective-permute-start.27 = (bf16[8,512,128]{2,1,0:T(8,128)(2,1)}, bf16[8,512,128]{2,1,0:T(8,128)(2,1)}, u32[]{:S(2)}, u32[]{:S(2)}) collective-permute-start(bf16[8,512,128]{2,1,0:T(8,128)(2,1)} %get-tuple-element.232), channel_id=1, source_target_pairs={{0,4},{4,0},{8,12},{12,8},{16,20},{20,16},{24,28},{28,24},{1,5},{5... | collective-permute-start | bytes 3145736 | tf_op jit(solution)/shard_map/ppermute | solution.py:816
  164.4 24.5 %collective-permute-start.26 = (bf16[8,512,128]{2,1,0:T(8,128)(2,1)}, bf16[8,512,128]{2,1,0:T(8,128)(2,1)}, u32[]{:S(2)}, u32[]{:S(2)}) collective-permute-start(bf16[8,512,128]{2,1,0:T(8,128)(2,1)} %get-tuple-element.257), channel_id=1, source_target_pairs={{0,2},{2,0},{1,3},{3,1},{4,6},{6,4},{5,7},{7,5},{8,10},{10,8},{9,1... | collective-permute-start | bytes 3145736 | tf_op jit(solution)/shard_map/ppermute | solution.py:824
  188.8 16.7 %collective-permute-start.25 = (bf16[2,584,1024]{2,1,0:T(8,128)(2,1)}, bf16[2,584,1024]{2,1,0:T(8,128)(2,1)S(1)}, u32[]{:S(2)}, u32[]{:S(2)}) collective-permute-start(bf16[2,584,1024]{2,1,0:T(8,128)(2,1)} %get-tuple-element.254.refs_5_), channel_id=1, source_target_pairs={{0,1},{1,0},{2,3},{3,2},{4,5},{5,4},{6,7},{7,6},{8,9},{9,8},{10,11... | collective-permute-start | bytes 7176200 | tf_op jit(solution)/shard_map/ppermute | solution.py:828
  193.8 21.4 %collective-permute-start.28 = (bf16[4,512,128]{2,1,0:T(8,128)(2,1)S(1)}, bf16[4,512,128]{2,1,0:T(8,128)(2,1)S(1)}, u32[]{:S(2)}, u32[]{:S(2)}) collective-permute-start(bf16[4,512,128]{2,1,0:T(8,128)(2,1)S(1)} %get-tuple-element.265), channel_id=1, source_target_pairs={{0,4},{4,0},{8,12},{12,8},{16,20},{20,16},{24,28},{28,24},{1,5},{5... | collective-permute-start | bytes 1572872 | tf_op jit(solution)/shard_map/ppermute | solution.py:816
  193.9 21.3 %collective-permute-start.29 = (bf16[4,512,128]{2,1,0:T(8,128)(2,1)S(1)}, bf16[4,512,128]{2,1,0:T(8,128)(2,1)S(1)}, u32[]{:S(2)}, u32[]{:S(2)}) collective-permute-start(bf16[4,512,128]{2,1,0:T(8,128)(2,1)S(1)} %get-tuple-element.267), channel_id=1, source_target_pairs={{0,2},{2,0},{1,3},{3,1},{4,6},{6,4},{5,7},{7,5},{8,10},{10,8},{9,1... | collective-permute-start | bytes 1572872 | tf_op jit(solution)/shard_map/ppermute | solution.py:824
  196.0 9.5 %copy-start.13 = (bf16[2,584,1024]{2,1,0:T(8,128)(2,1)S(1)}, bf16[2,584,1024]{2,1,0:T(8,128)(2,1)}, u32[]{:S(2)}) copy-start(bf16[2,584,1024]{2,1,0:T(8,128)(2,1)} %get-tuple-element.254.refs_5_) | copy-start | bytes 7176196
  203.4 28.4 %collective-permute-start.30 = (bf16[8,512,128]{2,1,0:T(8,128)(2,1)S(1)}, bf16[8,512,128]{2,1,0:T(8,128)(2,1)S(1)}, u32[]{:S(2)}, u32[]{:S(2)}) collective-permute-start(bf16[8,512,128]{2,1,0:T(8,128)(2,1)S(1)} %get-tuple-element.289), channel_id=1, source_target_pairs={{0,2},{2,0},{1,3},{3,1},{4,6},{6,4},{5,7},{7,5},{8,10},{10,8},{9,1... | collective-permute-start | bytes 3145736 | tf_op jit(solution)/shard_map/ppermute | solution.py:824
  203.5 28.3 %collective-permute-start.31 = (bf16[8,512,128]{2,1,0:T(8,128)(2,1)S(1)}, bf16[8,512,128]{2,1,0:T(8,128)(2,1)S(1)}, u32[]{:S(2)}, u32[]{:S(2)}) collective-permute-start(bf16[8,512,128]{2,1,0:T(8,128)(2,1)S(1)} %get-tuple-element.270), channel_id=1, source_target_pairs={{0,4},{4,0},{8,12},{12,8},{16,20},{20,16},{24,28},{28,24},{1,5},{5... | collective-permute-start | bytes 3145736 | tf_op jit(solution)/shard_map/ppermute | solution.py:816
  216.2 34.6 %collective-permute-start.34 = (bf16[1024,128]{1,0:T(8,128)(2,1)S(1)}, bf16[1024,128]{1,0:T(8,128)(2,1)S(1)}, u32[]{:S(2)}, u32[]{:S(2)}) collective-permute-start(bf16[1024,128]{1,0:T(8,128)(2,1)S(1)} %get-tuple-element.280), channel_id=1, source_target_pairs={{0,8},{4,12},{8,0},{12,4},{16,24},{20,28},{24,16},{28,20},{1,9},{5... | collective-permute-start | bytes 786440 | tf_op jit(solution)/shard_map/ppermute | solution.py:813
  216.8 39.2 %collective-permute-start.35 = (bf16[1024,128]{1,0:T(8,128)(2,1)S(1)}, bf16[1024,128]{1,0:T(8,128)(2,1)S(1)}, u32[]{:S(2)}, u32[]{:S(2)}) collective-permute-start(bf16[1024,128]{1,0:T(8,128)(2,1)S(1)} %get-tuple-element.281), channel_id=1, source_target_pairs={{0,16},{4,20},{8,24},{12,28},{16,0},{20,4},{24,8},{28,12},{1,17},{... | collective-permute-start | bytes 786440 | tf_op jit(solution)/shard_map/ppermute | solution.py:813
  219.2 37.4 %collective-permute-start.36 = (bf16[1024,128]{1,0:T(8,128)(2,1)S(1)}, bf16[1024,128]{1,0:T(8,128)(2,1)S(1)}, u32[]{:S(2)}, u32[]{:S(2)}) collective-permute-start(bf16[1024,128]{1,0:T(8,128)(2,1)S(1)} %get-tuple-element.282), channel_id=1, source_target_pairs={{0,24},{4,28},{8,16},{12,20},{16,8},{20,12},{24,0},{28,4},{1,25},{... | collective-permute-start | bytes 786440 | tf_op jit(solution)/shard_map/ppermute | solution.py:813
  233.2 26.3 %collective-permute-start.32 = (bf16[4,512,128]{2,1,0:T(8,128)(2,1)S(1)}, bf16[4,512,128]{2,1,0:T(8,128)(2,1)S(1)}, u32[]{:S(2)}, u32[]{:S(2)}) collective-permute-start(bf16[4,512,128]{2,1,0:T(8,128)(2,1)S(1)} %get-tuple-element.297), channel_id=1, source_target_pairs={{0,4},{4,0},{8,12},{12,8},{16,20},{20,16},{24,28},{28,24},{1,5},{5... | collective-permute-start | bytes 1572872 | tf_op jit(solution)/shard_map/ppermute | solution.py:816
  233.9 25.6 %collective-permute-start.33 = (bf16[4,512,128]{2,1,0:T(8,128)(2,1)S(1)}, bf16[4,512,128]{2,1,0:T(8,128)(2,1)S(1)}, u32[]{:S(2)}, u32[]{:S(2)}) collective-permute-start(bf16[4,512,128]{2,1,0:T(8,128)(2,1)S(1)} %get-tuple-element.299), channel_id=1, source_target_pairs={{0,2},{2,0},{1,3},{3,1},{4,6},{6,4},{5,7},{7,5},{8,10},{10,8},{9,1... | collective-permute-start | bytes 1572872 | tf_op jit(solution)/shard_map/ppermute | solution.py:824
  235.3 15.5 %copy-start.9 = (bf16[1168,1024]{1,0:T(8,128)(2,1)S(1)}, bf16[1168,1024]{1,0:T(8,128)(2,1)}, u32[]{:S(2)}) copy-start(bf16[1168,1024]{1,0:T(8,128)(2,1)} %get-tuple-element.249) | copy-start | bytes 7176196
  235.3 15.6 %copy-start.8 = (bf16[2,584,1024]{2,1,0:T(8,128)(2,1)S(1)}, bf16[2,584,1024]{2,1,0:T(8,128)(2,1)}, u32[]{:S(2)}) copy-start(bf16[2,584,1024]{2,1,0:T(8,128)(2,1)} %copy-done.7) | copy-start | bytes 7176196
  250.8 17.6 %collective-permute-start.37 = (bf16[2,584,1024]{2,1,0:T(8,128)(2,1)S(1)}, bf16[2,584,1024]{2,1,0:T(8,128)(2,1)S(1)}, u32[]{:S(2)}, u32[]{:S(2)}) collective-permute-start(bf16[2,584,1024]{2,1,0:T(8,128)(2,1)S(1)} %bitcast.97), channel_id=1, source_target_pairs={{0,1},{1,0},{2,3},{3,2},{4,5},{5,4},{6,7},{7,6},{8,9},{9,8},{10,11... | collective-permute-start | bytes 7176200 | tf_op jit(solution)/shard_map/ppermute | solution.py:828
  256.0 25.6 %collective-permute-start.38 = (bf16[8,512,128]{2,1,0:T(8,128)(2,1)S(1)}, bf16[8,512,128]{2,1,0:T(8,128)(2,1)S(1)}, u32[]{:S(2)}, u32[]{:S(2)}) collective-permute-start(bf16[8,512,128]{2,1,0:T(8,128)(2,1)S(1)} %get-tuple-element.304), channel_id=1, source_target_pairs={{0,2},{2,0},{1,3},{3,1},{4,6},{6,4},{5,7},{7,5},{8,10},{10,8},{9,1... | collective-permute-start | bytes 3145736 | tf_op jit(solution)/shard_map/ppermute | solution.py:824
  256.6 25.3 %collective-permute-start.39 = (bf16[8,512,128]{2,1,0:T(8,128)(2,1)S(1)}, bf16[8,512,128]{2,1,0:T(8,128)(2,1)S(1)}, u32[]{:S(2)}, u32[]{:S(2)}) collective-permute-start(bf16[8,512,128]{2,1,0:T(8,128)(2,1)S(1)} %get-tuple-element.305), channel_id=1, source_target_pairs={{0,4},{4,0},{8,12},{12,8},{16,20},{20,16},{24,28},{28,24},{1,5},{5... | collective-permute-start | bytes 3145736 | tf_op jit(solution)/shard_map/ppermute | solution.py:816
  260.4 19.2 %collective-permute-start.40 = (bf16[2,1024,128]{2,1,0:T(8,128)(2,1)S(1)}, bf16[2,1024,128]{2,1,0:T(8,128)(2,1)S(1)}, u32[]{:S(2)}, u32[]{:S(2)}) collective-permute-start(bf16[2,1024,128]{2,1,0:T(8,128)(2,1)S(1)} %get-tuple-element.323), channel_id=1, source_target_pairs={{0,8},{4,12},{8,0},{12,4},{16,24},{20,28},{24,16},{28,20},{1,9},{5... | collective-permute-start | bytes 1572872 | tf_op jit(solution)/shard_map/ppermute | solution.py:813
  279.5 7.7 %collective-permute-start.44 = (bf16[2,584,1024]{2,1,0:T(8,128)(2,1)S(1)}, bf16[2,584,1024]{2,1,0:T(8,128)(2,1)S(1)}, u32[]{:S(2)}, u32[]{:S(2)}) collective-permute-start(bf16[2,584,1024]{2,1,0:T(8,128)(2,1)S(1)} %grad_one.1.refs_9_), channel_id=1, source_target_pairs={{0,1},{1,0},{2,3},{3,2},{4,5},{5,4},{6,7},{7,6},{8,9},{9,8},{10,11... | collective-permute-start | bytes 7176200 | tf_op jit(solution)/shard_map/ppermute | solution.py:828
  283.3 13.3 %collective-permute-start.41 = (bf16[4,512,128]{2,1,0:T(8,128)(2,1)S(1)}, bf16[4,512,128]{2,1,0:T(8,128)(2,1)S(1)}, u32[]{:S(2)}, u32[]{:S(2)}) collective-permute-start(bf16[4,512,128]{2,1,0:T(8,128)(2,1)S(1)} %get-tuple-element.335), channel_id=1, source_target_pairs={{0,4},{4,0},{8,12},{12,8},{16,20},{20,16},{24,28},{28,24},{1,5},{5... | collective-permute-start | bytes 1572872 | tf_op jit(solution)/shard_map/ppermute | solution.py:816
  284.7 12.9 %collective-permute-start.42 = (bf16[4,512,128]{2,1,0:T(8,128)(2,1)S(1)}, bf16[4,512,128]{2,1,0:T(8,128)(2,1)S(1)}, u32[]{:S(2)}, u32[]{:S(2)}) collective-permute-start(bf16[4,512,128]{2,1,0:T(8,128)(2,1)S(1)} %get-tuple-element.337), channel_id=1, source_target_pairs={{0,2},{2,0},{1,3},{3,1},{4,6},{6,4},{5,7},{7,5},{8,10},{10,8},{9,1... | collective-permute-start | bytes 1572872 | tf_op jit(solution)/shard_map/ppermute | solution.py:824
  285.4 15.8 %collective-permute-start.43 = (bf16[1,1024,128]{2,1,0:T(8,128)(2,1)S(1)}, bf16[1,1024,128]{2,1,0:T(8,128)(2,1)S(1)}, u32[]{:S(2)}, u32[]{:S(2)}) collective-permute-start(bf16[1,1024,128]{2,1,0:T(8,128)(2,1)S(1)} %get-tuple-element.338), channel_id=1, source_target_pairs={{0,16},{4,20},{8,24},{12,28},{16,0},{20,4},{24,8},{28,12},{1,17},{... | collective-permute-start | bytes 786440 | tf_op jit(solution)/shard_map/ppermute | solution.py:813
  297.7 4.8 %collective-permute-start.45 = (f32[4,16,128]{2,1,0:T(8,128)S(1)}, f32[4,16,128]{2,1,0:T(8,128)S(1)}, u32[]{:S(2)}, u32[]{:S(2)}) collective-permute-start(f32[4,16,128]{2,1,0:T(8,128)S(1)} %get-tuple-element.352), channel_id=1, source_target_pairs={{0,4},{2,6},{4,0},{6,2},{8,12},{10,14},{12,8},{14,10},{16,20},{18,... | collective-permute-start | bytes 98312 | tf_op jit(solution)/shard_map/ppermute | solution.py:821
  298.3 4.2 %collective-permute-start.46 = (f32[4,16,128]{2,1,0:T(8,128)S(1)}, f32[4,16,128]{2,1,0:T(8,128)S(1)}, u32[]{:S(2)}, u32[]{:S(2)}) collective-permute-start(f32[4,16,128]{2,1,0:T(8,128)S(1)} %get-tuple-element.353), channel_id=1, source_target_pairs={{0,2},{2,0},{4,6},{6,4},{8,10},{10,8},{12,14},{14,12},{16,18},{18,... | collective-permute-start | bytes 98312 | tf_op jit(solution)/shard_map/ppermute | solution.py:821
  299.7 4.8 %collective-permute-start.47 = (f32[4,16,128]{2,1,0:T(8,128)S(1)}, f32[4,16,128]{2,1,0:T(8,128)S(1)}, u32[]{:S(2)}, u32[]{:S(2)}) collective-permute-start(f32[4,16,128]{2,1,0:T(8,128)S(1)} %get-tuple-element.354), channel_id=1, source_target_pairs={{0,6},{2,4},{4,2},{6,0},{8,14},{10,12},{12,10},{14,8},{16,22},{18,... | collective-permute-start | bytes 98312 | tf_op jit(solution)/shard_map/ppermute | solution.py:821
  306.2 11.7 %copy-start.33 = (bf16[1040,128]{1,0:T(8,128)(2,1)}, bf16[1040,128]{1,0:T(8,128)(2,1)S(1)}, u32[]{:S(2)}) copy-start(bf16[1040,128]{1,0:T(8,128)(2,1)S(1)} %get-tuple-element.361.refs_0_) | copy-start | bytes 798724
  306.2 11.7 %collective-permute-start.48 = (bf16[1040,128]{1,0:T(8,128)(2,1)}, bf16[1040,128]{1,0:T(8,128)(2,1)S(1)}, u32[]{:S(2)}, u32[]{:S(2)}) collective-permute-start(bf16[1040,128]{1,0:T(8,128)(2,1)} %get-tuple-element.356), channel_id=1, source_target_pairs={{0,8},{4,12},{8,0},{12,4},{16,24},{20,28},{24,16},{28,20},{1,9},{5... | collective-permute-start | bytes 798728 | tf_op jit(solution)/shard_map/ppermute | solution.py:813
  307.1 20.8 %collective-permute-start.49 = (bf16[1040,128]{1,0:T(8,128)(2,1)}, bf16[1040,128]{1,0:T(8,128)(2,1)S(1)}, u32[]{:S(2)}, u32[]{:S(2)}) collective-permute-start(bf16[1040,128]{1,0:T(8,128)(2,1)} %get-tuple-element.357), channel_id=1, source_target_pairs={{0,16},{4,20},{8,24},{12,28},{16,0},{20,4},{24,8},{28,12},{1,17},{... | collective-permute-start | bytes 798728 | tf_op jit(solution)/shard_map/ppermute | solution.py:813
  309.4 18.5 %collective-permute-start.50 = (bf16[1040,128]{1,0:T(8,128)(2,1)}, bf16[1040,128]{1,0:T(8,128)(2,1)S(1)}, u32[]{:S(2)}, u32[]{:S(2)}) collective-permute-start(bf16[1040,128]{1,0:T(8,128)(2,1)} %get-tuple-element.358), channel_id=1, source_target_pairs={{0,24},{4,28},{8,16},{12,20},{16,8},{20,12},{24,0},{28,4},{1,25},{... | collective-permute-start | bytes 798728 | tf_op jit(solution)/shard_map/ppermute | solution.py:813
  318.0 9.9 %copy-start.44 = (bf16[1040,128]{1,0:T(8,128)(2,1)}, bf16[1040,128]{1,0:T(8,128)(2,1)S(1)}, u32[]{:S(2)}) copy-start(bf16[1040,128]{1,0:T(8,128)(2,1)S(1)} %collective-permute-done.48.refs_1_) | copy-start | bytes 798724
  (34 other events, 126.8 us)

commit v8 on v7

--- a/solution.py
+++ b/solution.py
@@ -857,7 +857,7 @@
     return a_all, b_all
 
 
-def add_pieces(groups, cuts, outs, name):
+def add_pieces(groups, cuts, outs, name, smem=(), more=(), fill=None):
     arrays = [a for group in groups for a in group]
     starts = [sum(len(g) for g in groups[:i]) for i in range(len(groups))]
     last = {}
@@ -866,6 +866,7 @@
 
     def body(small, ins, outs_ref, scratch, loads):
         in_s, out_s = scratch[: len(arrays)], scratch[len(arrays) :]
+        more_s = out_s[len(outs) :]
         loaded = [loads.start([(ins[i], in_s[i]) for i in range(starts[g], starts[g] + len(groups[g]))]) for g in range(len(groups))]
         ready, done = set(), []
         for n, (g, spot, which, place) in enumerate(cuts):
@@ -879,16 +880,20 @@
             out_s[which][place] = total.astype(out_s[which].dtype)
             for w in sorted(w for w in last if last[w] == n):
                 done.append(loads.start([(out_s[w], outs_ref[w])]))
+        if fill is not None:
+            fill(small, out_s, more_s)
+            done.append(loads.start(list(zip(more_s, outs_ref[len(outs) :]))))
         for group in done:
             loads.wait(group)
 
     return call(
         body,
         arrays,
-        outs,
-        [pltpu.VMEM(a.shape, a.dtype) for a in arrays] + [pltpu.VMEM(o.shape, o.dtype) for o in outs],
+        list(outs) + list(more),
+        [pltpu.VMEM(a.shape, a.dtype) for a in list(arrays) + list(outs) + list(more)],
         name,
         0,
+        smem=smem,
         spare=8,
     )
 
@@ -955,13 +960,13 @@
         send, keep = add_pieces(groups, cuts, outs, self.name + "_half")
         self.left = kept
         self.state = [keep, grid.send_z(send, self.bit)]
-        return keep
-
-    def finish(self, gate, cuts, outs):
+        return keep, send
+
+    def finish(self, gate, cuts, outs, **extra):
         if self.bit:
             cuts = [((0, rows), which, place) for rows, which, place in cuts]
         cuts = [(0, rows, which, place) for rows, which, place in cuts]
-        return add_pieces([after(self.state, gate)], cuts, outs, self.name + "_sum")
+        return add_pieces([after(self.state, gate)], cuts, outs, self.name + "_sum", **extra)
 
 
 def join_kernel(pieces):
@@ -1342,11 +1347,11 @@
         ones = jnp.pad(one_sums.reshape(2, y_n, z_n, bd), ((0, 14), (0, 0), (0, 0), (0, wide - bd)))
         ones = ones.transpose(1, 2, 0, 3)
         small = [value + ones[n % y_n] for n, value in enumerate(small)]
-    small = after(small, qkv_rs.state)
+    grad_up = up_rs.finish(small[0], up_cuts, [sds((bd, fw), F32)])[0]
+    small = after(small, grad_up)
     got = small[:1]
     for n in range(1, tx * y_n):
         got.append(grid.send_xy(small[n], n // y_n, n % y_n))
-    grad_up = up_rs.finish(one_sums, up_cuts, [sds((bd, fw), F32)])[0]
     cuts, outs = [], [sds((3, bd, hw), F32), sds((hw, bd), F32)]
     last_rows = row0 + hh
     for h in range(2):
@@ -1365,7 +1370,27 @@
     layer_out = finish_layer(
         ids, keep, nv, middle, after(mlp_part, qkv_zs), mlp_recv, dp, aligned
     )
-    res = qkv_rs.finish(layer_out, cuts, outs)
+    share, own = bd // (2 * tx), None
+    if wide == bd == 128 and fw // dp == bd:
+        qv = hw // dp
+
+        def fill(small, out_s, more_s):
+            rows = out_s[2][...]
+            turned = pltpu.roll(rows, (128 - small[0][0]) % 128, 1)
+            more_s[0][0:1, :] = turned[0:1, :share]
+            more_s[0][1:2, :] = turned[2:3, :share]
+            more_s[1][0:1, :] = turned[1:2, :share]
+            more_s[1][1:4, :] = turned[3:6, :share]
+            more_s[2][...] = rows[6:8, :qv]
+            more_s[3][...] = rows[8:9, :]
+
+        shapes = [(2, share), (4, share), (2, qv), (1, bd)]
+        place = ((2 * me_x + core) * share)[None]
+        more = [sds(shape, F32) for shape in shapes]
+        res = qkv_rs.finish(layer_out, cuts, outs, smem=(place,), more=more, fill=fill)
+        own = res[3:]
+    else:
+        res = qkv_rs.finish(layer_out, cuts, outs)
     grad_qkv, grad_out = res[:2]
     if wide == bd:
         both = res[2]
@@ -1384,19 +1409,24 @@
 
         layer_out, grad_tokens = restore(layer_out), restore(grad_tokens)
 
-    share = bd // (2 * tx)
-    mine = lax.dynamic_slice(both[:6, :bd], (0, (2 * me_x + core) * share), (6, share))
-
+    if own is None:
+        mine = lax.dynamic_slice(both[:6, :bd], (0, (2 * me_x + core) * share), (6, share))
+        own = [
+            mine[0:3:2],
+            jnp.concatenate([mine[1:2], mine[3:6]]),
+            both[6:8, : hw // dp],
+            both[8:9, : fw // dp],
+        ]
     return (
         layer_out,
         grad_tokens,
-        mine[0:3:2],
-        jnp.concatenate([mine[1:2], mine[3:6]]),
+        own[0],
+        own[1],
         grad_qkv,
-        both[6:8, : hw // dp],
+        own[2],
         grad_out,
         grad_up,
-        both[8, : fw // dp],
+        own[3].reshape(fw // dp),
         grad_down,
     )
 

time: 341 us -> 335 us (0.982)
    unnamed x106 -> x102, local copies, waits for them, and re-layouts: 13.2 us -> 13.5 us
  transfers between devices with their start and end apart: 51 -> 51, of which waited for: 17 -> 17; matrix products, arithmetic and copies ran while one was open for 2% -> 2% of each run, Pallas kernels for 54% -> 55%
where the time goes in v8:
time: 335 us; the launch traced here: 330 us
  Pallas kernels  185 us (55%)
  starting transfers between devices  63.4 us (19%)
  waiting for transfers between devices  58.4 us (17%)
  local copies, waits for them, and re-layouts  18.6 us (6%)
  other arithmetic  3.52 us (1%)
    pallas_call x30, Pallas kernels, call(): pl.pallas_call(kernel, out_shape=outs, in_specs=[pl.BlockSpec(memory_spac...  185 us
    ppermute x17, starting transfers between devices, send_z(): lax.ppermute(value, 'dp', [(i, i ^ k * self.y) for i in range(self.dp)])  32.6 us
    ppermute x17, waiting for transfers between devices, send_z(): lax.ppermute(value, 'dp', [(i, i ^ k * self.y) for i in range(self.dp)])  27.9 us
    ppermute x12, waiting for transfers between devices, send_y(): return lax.ppermute(value, 'dp', [(i, i ^ k) for i in range(self.dp)])  22.1 us
    ppermute x12, starting transfers between devices, send_x(): return lax.ppermute(value, 'tx', [(i, i ^ k) for i in range(self.tx)])  14.5 us
    unnamed x102, local copies, waits for them, and re-layouts  13.5 us
    ppermute x12, starting transfers between devices, send_y(): return lax.ppermute(value, 'dp', [(i, i ^ k) for i in range(self.dp)])  11.6 us
  transfers between devices with their start and end apart: 51, of which 17 were waited for; matrix products, arithmetic and copies ran while one was open for 2% of the time, Pallas kernels for 55%

profile of v8, /device:TPU:0, one launch (start us, length us, event | category | flops | bytes accessed | tf_op | source)
XLA Modules:
  0.0 330.3 jit_solution(11717747349815470851)
XLA Ops:
  3.6 1.5 concatenate.23
  5.1 3.1 collective-permute-start
  8.2 2.6 collective-permute-start.1
  12.4 4.8 %arrange_pair.1 = (bf16[2,584,1024]{2,1,0:T(8,128)(2,1)}, bf16[2,584,1024]{2,1,0:T(8,128)(2,1)}) custom-call(s32[10]{0:T(128)} %stack.130.refs_0_, bf16[584,1024]{1,0:T(8,128)(2,1)} %refs_1_.1, bf16[584,1024]{1,0:T(8,128)(2,1)} %refs_2_.1, bf16[584,1024]{1,0:T(8,128)(2,1)} %copy-done.41, bf16[584,1024]{1,0:T(8,128)(2,1)} %collective-permute-done.4.refs_4_), custom_call_target="tpu_custom_call" | custom-call | flops 5750000128 | bytes 5750000 | tf_op jit(solution)/shard_map/arrange_pair/pallas_call | solution.py:94
  17.3 2.6 collective-permute-done
  19.9 9.9 %collective-permute-done.1 = bf16[1040,128]{1,0:T(8,128)(2,1)S(1)} collective-permute-done((bf16[1040,128]{1,0:T(8,128)(2,1)S(1)}, bf16[1040,128]{1,0:T(8,128)(2,1)S(1)}, u32[]{:S(2)}, u32[]{:S(2)}) %collective-permute-start.1) | collective-permute-done | bytes 266272 | tf_op jit(solution)/shard_map/ppermute | solution.py:813
  30.1 1.6 collective-permute-start.5
  31.8 1.6 collective-permute-start.7
  33.4 8.8 %collective-permute-done.5 = bf16[4,528,128]{2,1,0:T(8,128)(2,1)S(1)} collective-permute-done((bf16[4,528,128]{2,1,0:T(8,128)(2,1)S(1)}, bf16[4,528,128]{2,1,0:T(8,128)(2,1)S(1)}, u32[]{:S(2)}, u32[]{:S(2)}) %collective-permute-start.5) | collective-permute-done | bytes 540704 | tf_op jit(solution)/shard_map/ppermute | solution.py:816
  42.3 1.6 collective-permute-start.6
  46.3 6.2 %collective-permute-start.9 = (bf16[256,512]{1,0:T(8,128)(2,1)S(1)}, bf16[256,512]{1,0:T(8,128)(2,1)S(1)}, u32[]{:S(2)}, u32[]{:S(2)}) collective-permute-start(bf16[256,512]{1,0:T(8,128)(2,1)S(1)} %constant_dynamic-update-slice_fusion.10), channel_id=1, source_target_pairs={{0,8},{4,12},{8,0},{12,4},{16,24},{20,28},{24,16},{28,20},{1,9},{5... | collective-permute-start | bytes 786440 | tf_op jit(solution)/shard_map/ppermute | solution.py:813
  53.6 1.4 collective-permute-start.11
  55.0 11.0 %collective-permute-done.8.refs_6_.refs_10_.refs_11_.refs_15_ = bf16[8,512,128]{2,1,0:T(8,128)(2,1)} collective-permute-done((bf16[8,512,128]{2,1,0:T(8,128)(2,1)S(1)}, bf16[8,512,128]{2,1,0:T(8,128)(2,1)}, u32[]{:S(2)}, u32[]{:S(2)}) %collective-permute-start.8) | collective-permute-done | bytes 1048608 | tf_op jit(solution)/shard_map/ppermute | solution.py:816
  66.6 2.6 vectors.1
  69.2 3.7 %collective-permute-done.10 = bf16[256,512]{1,0:T(8,128)(2,1)S(1)} collective-permute-done((bf16[256,512]{1,0:T(8,128)(2,1)S(1)}, bf16[256,512]{1,0:T(8,128)(2,1)S(1)}, u32[]{:S(2)}, u32[]{:S(2)}) %collective-permute-start.10) | collective-permute-done | bytes 262176 | tf_op jit(solution)/shard_map/ppermute | solution.py:813
  74.9 14.7 %attn_forward.2 = (bf16[2,584,1024]{2,1,0:T(8,128)(2,1)S(1)}, bf16[2,584,512]{2,1,0:T(8,128)(2,1)S(1)}, bf16[2,584,512]{2,1,0:T(8,128)(2,1)S(1)}, bf16[2,584,512...) custom-call(f32[6,1024]{1,0:T(8,128)S(1)} %copy-done.20, ...), custom_call_target="tpu_custom_call" | custom-call | flops 18400000000 | bytes 18400000 | tf_op jit(solution)/shard_map/attn_forward/pallas_call | solution.py:94
  89.9 3.8 %collective-permute-start.18 = (bf16[1024,128]{1,0:T(8,128)(2,1)S(1)}, bf16[1024,128]{1,0:T(8,128)(2,1)S(1)}, u32[]{:S(2)}, u32[]{:S(2)}) collective-permute-start(bf16[1024,128]{1,0:T(8,128)(2,1)S(1)} %constant_dynamic-update-slice_fusion.16), channel_id=1, source_target_pairs={{0,8},{4,12},{8,0},{12,4},{16,24},{20,28},{24,16},{28,20},{1,9},{5... | collective-permute-start | bytes 786440 | tf_op jit(solution)/shard_map/ppermute | solution.py:813
  94.7 1.4 collective-permute-start.20
  98.3 15.5 %attn_forward.3 = (bf16[2,584,1024]{2,1,0:T(8,128)(2,1)S(1)}, bf16[2,584,512]{2,1,0:T(8,128)(2,1)S(1)}, bf16[2,584,512]{2,1,0:T(8,128)(2,1)S(1)}, bf16[2,584,512...) custom-call(f32[6,1024]{1,0:T(8,128)S(1)} %copy-done.20, ...), custom_call_target="tpu_custom_call", output_to_operand_aliasing={{0}: (3, {}), {1}: (4, {}), {2}: (5, {}), {3}: (6, {}), {4}... | custom-call | flops 18400000000 | bytes 18400000 | tf_op jit(solution)/shard_map/attn_forward/pallas_call | solution.py:94
  115.9 2.2 collective-permute-done.16
  118.1 1.7 broadcast_multiply_fusion
  122.3 1.4 collective-permute-start.22
  124.8 10.1 %mlp_up.2 = (f32[2,584,1024]{2,1,0:T(8,128)}, bf16[2,584,1024]{2,1,0:T(8,128)(2,1)}, bf16[2,584,2048]{2,1,0:T(8,128)(2,1)}, bf16[2,584,2048]{2,1,0:T(8,128)(2,1)}) custom-call(f32[2]{0:T(128)} %get-tuple-element.375.refs_0_.refs_1_, f32[6,1024]{1,0:T(8,128)} %get-tuple-element.199.refs_0_.refs_1_.refs_2_, f32[1,2048]{1,0:T(1,128)} %get-tuple-element.200.refs_2_, ...), custom_call_target="tpu_custom_call" | custom-call | flops 11500000256 | bytes 11500000 | tf_op jit(solution)/shard_map/mlp_up/pallas_call | solution.py:94
  135.2 1.4 collective-permute-done.22.refs_3_
  136.6 3.3 %join.1 = (bf16[8,512,128]{2,1,0:T(8,128)(2,1)}, bf16[8,512,128]{2,1,0:T(8,128)(2,1)}) custom-call(bf16[4,512,128]{2,1,0:T(8,128)(2,1)S(1)} %pad_maximum_fusion.4.refs_0_, bf16[4,512,128]{2,1,0:T(8,128)(2,1)} %collective-permute-done.21.refs_1_, bf16[4,512,128]{2,1,0:T(8,128)(2,1)} %pad_maximum_fusion.5.refs_2_, ...), custom_call_target="tpu_custom_call" | custom-call | flops 23000000 | bytes 23000 | tf_op jit(solution)/shard_map/join/pallas_call | solution.py:94
  140.0 1.4 collective-permute-start.23
  142.0 10.1 %mlp_up.3 = (f32[2,584,1024]{2,1,0:T(8,128)}, bf16[2,584,1024]{2,1,0:T(8,128)(2,1)}, bf16[2,584,2048]{2,1,0:T(8,128)(2,1)}, bf16[2,584,2048]{2,1,0:T(8,128)(2,1)}) custom-call(f32[2]{0:T(128)} %get-tuple-element.375.refs_0_.refs_1_, ...), custom_call_target="tpu_custom_call", output_to_operand_aliasing={{0}: (6, {}), {1}: (7, {}), {2}: (8, {}), {3}: (9, {})} | custom-call | flops 11500000256 | bytes 11500000 | tf_op jit(solution)/shard_map/mlp_up/pallas_call | solution.py:94
  152.1 10.7 %down_grad.1 = (bf16[8,512,128]{2,1,0:T(8,128)(2,1)}, bf16[8,512,128]{2,1,0:T(8,128)(2,1)}, bf16[8,512,128]{2,1,0:T(8,128)(2,1)}, bf16[8,512,128]{2,1,0:T(8,128)(2,1)}) custom-call(bf16[1168,2048]{1,0:T(8,128)(2,1)} %bitcast.123, bf16[1168,1024]{1,0:T(8,128)(2,1)} %bitcast.106), custom_call_target="tpu_custom_call" | custom-call | flops 12650000384 | bytes 12650000 | tf_op jit(solution)/shard_map/down_grad/pallas_call | solution.py:94
  162.9 1.5 collective-permute-start.27
  165.0 2.0 collective-permute-done.24.refs_6_
  167.0 21.8 %mlp_back.1 = (bf16[1168,2048]{1,0:T(8,128)(2,1)}, f32[1,2048]{1,0:T(1,128)}, bf16[2,584,1024]{2,1,0:T(8,128)(2,1)}, bf16[1168,1024]{1,0:T(8,128)(2,1)}) custom-call(bf16[1168,1024]{1,0:T(8,128)(2,1)} %bitcast.107, bf16[1168,2048]{1,0:T(8,128)(2,1)} %bitcast.124, bf16[1168,2048]{1,0:T(8,128)(2,1)} %bitcast.125, ...), custom_call_target="tpu_custom_call" | custom-call | flops 25300000768 | bytes 25300000 | tf_op jit(solution)/shard_map/mlp_back/pallas_call | solution.py:94
  191.3 2.5 down_add.1
  194.0 2.1 collective-permute-start.29
  196.1 7.4 %up_grad.1 = (bf16[8,512,128]{2,1,0:T(8,128)(2,1)S(1)}, bf16[8,512,128]{2,1,0:T(8,128)(2,1)S(1)}, bf16[8,512,128]{2,1,0:T(8,128)(2,1)S(1)}, bf16[8,512,128]{2,1,0:T(8,128)(2,1)S(1)}) custom-call(bf16[1168,1024]{1,0:T(8,128)(2,1)S(1)} %bitcast.104, bf16[1168,2048]{1,0:T(8,128)(2,1)S(1)} %copy-done.32), custom_call_target="tpu_custom_call" | custom-call | flops 12650000384 | bytes 12650000 | tf_op jit(solution)/shard_map/up_grad/pallas_call | solution.py:94
  203.5 1.9 collective-permute-start.31
  205.5 9.7 %middle_back.1 = (f32[584,1024]{1,0:T(8,128)S(1)}, bf16[2,584,1024]{2,1,0:T(8,128)(2,1)S(1)}, bf16[2,584,512]{2,1,0:T(8,128)(2,1)S(1)}, f32[4,1024]{1,0:T(4,128)S(1)}) custom-call(s32[10]{0:T(128)S(1)} %copy-done.23, f32[2]{0:T(128)S(1)} %copy-done.22, f32[6,1024]{1,0:T(8,128)S(1)} %copy-done.21, f32[2,584,1024]{2,1,0:T(8,128)} %get-tuple-element.232.refs_3_, ...), custom_call_target="tpu_custom_call" | custom-call | flops 23000000 | bytes 23000 | tf_op jit(solution)/shard_map/middle_back/pallas_call | solution.py:94
  216.8 2.4 collective-permute-start.35
  219.3 1.4 collective-permute-start.36
  220.7 3.1 out_grad.1
  223.8 8.0 %attn_first.1 = (bf16[3,2,584,128]{3,2,1,0:T(8,128)(2,1)S(1)}, f32[2,2,128]{2,1,0:T(2,128)S(1)}) custom-call(bf16[2,584,512]{2,1,0:T(8,128)(2,1)S(1)} %copy-done.15, bf16[2,584,512]{2,1,0:T(8,128)(2,1)S(1)} %copy-done.17, bf16[2,584,512]{2,1,0:T(8,128)(2,1)S(1)} %copy-done.19, bf16[2,584,512]{2,1,0:T(8,128)(2,1)S(1)} %get-tuple-element.319.refs_3_), custom_call_target="tpu_custom_call" | custom-call | flops 23000000 | bytes 23000 | tf_op jit(solution)/shard_map/attn_first/pallas_call | solution.py:94
  231.8 1.4 up_add.1
  233.9 1.4 collective-permute-start.33
  235.4 15.5 %attn_backward.2 = (bf16[3,4,584,128]{3,2,1,0:T(8,128)(2,1)S(1)}, f32[4,2,128]{2,1,0:T(2,128)S(1)}) custom-call(bf16[2,584,512]{2,1,0:T(8,128)(2,1)S(1)} %copy-done.15, bf16[2,584,512]{2,1,0:T(8,128)(2,1)S(1)} %copy-done.17, bf16[2,584,512]{2,1,0:T(8,128)(2,1)S(1)} %copy-done.19, bf16[2,584,512]{2,1,0:T(8,128)(2,1)S(1)} %get-tuple-element.319.refs_3_), custom_call_target="tpu_custom_call" | custom-call | flops 20700000256 | bytes 20700000 | tf_op jit(solution)/shard_map/attn_backward/pallas_call | solution.py:94
  250.9 5.1 %qkv_grad.1 = (bf16[8,512,128]{2,1,0:T(8,128)(2,1)S(1)}, bf16[8,512,128]{2,1,0:T(8,128)(2,1)S(1)}, bf16[8,512,128]{2,1,0:T(8,128)(2,1)S(1)}) custom-call(bf16[1168,1024]{1,0:T(8,128)(2,1)S(1)} %bitcast.95, bf16[3,1168,128]{2,1,0:T(8,128)(2,1)S(1)} %bitcast.101, ...), custom_call_target="tpu_custom_call", output_to_operand_aliasing={{0}: (3, {}), {1}: (4, {}), {2}: (5, {})} | custom-call | flops 8049999872 | bytes 8050000 | tf_op jit(solution)/shard_map/qkv_grad/pallas_call | solution.py:94
  256.7 1.4 collective-permute-start.39
  258.0 1.4 down_sum.1
  260.5 8.0 %attn_backward.3 = (bf16[3,2,584,128]{3,2,1,0:T(8,128)(2,1)S(1)}, f32[2,2,128]{2,1,0:T(2,128)S(1)}) custom-call(bf16[2,584,512]{2,1,0:T(8,128)(2,1)S(1)} %copy-done.15, bf16[2,584,512]{2,1,0:T(8,128)(2,1)S(1)} %copy-done.17, bf16[2,584,512]{2,1,0:T(8,128)(2,1)S(1)} %copy-done.19, bf16[2,584,512]{2,1,0:T(8,128)(2,1)S(1)} %get-tuple-element.319.refs_3_), custom_call_target="tpu_custom_call" | custom-call | flops 20700000256 | bytes 20700000 | tf_op jit(solution)/shard_map/attn_backward/pallas_call | solution.py:94
  268.5 1.4 copy-done.11
  269.9 2.6 qkv_keep.1.refs_0_
  272.5 7.1 %grad_one.1.refs_9_ = bf16[2,584,1024]{2,1,0:T(8,128)(2,1)S(1)} custom-call(bf16[3,1168,128]{2,1,0:T(8,128)(2,1)S(1)} %bitcast.102, bf16[6,1168,128]{2,1,0:T(8,128)(2,1)S(1)} %bitcast.100, bf16[3,1168,128]{2,1,0:T(8,128)(2,1)S(1)} %bitcast.94, bf16[8,528,128]{2,1,0:T(8,128)(2,1)S(1)} %copy-done.3, ...), custom_call_target="tpu_custom_call" | custom-call | flops 23000000 | bytes 23000 | tf_op jit(solution)/shard_map/grad_one/pallas_call | solution.py:94
  280.3 3.0 collective-permute-start.43
  283.4 1.4 qkv_add.1
  285.5 1.4 collective-permute-start.42
  286.9 7.2 %finish_tokens.1 = (bf16[584,1024]{1,0:T(8,128)(2,1)}, f32[2,1024]{1,0:T(2,128)}, f32[4,16,128]{2,1,0:T(8,128)S(1)}, f32[4,16,128]{2,1,0:T(8,128)S(1)}, f32[4,16...) custom-call(s32[10]{0:T(128)S(1)} %copy-done.23, f32[6,1024]{1,0:T(8,128)S(1)} %copy-done.21, ...), custom_call_target="tpu_custom_call" | custom-call | flops 10350000128 | bytes 10350000 | tf_op jit(solution)/shard_map/finish_tokens/pallas_call | solution.py:94
  294.1 1.8 collective-permute-done.43.refs_1_
  299.4 1.4 collective-permute-start.47
  302.4 1.8 collective-permute-done.47.refs_7_
  306.1 2.7 collective-permute-start.49
  308.7 1.7 collective-permute-start.50
  310.5 2.4 copy-done
  312.8 1.7 copy-done.12
  314.5 3.2 finish_layer.1
  318.1 9.5 %collective-permute-done.49.refs_3_ = bf16[1040,128]{1,0:T(8,128)(2,1)} collective-permute-done((bf16[1040,128]{1,0:T(8,128)(2,1)S(1)}, bf16[1040,128]{1,0:T(8,128)(2,1)}, u32[]{:S(2)}, u32[]{:S(2)}) %collective-permute-start.49) | collective-permute-done | bytes 266272 | tf_op jit(solution)/shard_map/ppermute | solution.py:813
  327.6 2.5 qkv_sum.1
  (204 shorter events, 37.2 us)
Async XLA Ops:
  0.6 10.8 %collective-permute-start.3 = (bf16[584,1024]{1,0:T(8,128)(2,1)}, bf16[584,1024]{1,0:T(8,128)(2,1)S(1)}, u32[]{:S(2)}, u32[]{:S(2)}) collective-permute-start(bf16[584,1024]{1,0:T(8,128)(2,1)} %refs_1_.1), channel_id=1, source_target_pairs={{0,1},{1,0},{2,3},{3,2},{4,5},{5,4},{6,7},{7,6},{8,9},{9,8},{10,11... | collective-permute-start | bytes 3588104 | tf_op jit(solution)/shard_map/ppermute | solution.py:828
  1.2 10.3 %collective-permute-start.4 = (bf16[584,1024]{1,0:T(8,128)(2,1)}, bf16[584,1024]{1,0:T(8,128)(2,1)}, u32[]{:S(2)}, u32[]{:S(2)}) collective-permute-start(bf16[584,1024]{1,0:T(8,128)(2,1)} %refs_2_.1), channel_id=1, source_target_pairs={{0,1},{1,0},{2,3},{3,2},{4,5},{5,4},{6,7},{7,6},{8,9},{9,8},{10,11... | collective-permute-start | bytes 3588104 | tf_op jit(solution)/shard_map/ppermute | solution.py:828
  5.1 14.8 %collective-permute-start = (bf16[1040,128]{1,0:T(8,128)(2,1)S(1)}, bf16[1040,128]{1,0:T(8,128)(2,1)S(1)}, u32[]{:S(2)}, u32[]{:S(2)}) collective-permute-start(bf16[1040,128]{1,0:T(8,128)(2,1)S(1)} %concatenate.23), channel_id=1, source_target_pairs={{0,8},{4,12},{8,0},{12,4},{16,24},{20,28},{24,16},{28,20},{1,9},{5... | collective-permute-start | bytes 798728 | tf_op jit(solution)/shard_map/ppermute | solution.py:813
  8.2 21.6 %collective-permute-start.1 = (bf16[1040,128]{1,0:T(8,128)(2,1)S(1)}, bf16[1040,128]{1,0:T(8,128)(2,1)S(1)}, u32[]{:S(2)}, u32[]{:S(2)}) collective-permute-start(bf16[1040,128]{1,0:T(8,128)(2,1)S(1)} %concatenate.23), channel_id=1, source_target_pairs={{0,16},{4,20},{8,24},{12,28},{16,0},{20,4},{24,8},{28,12},{1,17},{... | collective-permute-start | bytes 798728 | tf_op jit(solution)/shard_map/ppermute | solution.py:813
  10.8 19.0 %collective-permute-start.2 = (bf16[1040,128]{1,0:T(8,128)(2,1)S(1)}, bf16[1040,128]{1,0:T(8,128)(2,1)S(1)}, u32[]{:S(2)}, u32[]{:S(2)}) collective-permute-start(bf16[1040,128]{1,0:T(8,128)(2,1)S(1)} %concatenate.23), channel_id=1, source_target_pairs={{0,24},{4,28},{8,16},{12,20},{16,8},{20,12},{24,0},{28,4},{1,25},{... | collective-permute-start | bytes 798728 | tf_op jit(solution)/shard_map/ppermute | solution.py:813
  30.1 12.2 %collective-permute-start.5 = (bf16[4,528,128]{2,1,0:T(8,128)(2,1)S(1)}, bf16[4,528,128]{2,1,0:T(8,128)(2,1)S(1)}, u32[]{:S(2)}, u32[]{:S(2)}) collective-permute-start(bf16[4,528,128]{2,1,0:T(8,128)(2,1)S(1)} %pad_maximum_fusion), channel_id=1, source_target_pairs={{0,4},{4,0},{8,12},{12,8},{16,20},{20,16},{24,28},{28,24},{1,5},{5... | collective-permute-start | bytes 1622024 | tf_op jit(solution)/shard_map/ppermute | solution.py:816
  31.8 12.8 %collective-permute-start.7 = (bf16[4,512,128]{2,1,0:T(8,128)(2,1)S(1)}, bf16[4,512,128]{2,1,0:T(8,128)(2,1)S(1)}, u32[]{:S(2)}, u32[]{:S(2)}) collective-permute-start(bf16[4,512,128]{2,1,0:T(8,128)(2,1)S(1)} %pad_maximum_fusion.1), channel_id=1, source_target_pairs={{0,2},{2,0},{1,3},{3,1},{4,6},{6,4},{5,7},{7,5},{8,10},{10,8},{9,1... | collective-permute-start | bytes 1572872 | tf_op jit(solution)/shard_map/ppermute | solution.py:824
  33.4 12.2 %copy-start.40 = (s32[4]{0:T(128)S(1)}, s32[4]{0:T(128)}, u32[]{:S(2)}) copy-start(s32[4]{0:T(128)} %param.13) | copy-start | bytes 52
  33.4 12.8 %copy-start.38 = (bf16[1024,128]{1,0:T(8,128)(2,1)S(1)}, bf16[1024,128]{1,0:T(8,128)(2,1)}, u32[]{:S(2)}) copy-start(bf16[1024,128]{1,0:T(8,128)(2,1)} %param.21) | copy-start | bytes 786436
  33.4 12.8 %copy-start.39 = (bf16[128,1024]{1,0:T(8,128)(2,1)S(1)}, bf16[128,1024]{1,0:T(8,128)(2,1)}, u32[]{:S(2)}) copy-start(bf16[128,1024]{1,0:T(8,128)(2,1)} %param.19) | copy-start | bytes 786436
  42.3 24.3 %collective-permute-start.6 = (bf16[8,528,128]{2,1,0:T(8,128)(2,1)S(1)}, bf16[8,528,128]{2,1,0:T(8,128)(2,1)}, u32[]{:S(2)}, u32[]{:S(2)}) collective-permute-start(bf16[8,528,128]{2,1,0:T(8,128)(2,1)S(1)} %constant_dynamic-update-slice_fusion.refs_1_.refs_3_.refs_7_.refs_8_.refs_12_), channel_id=1, source_target_pairs={{0,2},{2,0},{1,3},{3,1},{4,6},{6,4},{5,7},{7,5},{8,10},{10,8},{9,1... | collective-permute-start | bytes 3244040 | tf_op jit(solution)/shard_map/ppermute | solution.py:824
  44.7 30.1 %copy-start.4 = (bf16[8,512,128]{2,1,0:T(8,128)(2,1)}, bf16[8,512,128]{2,1,0:T(8,128)(2,1)S(1)}, u32[]{:S(2)}) copy-start(bf16[8,512,128]{2,1,0:T(8,128)(2,1)S(1)} %constant_dynamic-update-slice_fusion.5.refs_5_.refs_9_.refs_10_.refs_14_) | copy-start | bytes 3145732
  44.7 21.3 %collective-permute-start.8 = (bf16[8,512,128]{2,1,0:T(8,128)(2,1)S(1)}, bf16[8,512,128]{2,1,0:T(8,128)(2,1)}, u32[]{:S(2)}, u32[]{:S(2)}) collective-permute-start(bf16[8,512,128]{2,1,0:T(8,128)(2,1)S(1)} %constant_dynamic-update-slice_fusion.5.refs_5_.refs_9_.refs_10_.refs_14_), channel_id=1, source_target_pairs={{0,4},{4,0},{8,12},{12,8},{16,20},{20,16},{24,28},{28,24},{1,5},{5... | collective-permute-start | bytes 3145736 | tf_op jit(solution)/shard_map/ppermute | solution.py:816
  46.3 22.9 %collective-permute-start.9 = (bf16[256,512]{1,0:T(8,128)(2,1)S(1)}, bf16[256,512]{1,0:T(8,128)(2,1)S(1)}, u32[]{:S(2)}, u32[]{:S(2)}) collective-permute-start(bf16[256,512]{1,0:T(8,128)(2,1)S(1)} %constant_dynamic-update-slice_fusion.10), channel_id=1, source_target_pairs={{0,8},{4,12},{8,0},{12,4},{16,24},{20,28},{24,16},{28,20},{1,9},{5... | collective-permute-start | bytes 786440 | tf_op jit(solution)/shard_map/ppermute | solution.py:813
  52.5 20.4 %collective-permute-start.10 = (bf16[256,512]{1,0:T(8,128)(2,1)S(1)}, bf16[256,512]{1,0:T(8,128)(2,1)S(1)}, u32[]{:S(2)}, u32[]{:S(2)}) collective-permute-start(bf16[256,512]{1,0:T(8,128)(2,1)S(1)} %constant_dynamic-update-slice_fusion.10), channel_id=1, source_target_pairs={{0,16},{4,20},{8,24},{12,28},{16,0},{20,4},{24,8},{28,12},{1,17},{... | collective-permute-start | bytes 786440 | tf_op jit(solution)/shard_map/ppermute | solution.py:813
  53.6 19.3 %collective-permute-start.11 = (bf16[256,512]{1,0:T(8,128)(2,1)S(1)}, bf16[256,512]{1,0:T(8,128)(2,1)S(1)}, u32[]{:S(2)}, u32[]{:S(2)}) collective-permute-start(bf16[256,512]{1,0:T(8,128)(2,1)S(1)} %constant_dynamic-update-slice_fusion.10), channel_id=1, source_target_pairs={{0,24},{4,28},{8,16},{12,20},{16,8},{20,12},{24,0},{28,4},{1,25},{... | collective-permute-start | bytes 786440 | tf_op jit(solution)/shard_map/ppermute | solution.py:813
  73.1 16.5 %collective-permute-start.12 = (bf16[4,128,512]{2,1,0:T(8,128)(2,1)S(1)}, bf16[4,128,512]{2,1,0:T(8,128)(2,1)S(1)}, u32[]{:S(2)}, u32[]{:S(2)}) collective-permute-start(bf16[4,128,512]{2,1,0:T(8,128)(2,1)S(1)} %pad_maximum_fusion.2), channel_id=1, source_target_pairs={{0,4},{4,0},{8,12},{12,8},{16,20},{20,16},{24,28},{28,24},{1,5},{5... | collective-permute-start | bytes 1572872 | tf_op jit(solution)/shard_map/ppermute | solution.py:816
  73.8 15.8 %collective-permute-start.13 = (bf16[4,128,512]{2,1,0:T(8,128)(2,1)S(1)}, bf16[4,128,512]{2,1,0:T(8,128)(2,1)S(1)}, u32[]{:S(2)}, u32[]{:S(2)}) collective-permute-start(bf16[4,128,512]{2,1,0:T(8,128)(2,1)S(1)} %pad_maximum_fusion.3), channel_id=1, source_target_pairs={{0,2},{2,0},{1,3},{3,1},{4,6},{6,4},{5,7},{7,5},{8,10},{10,8},{9,1... | collective-permute-start | bytes 1572872 | tf_op jit(solution)/shard_map/ppermute | solution.py:824
  89.6 28.5 %copy-start.24 = (bf16[584,1024]{1,0:T(8,128)(2,1)}, bf16[584,1024]{1,0:T(8,128)(2,1)S(1)}, u32[]{:S(2)}) copy-start(bf16[584,1024]{1,0:T(8,128)(2,1)S(1)} %get-tuple-element.223.refs_4_) | copy-start | bytes 3588100
  89.8 24.0 %copy-start.37 = (bf16[8,128,512]{2,1,0:T(8,128)(2,1)}, bf16[8,128,512]{2,1,0:T(8,128)(2,1)S(1)}, u32[]{:S(2)}) copy-start(bf16[8,128,512]{2,1,0:T(8,128)(2,1)S(1)} %constant_dynamic-update-slice_fusion.12) | copy-start | bytes 3145732
  89.8 24.0 %copy-start.36 = (bf16[8,128,512]{2,1,0:T(8,128)(2,1)}, bf16[8,128,512]{2,1,0:T(8,128)(2,1)S(1)}, u32[]{:S(2)}) copy-start(bf16[8,128,512]{2,1,0:T(8,128)(2,1)S(1)} %constant_dynamic-update-slice_fusion.14) | copy-start | bytes 3145732
  89.9 30.5 %collective-permute-start.18 = (bf16[1024,128]{1,0:T(8,128)(2,1)S(1)}, bf16[1024,128]{1,0:T(8,128)(2,1)S(1)}, u32[]{:S(2)}, u32[]{:S(2)}) collective-permute-start(bf16[1024,128]{1,0:T(8,128)(2,1)S(1)} %constant_dynamic-update-slice_fusion.16), channel_id=1, source_target_pairs={{0,8},{4,12},{8,0},{12,4},{16,24},{20,28},{24,16},{28,20},{1,9},{5... | collective-permute-start | bytes 786440 | tf_op jit(solution)/shard_map/ppermute | solution.py:813
  93.6 26.7 %collective-permute-start.19 = (bf16[1024,128]{1,0:T(8,128)(2,1)S(1)}, bf16[1024,128]{1,0:T(8,128)(2,1)S(1)}, u32[]{:S(2)}, u32[]{:S(2)}) collective-permute-start(bf16[1024,128]{1,0:T(8,128)(2,1)S(1)} %constant_dynamic-update-slice_fusion.16), channel_id=1, source_target_pairs={{0,16},{4,20},{8,24},{12,28},{16,0},{20,4},{24,8},{28,12},{1,17},{... | collective-permute-start | bytes 786440 | tf_op jit(solution)/shard_map/ppermute | solution.py:813
  94.7 25.6 %collective-permute-start.20 = (bf16[1024,128]{1,0:T(8,128)(2,1)S(1)}, bf16[1024,128]{1,0:T(8,128)(2,1)S(1)}, u32[]{:S(2)}, u32[]{:S(2)}) collective-permute-start(bf16[1024,128]{1,0:T(8,128)(2,1)S(1)} %constant_dynamic-update-slice_fusion.16), channel_id=1, source_target_pairs={{0,24},{4,28},{8,16},{12,20},{16,8},{20,12},{24,0},{28,4},{1,25},{... | collective-permute-start | bytes 786440 | tf_op jit(solution)/shard_map/ppermute | solution.py:813
  96.1 22.0 %collective-permute-start.16 = (bf16[8,128,512]{2,1,0:T(8,128)(2,1)S(1)}, bf16[8,128,512]{2,1,0:T(8,128)(2,1)S(1)}, u32[]{:S(2)}, u32[]{:S(2)}) collective-permute-start(bf16[8,128,512]{2,1,0:T(8,128)(2,1)S(1)} %constant_dynamic-update-slice_fusion.12), channel_id=1, source_target_pairs={{0,2},{2,0},{1,3},{3,1},{4,6},{6,4},{5,7},{7,5},{8,10},{10,8},{9,1... | collective-permute-start | bytes 3145736 | tf_op jit(solution)/shard_map/ppermute | solution.py:824
  97.3 22.6 %collective-permute-start.17 = (bf16[8,128,512]{2,1,0:T(8,128)(2,1)S(1)}, bf16[8,128,512]{2,1,0:T(8,128)(2,1)S(1)}, u32[]{:S(2)}, u32[]{:S(2)}) collective-permute-start(bf16[8,128,512]{2,1,0:T(8,128)(2,1)S(1)} %constant_dynamic-update-slice_fusion.14), channel_id=1, source_target_pairs={{0,4},{4,0},{8,12},{12,8},{16,20},{20,16},{24,28},{28,24},{1,5},{5... | collective-permute-start | bytes 3145736 | tf_op jit(solution)/shard_map/ppermute | solution.py:816
  98.3 19.8 %copy-start.1 = (bf16[2,584,1024]{2,1,0:T(8,128)(2,1)S(1)}, bf16[2,584,1024]{2,1,0:T(8,128)(2,1)}, u32[]{:S(2)}) copy-start(bf16[2,584,1024]{2,1,0:T(8,128)(2,1)} %get-tuple-element.233.refs_4_) | copy-start | bytes 7176196
  118.1 5.6 %collective-permute-start.15 = (bf16[584,1024]{1,0:T(8,128)(2,1)S(1)}, bf16[584,1024]{1,0:T(8,128)(2,1)S(1)}, u32[]{:S(2)}, u32[]{:S(2)}) collective-permute-start(bf16[584,1024]{1,0:T(8,128)(2,1)S(1)} %get-tuple-element.223.refs_4_), channel_id=1, source_target_pairs={{0,1},{1,0},{2,3},{3,2},{4,5},{5,4},{6,7},{7,6},{8,9},{9,8},{10,11... | collective-permute-start | bytes 3588104 | tf_op jit(solution)/shard_map/ppermute | solution.py:828
  119.9 22.2 %collective-permute-start.14 = (bf16[584,1024]{1,0:T(8,128)(2,1)}, bf16[584,1024]{1,0:T(8,128)(2,1)}, u32[]{:S(2)}, u32[]{:S(2)}) collective-permute-start(bf16[584,1024]{1,0:T(8,128)(2,1)} %get-tuple-element.222.refs_4_), channel_id=1, source_target_pairs={{0,1},{1,0},{2,3},{3,2},{4,5},{5,4},{6,7},{7,6},{8,9},{9,8},{10,11... | collective-permute-start | bytes 3588104 | tf_op jit(solution)/shard_map/ppermute | solution.py:828
  120.9 14.4 %collective-permute-start.21 = (bf16[4,512,128]{2,1,0:T(8,128)(2,1)S(1)}, bf16[4,512,128]{2,1,0:T(8,128)(2,1)}, u32[]{:S(2)}, u32[]{:S(2)}) collective-permute-start(bf16[4,512,128]{2,1,0:T(8,128)(2,1)S(1)} %pad_maximum_fusion.4.refs_0_), channel_id=1, source_target_pairs={{0,4},{4,0},{8,12},{12,8},{16,20},{20,16},{24,28},{28,24},{1,5},{5... | collective-permute-start | bytes 1572872 | tf_op jit(solution)/shard_map/ppermute | solution.py:816
  122.3 14.3 %collective-permute-start.22 = (bf16[4,512,128]{2,1,0:T(8,128)(2,1)}, bf16[4,512,128]{2,1,0:T(8,128)(2,1)}, u32[]{:S(2)}, u32[]{:S(2)}) collective-permute-start(bf16[4,512,128]{2,1,0:T(8,128)(2,1)} %pad_maximum_fusion.5.refs_2_), channel_id=1, source_target_pairs={{0,2},{2,0},{1,3},{3,1},{4,6},{6,4},{5,7},{7,5},{8,10},{10,8},{9,1... | collective-permute-start | bytes 1572872 | tf_op jit(solution)/shard_map/ppermute | solution.py:824
  140.0 25.1 %collective-permute-start.23 = (bf16[8,512,128]{2,1,0:T(8,128)(2,1)}, bf16[8,512,128]{2,1,0:T(8,128)(2,1)}, u32[]{:S(2)}, u32[]{:S(2)}) collective-permute-start(bf16[8,512,128]{2,1,0:T(8,128)(2,1)} %get-tuple-element.250.refs_3_), channel_id=1, source_target_pairs={{0,2},{2,0},{1,3},{3,1},{4,6},{6,4},{5,7},{7,5},{8,10},{10,8},{9,1... | collective-permute-start | bytes 3145736 | tf_op jit(solution)/shard_map/ppermute | solution.py:824
  141.4 25.6 %collective-permute-start.24 = (bf16[8,512,128]{2,1,0:T(8,128)(2,1)}, bf16[8,512,128]{2,1,0:T(8,128)(2,1)}, u32[]{:S(2)}, u32[]{:S(2)}) collective-permute-start(bf16[8,512,128]{2,1,0:T(8,128)(2,1)} %get-tuple-element.251.refs_5_), channel_id=1, source_target_pairs={{0,4},{4,0},{8,12},{12,8},{16,20},{20,16},{24,28},{28,24},{1,5},{5... | collective-permute-start | bytes 3145736 | tf_op jit(solution)/shard_map/ppermute | solution.py:816
  162.9 26.0 %collective-permute-start.27 = (bf16[8,512,128]{2,1,0:T(8,128)(2,1)}, bf16[8,512,128]{2,1,0:T(8,128)(2,1)}, u32[]{:S(2)}, u32[]{:S(2)}) collective-permute-start(bf16[8,512,128]{2,1,0:T(8,128)(2,1)} %get-tuple-element.235), channel_id=1, source_target_pairs={{0,4},{4,0},{8,12},{12,8},{16,20},{20,16},{24,28},{28,24},{1,5},{5... | collective-permute-start | bytes 3145736 | tf_op jit(solution)/shard_map/ppermute | solution.py:816
  164.4 24.5 %collective-permute-start.26 = (bf16[8,512,128]{2,1,0:T(8,128)(2,1)}, bf16[8,512,128]{2,1,0:T(8,128)(2,1)}, u32[]{:S(2)}, u32[]{:S(2)}) collective-permute-start(bf16[8,512,128]{2,1,0:T(8,128)(2,1)} %get-tuple-element.260), channel_id=1, source_target_pairs={{0,2},{2,0},{1,3},{3,1},{4,6},{6,4},{5,7},{7,5},{8,10},{10,8},{9,1... | collective-permute-start | bytes 3145736 | tf_op jit(solution)/shard_map/ppermute | solution.py:824
  188.8 16.7 %collective-permute-start.25 = (bf16[2,584,1024]{2,1,0:T(8,128)(2,1)}, bf16[2,584,1024]{2,1,0:T(8,128)(2,1)S(1)}, u32[]{:S(2)}, u32[]{:S(2)}) collective-permute-start(bf16[2,584,1024]{2,1,0:T(8,128)(2,1)} %get-tuple-element.257.refs_5_), channel_id=1, source_target_pairs={{0,1},{1,0},{2,3},{3,2},{4,5},{5,4},{6,7},{7,6},{8,9},{9,8},{10,11... | collective-permute-start | bytes 7176200 | tf_op jit(solution)/shard_map/ppermute | solution.py:828
  193.9 21.4 %collective-permute-start.28 = (bf16[4,512,128]{2,1,0:T(8,128)(2,1)S(1)}, bf16[4,512,128]{2,1,0:T(8,128)(2,1)S(1)}, u32[]{:S(2)}, u32[]{:S(2)}) collective-permute-start(bf16[4,512,128]{2,1,0:T(8,128)(2,1)S(1)} %get-tuple-element.268), channel_id=1, source_target_pairs={{0,4},{4,0},{8,12},{12,8},{16,20},{20,16},{24,28},{28,24},{1,5},{5... | collective-permute-start | bytes 1572872 | tf_op jit(solution)/shard_map/ppermute | solution.py:816
  194.0 21.3 %collective-permute-start.29 = (bf16[4,512,128]{2,1,0:T(8,128)(2,1)S(1)}, bf16[4,512,128]{2,1,0:T(8,128)(2,1)S(1)}, u32[]{:S(2)}, u32[]{:S(2)}) collective-permute-start(bf16[4,512,128]{2,1,0:T(8,128)(2,1)S(1)} %get-tuple-element.270), channel_id=1, source_target_pairs={{0,2},{2,0},{1,3},{3,1},{4,6},{6,4},{5,7},{7,5},{8,10},{10,8},{9,1... | collective-permute-start | bytes 1572872 | tf_op jit(solution)/shard_map/ppermute | solution.py:824
  196.0 9.5 %copy-start.6 = (bf16[8,512,128]{2,1,0:T(8,128)(2,1)S(1)}, bf16[8,512,128]{2,1,0:T(8,128)(2,1)}, u32[]{:S(2)}) copy-start(bf16[8,512,128]{2,1,0:T(8,128)(2,1)} %copy-done.4) | copy-start | bytes 3145732
  196.0 9.5 %copy-start.13 = (bf16[2,584,1024]{2,1,0:T(8,128)(2,1)S(1)}, bf16[2,584,1024]{2,1,0:T(8,128)(2,1)}, u32[]{:S(2)}) copy-start(bf16[2,584,1024]{2,1,0:T(8,128)(2,1)} %get-tuple-element.257.refs_5_) | copy-start | bytes 7176196
  196.0 9.5 %copy-start.21 = (f32[6,1024]{1,0:T(8,128)S(1)}, f32[6,1024]{1,0:T(8,128)}, u32[]{:S(2)}) copy-start(f32[6,1024]{1,0:T(8,128)} %get-tuple-element.199.refs_0_.refs_1_.refs_2_) | copy-start | bytes 73732
  203.4 28.4 %collective-permute-start.30 = (bf16[8,512,128]{2,1,0:T(8,128)(2,1)S(1)}, bf16[8,512,128]{2,1,0:T(8,128)(2,1)S(1)}, u32[]{:S(2)}, u32[]{:S(2)}) collective-permute-start(bf16[8,512,128]{2,1,0:T(8,128)(2,1)S(1)} %get-tuple-element.292), channel_id=1, source_target_pairs={{0,2},{2,0},{1,3},{3,1},{4,6},{6,4},{5,7},{7,5},{8,10},{10,8},{9,1... | collective-permute-start | bytes 3145736 | tf_op jit(solution)/shard_map/ppermute | solution.py:824
  203.5 28.3 %collective-permute-start.31 = (bf16[8,512,128]{2,1,0:T(8,128)(2,1)S(1)}, bf16[8,512,128]{2,1,0:T(8,128)(2,1)S(1)}, u32[]{:S(2)}, u32[]{:S(2)}) collective-permute-start(bf16[8,512,128]{2,1,0:T(8,128)(2,1)S(1)} %get-tuple-element.273), channel_id=1, source_target_pairs={{0,4},{4,0},{8,12},{12,8},{16,20},{20,16},{24,28},{28,24},{1,5},{5... | collective-permute-start | bytes 3145736 | tf_op jit(solution)/shard_map/ppermute | solution.py:816
  216.2 34.6 %collective-permute-start.34 = (bf16[1024,128]{1,0:T(8,128)(2,1)S(1)}, bf16[1024,128]{1,0:T(8,128)(2,1)S(1)}, u32[]{:S(2)}, u32[]{:S(2)}) collective-permute-start(bf16[1024,128]{1,0:T(8,128)(2,1)S(1)} %get-tuple-element.283), channel_id=1, source_target_pairs={{0,8},{4,12},{8,0},{12,4},{16,24},{20,28},{24,16},{28,20},{1,9},{5... | collective-permute-start | bytes 786440 | tf_op jit(solution)/shard_map/ppermute | solution.py:813
  216.8 39.2 %collective-permute-start.35 = (bf16[1024,128]{1,0:T(8,128)(2,1)S(1)}, bf16[1024,128]{1,0:T(8,128)(2,1)S(1)}, u32[]{:S(2)}, u32[]{:S(2)}) collective-permute-start(bf16[1024,128]{1,0:T(8,128)(2,1)S(1)} %get-tuple-element.284), channel_id=1, source_target_pairs={{0,16},{4,20},{8,24},{12,28},{16,0},{20,4},{24,8},{28,12},{1,17},{... | collective-permute-start | bytes 786440 | tf_op jit(solution)/shard_map/ppermute | solution.py:813
  219.3 37.4 %collective-permute-start.36 = (bf16[1024,128]{1,0:T(8,128)(2,1)S(1)}, bf16[1024,128]{1,0:T(8,128)(2,1)S(1)}, u32[]{:S(2)}, u32[]{:S(2)}) collective-permute-start(bf16[1024,128]{1,0:T(8,128)(2,1)S(1)} %get-tuple-element.285), channel_id=1, source_target_pairs={{0,24},{4,28},{8,16},{12,20},{16,8},{20,12},{24,0},{28,4},{1,25},{... | collective-permute-start | bytes 786440 | tf_op jit(solution)/shard_map/ppermute | solution.py:813
  233.2 26.3 %collective-permute-start.32 = (bf16[4,512,128]{2,1,0:T(8,128)(2,1)S(1)}, bf16[4,512,128]{2,1,0:T(8,128)(2,1)S(1)}, u32[]{:S(2)}, u32[]{:S(2)}) collective-permute-start(bf16[4,512,128]{2,1,0:T(8,128)(2,1)S(1)} %get-tuple-element.300), channel_id=1, source_target_pairs={{0,4},{4,0},{8,12},{12,8},{16,20},{20,16},{24,28},{28,24},{1,5},{5... | collective-permute-start | bytes 1572872 | tf_op jit(solution)/shard_map/ppermute | solution.py:816
  233.9 25.6 %collective-permute-start.33 = (bf16[4,512,128]{2,1,0:T(8,128)(2,1)S(1)}, bf16[4,512,128]{2,1,0:T(8,128)(2,1)S(1)}, u32[]{:S(2)}, u32[]{:S(2)}) collective-permute-start(bf16[4,512,128]{2,1,0:T(8,128)(2,1)S(1)} %get-tuple-element.302), channel_id=1, source_target_pairs={{0,2},{2,0},{1,3},{3,1},{4,6},{6,4},{5,7},{7,5},{8,10},{10,8},{9,1... | collective-permute-start | bytes 1572872 | tf_op jit(solution)/shard_map/ppermute | solution.py:824
  235.4 15.5 %copy-start.9 = (bf16[1168,1024]{1,0:T(8,128)(2,1)S(1)}, bf16[1168,1024]{1,0:T(8,128)(2,1)}, u32[]{:S(2)}) copy-start(bf16[1168,1024]{1,0:T(8,128)(2,1)} %get-tuple-element.252) | copy-start | bytes 7176196
  235.4 15.6 %copy-start.8 = (bf16[2,584,1024]{2,1,0:T(8,128)(2,1)S(1)}, bf16[2,584,1024]{2,1,0:T(8,128)(2,1)}, u32[]{:S(2)}) copy-start(bf16[2,584,1024]{2,1,0:T(8,128)(2,1)} %copy-done.7) | copy-start | bytes 7176196
  250.8 17.6 %collective-permute-start.37 = (bf16[2,584,1024]{2,1,0:T(8,128)(2,1)S(1)}, bf16[2,584,1024]{2,1,0:T(8,128)(2,1)S(1)}, u32[]{:S(2)}, u32[]{:S(2)}) collective-permute-start(bf16[2,584,1024]{2,1,0:T(8,128)(2,1)S(1)} %bitcast.97), channel_id=1, source_target_pairs={{0,1},{1,0},{2,3},{3,2},{4,5},{5,4},{6,7},{7,6},{8,9},{9,8},{10,11... | collective-permute-start | bytes 7176200 | tf_op jit(solution)/shard_map/ppermute | solution.py:828
  256.0 27.4 %collective-permute-start.38 = (bf16[8,512,128]{2,1,0:T(8,128)(2,1)S(1)}, bf16[8,512,128]{2,1,0:T(8,128)(2,1)S(1)}, u32[]{:S(2)}, u32[]{:S(2)}) collective-permute-start(bf16[8,512,128]{2,1,0:T(8,128)(2,1)S(1)} %get-tuple-element.307), channel_id=1, source_target_pairs={{0,2},{2,0},{1,3},{3,1},{4,6},{6,4},{5,7},{7,5},{8,10},{10,8},{9,1... | collective-permute-start | bytes 3145736 | tf_op jit(solution)/shard_map/ppermute | solution.py:824
  256.7 26.7 %collective-permute-start.39 = (bf16[8,512,128]{2,1,0:T(8,128)(2,1)S(1)}, bf16[8,512,128]{2,1,0:T(8,128)(2,1)S(1)}, u32[]{:S(2)}, u32[]{:S(2)}) collective-permute-start(bf16[8,512,128]{2,1,0:T(8,128)(2,1)S(1)} %get-tuple-element.308), channel_id=1, source_target_pairs={{0,4},{4,0},{8,12},{12,8},{16,20},{20,16},{24,28},{28,24},{1,5},{5... | collective-permute-start | bytes 3145736 | tf_op jit(solution)/shard_map/ppermute | solution.py:816
  260.4 19.2 %collective-permute-start.40 = (bf16[2,1024,128]{2,1,0:T(8,128)(2,1)S(1)}, bf16[2,1024,128]{2,1,0:T(8,128)(2,1)S(1)}, u32[]{:S(2)}, u32[]{:S(2)}) collective-permute-start(bf16[2,1024,128]{2,1,0:T(8,128)(2,1)S(1)} %get-tuple-element.318), channel_id=1, source_target_pairs={{0,8},{4,12},{8,0},{12,4},{16,24},{20,28},{24,16},{28,20},{1,9},{5... | collective-permute-start | bytes 1572872 | tf_op jit(solution)/shard_map/ppermute | solution.py:813
  279.6 7.4 %collective-permute-start.44 = (bf16[2,584,1024]{2,1,0:T(8,128)(2,1)S(1)}, bf16[2,584,1024]{2,1,0:T(8,128)(2,1)S(1)}, u32[]{:S(2)}, u32[]{:S(2)}) collective-permute-start(bf16[2,584,1024]{2,1,0:T(8,128)(2,1)S(1)} %grad_one.1.refs_9_), channel_id=1, source_target_pairs={{0,1},{1,0},{2,3},{3,2},{4,5},{5,4},{6,7},{7,6},{8,9},{9,8},{10,11... | collective-permute-start | bytes 7176200 | tf_op jit(solution)/shard_map/ppermute | solution.py:828
  280.3 15.6 %collective-permute-start.43 = (bf16[1,1024,128]{2,1,0:T(8,128)(2,1)S(1)}, bf16[1,1024,128]{2,1,0:T(8,128)(2,1)S(1)}, u32[]{:S(2)}, u32[]{:S(2)}) collective-permute-start(bf16[1,1024,128]{2,1,0:T(8,128)(2,1)S(1)} %get-tuple-element.333), channel_id=1, source_target_pairs={{0,16},{4,20},{8,24},{12,28},{16,0},{20,4},{24,8},{28,12},{1,17},{... | collective-permute-start | bytes 786440 | tf_op jit(solution)/shard_map/ppermute | solution.py:813
  284.8 16.1 %collective-permute-start.41 = (bf16[4,512,128]{2,1,0:T(8,128)(2,1)S(1)}, bf16[4,512,128]{2,1,0:T(8,128)(2,1)S(1)}, u32[]{:S(2)}, u32[]{:S(2)}) collective-permute-start(bf16[4,512,128]{2,1,0:T(8,128)(2,1)S(1)} %get-tuple-element.339), channel_id=1, source_target_pairs={{0,4},{4,0},{8,12},{12,8},{16,20},{20,16},{24,28},{28,24},{1,5},{5... | collective-permute-start | bytes 1572872 | tf_op jit(solution)/shard_map/ppermute | solution.py:816
  285.5 15.4 %collective-permute-start.42 = (bf16[4,512,128]{2,1,0:T(8,128)(2,1)S(1)}, bf16[4,512,128]{2,1,0:T(8,128)(2,1)S(1)}, u32[]{:S(2)}, u32[]{:S(2)}) collective-permute-start(bf16[4,512,128]{2,1,0:T(8,128)(2,1)S(1)} %get-tuple-element.341), channel_id=1, source_target_pairs={{0,2},{2,0},{1,3},{3,1},{4,6},{6,4},{5,7},{7,5},{8,10},{10,8},{9,1... | collective-permute-start | bytes 1572872 | tf_op jit(solution)/shard_map/ppermute | solution.py:824
  297.3 4.0 %collective-permute-start.45 = (f32[4,16,128]{2,1,0:T(8,128)S(1)}, f32[4,16,128]{2,1,0:T(8,128)S(1)}, u32[]{:S(2)}, u32[]{:S(2)}) collective-permute-start(f32[4,16,128]{2,1,0:T(8,128)S(1)} %get-tuple-element.355), channel_id=1, source_target_pairs={{0,4},{2,6},{4,0},{6,2},{8,12},{10,14},{12,8},{14,10},{16,20},{18,... | collective-permute-start | bytes 98312 | tf_op jit(solution)/shard_map/ppermute | solution.py:821
  298.2 4.2 %collective-permute-start.46 = (f32[4,16,128]{2,1,0:T(8,128)S(1)}, f32[4,16,128]{2,1,0:T(8,128)S(1)}, u32[]{:S(2)}, u32[]{:S(2)}) collective-permute-start(f32[4,16,128]{2,1,0:T(8,128)S(1)} %get-tuple-element.356), channel_id=1, source_target_pairs={{0,2},{2,0},{4,6},{6,4},{8,10},{10,8},{12,14},{14,12},{16,18},{18,... | collective-permute-start | bytes 98312 | tf_op jit(solution)/shard_map/ppermute | solution.py:821
  299.4 4.8 %collective-permute-start.47 = (f32[4,16,128]{2,1,0:T(8,128)S(1)}, f32[4,16,128]{2,1,0:T(8,128)S(1)}, u32[]{:S(2)}, u32[]{:S(2)}) collective-permute-start(f32[4,16,128]{2,1,0:T(8,128)S(1)} %get-tuple-element.357), channel_id=1, source_target_pairs={{0,6},{2,4},{4,2},{6,0},{8,14},{10,12},{12,10},{14,8},{16,22},{18,... | collective-permute-start | bytes 98312 | tf_op jit(solution)/shard_map/ppermute | solution.py:821
  306.1 12.0 %collective-permute-start.48 = (bf16[1040,128]{1,0:T(8,128)(2,1)S(1)}, bf16[1040,128]{1,0:T(8,128)(2,1)}, u32[]{:S(2)}, u32[]{:S(2)}) collective-permute-start(bf16[1040,128]{1,0:T(8,128)(2,1)S(1)} %get-tuple-element.359), channel_id=1, source_target_pairs={{0,8},{4,12},{8,0},{12,4},{16,24},{20,28},{24,16},{28,20},{1,9},{5... | collective-permute-start | bytes 798728 | tf_op jit(solution)/shard_map/ppermute | solution.py:813
  306.1 21.5 %collective-permute-start.49 = (bf16[1040,128]{1,0:T(8,128)(2,1)S(1)}, bf16[1040,128]{1,0:T(8,128)(2,1)}, u32[]{:S(2)}, u32[]{:S(2)}) collective-permute-start(bf16[1040,128]{1,0:T(8,128)(2,1)S(1)} %get-tuple-element.360), channel_id=1, source_target_pairs={{0,16},{4,20},{8,24},{12,28},{16,0},{20,4},{24,8},{28,12},{1,17},{... | collective-permute-start | bytes 798728 | tf_op jit(solution)/shard_map/ppermute | solution.py:813
  308.7 18.8 %collective-permute-start.50 = (bf16[1040,128]{1,0:T(8,128)(2,1)S(1)}, bf16[1040,128]{1,0:T(8,128)(2,1)}, u32[]{:S(2)}, u32[]{:S(2)}) collective-permute-start(bf16[1040,128]{1,0:T(8,128)(2,1)S(1)} %get-tuple-element.361), channel_id=1, source_target_pairs={{0,24},{4,28},{8,16},{12,20},{16,8},{20,12},{24,0},{28,4},{1,25},{... | collective-permute-start | bytes 798728 | tf_op jit(solution)/shard_map/ppermute | solution.py:813
  (32 other events, 104.4 us)

commit v9 on v8

--- a/solution.py
+++ b/solution.py
@@ -123,15 +123,15 @@
     return jax.ShapeDtypeStruct(shape, dtype)
 
 
-def arrange_pair(ids, own, other, nd):
+def arrange_pair(ids, keep, own, other, nd):
     n = len(own)
     rows, width = own[0].shape
     bd = width // nd
 
     def body(small, ins, outs, scratch, loads):
-        (ids_ref,) = small
+        ids_ref, keep_ref = small
         mine = ids_ref[0]
-        in_s, out_s = scratch[: 2 * n], scratch[2 * n :]
+        in_s, out_s, kept_s = scratch[: 2 * n], scratch[2 * n : 4 * n], scratch[4 * n :]
         groups = [loads.start([(ins[i], in_s[i])]) for i in range(2 * n)]
         done = []
         for i in range(2 * n):
@@ -141,17 +141,21 @@
                 out_s[i][:, p * bd : (p + 1) * bd] = in_s[i][:, src]
             spot = mine if i < n else 1 - mine
             done.append(loads.start([(out_s[i], outs[i % n].at[spot])]))
+            if i % n == n - 1:
+                kept = kept_s[i // n]
+                kept[...] = (out_s[i][...].astype(F32) * keep_ref[spot]).astype(BF)
+                done.append(loads.start([(kept, outs[n].at[spot])]))
         for group in done:
             loads.wait(group)
 
     return call(
         body,
         list(own) + list(other),
-        [sds((2, rows, width), BF)] * n,
-        [pltpu.VMEM((rows, width), BF)] * (4 * n),
+        [sds((2, rows, width), BF)] * (n + 1),
+        [pltpu.VMEM((rows, width), BF)] * (4 * n + 2),
         "arrange_pair",
         0,
-        smem=(ids,),
+        smem=(ids, keep),
     )
 
 
@@ -1055,7 +1059,7 @@
     own = [tokens, cotangent]
     other = [swap_core(value) for value in own]
     if aligned:
-        tok, cot = arrange_pair(ids, own, other, dp)
+        tok, cot, grad_top = arrange_pair(ids, keep, own, other, dp)
     else:
 
         def arrange(own, other):
@@ -1064,6 +1068,7 @@
             return from_abs(pair, 2).reshape(2, seq, width)
 
         tok, cot = [arrange(own[i], other[i]) for i in range(2)]
+        grad_top = cot * keep.astype(BF)[:, None, None]
     c1_z = gather_z(grid, first_a, first_b, gate=tok)
     c1_h = gather_first(grid, *c1_z)
     c1_h = join(c1_h)
@@ -1079,7 +1084,6 @@
         tail = xor_blocks(to_rel(tail, 1), me_d, 1)
         bq = tail[:, :, :2, : hw // dp].transpose(2, 0, 1, 3).reshape(2, ext).astype(F32)
         bu = tail[:, :, 2, : fw // dp].reshape(1, hid).astype(F32)
-    grad_top = cot * keep.astype(BF)[:, None, None]
 
     up_z = gather_z(grid, *up_halves, gate=nv)
     up_h = gather_first(grid, *up_z)

time: 335 us -> 340 us (1.015)
  local copies, waits for them, and re-layouts: 18.6 us -> 27.3 us
  starting transfers between devices: 63.4 us -> 58.1 us
    ppermute x12, waiting for transfers between devices: 22.1 us -> 28.9 us  [send_y(): return lax.ppermute(value, 'dp', [(i, i ^ k) for i in range(self.dp)])]
    unnamed x102 -> x110, local copies, waits for them, and re-layouts: 13.5 us -> 20.2 us
    ppermute x17, starting transfers between devices: 32.6 us -> 26.6 us  [send_z(): lax.ppermute(value, 'dp', [(i, i ^ k * self.y) for i in range(self.dp)])]
    ppermute x12, waiting for transfers between devices: 4.97 us -> 0.75 us  [send_x(): return lax.ppermute(value, 'tx', [(i, i ^ k) for i in range(self.tx)])]
  transfers between devices with their start and end apart: 51 -> 51, of which waited for: 17 -> 11; matrix products, arithmetic and copies ran while one was open for 2% -> 2% of each run, Pallas kernels for 55% -> 54%
where the time goes in v9:
time: 340 us; the launch traced here: 334 us
  Pallas kernels  186 us (55%)
  waiting for transfers between devices  58.6 us (17%)
  starting transfers between devices  58.1 us (17%)
  local copies, waits for them, and re-layouts  27.3 us (8%)
    pallas_call x30, Pallas kernels, call(): pl.pallas_call(kernel, out_shape=outs, in_specs=[pl.BlockSpec(memory_spac...  186 us
    ppermute x12, waiting for transfers between devices, send_y(): return lax.ppermute(value, 'dp', [(i, i ^ k) for i in range(self.dp)])  28.9 us
    ppermute x17, starting transfers between devices, send_z(): lax.ppermute(value, 'dp', [(i, i ^ k * self.y) for i in range(self.dp)])  26.6 us
    ppermute x17, waiting for transfers between devices, send_z(): lax.ppermute(value, 'dp', [(i, i ^ k * self.y) for i in range(self.dp)])  26.1 us
    unnamed x110, local copies, waits for them, and re-layouts  20.2 us
    ppermute x12, starting transfers between devices, send_y(): return lax.ppermute(value, 'dp', [(i, i ^ k) for i in range(self.dp)])  13.9 us
    ppermute x12, starting transfers between devices, send_x(): return lax.ppermute(value, 'tx', [(i, i ^ k) for i in range(self.tx)])  12.7 us
  transfers between devices with their start and end apart: 51, of which 11 were waited for; matrix products, arithmetic and copies ran while one was open for 2% of the time, Pallas kernels for 54%

profile of v9, /device:TPU:0, one launch (start us, length us, event | category | flops | bytes accessed | tf_op | source)
XLA Modules:
  0.0 334.2 jit_solution(18355975758618118633)
XLA Ops:
  3.6 1.5 concatenate.23
  5.1 5.1 %collective-permute-start.2 = (bf16[1040,128]{1,0:T(8,128)(2,1)S(1)}, bf16[1040,128]{1,0:T(8,128)(2,1)S(1)}, u32[]{:S(2)}, u32[]{:S(2)}) collective-permute-start(bf16[1040,128]{1,0:T(8,128)(2,1)S(1)} %concatenate.23), channel_id=1, source_target_pairs={{0,24},{4,28},{8,16},{12,20},{16,8},{20,12},{24,0},{28,4},{1,25},{... | collective-permute-start | bytes 798728 | tf_op jit(solution)/shard_map/ppermute | solution.py:817
  11.5 1.2 dynamic-slice_convert_fusion.refs_1_.refs_0_
  13.8 5.6 %arrange_pair.1 = (bf16[2,584,1024]{2,1,0:T(8,128)(2,1)}, bf16[2,584,1024]{2,1,0:T(8,128)(2,1)}, bf16[2,584,1024]{2,1,0:T(8,128)(2,1)}) custom-call(s32[10]{0:T(128)} %stack.130.refs_0_, f32[2]{0:T(128)} %dynamic-slice_convert_fusion.refs_1_.refs_0_, bf16[584,1024]{1,0:T(8,128)(2,1)} %refs_2_.1, bf16[584,1024]{1,0:T(8,128)(2,1)} %refs_3_.1, ...), custom_call_target="tpu_custom_call" | custom-call | flops 5750000128 | bytes 5750000 | tf_op jit(solution)/shard_map/arrange_pair/pallas_call | solution.py:94
  19.4 13.7 %collective-permute-done.1 = bf16[1040,128]{1,0:T(8,128)(2,1)S(1)} collective-permute-done((bf16[1040,128]{1,0:T(8,128)(2,1)S(1)}, bf16[1040,128]{1,0:T(8,128)(2,1)S(1)}, u32[]{:S(2)}, u32[]{:S(2)}) %collective-permute-start.1) | collective-permute-done | bytes 266272 | tf_op jit(solution)/shard_map/ppermute | solution.py:817
  33.4 1.6 collective-permute-start.7
  35.0 1.6 collective-permute-start.5
  36.8 11.4 %collective-permute-done.5 = bf16[4,528,128]{2,1,0:T(8,128)(2,1)S(1)} collective-permute-done((bf16[4,528,128]{2,1,0:T(8,128)(2,1)S(1)}, bf16[4,528,128]{2,1,0:T(8,128)(2,1)S(1)}, u32[]{:S(2)}, u32[]{:S(2)}) %collective-permute-start.5) | collective-permute-done | bytes 540704 | tf_op jit(solution)/shard_map/ppermute | solution.py:820
  49.0 1.6 collective-permute-start.8
  50.7 2.5 collective-permute-start.11
  53.2 1.9 collective-permute-start.9
  55.1 16.7 %collective-permute-done.8.refs_6_.refs_10_.refs_11_.refs_15_ = bf16[8,512,128]{2,1,0:T(8,128)(2,1)S(1)} collective-permute-done((bf16[8,512,128]{2,1,0:T(8,128)(2,1)S(1)}, bf16[8,512,128]{2,1,0:T(8,128)(2,1)S(1)}, u32[]{:S(2)}, u32[]{:S(2)}) %collective-permute-start.8) | collective-permute-done | bytes 1048608 | tf_op jit(solution)/shard_map/ppermute | solution.py:820
  73.9 2.6 vectors.1
  78.8 1.6 collective-permute-start.12
  80.4 1.6 collective-permute-start.13
  82.0 1.7 copy-done.32
  83.7 15.0 %attn_forward.2 = (bf16[2,584,1024]{2,1,0:T(8,128)(2,1)S(1)}, bf16[2,584,512]{2,1,0:T(8,128)(2,1)S(1)}, bf16[2,584,512]{2,1,0:T(8,128)(2,1)S(1)}, bf16[2,584,512...) custom-call(f32[6,1024]{1,0:T(8,128)S(1)} %copy-done.22, ...), custom_call_target="tpu_custom_call" | custom-call | flops 18400000000 | bytes 18400000 | tf_op jit(solution)/shard_map/attn_forward/pallas_call | solution.py:94
  99.0 2.5 collective-permute-start.20
  101.5 1.9 collective-permute-start.18
  104.6 16.0 %attn_forward.3 = (bf16[2,584,1024]{2,1,0:T(8,128)(2,1)S(1)}, bf16[2,584,512]{2,1,0:T(8,128)(2,1)S(1)}, bf16[2,584,512]{2,1,0:T(8,128)(2,1)S(1)}, bf16[2,584,512...) custom-call(f32[6,1024]{1,0:T(8,128)S(1)} %copy-done.22, ...), custom_call_target="tpu_custom_call", output_to_operand_aliasing={{0}: (3, {}), {1}: (4, {}), {2}: (5, {}), {3}: (6, {}), {4}... | custom-call | flops 18400000000 | bytes 18400000 | tf_op jit(solution)/shard_map/attn_forward/pallas_call | solution.py:94
  126.2 1.4 collective-permute-start.21
  128.4 1.5 collective-permute-start.22
  130.9 10.2 %mlp_up.2 = (f32[2,584,1024]{2,1,0:T(8,128)}, bf16[2,584,1024]{2,1,0:T(8,128)(2,1)}, bf16[2,584,2048]{2,1,0:T(8,128)(2,1)}, bf16[2,584,2048]{2,1,0:T(8,128)(2,1)}) custom-call(f32[2]{0:T(128)} %dynamic-slice_convert_fusion.refs_1_.refs_0_, f32[6,1024]{1,0:T(8,128)} %get-tuple-element.200.refs_0_.refs_1_.refs_2_, f32[1,2048]{1,0:T(1,128)} %get-tuple-element.201.refs_2_, ...), custom_call_target="tpu_custom_call" | custom-call | flops 11500000256 | bytes 11500000 | tf_op jit(solution)/shard_map/mlp_up/pallas_call | solution.py:94
  141.8 2.9 join.1
  144.8 1.6 collective-permute-start.23
  146.8 10.1 %mlp_up.3 = (f32[2,584,1024]{2,1,0:T(8,128)}, bf16[2,584,1024]{2,1,0:T(8,128)(2,1)}, bf16[2,584,2048]{2,1,0:T(8,128)(2,1)}, bf16[2,584,2048]{2,1,0:T(8,128)(2,1)}) custom-call(f32[2]{0:T(128)} %dynamic-slice_convert_fusion.refs_1_.refs_0_, ...), custom_call_target="tpu_custom_call", output_to_operand_aliasing={{0}: (6, {}), {1}: (7, {}), {2}: (8, {}), {3}: (9, {})} | custom-call | flops 11500000256 | bytes 11500000 | tf_op jit(solution)/shard_map/mlp_up/pallas_call | solution.py:94
  157.0 10.7 %down_grad.1 = (bf16[8,512,128]{2,1,0:T(8,128)(2,1)}, bf16[8,512,128]{2,1,0:T(8,128)(2,1)}, bf16[8,512,128]{2,1,0:T(8,128)(2,1)}, bf16[8,512,128]{2,1,0:T(8,128)(2,1)}) custom-call(bf16[1168,2048]{1,0:T(8,128)(2,1)} %bitcast.121, bf16[1168,1024]{1,0:T(8,128)(2,1)} %bitcast.124), custom_call_target="tpu_custom_call" | custom-call | flops 12650000384 | bytes 12650000 | tf_op jit(solution)/shard_map/down_grad/pallas_call | solution.py:94
  167.7 1.6 collective-permute-start.27
  170.5 21.7 %mlp_back.1 = (bf16[1168,2048]{1,0:T(8,128)(2,1)}, f32[1,2048]{1,0:T(1,128)}, bf16[2,584,1024]{2,1,0:T(8,128)(2,1)}, bf16[1168,1024]{1,0:T(8,128)(2,1)}) custom-call(bf16[1168,1024]{1,0:T(8,128)(2,1)} %bitcast.125, bf16[1168,2048]{1,0:T(8,128)(2,1)} %bitcast.122, bf16[1168,2048]{1,0:T(8,128)(2,1)} %bitcast.123, ...), custom_call_target="tpu_custom_call" | custom-call | flops 25300000768 | bytes 25300000 | tf_op jit(solution)/shard_map/mlp_back/pallas_call | solution.py:94
  192.4 1.2 copy-done.30
  193.6 1.2 copy-done.31
  194.8 2.5 down_add.1
  198.9 7.4 %up_grad.1 = (bf16[8,512,128]{2,1,0:T(8,128)(2,1)S(1)}, bf16[8,512,128]{2,1,0:T(8,128)(2,1)S(1)}, bf16[8,512,128]{2,1,0:T(8,128)(2,1)S(1)}, bf16[8,512,128]{2,1,0:T(8,128)(2,1)S(1)}) custom-call(bf16[1168,1024]{1,0:T(8,128)(2,1)S(1)} %bitcast.104, bf16[1168,2048]{1,0:T(8,128)(2,1)S(1)} %copy-done.34), custom_call_target="tpu_custom_call" | custom-call | flops 12650000384 | bytes 12650000 | tf_op jit(solution)/shard_map/up_grad/pallas_call | solution.py:94
  206.3 1.6 collective-permute-start.30
  209.0 9.9 %middle_back.1 = (f32[584,1024]{1,0:T(8,128)S(1)}, bf16[2,584,1024]{2,1,0:T(8,128)(2,1)S(1)}, bf16[2,584,512]{2,1,0:T(8,128)(2,1)S(1)}, f32[4,1024]{1,0:T(4,128)S(1)}) custom-call(s32[10]{0:T(128)S(1)} %copy-done.24, f32[2]{0:T(128)S(1)} %copy-done.25, f32[6,1024]{1,0:T(8,128)S(1)} %copy-done.23, f32[2,584,1024]{2,1,0:T(8,128)} %get-tuple-element.233.refs_3_, ...), custom_call_target="tpu_custom_call" | custom-call | flops 23000000 | bytes 23000 | tf_op jit(solution)/shard_map/middle_back/pallas_call | solution.py:94
  220.0 2.9 collective-permute-start.35
  222.9 1.4 collective-permute-start.36
  224.3 3.1 out_grad.1
  227.5 8.0 %attn_first.1 = (bf16[3,2,584,128]{3,2,1,0:T(8,128)(2,1)S(1)}, f32[2,2,128]{2,1,0:T(2,128)S(1)}) custom-call(bf16[2,584,512]{2,1,0:T(8,128)(2,1)S(1)} %copy-done.17, bf16[2,584,512]{2,1,0:T(8,128)(2,1)S(1)} %copy-done.19, bf16[2,584,512]{2,1,0:T(8,128)(2,1)S(1)} %copy-done.21, bf16[2,584,512]{2,1,0:T(8,128)(2,1)S(1)} %get-tuple-element.321.refs_3_), custom_call_target="tpu_custom_call" | custom-call | flops 23000000 | bytes 23000 | tf_op jit(solution)/shard_map/attn_first/pallas_call | solution.py:94
  235.5 1.4 up_add.1
  238.4 15.5 %attn_backward.2 = (bf16[3,4,584,128]{3,2,1,0:T(8,128)(2,1)S(1)}, f32[4,2,128]{2,1,0:T(2,128)S(1)}) custom-call(bf16[2,584,512]{2,1,0:T(8,128)(2,1)S(1)} %copy-done.17, bf16[2,584,512]{2,1,0:T(8,128)(2,1)S(1)} %copy-done.19, bf16[2,584,512]{2,1,0:T(8,128)(2,1)S(1)} %copy-done.21, bf16[2,584,512]{2,1,0:T(8,128)(2,1)S(1)} %get-tuple-element.321.refs_3_), custom_call_target="tpu_custom_call" | custom-call | flops 20700000256 | bytes 20700000 | tf_op jit(solution)/shard_map/attn_backward/pallas_call | solution.py:94
  253.9 5.1 %qkv_grad.1 = (bf16[8,512,128]{2,1,0:T(8,128)(2,1)S(1)}, bf16[8,512,128]{2,1,0:T(8,128)(2,1)S(1)}, bf16[8,512,128]{2,1,0:T(8,128)(2,1)S(1)}) custom-call(bf16[1168,1024]{1,0:T(8,128)(2,1)S(1)} %bitcast.95, bf16[3,1168,128]{2,1,0:T(8,128)(2,1)S(1)} %bitcast.101, ...), custom_call_target="tpu_custom_call", output_to_operand_aliasing={{0}: (3, {}), {1}: (4, {}), {2}: (5, {})} | custom-call | flops 8049999872 | bytes 8050000 | tf_op jit(solution)/shard_map/qkv_grad/pallas_call | solution.py:94
  259.0 1.5 collective-permute-start.38
  260.6 1.1 collective-permute-start.39
  261.7 1.4 down_sum.1
  264.1 8.0 %attn_backward.3 = (bf16[3,2,584,128]{3,2,1,0:T(8,128)(2,1)S(1)}, f32[2,2,128]{2,1,0:T(2,128)S(1)}) custom-call(bf16[2,584,512]{2,1,0:T(8,128)(2,1)S(1)} %copy-done.17, bf16[2,584,512]{2,1,0:T(8,128)(2,1)S(1)} %copy-done.19, bf16[2,584,512]{2,1,0:T(8,128)(2,1)S(1)} %copy-done.21, bf16[2,584,512]{2,1,0:T(8,128)(2,1)S(1)} %get-tuple-element.321.refs_3_), custom_call_target="tpu_custom_call" | custom-call | flops 20700000256 | bytes 20700000 | tf_op jit(solution)/shard_map/attn_backward/pallas_call | solution.py:94
  272.1 1.4 copy-done.13
  273.5 2.6 qkv_keep.1.refs_0_
  276.1 6.5 %grad_one.1.refs_9_ = bf16[2,584,1024]{2,1,0:T(8,128)(2,1)S(1)} custom-call(bf16[3,1168,128]{2,1,0:T(8,128)(2,1)S(1)} %bitcast.102, bf16[6,1168,128]{2,1,0:T(8,128)(2,1)S(1)} %bitcast.100, bf16[3,1168,128]{2,1,0:T(8,128)(2,1)S(1)} %bitcast.94, bf16[8,528,128]{2,1,0:T(8,128)(2,1)S(1)} %copy-done.2, bf16[8,528,128]{2,1,0:T(8,128)(2,1)S(1)} %copy-done.4, ...), custom_call_target="tpu_custom_call" | custom-call | flops 23000000 | bytes 23000 | tf_op jit(solution)/shard_map/grad_one/pallas_call | solution.py:94
  283.4 3.1 collective-permute-start.43
  286.5 1.4 qkv_add.1
  289.4 7.2 %finish_tokens.1 = (bf16[584,1024]{1,0:T(8,128)(2,1)}, f32[2,1024]{1,0:T(2,128)}, f32[4,16,128]{2,1,0:T(8,128)S(1)}, f32[4,16,128]{2,1,0:T(8,128)S(1)}, f32[4,16...) custom-call(s32[10]{0:T(128)S(1)} %copy-done.24, f32[6,1024]{1,0:T(8,128)S(1)} %copy-done.23, ...), custom_call_target="tpu_custom_call" | custom-call | flops 10350000128 | bytes 10350000 | tf_op jit(solution)/shard_map/finish_tokens/pallas_call | solution.py:94
  296.6 2.5 collective-permute-done.43.refs_1_
  299.0 1.3 up_sum.1
  301.9 2.0 collective-permute-start.47
  305.4 1.4 collective-permute-done.47.refs_7_
  306.7 1.6 qkv_addz.1
  309.1 2.7 collective-permute-start.49
  311.7 1.7 collective-permute-start.50
  313.5 2.4 copy-done
  315.8 1.7 copy-done.14
  317.5 3.2 finish_layer.1
  320.8 9.8 %collective-permute-done.49.refs_3_ = bf16[1040,128]{1,0:T(8,128)(2,1)S(1)} collective-permute-done((bf16[1040,128]{1,0:T(8,128)(2,1)}, bf16[1040,128]{1,0:T(8,128)(2,1)S(1)}, u32[]{:S(2)}, u32[]{:S(2)}) %collective-permute-start.49) | collective-permute-done | bytes 266272 | tf_op jit(solution)/shard_map/ppermute | solution.py:817
  331.4 2.5 qkv_sum.1
  (211 shorter events, 35.3 us)
Async XLA Ops:
  0.6 12.1 %collective-permute-start.3 = (bf16[584,1024]{1,0:T(8,128)(2,1)}, bf16[584,1024]{1,0:T(8,128)(2,1)S(1)}, u32[]{:S(2)}, u32[]{:S(2)}) collective-permute-start(bf16[584,1024]{1,0:T(8,128)(2,1)} %refs_2_.1), channel_id=1, source_target_pairs={{0,1},{1,0},{2,3},{3,2},{4,5},{5,4},{6,7},{7,6},{8,9},{9,8},{10,11... | collective-permute-start | bytes 3588104 | tf_op jit(solution)/shard_map/ppermute | solution.py:832
  1.2 11.6 %collective-permute-start.4 = (bf16[584,1024]{1,0:T(8,128)(2,1)}, bf16[584,1024]{1,0:T(8,128)(2,1)}, u32[]{:S(2)}, u32[]{:S(2)}) collective-permute-start(bf16[584,1024]{1,0:T(8,128)(2,1)} %refs_3_.1), channel_id=1, source_target_pairs={{0,1},{1,0},{2,3},{3,2},{4,5},{5,4},{6,7},{7,6},{8,9},{9,8},{10,11... | collective-permute-start | bytes 3588104 | tf_op jit(solution)/shard_map/ppermute | solution.py:832
  5.1 14.3 %collective-permute-start.2 = (bf16[1040,128]{1,0:T(8,128)(2,1)S(1)}, bf16[1040,128]{1,0:T(8,128)(2,1)S(1)}, u32[]{:S(2)}, u32[]{:S(2)}) collective-permute-start(bf16[1040,128]{1,0:T(8,128)(2,1)S(1)} %concatenate.23), channel_id=1, source_target_pairs={{0,24},{4,28},{8,16},{12,20},{16,8},{20,12},{24,0},{28,4},{1,25},{... | collective-permute-start | bytes 798728 | tf_op jit(solution)/shard_map/ppermute | solution.py:817
  10.2 22.9 %collective-permute-start.1 = (bf16[1040,128]{1,0:T(8,128)(2,1)S(1)}, bf16[1040,128]{1,0:T(8,128)(2,1)S(1)}, u32[]{:S(2)}, u32[]{:S(2)}) collective-permute-start(bf16[1040,128]{1,0:T(8,128)(2,1)S(1)} %concatenate.23), channel_id=1, source_target_pairs={{0,16},{4,20},{8,24},{12,28},{16,0},{20,4},{24,8},{28,12},{1,17},{... | collective-permute-start | bytes 798728 | tf_op jit(solution)/shard_map/ppermute | solution.py:817
  10.2 22.9 %collective-permute-start = (bf16[1040,128]{1,0:T(8,128)(2,1)S(1)}, bf16[1040,128]{1,0:T(8,128)(2,1)S(1)}, u32[]{:S(2)}, u32[]{:S(2)}) collective-permute-start(bf16[1040,128]{1,0:T(8,128)(2,1)S(1)} %concatenate.23), channel_id=1, source_target_pairs={{0,8},{4,12},{8,0},{12,4},{16,24},{20,28},{24,16},{28,20},{1,9},{5... | collective-permute-start | bytes 798728 | tf_op jit(solution)/shard_map/ppermute | solution.py:817
  33.4 15.5 %collective-permute-start.7 = (bf16[4,512,128]{2,1,0:T(8,128)(2,1)S(1)}, bf16[4,512,128]{2,1,0:T(8,128)(2,1)S(1)}, u32[]{:S(2)}, u32[]{:S(2)}) collective-permute-start(bf16[4,512,128]{2,1,0:T(8,128)(2,1)S(1)} %pad_maximum_fusion.1), channel_id=1, source_target_pairs={{0,2},{2,0},{1,3},{3,1},{4,6},{6,4},{5,7},{7,5},{8,10},{10,8},{9,1... | collective-permute-start | bytes 1572872 | tf_op jit(solution)/shard_map/ppermute | solution.py:828
  35.0 13.2 %collective-permute-start.5 = (bf16[4,528,128]{2,1,0:T(8,128)(2,1)S(1)}, bf16[4,528,128]{2,1,0:T(8,128)(2,1)S(1)}, u32[]{:S(2)}, u32[]{:S(2)}) collective-permute-start(bf16[4,528,128]{2,1,0:T(8,128)(2,1)S(1)} %pad_maximum_fusion), channel_id=1, source_target_pairs={{0,4},{4,0},{8,12},{12,8},{16,20},{20,16},{24,28},{28,24},{1,5},{5... | collective-permute-start | bytes 1622024 | tf_op jit(solution)/shard_map/ppermute | solution.py:820
  36.7 13.8 %copy-start.40 = (bf16[128,1024]{1,0:T(8,128)(2,1)S(1)}, bf16[128,1024]{1,0:T(8,128)(2,1)}, u32[]{:S(2)}) copy-start(bf16[128,1024]{1,0:T(8,128)(2,1)} %param.19) | copy-start | bytes 786436
  36.8 13.8 %copy-start.41 = (bf16[1024,128]{1,0:T(8,128)(2,1)S(1)}, bf16[1024,128]{1,0:T(8,128)(2,1)}, u32[]{:S(2)}) copy-start(bf16[1024,128]{1,0:T(8,128)(2,1)} %param.21) | copy-start | bytes 786436
  48.3 24.6 %collective-permute-start.6 = (bf16[8,528,128]{2,1,0:T(8,128)(2,1)S(1)}, bf16[8,528,128]{2,1,0:T(8,128)(2,1)S(1)}, u32[]{:S(2)}, u32[]{:S(2)}) collective-permute-start(bf16[8,528,128]{2,1,0:T(8,128)(2,1)S(1)} %constant_dynamic-update-slice_fusion.refs_1_.refs_3_.refs_7_.refs_8_.refs_12_), channel_id=1, source_target_pairs={{0,2},{2,0},{1,3},{3,1},{4,6},{6,4},{5,7},{7,5},{8,10},{10,8},{9,1... | collective-permute-start | bytes 3244040 | tf_op jit(solution)/shard_map/ppermute | solution.py:828
  49.0 22.9 %collective-permute-start.8 = (bf16[8,512,128]{2,1,0:T(8,128)(2,1)S(1)}, bf16[8,512,128]{2,1,0:T(8,128)(2,1)S(1)}, u32[]{:S(2)}, u32[]{:S(2)}) collective-permute-start(bf16[8,512,128]{2,1,0:T(8,128)(2,1)S(1)} %constant_dynamic-update-slice_fusion.5.refs_5_.refs_9_.refs_10_.refs_14_), channel_id=1, source_target_pairs={{0,4},{4,0},{8,12},{12,8},{16,20},{20,16},{24,28},{28,24},{1,5},{5... | collective-permute-start | bytes 3145736 | tf_op jit(solution)/shard_map/ppermute | solution.py:820
  50.7 25.8 %collective-permute-start.11 = (bf16[256,512]{1,0:T(8,128)(2,1)S(1)}, bf16[256,512]{1,0:T(8,128)(2,1)S(1)}, u32[]{:S(2)}, u32[]{:S(2)}) collective-permute-start(bf16[256,512]{1,0:T(8,128)(2,1)S(1)} %constant_dynamic-update-slice_fusion.10), channel_id=1, source_target_pairs={{0,24},{4,28},{8,16},{12,20},{16,8},{20,12},{24,0},{28,4},{1,25},{... | collective-permute-start | bytes 786440 | tf_op jit(solution)/shard_map/ppermute | solution.py:817
  53.2 23.3 %collective-permute-start.10 = (bf16[256,512]{1,0:T(8,128)(2,1)S(1)}, bf16[256,512]{1,0:T(8,128)(2,1)}, u32[]{:S(2)}, u32[]{:S(2)}) collective-permute-start(bf16[256,512]{1,0:T(8,128)(2,1)S(1)} %constant_dynamic-update-slice_fusion.10), channel_id=1, source_target_pairs={{0,16},{4,20},{8,24},{12,28},{16,0},{20,4},{24,8},{28,12},{1,17},{... | collective-permute-start | bytes 786440 | tf_op jit(solution)/shard_map/ppermute | solution.py:817
  53.2 23.3 %collective-permute-start.9 = (bf16[256,512]{1,0:T(8,128)(2,1)S(1)}, bf16[256,512]{1,0:T(8,128)(2,1)}, u32[]{:S(2)}, u32[]{:S(2)}) collective-permute-start(bf16[256,512]{1,0:T(8,128)(2,1)S(1)} %constant_dynamic-update-slice_fusion.10), channel_id=1, source_target_pairs={{0,8},{4,12},{8,0},{12,4},{16,24},{20,28},{24,16},{28,20},{1,9},{5... | collective-permute-start | bytes 786440 | tf_op jit(solution)/shard_map/ppermute | solution.py:817
  78.8 19.9 %collective-permute-start.12 = (bf16[4,128,512]{2,1,0:T(8,128)(2,1)S(1)}, bf16[4,128,512]{2,1,0:T(8,128)(2,1)S(1)}, u32[]{:S(2)}, u32[]{:S(2)}) collective-permute-start(bf16[4,128,512]{2,1,0:T(8,128)(2,1)S(1)} %pad_maximum_fusion.2), channel_id=1, source_target_pairs={{0,4},{4,0},{8,12},{12,8},{16,20},{20,16},{24,28},{28,24},{1,5},{5... | collective-permute-start | bytes 1572872 | tf_op jit(solution)/shard_map/ppermute | solution.py:820
  80.4 18.3 %collective-permute-start.13 = (bf16[4,128,512]{2,1,0:T(8,128)(2,1)S(1)}, bf16[4,128,512]{2,1,0:T(8,128)(2,1)S(1)}, u32[]{:S(2)}, u32[]{:S(2)}) collective-permute-start(bf16[4,128,512]{2,1,0:T(8,128)(2,1)S(1)} %pad_maximum_fusion.3), channel_id=1, source_target_pairs={{0,2},{2,0},{1,3},{3,1},{4,6},{6,4},{5,7},{7,5},{8,10},{10,8},{9,1... | collective-permute-start | bytes 1572872 | tf_op jit(solution)/shard_map/ppermute | solution.py:828
  98.7 26.1 %copy-start.26 = (bf16[584,1024]{1,0:T(8,128)(2,1)}, bf16[584,1024]{1,0:T(8,128)(2,1)S(1)}, u32[]{:S(2)}) copy-start(bf16[584,1024]{1,0:T(8,128)(2,1)S(1)} %get-tuple-element.224.refs_4_) | copy-start | bytes 3588100
  98.8 21.8 %copy-start.39 = (bf16[8,128,512]{2,1,0:T(8,128)(2,1)}, bf16[8,128,512]{2,1,0:T(8,128)(2,1)S(1)}, u32[]{:S(2)}) copy-start(bf16[8,128,512]{2,1,0:T(8,128)(2,1)S(1)} %constant_dynamic-update-slice_fusion.12) | copy-start | bytes 3145732
  98.9 21.7 %copy-start.38 = (bf16[8,128,512]{2,1,0:T(8,128)(2,1)}, bf16[8,128,512]{2,1,0:T(8,128)(2,1)S(1)}, u32[]{:S(2)}) copy-start(bf16[8,128,512]{2,1,0:T(8,128)(2,1)S(1)} %constant_dynamic-update-slice_fusion.14) | copy-start | bytes 3145732
  99.0 26.4 %collective-permute-start.20 = (bf16[1024,128]{1,0:T(8,128)(2,1)S(1)}, bf16[1024,128]{1,0:T(8,128)(2,1)S(1)}, u32[]{:S(2)}, u32[]{:S(2)}) collective-permute-start(bf16[1024,128]{1,0:T(8,128)(2,1)S(1)} %constant_dynamic-update-slice_fusion.16), channel_id=1, source_target_pairs={{0,24},{4,28},{8,16},{12,20},{16,8},{20,12},{24,0},{28,4},{1,25},{... | collective-permute-start | bytes 786440 | tf_op jit(solution)/shard_map/ppermute | solution.py:817
  101.5 23.9 %collective-permute-start.19 = (bf16[1024,128]{1,0:T(8,128)(2,1)S(1)}, bf16[1024,128]{1,0:T(8,128)(2,1)S(1)}, u32[]{:S(2)}, u32[]{:S(2)}) collective-permute-start(bf16[1024,128]{1,0:T(8,128)(2,1)S(1)} %constant_dynamic-update-slice_fusion.16), channel_id=1, source_target_pairs={{0,16},{4,20},{8,24},{12,28},{16,0},{20,4},{24,8},{28,12},{1,17},{... | collective-permute-start | bytes 786440 | tf_op jit(solution)/shard_map/ppermute | solution.py:817
  101.5 23.9 %collective-permute-start.18 = (bf16[1024,128]{1,0:T(8,128)(2,1)S(1)}, bf16[1024,128]{1,0:T(8,128)(2,1)S(1)}, u32[]{:S(2)}, u32[]{:S(2)}) collective-permute-start(bf16[1024,128]{1,0:T(8,128)(2,1)S(1)} %constant_dynamic-update-slice_fusion.16), channel_id=1, source_target_pairs={{0,8},{4,12},{8,0},{12,4},{16,24},{20,28},{24,16},{28,20},{1,9},{5... | collective-permute-start | bytes 786440 | tf_op jit(solution)/shard_map/ppermute | solution.py:817
  103.4 21.4 %collective-permute-start.17 = (bf16[8,128,512]{2,1,0:T(8,128)(2,1)S(1)}, bf16[8,128,512]{2,1,0:T(8,128)(2,1)S(1)}, u32[]{:S(2)}, u32[]{:S(2)}) collective-permute-start(bf16[8,128,512]{2,1,0:T(8,128)(2,1)S(1)} %constant_dynamic-update-slice_fusion.14), channel_id=1, source_target_pairs={{0,4},{4,0},{8,12},{12,8},{16,20},{20,16},{24,28},{28,24},{1,5},{5... | collective-permute-start | bytes 3145736 | tf_op jit(solution)/shard_map/ppermute | solution.py:820
  103.9 20.9 %collective-permute-start.16 = (bf16[8,128,512]{2,1,0:T(8,128)(2,1)S(1)}, bf16[8,128,512]{2,1,0:T(8,128)(2,1)S(1)}, u32[]{:S(2)}, u32[]{:S(2)}) collective-permute-start(bf16[8,128,512]{2,1,0:T(8,128)(2,1)S(1)} %constant_dynamic-update-slice_fusion.12), channel_id=1, source_target_pairs={{0,2},{2,0},{1,3},{3,1},{4,6},{6,4},{5,7},{7,5},{8,10},{10,8},{9,1... | collective-permute-start | bytes 3145736 | tf_op jit(solution)/shard_map/ppermute | solution.py:828
  124.8 5.1 %collective-permute-start.15 = (bf16[584,1024]{1,0:T(8,128)(2,1)S(1)}, bf16[584,1024]{1,0:T(8,128)(2,1)S(1)}, u32[]{:S(2)}, u32[]{:S(2)}) collective-permute-start(bf16[584,1024]{1,0:T(8,128)(2,1)S(1)} %get-tuple-element.224.refs_4_), channel_id=1, source_target_pairs={{0,1},{1,0},{2,3},{3,2},{4,5},{5,4},{6,7},{7,6},{8,9},{9,8},{10,11... | collective-permute-start | bytes 3588104 | tf_op jit(solution)/shard_map/ppermute | solution.py:832
  124.9 22.0 %collective-permute-start.14 = (bf16[584,1024]{1,0:T(8,128)(2,1)}, bf16[584,1024]{1,0:T(8,128)(2,1)}, u32[]{:S(2)}, u32[]{:S(2)}) collective-permute-start(bf16[584,1024]{1,0:T(8,128)(2,1)} %get-tuple-element.223.refs_4_), channel_id=1, source_target_pairs={{0,1},{1,0},{2,3},{3,2},{4,5},{5,4},{6,7},{7,6},{8,9},{9,8},{10,11... | collective-permute-start | bytes 3588104 | tf_op jit(solution)/shard_map/ppermute | solution.py:832
  126.2 14.9 %collective-permute-start.21 = (bf16[4,512,128]{2,1,0:T(8,128)(2,1)S(1)}, bf16[4,512,128]{2,1,0:T(8,128)(2,1)}, u32[]{:S(2)}, u32[]{:S(2)}) collective-permute-start(bf16[4,512,128]{2,1,0:T(8,128)(2,1)S(1)} %pad_maximum_fusion.4.refs_0_), channel_id=1, source_target_pairs={{0,4},{4,0},{8,12},{12,8},{16,20},{20,16},{24,28},{28,24},{1,5},{5... | collective-permute-start | bytes 1572872 | tf_op jit(solution)/shard_map/ppermute | solution.py:820
  128.4 13.4 %collective-permute-start.22 = (bf16[4,512,128]{2,1,0:T(8,128)(2,1)}, bf16[4,512,128]{2,1,0:T(8,128)(2,1)}, u32[]{:S(2)}, u32[]{:S(2)}) collective-permute-start(bf16[4,512,128]{2,1,0:T(8,128)(2,1)} %pad_maximum_fusion.5.refs_2_), channel_id=1, source_target_pairs={{0,2},{2,0},{1,3},{3,1},{4,6},{6,4},{5,7},{7,5},{8,10},{10,8},{9,1... | collective-permute-start | bytes 1572872 | tf_op jit(solution)/shard_map/ppermute | solution.py:828
  144.8 25.1 %collective-permute-start.23 = (bf16[8,512,128]{2,1,0:T(8,128)(2,1)}, bf16[8,512,128]{2,1,0:T(8,128)(2,1)}, u32[]{:S(2)}, u32[]{:S(2)}) collective-permute-start(bf16[8,512,128]{2,1,0:T(8,128)(2,1)} %get-tuple-element.251.refs_3_), channel_id=1, source_target_pairs={{0,2},{2,0},{1,3},{3,1},{4,6},{6,4},{5,7},{7,5},{8,10},{10,8},{9,1... | collective-permute-start | bytes 3145736 | tf_op jit(solution)/shard_map/ppermute | solution.py:828
  146.3 24.2 %collective-permute-start.24 = (bf16[8,512,128]{2,1,0:T(8,128)(2,1)}, bf16[8,512,128]{2,1,0:T(8,128)(2,1)}, u32[]{:S(2)}, u32[]{:S(2)}) collective-permute-start(bf16[8,512,128]{2,1,0:T(8,128)(2,1)} %get-tuple-element.252.refs_5_), channel_id=1, source_target_pairs={{0,4},{4,0},{8,12},{12,8},{16,20},{20,16},{24,28},{28,24},{1,5},{5... | collective-permute-start | bytes 3145736 | tf_op jit(solution)/shard_map/ppermute | solution.py:820
  167.7 24.6 %collective-permute-start.27 = (bf16[8,512,128]{2,1,0:T(8,128)(2,1)}, bf16[8,512,128]{2,1,0:T(8,128)(2,1)}, u32[]{:S(2)}, u32[]{:S(2)}) collective-permute-start(bf16[8,512,128]{2,1,0:T(8,128)(2,1)} %get-tuple-element.236), channel_id=1, source_target_pairs={{0,4},{4,0},{8,12},{12,8},{16,20},{20,16},{24,28},{28,24},{1,5},{5... | collective-permute-start | bytes 3145736 | tf_op jit(solution)/shard_map/ppermute | solution.py:820
  169.3 23.0 %collective-permute-start.26 = (bf16[8,512,128]{2,1,0:T(8,128)(2,1)}, bf16[8,512,128]{2,1,0:T(8,128)(2,1)}, u32[]{:S(2)}, u32[]{:S(2)}) collective-permute-start(bf16[8,512,128]{2,1,0:T(8,128)(2,1)} %get-tuple-element.262), channel_id=1, source_target_pairs={{0,2},{2,0},{1,3},{3,1},{4,6},{6,4},{5,7},{7,5},{8,10},{10,8},{9,1... | collective-permute-start | bytes 3145736 | tf_op jit(solution)/shard_map/ppermute | solution.py:828
  192.2 16.7 %collective-permute-start.25 = (bf16[2,584,1024]{2,1,0:T(8,128)(2,1)}, bf16[2,584,1024]{2,1,0:T(8,128)(2,1)S(1)}, u32[]{:S(2)}, u32[]{:S(2)}) collective-permute-start(bf16[2,584,1024]{2,1,0:T(8,128)(2,1)} %get-tuple-element.259.refs_5_), channel_id=1, source_target_pairs={{0,1},{1,0},{2,3},{3,2},{4,5},{5,4},{6,7},{7,6},{8,9},{9,8},{10,11... | collective-permute-start | bytes 7176200 | tf_op jit(solution)/shard_map/ppermute | solution.py:832
  197.3 21.5 %collective-permute-start.28 = (bf16[4,512,128]{2,1,0:T(8,128)(2,1)S(1)}, bf16[4,512,128]{2,1,0:T(8,128)(2,1)S(1)}, u32[]{:S(2)}, u32[]{:S(2)}) collective-permute-start(bf16[4,512,128]{2,1,0:T(8,128)(2,1)S(1)} %get-tuple-element.270), channel_id=1, source_target_pairs={{0,4},{4,0},{8,12},{12,8},{16,20},{20,16},{24,28},{28,24},{1,5},{5... | collective-permute-start | bytes 1572872 | tf_op jit(solution)/shard_map/ppermute | solution.py:820
  198.3 20.6 %collective-permute-start.29 = (bf16[4,512,128]{2,1,0:T(8,128)(2,1)S(1)}, bf16[4,512,128]{2,1,0:T(8,128)(2,1)S(1)}, u32[]{:S(2)}, u32[]{:S(2)}) collective-permute-start(bf16[4,512,128]{2,1,0:T(8,128)(2,1)S(1)} %get-tuple-element.272), channel_id=1, source_target_pairs={{0,2},{2,0},{1,3},{3,1},{4,6},{6,4},{5,7},{7,5},{8,10},{10,8},{9,1... | collective-permute-start | bytes 1572872 | tf_op jit(solution)/shard_map/ppermute | solution.py:828
  198.9 10.1 %copy-start.7 = (bf16[8,512,128]{2,1,0:T(8,128)(2,1)S(1)}, bf16[8,512,128]{2,1,0:T(8,128)(2,1)}, u32[]{:S(2)}) copy-start(bf16[8,512,128]{2,1,0:T(8,128)(2,1)} %copy-done.5) | copy-start | bytes 3145732
  198.9 10.1 %copy-start.10 = (bf16[2,584,1024]{2,1,0:T(8,128)(2,1)S(1)}, bf16[2,584,1024]{2,1,0:T(8,128)(2,1)}, u32[]{:S(2)}) copy-start(bf16[2,584,1024]{2,1,0:T(8,128)(2,1)} %get-tuple-element.258.refs_4_) | copy-start | bytes 7176196
  198.9 10.1 %copy-start.15 = (bf16[2,584,1024]{2,1,0:T(8,128)(2,1)S(1)}, bf16[2,584,1024]{2,1,0:T(8,128)(2,1)}, u32[]{:S(2)}) copy-start(bf16[2,584,1024]{2,1,0:T(8,128)(2,1)} %get-tuple-element.259.refs_5_) | copy-start | bytes 7176196
  198.9 10.1 %copy-start.23 = (f32[6,1024]{1,0:T(8,128)S(1)}, f32[6,1024]{1,0:T(8,128)}, u32[]{:S(2)}) copy-start(f32[6,1024]{1,0:T(8,128)} %get-tuple-element.200.refs_0_.refs_1_.refs_2_) | copy-start | bytes 73732
  198.9 10.1 %copy-start.24 = (s32[10]{0:T(128)S(1)}, s32[10]{0:T(128)}, u32[]{:S(2)}) copy-start(s32[10]{0:T(128)} %stack.130.refs_0_) | copy-start | bytes 124
  198.9 10.1 %copy-start.25 = (f32[2]{0:T(128)S(1)}, f32[2]{0:T(128)}, u32[]{:S(2)}) copy-start(f32[2]{0:T(128)} %dynamic-slice_convert_fusion.refs_1_.refs_0_) | copy-start | bytes 28
  206.3 29.2 %collective-permute-start.30 = (bf16[8,512,128]{2,1,0:T(8,128)(2,1)S(1)}, bf16[8,512,128]{2,1,0:T(8,128)(2,1)S(1)}, u32[]{:S(2)}, u32[]{:S(2)}) collective-permute-start(bf16[8,512,128]{2,1,0:T(8,128)(2,1)S(1)} %get-tuple-element.294), channel_id=1, source_target_pairs={{0,2},{2,0},{1,3},{3,1},{4,6},{6,4},{5,7},{7,5},{8,10},{10,8},{9,1... | collective-permute-start | bytes 3145736 | tf_op jit(solution)/shard_map/ppermute | solution.py:828
  207.8 27.6 %collective-permute-start.31 = (bf16[8,512,128]{2,1,0:T(8,128)(2,1)S(1)}, bf16[8,512,128]{2,1,0:T(8,128)(2,1)S(1)}, u32[]{:S(2)}, u32[]{:S(2)}) collective-permute-start(bf16[8,512,128]{2,1,0:T(8,128)(2,1)S(1)} %get-tuple-element.275), channel_id=1, source_target_pairs={{0,4},{4,0},{8,12},{12,8},{16,20},{20,16},{24,28},{28,24},{1,5},{5... | collective-permute-start | bytes 3145736 | tf_op jit(solution)/shard_map/ppermute | solution.py:820
  219.8 34.0 %collective-permute-start.34 = (bf16[1024,128]{1,0:T(8,128)(2,1)S(1)}, bf16[1024,128]{1,0:T(8,128)(2,1)S(1)}, u32[]{:S(2)}, u32[]{:S(2)}) collective-permute-start(bf16[1024,128]{1,0:T(8,128)(2,1)S(1)} %get-tuple-element.285), channel_id=1, source_target_pairs={{0,8},{4,12},{8,0},{12,4},{16,24},{20,28},{24,16},{28,20},{1,9},{5... | collective-permute-start | bytes 786440 | tf_op jit(solution)/shard_map/ppermute | solution.py:817
  220.0 39.0 %collective-permute-start.35 = (bf16[1024,128]{1,0:T(8,128)(2,1)S(1)}, bf16[1024,128]{1,0:T(8,128)(2,1)S(1)}, u32[]{:S(2)}, u32[]{:S(2)}) collective-permute-start(bf16[1024,128]{1,0:T(8,128)(2,1)S(1)} %get-tuple-element.286), channel_id=1, source_target_pairs={{0,16},{4,20},{8,24},{12,28},{16,0},{20,4},{24,8},{28,12},{1,17},{... | collective-permute-start | bytes 786440 | tf_op jit(solution)/shard_map/ppermute | solution.py:817
  222.9 37.7 %collective-permute-start.36 = (bf16[1024,128]{1,0:T(8,128)(2,1)S(1)}, bf16[1024,128]{1,0:T(8,128)(2,1)S(1)}, u32[]{:S(2)}, u32[]{:S(2)}) collective-permute-start(bf16[1024,128]{1,0:T(8,128)(2,1)S(1)} %get-tuple-element.287), channel_id=1, source_target_pairs={{0,24},{4,28},{8,16},{12,20},{16,8},{20,12},{24,0},{28,4},{1,25},{... | collective-permute-start | bytes 786440 | tf_op jit(solution)/shard_map/ppermute | solution.py:817
  236.8 26.3 %collective-permute-start.32 = (bf16[4,512,128]{2,1,0:T(8,128)(2,1)S(1)}, bf16[4,512,128]{2,1,0:T(8,128)(2,1)S(1)}, u32[]{:S(2)}, u32[]{:S(2)}) collective-permute-start(bf16[4,512,128]{2,1,0:T(8,128)(2,1)S(1)} %get-tuple-element.302), channel_id=1, source_target_pairs={{0,4},{4,0},{8,12},{12,8},{16,20},{20,16},{24,28},{28,24},{1,5},{5... | collective-permute-start | bytes 1572872 | tf_op jit(solution)/shard_map/ppermute | solution.py:820
  237.8 25.3 %collective-permute-start.33 = (bf16[4,512,128]{2,1,0:T(8,128)(2,1)S(1)}, bf16[4,512,128]{2,1,0:T(8,128)(2,1)S(1)}, u32[]{:S(2)}, u32[]{:S(2)}) collective-permute-start(bf16[4,512,128]{2,1,0:T(8,128)(2,1)S(1)} %get-tuple-element.304), channel_id=1, source_target_pairs={{0,2},{2,0},{1,3},{3,1},{4,6},{6,4},{5,7},{7,5},{8,10},{10,8},{9,1... | collective-permute-start | bytes 1572872 | tf_op jit(solution)/shard_map/ppermute | solution.py:828
  238.4 15.5 %copy-start.11 = (bf16[1168,1024]{1,0:T(8,128)(2,1)S(1)}, bf16[1168,1024]{1,0:T(8,128)(2,1)}, u32[]{:S(2)}) copy-start(bf16[1168,1024]{1,0:T(8,128)(2,1)} %get-tuple-element.253) | copy-start | bytes 7176196
  238.4 15.6 %copy-start.9 = (bf16[2,584,1024]{2,1,0:T(8,128)(2,1)S(1)}, bf16[2,584,1024]{2,1,0:T(8,128)(2,1)}, u32[]{:S(2)}) copy-start(bf16[2,584,1024]{2,1,0:T(8,128)(2,1)} %copy-done.8) | copy-start | bytes 7176196
  253.9 18.2 %collective-permute-start.37 = (bf16[2,584,1024]{2,1,0:T(8,128)(2,1)S(1)}, bf16[2,584,1024]{2,1,0:T(8,128)(2,1)S(1)}, u32[]{:S(2)}, u32[]{:S(2)}) collective-permute-start(bf16[2,584,1024]{2,1,0:T(8,128)(2,1)S(1)} %bitcast.97), channel_id=1, source_target_pairs={{0,1},{1,0},{2,3},{3,2},{4,5},{5,4},{6,7},{7,6},{8,9},{9,8},{10,11... | collective-permute-start | bytes 7176200 | tf_op jit(solution)/shard_map/ppermute | solution.py:832
  259.0 27.5 %collective-permute-start.38 = (bf16[8,512,128]{2,1,0:T(8,128)(2,1)S(1)}, bf16[8,512,128]{2,1,0:T(8,128)(2,1)S(1)}, u32[]{:S(2)}, u32[]{:S(2)}) collective-permute-start(bf16[8,512,128]{2,1,0:T(8,128)(2,1)S(1)} %get-tuple-element.309), channel_id=1, source_target_pairs={{0,2},{2,0},{1,3},{3,1},{4,6},{6,4},{5,7},{7,5},{8,10},{10,8},{9,1... | collective-permute-start | bytes 3145736 | tf_op jit(solution)/shard_map/ppermute | solution.py:828
  260.6 25.9 %collective-permute-start.39 = (bf16[8,512,128]{2,1,0:T(8,128)(2,1)S(1)}, bf16[8,512,128]{2,1,0:T(8,128)(2,1)S(1)}, u32[]{:S(2)}, u32[]{:S(2)}) collective-permute-start(bf16[8,512,128]{2,1,0:T(8,128)(2,1)S(1)} %get-tuple-element.310), channel_id=1, source_target_pairs={{0,4},{4,0},{8,12},{12,8},{16,20},{20,16},{24,28},{28,24},{1,5},{5... | collective-permute-start | bytes 3145736 | tf_op jit(solution)/shard_map/ppermute | solution.py:820
  264.0 18.7 %collective-permute-start.40 = (bf16[2,1024,128]{2,1,0:T(8,128)(2,1)S(1)}, bf16[2,1024,128]{2,1,0:T(8,128)(2,1)S(1)}, u32[]{:S(2)}, u32[]{:S(2)}) collective-permute-start(bf16[2,1024,128]{2,1,0:T(8,128)(2,1)S(1)} %get-tuple-element.320), channel_id=1, source_target_pairs={{0,8},{4,12},{8,0},{12,4},{16,24},{20,28},{24,16},{28,20},{1,9},{5... | collective-permute-start | bytes 1572872 | tf_op jit(solution)/shard_map/ppermute | solution.py:817
  282.6 6.7 %collective-permute-start.44 = (bf16[2,584,1024]{2,1,0:T(8,128)(2,1)S(1)}, bf16[2,584,1024]{2,1,0:T(8,128)(2,1)S(1)}, u32[]{:S(2)}, u32[]{:S(2)}) collective-permute-start(bf16[2,584,1024]{2,1,0:T(8,128)(2,1)S(1)} %grad_one.1.refs_9_), channel_id=1, source_target_pairs={{0,1},{1,0},{2,3},{3,2},{4,5},{5,4},{6,7},{7,6},{8,9},{9,8},{10,11... | collective-permute-start | bytes 7176200 | tf_op jit(solution)/shard_map/ppermute | solution.py:832
  283.4 15.6 %collective-permute-start.43 = (bf16[1,1024,128]{2,1,0:T(8,128)(2,1)S(1)}, bf16[1,1024,128]{2,1,0:T(8,128)(2,1)S(1)}, u32[]{:S(2)}, u32[]{:S(2)}) collective-permute-start(bf16[1,1024,128]{2,1,0:T(8,128)(2,1)S(1)} %get-tuple-element.335), channel_id=1, source_target_pairs={{0,16},{4,20},{8,24},{12,28},{16,0},{20,4},{24,8},{28,12},{1,17},{... | collective-permute-start | bytes 786440 | tf_op jit(solution)/shard_map/ppermute | solution.py:817
  287.9 16.1 %collective-permute-start.41 = (bf16[4,512,128]{2,1,0:T(8,128)(2,1)S(1)}, bf16[4,512,128]{2,1,0:T(8,128)(2,1)S(1)}, u32[]{:S(2)}, u32[]{:S(2)}) collective-permute-start(bf16[4,512,128]{2,1,0:T(8,128)(2,1)S(1)} %get-tuple-element.341), channel_id=1, source_target_pairs={{0,4},{4,0},{8,12},{12,8},{16,20},{20,16},{24,28},{28,24},{1,5},{5... | collective-permute-start | bytes 1572872 | tf_op jit(solution)/shard_map/ppermute | solution.py:820
  288.9 15.1 %collective-permute-start.42 = (bf16[4,512,128]{2,1,0:T(8,128)(2,1)S(1)}, bf16[4,512,128]{2,1,0:T(8,128)(2,1)S(1)}, u32[]{:S(2)}, u32[]{:S(2)}) collective-permute-start(bf16[4,512,128]{2,1,0:T(8,128)(2,1)S(1)} %get-tuple-element.343), channel_id=1, source_target_pairs={{0,2},{2,0},{1,3},{3,1},{4,6},{6,4},{5,7},{7,5},{8,10},{10,8},{9,1... | collective-permute-start | bytes 1572872 | tf_op jit(solution)/shard_map/ppermute | solution.py:828
  300.4 4.0 %collective-permute-start.45 = (f32[4,16,128]{2,1,0:T(8,128)S(1)}, f32[4,16,128]{2,1,0:T(8,128)S(1)}, u32[]{:S(2)}, u32[]{:S(2)}) collective-permute-start(f32[4,16,128]{2,1,0:T(8,128)S(1)} %get-tuple-element.357), channel_id=1, source_target_pairs={{0,4},{2,6},{4,0},{6,2},{8,12},{10,14},{12,8},{14,10},{16,20},{18,... | collective-permute-start | bytes 98312 | tf_op jit(solution)/shard_map/ppermute | solution.py:825
  301.4 4.0 %collective-permute-start.46 = (f32[4,16,128]{2,1,0:T(8,128)S(1)}, f32[4,16,128]{2,1,0:T(8,128)S(1)}, u32[]{:S(2)}, u32[]{:S(2)}) collective-permute-start(f32[4,16,128]{2,1,0:T(8,128)S(1)} %get-tuple-element.358), channel_id=1, source_target_pairs={{0,2},{2,0},{4,6},{6,4},{8,10},{10,8},{12,14},{14,12},{16,18},{18,... | collective-permute-start | bytes 98312 | tf_op jit(solution)/shard_map/ppermute | solution.py:825
  301.9 4.8 %collective-permute-start.47 = (f32[4,16,128]{2,1,0:T(8,128)S(1)}, f32[4,16,128]{2,1,0:T(8,128)S(1)}, u32[]{:S(2)}, u32[]{:S(2)}) collective-permute-start(f32[4,16,128]{2,1,0:T(8,128)S(1)} %get-tuple-element.359), channel_id=1, source_target_pairs={{0,6},{2,4},{4,2},{6,0},{8,14},{10,12},{12,10},{14,8},{16,22},{18,... | collective-permute-start | bytes 98312 | tf_op jit(solution)/shard_map/ppermute | solution.py:825
  309.1 11.7 %collective-permute-start.48 = (bf16[1040,128]{1,0:T(8,128)(2,1)}, bf16[1040,128]{1,0:T(8,128)(2,1)S(1)}, u32[]{:S(2)}, u32[]{:S(2)}) collective-permute-start(bf16[1040,128]{1,0:T(8,128)(2,1)} %get-tuple-element.361), channel_id=1, source_target_pairs={{0,8},{4,12},{8,0},{12,4},{16,24},{20,28},{24,16},{28,20},{1,9},{5... | collective-permute-start | bytes 798728 | tf_op jit(solution)/shard_map/ppermute | solution.py:817
  309.1 21.6 %collective-permute-start.49 = (bf16[1040,128]{1,0:T(8,128)(2,1)}, bf16[1040,128]{1,0:T(8,128)(2,1)S(1)}, u32[]{:S(2)}, u32[]{:S(2)}) collective-permute-start(bf16[1040,128]{1,0:T(8,128)(2,1)} %get-tuple-element.362), channel_id=1, source_target_pairs={{0,16},{4,20},{8,24},{12,28},{16,0},{20,4},{24,8},{28,12},{1,17},{... | collective-permute-start | bytes 798728 | tf_op jit(solution)/shard_map/ppermute | solution.py:817
  311.7 18.9 %collective-permute-start.50 = (bf16[1040,128]{1,0:T(8,128)(2,1)S(1)}, bf16[1040,128]{1,0:T(8,128)(2,1)S(1)}, u32[]{:S(2)}, u32[]{:S(2)}) collective-permute-start(bf16[1040,128]{1,0:T(8,128)(2,1)S(1)} %get-tuple-element.363), channel_id=1, source_target_pairs={{0,24},{4,28},{8,16},{12,20},{16,8},{20,12},{24,0},{28,4},{1,25},{... | collective-permute-start | bytes 798728 | tf_op jit(solution)/shard_map/ppermute | solution.py:817
  (36 other events, 100.2 us)
